TPU v7x, 32 devices: a whole 2x2x4 slice. The times are simulated.
32 devices in a mesh: fsdp: 8 (over y, x, core), tensor: 4 (over z).
Axes of the slice: x: 2, y: 2, z: 4, core: 2. Of those that a mesh axis runs over, the one named last changes fastest.
Arguments:
- latents: bfloat16 [16, 1024, 1152], P('fsdp', 'tensor'), may hold values from -6 to 6
- conditioning: bfloat16 [16, 1152], P('fsdp'), may hold values from -6 to 6
- mod_weight: bfloat16 [1152, 6, 1152], P('fsdp', None, 'tensor'), may hold values from -0.1875 to 0.1875
- mod_bias: bfloat16 [6, 1152], P(None, 'tensor'), may hold values from -3 to 3
- in_weight: bfloat16 [3, 1152, 1152], P(None, 'fsdp', 'tensor'), may hold values from -0.1875 to 0.1875
- query_value_bias: bfloat16 [2, 1152], P(None, 'tensor'), may hold values from -3 to 3
- out_weight: bfloat16 [1152, 1152], P('tensor', 'fsdp'), may hold values from -1.5 to 1.5
- branch_bias: bfloat16 [2, 1152], replicated, may hold values from -3 to 3
- up_weight: bfloat16 [1152, 4608], P('fsdp', 'tensor'), may hold values from -0.1875 to 0.1875
- up_bias: bfloat16 [4608], P('tensor'), may hold values from -3 to 3
- down_weight: bfloat16 [4608, 1152], P('tensor', 'fsdp'), may hold values from -0.1875 to 0.1875
- cotangent: bfloat16 [16, 1024, 1152], P('fsdp', 'tensor'), may hold values from -6 to 6
Outputs:
- block_out: bfloat16 [16, 1024, 1152], P('fsdp', 'tensor')
- latent_grad: bfloat16 [16, 1024, 1152], P('fsdp', 'tensor')
- cond_grad: float32 [16, 1152], P('fsdp')
- mod_weight_grad: float32 [1152, 6, 1152], P('fsdp', None, 'tensor')
- mod_bias_grad: float32 [6, 1152], P(None, 'tensor')
- in_weight_grad: float32 [3, 1152, 1152], P(None, 'fsdp', 'tensor')
- query_value_bias_grad: float32 [2, 1152], P(None, 'tensor')
- out_weight_grad: float32 [1152, 1152], P('tensor', 'fsdp')
- branch_bias_grad: float32 [2, 1152], replicated
- up_weight_grad: float32 [1152, 4608], P('fsdp', 'tensor')
- up_bias_grad: float32 [4608], P('tensor')
- down_weight_grad: float32 [4608, 1152], P('tensor', 'fsdp')
All inputs are finite; a program needn't handle non-finite values.
Results may differ from a plain program's by a relative error of at most 0.02.
Values may be sent and summed in bfloat16 or wider, within the bound.
No kernel may reach another device: no remote copies, remote signals or barrier semaphores. Data moves between devices by JAX's collectives and lax.ppermute only.
A program may use at most 256 MiB of HBM per device.

v0:
```python
import jax
import jax.numpy as jnp
from jax import lax
from jax.sharding import PartitionSpec as P

HEAD_DIM = 72


eps_norm = 1e-06
tanh_coeff = 0.7978845608028654
cubic_coeff = 0.044715


def gelu_tanh(inputs):
    inner = tanh_coeff * (inputs + cubic_coeff * inputs * inputs * inputs)
    return 0.5 * inputs * (1.0 + jnp.tanh(inner))


def normalize(values):
    centre = values - jnp.mean(values, axis=-1, keepdims=True)
    spread = jnp.mean(centre * centre, axis=-1, keepdims=True)
    return centre * lax.rsqrt(spread + eps_norm)


def fetch(shards):
    return (
        lax.all_gather(shards[0], "fsdp", axis=1, tiled=True),
        lax.all_gather(shards[1], "fsdp", axis=1, tiled=True),
        lax.all_gather(shards[2], "fsdp", axis=0, tiled=True),
        lax.all_gather(shards[3], "fsdp", axis=1, tiled=True),
        lax.all_gather(shards[4], "fsdp", axis=0, tiled=True),
    )


def body(
    latents,
    conditioning,
    mod_weight,
    mod_bias,
    in_weight,
    query_value_bias,
    out_weight,
    branch_bias,
    up_weight,
    up_bias,
    down_weight,
    cotangent,
):
    images, row_count, width = latents.shape
    local_cols = in_weight.shape[2]
    local_units = up_weight.shape[1]
    heads_here = local_cols // HEAD_DIM
    tensor_count = lax.axis_size("tensor")
    seq_len = row_count * tensor_count
    score_scale = HEAD_DIM ** (-0.5)
    highest = lax.Precision.HIGHEST
    ada_bias = mod_bias.astype(jnp.float32)
    triple_bias = jnp.stack(
        [query_value_bias[0], jnp.zeros_like(query_value_bias[0]), query_value_bias[1]]
    ).astype(jnp.float32)
    attn_bias = branch_bias[0].astype(jnp.float32)
    ffn_bias = branch_bias[1].astype(jnp.float32)
    unit_bias = up_bias.astype(jnp.float32)
    local_shards = (in_weight, out_weight, up_weight, down_weight, mod_weight)

    def one_image(carry, item):
        latent_rows, cond_row, grad_rows_low = item
        forward_set = fetch(local_shards)
        triple_w, proj_w, up_w, down_w, ada_w = forward_set
        latent_f = latent_rows.astype(jnp.float32)
        grad_rows = grad_rows_low.astype(jnp.float32)
        silu_out, silu_back = jax.vjp(jax.nn.silu, cond_row.astype(jnp.float32))
        silu_low = silu_out.astype(jnp.bfloat16)
        mod_part = (
            jnp.einsum("d,dcj->cj", silu_low, ada_w, preferred_element_type=jnp.float32) + ada_bias
        )
        modulation = lax.all_gather(mod_part, "tensor", axis=1, tiled=True)
        shift_first, scale_first, gate_first = (modulation[0], modulation[1], modulation[2])
        shift_second, scale_second, gate_second = (modulation[3], modulation[4], modulation[5])
        norm_first, norm_back_first = jax.vjp(normalize, latent_f)
        h_first = (norm_first * (1.0 + scale_first) + shift_first).astype(jnp.bfloat16)
        first_all = lax.all_gather(h_first, "tensor", axis=0, tiled=True)
        triple = (
            jnp.einsum("sd,cde->sce", first_all, triple_w, preferred_element_type=jnp.float32)
            + triple_bias
        )
        triple_low = triple.astype(jnp.bfloat16)
        queries = triple_low[:, 0].reshape(seq_len, heads_here, HEAD_DIM)
        key_rows = triple_low[:, 1].reshape(seq_len, heads_here, HEAD_DIM)
        value_rows = triple_low[:, 2].reshape(seq_len, heads_here, HEAD_DIM)
        scores = (
            jnp.einsum("qhe,khe->hqk", queries, key_rows, preferred_element_type=jnp.float32)
            * score_scale
        )
        top_score = jnp.max(scores, axis=-1, keepdims=True)
        log_total = top_score + jnp.log(
            jnp.sum(jnp.exp(scores - top_score), axis=-1, keepdims=True)
        )
        probs_low = jnp.exp(scores - log_total).astype(jnp.bfloat16)
        mixed = jnp.einsum(
            "hqk,khe->qhe", probs_low, value_rows, preferred_element_type=jnp.float32
        )
        mixed_low = mixed.reshape(seq_len, local_cols).astype(jnp.bfloat16)
        piece = mixed_low
        attn_branch = (
            lax.psum_scatter(
                jnp.dot(piece, proj_w, preferred_element_type=jnp.float32).astype(jnp.bfloat16),
                "tensor",
                scatter_dimension=0,
                tiled=True,
            ).astype(jnp.float32)
            + attn_bias
        )
        resid = latent_f + gate_first * attn_branch
        norm_second, norm_back_second = jax.vjp(normalize, resid)
        h_second = (norm_second * (1.0 + scale_second) + shift_second).astype(jnp.bfloat16)
        second_all = lax.all_gather(h_second, "tensor", axis=0, tiled=True)
        pre_act = jnp.dot(second_all, up_w, preferred_element_type=jnp.float32) + unit_bias
        act_value, gelu_back = jax.vjp(gelu_tanh, pre_act)
        hidden_low = act_value.astype(jnp.bfloat16)
        piece = hidden_low
        ffn_branch = (
            lax.psum_scatter(
                jnp.dot(piece, down_w, preferred_element_type=jnp.float32).astype(jnp.bfloat16),
                "tensor",
                scatter_dimension=0,
                tiled=True,
            ).astype(jnp.float32)
            + ffn_bias
        )
        block_rows = (resid + gate_second * ffn_branch).astype(jnp.bfloat16)
        tied = lax.optimization_barrier((local_shards, block_rows))
        back_set = fetch(tied[0])
        block_rows = tied[1]
        triple_w, proj_w, up_w, down_w, ada_w = back_set
        ffn_grad = (grad_rows * gate_second).astype(jnp.bfloat16)
        ffn_all = lax.all_gather(ffn_grad, "tensor", axis=0, tiled=True)
        hidden_grad = jnp.einsum("sd,fd->sf", ffn_all, down_w, preferred_element_type=jnp.float32)
        down_step = jnp.einsum("sf,sd->fd", hidden_low, ffn_all, preferred_element_type=jnp.float32)
        pre_grad = gelu_back(hidden_grad)[0].astype(jnp.bfloat16)
        up_step = jnp.einsum("sd,sf->df", second_all, pre_grad, preferred_element_type=jnp.float32)
        unit_step = jnp.sum(pre_grad.astype(jnp.float32), axis=0)
        piece = pre_grad
        second_grad = lax.psum_scatter(
            jnp.einsum("sf,df->sd", piece, up_w, preferred_element_type=jnp.float32).astype(
                jnp.bfloat16
            ),
            "tensor",
            scatter_dimension=0,
            tiled=True,
        ).astype(jnp.float32)
        resid_grad = grad_rows + norm_back_second(second_grad * (1.0 + scale_second))[0]
        attn_grad = (resid_grad * gate_first).astype(jnp.bfloat16)
        attn_all = lax.all_gather(attn_grad, "tensor", axis=0, tiled=True)
        proj_step = jnp.einsum("se,sd->ed", mixed_low, attn_all, preferred_element_type=jnp.float32)
        mixed_grad = jnp.einsum("sd,ed->se", attn_all, proj_w, preferred_element_type=jnp.float32)
        mixed_grad = mixed_grad.astype(jnp.bfloat16).reshape(seq_len, heads_here, HEAD_DIM)
        scores_again = (
            jnp.einsum("qhe,khe->hqk", queries, key_rows, preferred_element_type=jnp.float32)
            * score_scale
        )
        probs = jnp.exp(scores_again - log_total)
        probs_again = probs.astype(jnp.bfloat16)
        value_grad = jnp.einsum(
            "hqk,qhe->khe", probs_again, mixed_grad, preferred_element_type=jnp.float32
        )
        probs_grad = jnp.einsum(
            "qhe,khe->hqk", mixed_grad, value_rows, preferred_element_type=jnp.float32
        )
        score_grad = (
            probs * (probs_grad - jnp.sum(probs_grad * probs, axis=-1, keepdims=True))
        ).astype(jnp.bfloat16)
        query_grad = (
            jnp.einsum("hqk,khe->qhe", score_grad, key_rows, preferred_element_type=jnp.float32)
            * score_scale
        )
        key_grad = (
            jnp.einsum("hqk,qhe->khe", score_grad, queries, preferred_element_type=jnp.float32)
            * score_scale
        )
        triple_grad = (
            jnp.stack([query_grad, key_grad, value_grad], axis=1)
            .reshape(seq_len, 3, local_cols)
            .astype(jnp.bfloat16)
        )
        triple_step = jnp.einsum(
            "sd,sce->cde", first_all, triple_grad, preferred_element_type=jnp.float32
        )
        triple_sums = jnp.sum(triple_grad.astype(jnp.float32), axis=0)
        pair_step = jnp.stack([triple_sums[0], triple_sums[2]])
        piece = triple_grad
        first_grad = lax.psum_scatter(
            jnp.einsum("sce,cde->sd", piece, triple_w, preferred_element_type=jnp.float32).astype(
                jnp.bfloat16
            ),
            "tensor",
            scatter_dimension=0,
            tiled=True,
        ).astype(jnp.float32)
        latent_grad_rows = (
            resid_grad + norm_back_first(first_grad * (1.0 + scale_first))[0]
        ).astype(jnp.bfloat16)
        mod_grad_rows = jnp.stack(
            [
                jnp.sum(first_grad, axis=0),
                jnp.sum(first_grad * norm_first, axis=0),
                jnp.sum(resid_grad * attn_branch, axis=0),
                jnp.sum(second_grad, axis=0),
                jnp.sum(second_grad * norm_second, axis=0),
                jnp.sum(grad_rows * ffn_branch, axis=0),
            ]
        )
        mod_grad_own = lax.psum_scatter(mod_grad_rows, "tensor", scatter_dimension=1, tiled=True)
        ada_step = jnp.einsum(
            "d,cj->dcj", silu_low.astype(jnp.float32), mod_grad_own, precision=highest
        )
        silu_grad = jnp.einsum(
            "cj,dcj->d", mod_grad_own, ada_w.astype(jnp.float32), precision=highest
        )
        cond_part = silu_back(silu_grad)[0]
        branch_step = jnp.stack(
            [
                jnp.sum(attn_grad.astype(jnp.float32), axis=0),
                jnp.sum(ffn_grad.astype(jnp.float32), axis=0),
            ]
        )
        steps_now = (
            triple_step,
            proj_step,
            up_step,
            down_step,
            ada_step,
            pair_step,
            unit_step,
            branch_step,
            mod_grad_own,
        )
        new_carry = jax.tree.map(jnp.add, carry, steps_now)
        return (new_carry, (block_rows, latent_grad_rows, cond_part))

    zero_carry = (
        jnp.zeros((3, width, local_cols), jnp.float32),
        jnp.zeros((local_cols, width), jnp.float32),
        jnp.zeros((width, local_units), jnp.float32),
        jnp.zeros((local_units, width), jnp.float32),
        jnp.zeros((width, 6, local_cols), jnp.float32),
        jnp.zeros((2, local_cols), jnp.float32),
        jnp.zeros((local_units,), jnp.float32),
        jnp.zeros((2, width), jnp.float32),
        jnp.zeros((6, local_cols), jnp.float32),
    )
    totals, outputs = lax.scan(one_image, zero_carry, (latents, conditioning, cotangent))
    block_out, latent_grad, cond_parts = outputs
    cond_grad, branch_part = lax.psum((cond_parts, totals[7]), "tensor")
    pair_grad, unit_grad, ada_bias_grad, branch_total = lax.psum(
        (totals[5], totals[6], totals[8], branch_part), "fsdp"
    )
    triple_grad_own, proj_grad_own, up_grad_own, down_grad_own, ada_grad_own = (
        lax.psum_scatter(
            totals[0].astype(jnp.bfloat16), "fsdp", scatter_dimension=1, tiled=True
        ).astype(jnp.float32),
        lax.psum_scatter(
            totals[1].astype(jnp.bfloat16), "fsdp", scatter_dimension=1, tiled=True
        ).astype(jnp.float32),
        lax.psum_scatter(
            totals[2].astype(jnp.bfloat16), "fsdp", scatter_dimension=0, tiled=True
        ).astype(jnp.float32),
        lax.psum_scatter(
            totals[3].astype(jnp.bfloat16), "fsdp", scatter_dimension=1, tiled=True
        ).astype(jnp.float32),
        lax.psum_scatter(
            totals[4].astype(jnp.bfloat16), "fsdp", scatter_dimension=0, tiled=True
        ).astype(jnp.float32),
    )
    return (
        block_out,
        latent_grad,
        cond_grad,
        ada_grad_own,
        ada_bias_grad,
        triple_grad_own,
        pair_grad,
        proj_grad_own,
        branch_total,
        up_grad_own,
        unit_grad,
        down_grad_own,
    )


def solution(mesh):
    in_specs = (
        P("fsdp", "tensor", None),
        P("fsdp", None),
        P("fsdp", None, "tensor"),
        P(None, "tensor"),
        P(None, "fsdp", "tensor"),
        P(None, "tensor"),
        P("tensor", "fsdp"),
        P(),
        P("fsdp", "tensor"),
        P("tensor"),
        P("tensor", "fsdp"),
        P("fsdp", "tensor", None),
    )
    out_specs = (
        P("fsdp", "tensor", None),
        P("fsdp", "tensor", None),
        P("fsdp", None),
        P("fsdp", None, "tensor"),
        P(None, "tensor"),
        P(None, "fsdp", "tensor"),
        P(None, "tensor"),
        P("tensor", "fsdp"),
        P(),
        P("fsdp", "tensor"),
        P("tensor"),
        P("tensor", "fsdp"),
    )
    return jax.shard_map(body, mesh=mesh, in_specs=in_specs, out_specs=out_specs, check_vma=False)
```

profile of v0, /device:TPU:10, one launch (start us, length us, event | category | flops | bytes accessed | tf_op | source)
XLA Modules:
  0.0 1839.6 jit_solution(16392404143528849452)
XLA Ops:
  12.4 1583.9 %while.33 = (s32[]{:T(128)}, f32[3,1152,288]{1,2,0:T(8,128)}, f32[288,1152]{1,0:T(8,128)}, f32[1152,1152]{1,0:T(8,128)}, f32[1152,1152]{1,0:T(8,128)}, /*index=5...) while((s32[]{:T(128)}, f32[3,1152,288]{1,2,0:T(8,128)}, ...), condition=%wide.region_27.28_spmd.clone, body=%wide.region_0.27_spmd.clone.sunk | while | flops 28319299584 | bytes 661806848 | solution.py:252
  17.3 40.4 %all-gather.17.cloned.1.call-done = bf16[1152,6,288]{2,0,1:T(8,128)(2,1)} async-done(((bf16[144,6,288]{2,0,1:T(8,128)(2,1)}), bf16[1152,6,288]{2,0,1:T(8,128)(2,1)}) %all-gather.17.cloned.1.call-update) | async-done | bytes 3981328 | tf_op jit(solution)/shard_map/while/body/eval_jaxpr/all_gather | solution.py:31
  92.2 51.2 %all-gather.19.cloned.1.call-done = bf16[1024,1152]{1,0:T(8,128)(2,1)} async-done(((bf16[256,1152]{1,0:T(8,128)(2,1)}), bf16[1024,1152]{1,0:T(8,128)(2,1)}) %all-gather.19.cloned.1.call-update) | async-done | bytes 2359312 | tf_op jit(solution)/shard_map/while/body/eval_jaxpr/all_gather | solution.py:82
  178.2 46.8 %reduce-scatter.31.cloned.1.call-done = bf16[256,1152]{1,0:T(8,128)(2,1)} async-done(((bf16[1024,1152]{1,0:T(8,128)(2,1)}), bf16[256,1152]{1,0:T(8,128)(2,1)}) %reduce-scatter.31.cloned.1.call-update) | async-done | bytes 589840 | tf_op jit(solution)/shard_map/while/body/eval_jaxpr/reduce_scatter | solution.py:106
  257.6 50.9 %all-gather.23.cloned.1.call-done = bf16[1024,1152]{1,0:T(8,128)(2,1)} async-done(((bf16[256,1152]{1,0:T(8,128)(2,1)}), bf16[1024,1152]{1,0:T(8,128)(2,1)}) %all-gather.23.cloned.1.call-update) | async-done | bytes 2359312 | tf_op jit(solution)/shard_map/while/body/eval_jaxpr/all_gather | solution.py:117
  350.0 47.0 %reduce-scatter.33.cloned.1.call-done = bf16[256,1152]{1,0:T(8,128)(2,1)} async-done(((bf16[1024,1152]{1,0:T(8,128)(2,1)}), bf16[256,1152]{1,0:T(8,128)(2,1)}) %reduce-scatter.33.cloned.1.call-update) | async-done | bytes 589840 | tf_op jit(solution)/shard_map/while/body/eval_jaxpr/reduce_scatter | solution.py:123
  401.3 48.1 %all-gather.29.cloned.1.call-done = bf16[1024,1152]{1,0:T(8,128)(2,1)} async-done(((bf16[256,1152]{1,0:T(8,128)(2,1)}), bf16[1024,1152]{1,0:T(8,128)(2,1)}) %all-gather.29.cloned.1.call-update) | async-done | bytes 2359312 | tf_op jit(solution)/shard_map/while/body/eval_jaxpr/all_gather | solution.py:137
  521.5 47.0 %reduce-scatter.35.cloned.1.call-done = bf16[256,1152]{1,0:T(8,128)(2,1)} async-done(((bf16[1024,1152]{1,0:T(8,128)(2,1)}), bf16[256,1152]{1,0:T(8,128)(2,1)}) %reduce-scatter.35.cloned.1.call-update) | async-done | bytes 589840 | tf_op jit(solution)/shard_map/while/body/eval_jaxpr/reduce_scatter | solution.py:144
  585.3 38.7 %all-gather.35.cloned.1.call-done = bf16[1024,1152]{1,0:T(8,128)(2,1)} async-done(((bf16[256,1152]{1,0:T(8,128)(2,1)}), bf16[1024,1152]{1,0:T(8,128)(2,1)}) %all-gather.35.cloned.1.call-update) | async-done | bytes 2359312 | tf_op jit(solution)/shard_map/while/body/eval_jaxpr/all_gather | solution.py:154
  672.6 46.0 %reduce-scatter.37.cloned.1.call-done = bf16[256,1152]{1,0:T(8,128)(2,1)} async-done(((bf16[1024,1152]{1,0:T(8,128)(2,1)}), bf16[256,1152]{1,0:T(8,128)(2,1)}) %reduce-scatter.37.cloned.1.call-update) | async-done | bytes 589840 | tf_op jit(solution)/shard_map/while/body/eval_jaxpr/reduce_scatter | solution.py:192
  750.5 36.7 %all-gather.39.cloned.1.call-done = bf16[1152,6,288]{2,0,1:T(8,128)(2,1)} async-done(((bf16[144,6,288]{2,0,1:T(8,128)(2,1)}), bf16[1152,6,288]{2,0,1:T(8,128)(2,1)}) %all-gather.39.cloned.1.call-update) | async-done | bytes 3981328 | tf_op jit(solution)/shard_map/while/body/eval_jaxpr/all_gather | solution.py:31
  805.4 39.1 %all-gather.17.cloned.1.call-done = bf16[1152,6,288]{2,0,1:T(8,128)(2,1)} async-done(((bf16[144,6,288]{2,0,1:T(8,128)(2,1)}), bf16[1152,6,288]{2,0,1:T(8,128)(2,1)}) %all-gather.17.cloned.1.call-update) | async-done | bytes 3981328 | tf_op jit(solution)/shard_map/while/body/eval_jaxpr/all_gather | solution.py:31
  879.1 51.0 %all-gather.19.cloned.1.call-done = bf16[1024,1152]{1,0:T(8,128)(2,1)} async-done(((bf16[256,1152]{1,0:T(8,128)(2,1)}), bf16[1024,1152]{1,0:T(8,128)(2,1)}) %all-gather.19.cloned.1.call-update) | async-done | bytes 2359312 | tf_op jit(solution)/shard_map/while/body/eval_jaxpr/all_gather | solution.py:82
  964.7 46.7 %reduce-scatter.31.cloned.1.call-done = bf16[256,1152]{1,0:T(8,128)(2,1)} async-done(((bf16[1024,1152]{1,0:T(8,128)(2,1)}), bf16[256,1152]{1,0:T(8,128)(2,1)}) %reduce-scatter.31.cloned.1.call-update) | async-done | bytes 589840 | tf_op jit(solution)/shard_map/while/body/eval_jaxpr/reduce_scatter | solution.py:106
  1044.1 51.1 %all-gather.23.cloned.1.call-done = bf16[1024,1152]{1,0:T(8,128)(2,1)} async-done(((bf16[256,1152]{1,0:T(8,128)(2,1)}), bf16[1024,1152]{1,0:T(8,128)(2,1)}) %all-gather.23.cloned.1.call-update) | async-done | bytes 2359312 | tf_op jit(solution)/shard_map/while/body/eval_jaxpr/all_gather | solution.py:117
  1136.5 47.0 %reduce-scatter.33.cloned.1.call-done = bf16[256,1152]{1,0:T(8,128)(2,1)} async-done(((bf16[1024,1152]{1,0:T(8,128)(2,1)}), bf16[256,1152]{1,0:T(8,128)(2,1)}) %reduce-scatter.33.cloned.1.call-update) | async-done | bytes 589840 | tf_op jit(solution)/shard_map/while/body/eval_jaxpr/reduce_scatter | solution.py:123
  1188.1 47.9 %all-gather.29.cloned.1.call-done = bf16[1024,1152]{1,0:T(8,128)(2,1)} async-done(((bf16[256,1152]{1,0:T(8,128)(2,1)}), bf16[1024,1152]{1,0:T(8,128)(2,1)}) %all-gather.29.cloned.1.call-update) | async-done | bytes 2359312 | tf_op jit(solution)/shard_map/while/body/eval_jaxpr/all_gather | solution.py:137
  1308.0 47.0 %reduce-scatter.35.cloned.1.call-done = bf16[256,1152]{1,0:T(8,128)(2,1)} async-done(((bf16[1024,1152]{1,0:T(8,128)(2,1)}), bf16[256,1152]{1,0:T(8,128)(2,1)}) %reduce-scatter.35.cloned.1.call-update) | async-done | bytes 589840 | tf_op jit(solution)/shard_map/while/body/eval_jaxpr/reduce_scatter | solution.py:144
  1371.8 38.7 %all-gather.35.cloned.1.call-done = bf16[1024,1152]{1,0:T(8,128)(2,1)} async-done(((bf16[256,1152]{1,0:T(8,128)(2,1)}), bf16[1024,1152]{1,0:T(8,128)(2,1)}) %all-gather.35.cloned.1.call-update) | async-done | bytes 2359312 | tf_op jit(solution)/shard_map/while/body/eval_jaxpr/all_gather | solution.py:154
  1459.2 46.0 %reduce-scatter.37.cloned.1.call-done = bf16[256,1152]{1,0:T(8,128)(2,1)} async-done(((bf16[1024,1152]{1,0:T(8,128)(2,1)}), bf16[256,1152]{1,0:T(8,128)(2,1)}) %reduce-scatter.37.cloned.1.call-update) | async-done | bytes 589840 | tf_op jit(solution)/shard_map/while/body/eval_jaxpr/reduce_scatter | solution.py:192
  1541.2 32.7 %all-gather.39.cloned.1.call-done = bf16[1152,6,288]{2,0,1:T(8,128)(2,1)} async-done(((bf16[144,6,288]{2,0,1:T(8,128)(2,1)}), bf16[1152,6,288]{2,0,1:T(8,128)(2,1)}) %all-gather.39.cloned.1.call-update) | async-done | bytes 3981328 | tf_op jit(solution)/shard_map/while/body/eval_jaxpr/all_gather | solution.py:31
  1683.1 44.1 %reduce-scatter.21.cloned.1.call-done = bf16[144,1152]{1,0:T(8,128)(2,1)} async-done(((bf16[1152,1152]{1,0:T(8,128)(2,1)}), bf16[144,1152]{1,0:T(8,128)(2,1)}) %reduce-scatter.21.cloned.1.call-update) | async-done | bytes 331792 | tf_op jit(solution)/shard_map/reduce_scatter | solution.py:265
  1729.0 45.7 %reduce-scatter.23.cloned.1.call-done = bf16[1152,144]{0,1:T(8,128)(2,1)} async-done(((bf16[1152,1152]{0,1:T(8,128)(2,1)}), bf16[1152,144]{0,1:T(8,128)(2,1)}) %reduce-scatter.23.cloned.1.call-update) | async-done | bytes 331792 | tf_op jit(solution)/shard_map/reduce_scatter | solution.py:268
  1776.5 52.5 %reduce-scatter.25.cloned.1.call-done = bf16[144,1728]{1,0:T(8,128)(2,1)} async-done(((bf16[1152,1728]{1,0:T(8,128)(2,1)}), bf16[144,1728]{1,0:T(8,128)(2,1)}) %reduce-scatter.25.cloned.1.call-update) | async-done | bytes 497680
  (424 shorter events, 775.2 us)
Async XLA Ops:
  13.9 129.5 %all-gather.19.cloned.1.call-start = ((), (), s32[]{:S(2)}) async-start(), calls=%async_computation.16 | async-start | bytes 2949120 | tf_op jit(solution)/shard_map/while/body/eval_jaxpr/all_gather | solution.py:82
  75.5 149.5 %reduce-scatter.31.cloned.1.call-start = ((), (), s32[]{:S(2)}) async-start(), calls=%async_computation.18 | async-start | bytes 2949120 | tf_op jit(solution)/shard_map/while/body/eval_jaxpr/reduce_scatter | solution.py:106
  178.1 130.4 %all-gather.23.cloned.1.call-start = ((), (), s32[]{:S(2)}) async-start(), calls=%async_computation.19 | async-start | bytes 2949120 | tf_op jit(solution)/shard_map/while/body/eval_jaxpr/all_gather | solution.py:117
  229.2 111.9 %all-gather.27.cloned.1.call-start = ((), (), s32[]{:S(2)}) async-start(), calls=%async_computation.21 | async-start | bytes 2985984 | tf_op jit(solution)/shard_map/while/body/eval_jaxpr/all_gather | solution.py:30
  230.0 167.1 %reduce-scatter.33.cloned.1.call-start = ((), (), s32[]{:S(2)}) async-start(), calls=%async_computation.22 | async-start | bytes 2949120 | tf_op jit(solution)/shard_map/while/body/eval_jaxpr/reduce_scatter | solution.py:123
  349.9 99.5 %all-gather.29.cloned.1.call-start = ((), (), s32[]{:S(2)}) async-start(), calls=%async_computation.23 | async-start | bytes 2949120 | tf_op jit(solution)/shard_map/while/body/eval_jaxpr/all_gather | solution.py:137
  400.4 113.7 %all-gather.33.cloned.1.call-start = ((), (), s32[]{:S(2)}) async-start(), calls=%async_computation.25 | async-start | bytes 2985984 | tf_op jit(solution)/shard_map/while/body/eval_jaxpr/all_gather | solution.py:29
  401.1 167.4 %reduce-scatter.35.cloned.1.call-start = ((), (), s32[]{:S(2)}) async-start(), calls=%async_computation.26 | async-start | bytes 2949120 | tf_op jit(solution)/shard_map/while/body/eval_jaxpr/reduce_scatter | solution.py:144
  521.5 102.5 %all-gather.35.cloned.1.call-start = ((), (), s32[]{:S(2)}) async-start(), calls=%async_computation.27 | async-start | bytes 2949120 | tf_op jit(solution)/shard_map/while/body/eval_jaxpr/all_gather | solution.py:154
  574.4 89.5 %all-gather.37.cloned.1.call-start = ((), (), s32[]{:S(2)}) async-start(), calls=%async_computation.28 | async-start | bytes 2985984 | tf_op jit(solution)/shard_map/while/body/eval_jaxpr/all_gather | solution.py:27
  585.1 133.6 %reduce-scatter.37.cloned.1.call-start = ((), (), s32[]{:S(2)}) async-start(), calls=%async_computation.29 | async-start | bytes 2949120 | tf_op jit(solution)/shard_map/while/body/eval_jaxpr/reduce_scatter | solution.py:192
  802.0 128.1 %all-gather.19.cloned.1.call-start = ((), (), s32[]{:S(2)}) async-start(), calls=%async_computation.16 | async-start | bytes 2949120 | tf_op jit(solution)/shard_map/while/body/eval_jaxpr/all_gather | solution.py:82
  862.3 149.1 %reduce-scatter.31.cloned.1.call-start = ((), (), s32[]{:S(2)}) async-start(), calls=%async_computation.18 | async-start | bytes 2949120 | tf_op jit(solution)/shard_map/while/body/eval_jaxpr/reduce_scatter | solution.py:106
  964.6 130.6 %all-gather.23.cloned.1.call-start = ((), (), s32[]{:S(2)}) async-start(), calls=%async_computation.19 | async-start | bytes 2949120 | tf_op jit(solution)/shard_map/while/body/eval_jaxpr/all_gather | solution.py:117
  1015.6 112.0 %all-gather.27.cloned.1.call-start = ((), (), s32[]{:S(2)}) async-start(), calls=%async_computation.21 | async-start | bytes 2985984 | tf_op jit(solution)/shard_map/while/body/eval_jaxpr/all_gather | solution.py:30
  1016.2 167.4 %reduce-scatter.33.cloned.1.call-start = ((), (), s32[]{:S(2)}) async-start(), calls=%async_computation.22 | async-start | bytes 2949120 | tf_op jit(solution)/shard_map/while/body/eval_jaxpr/reduce_scatter | solution.py:123
  1136.4 99.5 %all-gather.29.cloned.1.call-start = ((), (), s32[]{:S(2)}) async-start(), calls=%async_computation.23 | async-start | bytes 2949120 | tf_op jit(solution)/shard_map/while/body/eval_jaxpr/all_gather | solution.py:137
  1186.9 113.7 %all-gather.33.cloned.1.call-start = ((), (), s32[]{:S(2)}) async-start(), calls=%async_computation.25 | async-start | bytes 2985984 | tf_op jit(solution)/shard_map/while/body/eval_jaxpr/all_gather | solution.py:29
  1187.7 167.4 %reduce-scatter.35.cloned.1.call-start = ((), (), s32[]{:S(2)}) async-start(), calls=%async_computation.26 | async-start | bytes 2949120 | tf_op jit(solution)/shard_map/while/body/eval_jaxpr/reduce_scatter | solution.py:144
  1308.0 102.6 %all-gather.35.cloned.1.call-start = ((), (), s32[]{:S(2)}) async-start(), calls=%async_computation.27 | async-start | bytes 2949120 | tf_op jit(solution)/shard_map/while/body/eval_jaxpr/all_gather | solution.py:154
  1371.6 133.5 %reduce-scatter.37.cloned.1.call-start = ((), (), s32[]{:S(2)}) async-start(), calls=%async_computation.29 | async-start | bytes 2949120 | tf_op jit(solution)/shard_map/while/body/eval_jaxpr/reduce_scatter | solution.py:192
  1613.0 114.1 %reduce-scatter.21.cloned.1.call-start = ((), (), s32[]{:S(2)}) async-start(), calls=%async_computation.10 | async-start | bytes 2985984 | tf_op jit(solution)/shard_map/reduce_scatter | solution.py:265
  1617.4 157.3 %reduce-scatter.23.cloned.1.call-start = ((), (), s32[]{:S(2)}) async-start(), calls=%async_computation.11 | async-start | bytes 2985984 | tf_op jit(solution)/shard_map/reduce_scatter | solution.py:268
  1623.3 205.8 %reduce-scatter.25.cloned.1.call-start = ((), (), s32[]{:S(2)}) async-start(), calls=%async_computation.12 | async-start | bytes 4644864
  (82 other events, 1981.3 us)
Sparse Core Ops, SparseCore 0:
  15.1 42.5 all-gather.16
  59.6 32.6 all-gather.20
  94.4 48.9 all-gather.18
  177.6 47.3 reduce-scatter.30
  226.7 30.8 all-gather.24
  259.6 48.8 all-gather.22
  350.0 46.9 reduce-scatter.32
  399.9 49.4 all-gather.28
  521.6 46.9 reduce-scatter.34
  574.5 49.4 all-gather.34
  671.2 47.4 reduce-scatter.36
  744.8 42.3 all-gather.38
  803.1 41.3 all-gather.16
  846.4 32.6 all-gather.20
  881.1 48.9 all-gather.18
  964.0 47.3 reduce-scatter.30
  1013.2 30.8 all-gather.24
  1046.3 48.8 all-gather.22
  1136.6 46.9 reduce-scatter.32
  1186.4 49.4 all-gather.28
  1308.1 46.9 reduce-scatter.34
  1361.0 49.4 all-gather.34
  1457.7 47.3 reduce-scatter.36
  1531.4 42.4 all-gather.38
  (10 shorter events, 283.6 us)
Sparse Core Ops, SparseCore 1:
  1600.6 34.9 reduce-scatter.28
  1639.2 40.8 reduce-scatter.26
  1683.5 43.6 reduce-scatter.20
  1731.0 43.6 reduce-scatter.22
  1778.1 50.9 reduce-scatter.24
where the time goes:
time: 1840 us
  waiting for transfers between devices  1270 us (69%)
  matrix products  252 us (14%)
  other arithmetic  115 us (6%)
  blocking collectives  110 us (6%)
  local copies, waits for them, and re-layouts  63.8 us (3%)
    all_gather x4, waiting for transfers between devices, fetch(): lax.all_gather(shards[4], 'fsdp', axis=0, tiled=True)  149 us
    all_gather x4, waiting for transfers between devices, fetch(): lax.all_gather(shards[3], 'fsdp', axis=1, tiled=True)  114 us
    all_gather x2, waiting for transfers between devices, one_image(): first_all = lax.all_gather(h_first, 'tensor', axis=0, tiled=True)  102 us
    all_gather x2, waiting for transfers between devices, one_image(): second_all = lax.all_gather(h_second, 'tensor', axis=0, tiled=True)  102 us
    all_gather x4, waiting for transfers between devices, fetch(): lax.all_gather(shards[2], 'fsdp', axis=0, tiled=True)  100 us
    all_gather x2, waiting for transfers between devices, one_image(): ffn_all = lax.all_gather(ffn_grad, 'tensor', axis=0, tiled=True)  96 us
    reduce_scatter x2, waiting for transfers between devices, one_image(): lax.psum_scatter(jnp.dot(piece, down_w, preferred_element_type=jnp.float3...  94.1 us
    reduce_scatter x2, waiting for transfers between devices, one_image(): lax.psum_scatter(jnp.einsum('sf,df->sd', piece, up_w, preferred_element_t...  94.1 us
  transfers between devices with their start and end apart: 39, of which 34 were waited for; matrix products, arithmetic and copies ran while one was open for 13% of the time, Pallas kernels for 0%

commit v1 on v0

v1 whole, which is shorter than its diff:
```python
import functools

import jax
import jax.numpy as jnp
from jax import lax
from jax.experimental import pallas as pl
from jax.experimental.pallas import tpu as pltpu
from jax.sharding import PartitionSpec as P

HEAD_DIM = 72
EPS = 1e-06
TANH_C = 0.7978845608028654
CUBIC = 0.044715
LOG2E = 1.4426950408889634
VMEM_BYTES = 56 << 20
ROWS = 16
BF = jnp.bfloat16
F32 = jnp.float32
BOTH = ("fsdp", "tensor")


def dotg(a, b, ca, cb):
    return lax.dot_general(a, b, (((ca,), (cb,)), ((), ())), preferred_element_type=F32)


class Geo:
    def __init__(self, fsdp, tensor, dim):
        self.F, self.T, self.P = fsdp, tensor, fsdp // 2
        self.Th = tensor // 2
        self.D = dim
        self.R = dim // fsdp
        self.bits = [1 << b for b in range((self.P - 1).bit_length())]
        self.order = (self.orders(self.bits[::-1]), self.orders(self.bits))
        self.direct = self.R % 16 == 0

    @staticmethod
    def orders(msb_first):
        vals = [0]
        for bit in reversed(msb_first):
            vals = vals + [v | bit for v in vals]
        return vals


def reorder(x, index, axis=0):
    return jnp.stack([lax.dynamic_index_in_dim(x, i, axis, keepdims=False) for i in index], axis)


def flip_pair(x, bit, geo):
    return lax.ppermute(x, "fsdp", [(i, i ^ (2 * bit)) for i in range(geo.F)])


def flip_core(x, geo):
    return lax.ppermute(x, "fsdp", [(i, i ^ 1) for i in range(geo.F)])


def flip_tensor(x, k, geo):
    return lax.ppermute(x, "tensor", [(i, i ^ k) for i in range(geo.T)])


def gather_weight(shard, geo):
    parts = [shard] + [flip_tensor(shard, k, geo) for k in range(1, geo.T)]
    halves = []
    for half in range(2):
        buf = jnp.stack(parts[half * geo.Th : (half + 1) * geo.Th])[None]
        bits = geo.bits if half == 0 else geo.bits[::-1]
        for bit in bits[:-1]:
            buf = jnp.concatenate([buf, flip_pair(buf, bit, geo)])
        own = [buf, flip_pair(buf, bits[-1], geo)]
        other = [flip_core(a, geo) for a in own]
        halves.append(own + other)
    return halves


class Gathered:
    def __init__(self, halves, geo, scal):
        self.geo = geo
        if not geo.direct:
            fixed = []
            for half, arrays in enumerate(halves):
                at = [geo.order[half].index(rel) for rel in range(geo.P)]
                lookup = jnp.array(at, jnp.int32)
                blocks = jnp.concatenate(arrays)
                blocks = reorder(
                    blocks,
                    [
                        lookup[(f // 2) ^ scal[0]] + geo.P * ((f % 2) ^ scal[1])
                        for f in range(geo.F)
                    ],
                )
                _, th, k, r, w = blocks.shape
                fixed.append([blocks.transpose(1, 2, 0, 3, 4).reshape(1, th, k, geo.D, w)])
            halves = fixed
        self.arrays = halves[0] + halves[1]
        self.n = len(halves[0])
        self.width = self.arrays[0].shape[-1]

    def specs(self, plane, count):
        th = self.geo.Th
        out = []
        for idx, a in enumerate(self.arrays):
            block = (a.shape[0], 1, count, a.shape[3], a.shape[4])
            if idx < self.n:
                out.append(pl.BlockSpec(block, lambda j, s: (0, jnp.minimum(j, th - 1), plane, 0, 0)))
            else:
                out.append(pl.BlockSpec(block, lambda j, s: (0, jnp.maximum(j - th, 0), plane, 0, 0)))
        return out

    def assemble(self, j, s_ref, refs, dst):
        geo = self.geo
        for half in range(2):

            @pl.when((j < geo.Th) if half == 0 else (j >= geo.Th))
            def _():
                for at in range(self.n):
                    ref = refs[half * self.n + at]
                    n, _, count, rows, _ = ref.shape
                    for i in range(n):
                        if geo.direct:
                            rel = geo.order[half][(at % 2) * n + i]
                            place = 2 * (s_ref[0] ^ rel) + (s_ref[1] ^ (at // 2))
                            place = pl.multiple_of(place * rows, rows)
                        else:
                            place = 0
                        for q in range(count):
                            dst[q, pl.ds(place, rows), :] = ref[i, 0, q]


def scatter_grad(pieces, geo):
    def add(a, b):
        return a.astype(F32) + b.astype(F32)

    halves = []
    for half in range(2):
        keep, send = pieces[2 * half], pieces[2 * half + 1]
        bits = geo.bits[::-1] if half == 0 else geo.bits
        for at, bit in enumerate(bits):
            got = flip_pair(send, bit, geo)
            if at == len(bits) - 1:
                halves.append(add(keep, got)[0].astype(BF))
            else:
                m = keep.shape[0] // 2
                send = add(keep[m:], got[m:]).astype(BF)
                keep = add(keep[:m], got[:m]).astype(BF)
    keep, send = halves
    size = geo.Th
    while True:
        got = flip_tensor(send, size, geo)
        if size == 1:
            return add(keep, got)[0]
        size //= 2
        send = add(keep[size:], got[size:]).astype(BF)
        keep = add(keep[:size], got[:size]).astype(BF)


def params():
    return pltpu.CompilerParams(vmem_limit_bytes=VMEM_BYTES)


def cost(flops, size):
    return pl.CostEstimate(flops=int(flops), bytes_accessed=int(size), transcendentals=0)


def whole(shape):
    zeros = (0,) * len(shape)
    return pl.BlockSpec(shape, lambda j, s: zeros)


def chunked(total, want):
    return want if total % want == 0 else total


def norm_of(v):
    centre = v - jnp.mean(v, axis=-1, keepdims=True)
    inv = lax.rsqrt(jnp.mean(centre * centre, axis=-1, keepdims=True) + EPS)
    return centre * inv, inv


def norm_back(norm, inv, g):
    return (
        g
        - jnp.mean(g, axis=-1, keepdims=True)
        - norm * jnp.mean(g * norm, axis=-1, keepdims=True)
    ) * inv


def fold_rows(v):
    return v.reshape(v.shape[0] // 8, 8, v.shape[1]).sum(axis=0)


def in_proj(scal, x, mod, wt, bias, geo):
    n, d = x.shape
    w = wt.width
    nw = len(wt.arrays)

    def kernel(s, x_ref, m_ref, b_ref, *refs):
        w_refs, (h_ref, q_ref, kv_ref, wbuf) = refs[:nw], refs[nw:]
        j = pl.program_id(0)

        @pl.when(j == 0)
        def _():
            @pl.loop(0, n // ROWS)
            def _(i):
                at = pl.ds(pl.multiple_of(i * ROWS, ROWS), ROWS)
                norm, _ = norm_of(x_ref[at, :].astype(F32))
                h_ref[at, :] = (norm * (1.0 + m_ref[1:2, :]) + m_ref[0:1, :]).astype(BF)

        wt.assemble(j, s, w_refs, wbuf)
        for q in range(3):
            y = dotg(h_ref[...], wbuf[q], 1, 0) + b_ref[0, q]
            if q == 0:
                q_ref[0] = y.astype(BF)
            else:
                kv_ref[0, q - 1] = y.astype(BF)

    return pl.pallas_call(
        kernel,
        grid_spec=pltpu.PrefetchScalarGridSpec(
            num_scalar_prefetch=1,
            grid=(geo.T,),
            in_specs=[
                whole((n, d)),
                whole(mod.shape),
                pl.BlockSpec((1, 3, 1, w), lambda j, s: (s[2] ^ j, 0, 0, 0)),
                *wt.specs(0, 3),
            ],
            out_specs=[
                whole((n, d)),
                pl.BlockSpec((1, n, w), lambda j, s: (j, 0, 0)),
                pl.BlockSpec((1, 2, n, w), lambda j, s: (j, 0, 0, 0)),
            ],
            scratch_shapes=[pltpu.VMEM((3, d, w), BF)],
        ),
        out_shape=[
            jax.ShapeDtypeStruct((n, d), BF),
            jax.ShapeDtypeStruct((geo.T, n, w), BF),
            jax.ShapeDtypeStruct((geo.T, 2, n, w), BF),
        ],
        compiler_params=params(),
        cost_estimate=cost(6 * n * d * d, 6 * d * d + 8 * n * d),
        name="in_proj",
    )(scal, x, mod, bias, *wt.arrays)


def attn_fwd(q, kv, kvo):
    z, n, w = q.shape
    heads = w // HEAD_DIM
    c = HEAD_DIM**-0.5 * LOG2E

    def kernel(q_ref, kv_ref, kvo_ref, o_ref, lse_ref):
        outs = []
        for h in range(heads):
            sl = slice(h * HEAD_DIM, (h + 1) * HEAD_DIM)
            qh = q_ref[0, :, sl]
            sa = dotg(kv_ref[0, 0, :, sl], qh, 1, 1) * c
            sb = dotg(kvo_ref[0, 0, :, sl], qh, 1, 1) * c
            top = jnp.maximum(
                jnp.max(sa, axis=0, keepdims=True), jnp.max(sb, axis=0, keepdims=True)
            )
            pa, pb = jnp.exp2(sa - top), jnp.exp2(sb - top)
            total = jnp.sum(pa, axis=0, keepdims=True) + jnp.sum(pb, axis=0, keepdims=True)
            o = dotg(kv_ref[0, 1, :, sl], pa.astype(BF), 0, 0)
            o = o + dotg(kvo_ref[0, 1, :, sl], pb.astype(BF), 0, 0)
            outs.append(o / total)
            lse_ref[0, h : h + 1, :] = top + jnp.log2(total)
        o_ref[0] = jnp.concatenate(outs, axis=0).T.astype(BF)

    s3 = pl.BlockSpec((1, n, w), lambda j: (j, 0, 0))
    s4 = pl.BlockSpec((1, 2, n, w), lambda j: (j, 0, 0, 0))
    sl = pl.BlockSpec((1, heads, n), lambda j: (j, 0, 0))
    return pl.pallas_call(
        kernel,
        grid=(z,),
        in_specs=[s3, s4, s4],
        out_specs=[s3, sl],
        out_shape=[
            jax.ShapeDtypeStruct((z, n, w), BF),
            jax.ShapeDtypeStruct((z, heads, n), F32),
        ],
        compiler_params=params(),
        cost_estimate=cost(30 * 1e9, 14 * z * n * w),
        name="attn_fwd",
    )(q, kv, kvo)


def attn_bwd(q, kv, kvo, o, do, lse):
    z, n, w = q.shape
    heads = w // HEAD_DIM
    scale = HEAD_DIM**-0.5
    c = scale * LOG2E

    def kernel(q_ref, kv_ref, kvo_ref, o_ref, do_ref, lse_ref, dq_ref, dkv_ref, dkvo_ref, sum_ref):
        both = (do_ref[0].astype(F32) * o_ref[0].astype(F32)).T
        dqs, parts = [], [[[], []], [[], []]]
        for h in range(heads):
            sl = slice(h * HEAD_DIM, (h + 1) * HEAD_DIM)
            qh, doh = q_ref[0, :, sl], do_ref[0, :, sl]
            delta = jnp.sum(both[sl], axis=0, keepdims=True)
            lse_h = lse_ref[0, h : h + 1, :]
            dq = None
            for i, ref in enumerate((kv_ref, kvo_ref)):
                k, v = ref[0, 0, :, sl], ref[0, 1, :, sl]
                p = jnp.exp2(dotg(k, qh, 1, 1) * c - lse_h)
                ds = (p * (dotg(v, doh, 1, 1) - delta)).astype(BF)
                parts[i][1].append(dotg(doh, p.astype(BF), 0, 1))
                parts[i][0].append(dotg(qh, ds, 0, 1) * scale)
                got = dotg(k, ds, 0, 0)
                dq = got if dq is None else dq + got
            dqs.append(dq * scale)
        dq = jnp.concatenate(dqs, axis=0).T
        dq_ref[0] = dq.astype(BF)
        sum_ref[0, 0:1, :] = jnp.sum(dq, axis=0, keepdims=True)
        dv_sum = None
        for i, ref in enumerate((dkv_ref, dkvo_ref)):
            for at in range(2):
                full = jnp.concatenate(parts[i][at], axis=0).T
                ref[0, at] = full.astype(BF)
                if at == 1:
                    now = jnp.sum(full, axis=0, keepdims=True)
                    dv_sum = now if dv_sum is None else dv_sum + now
        sum_ref[0, 1:2, :] = dv_sum

    s3 = pl.BlockSpec((1, n, w), lambda j: (j, 0, 0))
    s4 = pl.BlockSpec((1, 2, n, w), lambda j: (j, 0, 0, 0))
    sl = pl.BlockSpec((1, heads, n), lambda j: (j, 0, 0))
    return pl.pallas_call(
        kernel,
        grid=(z,),
        in_specs=[s3, s4, s4, s3, s3, sl],
        out_specs=[s3, s4, s4, pl.BlockSpec((1, 2, w), lambda j: (j, 0, 0))],
        out_shape=[
            jax.ShapeDtypeStruct((z, n, w), BF),
            jax.ShapeDtypeStruct((z, 2, n, w), BF),
            jax.ShapeDtypeStruct((z, 2, n, w), BF),
            jax.ShapeDtypeStruct((z, 2, w), F32),
        ],
        compiler_params=params(),
        cost_estimate=cost(50 * 1e9, 24 * z * n * w),
        name="attn_bwd",
    )(q, kv, kvo, o, do, lse)


def out_proj(scal, mixed, x, mod, bias, wt, geo):
    _, n, w = mixed.shape
    d = geo.D
    nw = len(wt.arrays)

    def kernel(s, y_ref, x_ref, m_ref, b_ref, *refs):
        w_refs, (attn_ref, resid_ref, h_ref, wbuf) = refs[:nw], refs[nw:]
        j = pl.program_id(0)
        wt.assemble(j, s, w_refs, wbuf)
        part = dotg(y_ref[0], wbuf[0], 1, 1)

        @pl.when(j == 0)
        def _():
            attn_ref[...] = part

        @pl.when(j > 0)
        def _():
            attn_ref[...] += part

        @pl.when(j == geo.T - 1)
        def _():
            @pl.loop(0, n // ROWS)
            def _(i):
                at = pl.ds(pl.multiple_of(i * ROWS, ROWS), ROWS)
                attn = attn_ref[at, :] + b_ref[...]
                attn_ref[at, :] = attn
                resid = x_ref[at, :].astype(F32) + m_ref[2:3, :] * attn
                resid_ref[at, :] = resid
                norm, _ = norm_of(resid)
                h_ref[at, :] = (norm * (1.0 + m_ref[4:5, :]) + m_ref[3:4, :]).astype(BF)

    return pl.pallas_call(
        kernel,
        grid_spec=pltpu.PrefetchScalarGridSpec(
            num_scalar_prefetch=1,
            grid=(geo.T,),
            in_specs=[
                pl.BlockSpec((1, n, w), lambda j, s: (j, 0, 0)),
                whole((n, d)),
                whole(mod.shape),
                whole((1, d)),
                *wt.specs(3, 1),
            ],
            out_specs=[whole((n, d))] * 3,
            scratch_shapes=[pltpu.VMEM((1, d, w), BF)],
        ),
        out_shape=[
            jax.ShapeDtypeStruct((n, d), F32),
            jax.ShapeDtypeStruct((n, d), F32),
            jax.ShapeDtypeStruct((n, d), BF),
        ],
        compiler_params=params(),
        cost_estimate=cost(2 * n * d * d, 2 * d * d + 14 * n * d),
        name="out_proj",
    )(scal, mixed, x, mod, bias, *wt.arrays)


def up_proj(scal, h, bias, wt, geo):
    n, d = h.shape
    w = wt.width
    nw = len(wt.arrays)
    step = chunked(w, 384)

    def kernel(s, h_ref, b_ref, *refs):
        w_refs, (hid_ref, gp_ref, wbuf) = refs[:nw], refs[nw:]
        j = pl.program_id(0)
        wt.assemble(j, s, w_refs, wbuf)
        for at in range(0, w, step):
            cols = slice(at, at + step)
            u = dotg(h_ref[...], wbuf[0, :, cols], 1, 0) + b_ref[0, :, cols]
            sq = u * u
            t = jnp.tanh(TANH_C * (u + CUBIC * sq * u))
            half = 0.5 * (1.0 + t)
            hid_ref[0, :, cols] = (u * half).astype(BF)
            slope = TANH_C * (1.0 + 3.0 * CUBIC * sq)
            gp_ref[0, :, cols] = (half + 0.5 * u * (1.0 - t * t) * slope).astype(BF)

    out = pl.BlockSpec((1, n, w), lambda j, s: (j, 0, 0))
    return pl.pallas_call(
        kernel,
        grid_spec=pltpu.PrefetchScalarGridSpec(
            num_scalar_prefetch=1,
            grid=(geo.T,),
            in_specs=[
                whole((n, d)),
                pl.BlockSpec((1, 1, w), lambda j, s: (s[2] ^ j, 0, 0)),
                *wt.specs(0, 1),
            ],
            out_specs=[out, out],
            scratch_shapes=[pltpu.VMEM((1, d, w), BF)],
        ),
        out_shape=[jax.ShapeDtypeStruct((geo.T, n, w), BF)] * 2,
        compiler_params=params(),
        cost_estimate=cost(2 * n * d * w * geo.T, 2 * geo.T * w * (d + 2 * n)),
        name="up_proj",
    )(scal, h, bias, *wt.arrays)


def down_proj(scal, hidden, resid, cot, mod, bias, wt, geo):
    _, n, w = hidden.shape
    d = geo.D
    nw = len(wt.arrays)

    def kernel(s, y_ref, r_ref, c_ref, m_ref, b_ref, *refs):
        w_refs, (out_ref, sum_ref, wbuf, acc) = refs[:nw], refs[nw:]
        j = pl.program_id(0)
        wt.assemble(j, s, w_refs, wbuf)
        part = dotg(y_ref[0], wbuf[0], 1, 1)

        @pl.when(j == 0)
        def _():
            acc[...] = part
            sum_ref[...] = jnp.zeros_like(sum_ref)

        @pl.when(j > 0)
        def _():
            acc[...] += part

        @pl.when(j == geo.T - 1)
        def _():
            @pl.loop(0, n // ROWS)
            def _(i):
                at = pl.ds(pl.multiple_of(i * ROWS, ROWS), ROWS)
                ffn = acc[at, :] + b_ref[...]
                out_ref[at, :] = (r_ref[at, :] + m_ref[5:6, :] * ffn).astype(BF)
                sum_ref[...] += fold_rows(c_ref[at, :].astype(F32) * ffn)

    return pl.pallas_call(
        kernel,
        grid_spec=pltpu.PrefetchScalarGridSpec(
            num_scalar_prefetch=1,
            grid=(geo.T,),
            in_specs=[
                pl.BlockSpec((1, n, w), lambda j, s: (j, 0, 0)),
                whole((n, d)),
                whole((n, d)),
                whole(mod.shape),
                whole((1, d)),
                *wt.specs(0, 1),
            ],
            out_specs=[whole((n, d)), whole((8, d))],
            scratch_shapes=[pltpu.VMEM((1, d, w), BF), pltpu.VMEM((n, d), F32)],
        ),
        out_shape=[jax.ShapeDtypeStruct((n, d), BF), jax.ShapeDtypeStruct((8, d), F32)],
        compiler_params=params(),
        cost_estimate=cost(2 * n * d * w * geo.T, 2 * geo.T * w * (d + n) + 8 * n * d),
        name="down_proj",
    )(scal, hidden, resid, cot, mod, bias, *wt.arrays)


def pre_back(scal, g, gp, wt, geo):
    n, d = g.shape
    w = wt.width
    nw = len(wt.arrays)
    step = chunked(w, 384)

    def kernel(s, g_ref, gp_ref, *refs):
        w_refs, (out_ref, sum_ref, wbuf) = refs[:nw], refs[nw:]
        j = pl.program_id(0)
        wt.assemble(j, s, w_refs, wbuf)
        for at in range(0, w, step):
            cols = slice(at, at + step)
            y = dotg(g_ref[...], wbuf[0, :, cols], 1, 0) * gp_ref[0, :, cols].astype(F32)
            out_ref[0, :, cols] = y.astype(BF)
            sum_ref[0, :, cols] = jnp.sum(y, axis=0, keepdims=True)

    out = pl.BlockSpec((1, n, w), lambda j, s: (j, 0, 0))
    return pl.pallas_call(
        kernel,
        grid_spec=pltpu.PrefetchScalarGridSpec(
            num_scalar_prefetch=1,
            grid=(geo.T,),
            in_specs=[whole((n, d)), out, *wt.specs(0, 1)],
            out_specs=[out, pl.BlockSpec((1, 1, w), lambda j, s: (j, 0, 0))],
            scratch_shapes=[pltpu.VMEM((1, d, w), BF)],
        ),
        out_shape=[
            jax.ShapeDtypeStruct((geo.T, n, w), BF),
            jax.ShapeDtypeStruct((geo.T, 1, w), F32),
        ],
        compiler_params=params(),
        cost_estimate=cost(2 * n * d * w * geo.T, 2 * geo.T * w * (d + 2 * n)),
        name="pre_back",
    )(scal, g, gp, *wt.arrays)


def second_back(scal, pre, resid, attn, cot, mod, wt, geo):
    _, n, w = pre.shape
    d = geo.D
    nw = len(wt.arrays)

    def kernel(s, y_ref, r_ref, a_ref, c_ref, m_ref, *refs):
        w_refs, (rg_ref, ag_ref, sum_ref, wbuf, acc) = refs[:nw], refs[nw:]
        j = pl.program_id(0)
        wt.assemble(j, s, w_refs, wbuf)
        part = dotg(y_ref[0], wbuf[0], 1, 1)

        @pl.when(j == 0)
        def _():
            acc[...] = part
            sum_ref[...] = jnp.zeros_like(sum_ref)

        @pl.when(j > 0)
        def _():
            acc[...] += part

        @pl.when(j == geo.T - 1)
        def _():
            @pl.loop(0, n // ROWS)
            def _(i):
                at = pl.ds(pl.multiple_of(i * ROWS, ROWS), ROWS)
                g = acc[at, :]
                norm, inv = norm_of(r_ref[at, :])
                rg = c_ref[at, :].astype(F32) + norm_back(norm, inv, g * (1.0 + m_ref[4:5, :]))
                rg_ref[at, :] = rg
                ag = rg * m_ref[2:3, :]
                ag_ref[at, :] = ag.astype(BF)
                sum_ref[0] += fold_rows(rg * a_ref[at, :])
                sum_ref[1] += fold_rows(g)
                sum_ref[2] += fold_rows(g * norm)
                sum_ref[3] += fold_rows(ag)

    return pl.pallas_call(
        kernel,
        grid_spec=pltpu.PrefetchScalarGridSpec(
            num_scalar_prefetch=1,
            grid=(geo.T,),
            in_specs=[
                pl.BlockSpec((1, n, w), lambda j, s: (j, 0, 0)),
                whole((n, d)),
                whole((n, d)),
                whole((n, d)),
                whole(mod.shape),
                *wt.specs(0, 1),
            ],
            out_specs=[whole((n, d)), whole((n, d)), whole((4, 8, d))],
            scratch_shapes=[pltpu.VMEM((1, d, w), BF), pltpu.VMEM((n, d), F32)],
        ),
        out_shape=[
            jax.ShapeDtypeStruct((n, d), F32),
            jax.ShapeDtypeStruct((n, d), BF),
            jax.ShapeDtypeStruct((4, 8, d), F32),
        ],
        compiler_params=params(),
        cost_estimate=cost(2 * n * d * w * geo.T, 2 * geo.T * w * (d + n) + 18 * n * d),
        name="second_back",
    )(scal, pre, resid, attn, cot, mod, *wt.arrays)


def mixed_back(scal, g, wt, geo):
    n, d = g.shape
    w = wt.width
    nw = len(wt.arrays)

    def kernel(s, g_ref, *refs):
        w_refs, (out_ref, wbuf) = refs[:nw], refs[nw:]
        wt.assemble(pl.program_id(0), s, w_refs, wbuf)
        out_ref[0] = dotg(g_ref[...], wbuf[0], 1, 0).astype(BF)

    return pl.pallas_call(
        kernel,
        grid_spec=pltpu.PrefetchScalarGridSpec(
            num_scalar_prefetch=1,
            grid=(geo.T,),
            in_specs=[whole((n, d)), *wt.specs(3, 1)],
            out_specs=pl.BlockSpec((1, n, w), lambda j, s: (j, 0, 0)),
            scratch_shapes=[pltpu.VMEM((1, d, w), BF)],
        ),
        out_shape=jax.ShapeDtypeStruct((geo.T, n, w), BF),
        compiler_params=params(),
        cost_estimate=cost(2 * n * d * d, 2 * d * d + 4 * n * d),
        name="mixed_back",
    )(scal, g, *wt.arrays)


def first_back(scal, dq, dkv, x, rg, mod, wt, geo):
    _, n, w = dq.shape
    d = geo.D
    nw = len(wt.arrays)

    def kernel(s, q_ref, kv_ref, x_ref, r_ref, m_ref, *refs):
        w_refs, (out_ref, sum_ref, wbuf, acc) = refs[:nw], refs[nw:]
        j = pl.program_id(0)
        wt.assemble(j, s, w_refs, wbuf)
        part = dotg(q_ref[0], wbuf[0], 1, 1)
        part += dotg(kv_ref[0, 0], wbuf[1], 1, 1)
        part += dotg(kv_ref[0, 1], wbuf[2], 1, 1)

        @pl.when(j == 0)
        def _():
            acc[...] = part
            sum_ref[...] = jnp.zeros_like(sum_ref)

        @pl.when(j > 0)
        def _():
            acc[...] += part

        @pl.when(j == geo.T - 1)
        def _():
            @pl.loop(0, n // ROWS)
            def _(i):
                at = pl.ds(pl.multiple_of(i * ROWS, ROWS), ROWS)
                g = acc[at, :]
                norm, inv = norm_of(x_ref[at, :].astype(F32))
                back = norm_back(norm, inv, g * (1.0 + m_ref[1:2, :]))
                out_ref[at, :] = (r_ref[at, :] + back).astype(BF)
                sum_ref[0] += fold_rows(g)
                sum_ref[1] += fold_rows(g * norm)

    return pl.pallas_call(
        kernel,
        grid_spec=pltpu.PrefetchScalarGridSpec(
            num_scalar_prefetch=1,
            grid=(geo.T,),
            in_specs=[
                pl.BlockSpec((1, n, w), lambda j, s: (j, 0, 0)),
                pl.BlockSpec((1, 2, n, w), lambda j, s: (j, 0, 0, 0)),
                whole((n, d)),
                whole((n, d)),
                whole(mod.shape),
                *wt.specs(0, 3),
            ],
            out_specs=[whole((n, d)), whole((2, 8, d))],
            scratch_shapes=[pltpu.VMEM((3, d, w), BF), pltpu.VMEM((n, d), F32)],
        ),
        out_shape=[jax.ShapeDtypeStruct((n, d), BF), jax.ShapeDtypeStruct((2, 8, d), F32)],
        compiler_params=params(),
        cost_estimate=cost(6 * n * d * d, 6 * d * d + 16 * n * d),
        name="first_back",
    )(scal, dq, dkv, x, rg, mod, *wt.arrays)


def weight_grad(scal, a_own, a_other, bs, geo, name):
    w = bs[0][0].shape[-1]
    n = a_own.shape[0]
    pr = geo.P * geo.R
    th = geo.Th
    planes = sum(b[0].shape[1] for b in bs)
    flat = [part for pair in bs for part in pair]
    nb = len(flat)
    half_n = geo.P // 2
    if not geo.direct:

        def pick(a):
            cols = a.reshape(n, geo.P, 2, geo.R)
            cols = jnp.where(scal[1] == 0, cols[:, :, 0], cols[:, :, 1])
            return cols.reshape(n, pr).T

        a_own, a_other = pick(a_own), pick(a_other)

    def kernel(s, a_ref, ao_ref, *refs):
        b_refs, outs = refs[:nb], refs[nb:]
        if geo.direct:
            outs, ats = outs[:-2], outs[-2:]
        else:
            ats = (a_ref, ao_ref)
        j = pl.program_id(0)

        if geo.direct:

            @pl.when(j == 0)
            def _():
                for ref, at in ((a_ref, ats[0]), (ao_ref, ats[1])):
                    flip = ref[...].T
                    for p in range(geo.P):
                        even = flip[2 * p * geo.R : (2 * p + 1) * geo.R]
                        odd = flip[(2 * p + 1) * geo.R : (2 * p + 2) * geo.R]
                        at[p * geo.R : (p + 1) * geo.R, :] = jnp.where(s[1] == 0, even, odd)

        plane = 0
        for at in range(nb // 2):
            own, other = b_refs[2 * at], b_refs[2 * at + 1]
            for q in range(own.shape[1]):
                full = dotg(ats[0][...], own[0, q], 1, 0) + dotg(ats[1][...], other[0, q], 1, 0)
                full = full.astype(BF)
                if not geo.direct:
                    outs[0][0, plane] = full
                else:
                    for half in range(2):

                        @pl.when((j < th) if half == 0 else (j >= th))
                        def _():
                            for i, rel in enumerate(geo.order[half]):
                                src = s[0] ^ rel
                                ref = outs[2 * half + i // half_n]
                                for p in range(geo.P):

                                    @pl.when(src == p)
                                    def _():
                                        ref[i % half_n, 0, plane] = full[
                                            p * geo.R : (p + 1) * geo.R
                                        ]

                plane += 1

    if geo.direct:
        a_block = (half_n, 1, planes, geo.R, w)
        specs = [
            pl.BlockSpec(a_block, lambda j, s: (0, jnp.minimum(j, th - 1), 0, 0, 0)),
            pl.BlockSpec(a_block, lambda j, s: (0, jnp.minimum(j, th - 1), 0, 0, 0)),
            pl.BlockSpec(a_block, lambda j, s: (0, jnp.maximum(j - th, 0), 0, 0, 0)),
            pl.BlockSpec(a_block, lambda j, s: (0, jnp.maximum(j - th, 0), 0, 0, 0)),
        ]
        shapes = [jax.ShapeDtypeStruct((half_n, th, planes, geo.R, w), BF)] * 4
        scratch = [pltpu.VMEM((pr, n), BF)] * 2
    else:
        specs = [pl.BlockSpec((1, planes, pr, w), lambda j, s: (j, 0, 0, 0))]
        shapes = [jax.ShapeDtypeStruct((geo.T, planes, pr, w), BF)]
        scratch = []

    got = pl.pallas_call(
        kernel,
        grid_spec=pltpu.PrefetchScalarGridSpec(
            num_scalar_prefetch=1,
            grid=(geo.T,),
            in_specs=[
                whole(a_own.shape),
                whole(a_other.shape),
                *[
                    pl.BlockSpec((1,) + b.shape[1:], lambda j, s: (j, 0, 0, 0))
                    for b in flat
                ],
            ],
            out_specs=specs,
            scratch_shapes=scratch,
        ),
        out_shape=shapes,
        compiler_params=params(),
        cost_estimate=cost(
            4 * pr * n * w * planes * geo.T, 2 * geo.T * planes * w * (pr + 2 * n)
        ),
        name=name,
    )(scal, a_own, a_other, *flat)
    if geo.direct:
        return got
    blocks = got[0].reshape(geo.T, planes, geo.P, geo.R, w)
    out = []
    for half in range(2):
        part = blocks[half * th : (half + 1) * th]
        part = reorder(part, [scal[0] ^ rel for rel in geo.order[half]], 2)
        part = part.transpose(2, 0, 1, 3, 4)
        out += [part[:half_n], part[half_n:]]
    return out


def body(
    latents,
    conditioning,
    mod_weight,
    mod_bias,
    in_weight,
    query_value_bias,
    out_weight,
    branch_bias,
    up_weight,
    up_bias,
    down_weight,
    cotangent,
):
    images, row_count, width = latents.shape
    geo = Geo(lax.axis_size("fsdp"), lax.axis_size("tensor"), width)
    F, T = geo.F, geo.T
    assert 2 * images == T
    highest = lax.Precision.HIGHEST
    fi = lax.axis_index("fsdp")
    ti = lax.axis_index("tensor")
    pair, core = fi // 2, fi % 2
    scal = jnp.stack([pair, core, ti]).astype(jnp.int32)
    cols = in_weight.shape[2]
    units = up_weight.shape[1]

    def places(k):
        return [
            ((2 * p + c) * T + t, (2 * p + t // images) * T + c * images + (t % images + k) % images)
            for p in range(geo.P)
            for c in range(2)
            for t in range(T)
        ]

    def to_chip(arr):
        got = []
        for k in range(images):
            item = lax.dynamic_index_in_dim(arr, (ti + k) % images, 0, keepdims=False)
            got.append(lax.ppermute(item, BOTH, places(k)))
        return jnp.concatenate(got)

    def from_chip(arr):
        got = []
        for k in range(images):
            back = [(dst, src) for src, dst in places(k)]
            got.append(lax.ppermute(arr[k * row_count : (k + 1) * row_count], BOTH, back))
        return reorder(jnp.stack(got), [(i - ti) % images for i in range(images)])

    attn_shard = jnp.concatenate([in_weight, out_weight.T[None]])
    attn_halves = gather_weight(attn_shard, geo)
    x = to_chip(latents)
    up_halves = gather_weight(up_weight[None], geo)
    down_halves = gather_weight(down_weight.T[None], geo)
    cot = to_chip(cotangent)

    info = jnp.concatenate([conditioning.reshape(-1), query_value_bias.reshape(-1), up_bias])
    info = lax.all_gather(info, BOTH, axis=0).reshape(F, T, -1)
    cond_all = info[:, 0, : images * width].reshape(F * images, width)
    qv_bias = info[0, :, images * width : images * width + 2 * cols].reshape(T, 2, 1, cols)
    unit_bias = info[0, :, images * width + 2 * cols :].reshape(T, 1, units).astype(F32)
    triple_bias = jnp.stack(
        [qv_bias[:, 0], jnp.zeros_like(qv_bias[:, 0]), qv_bias[:, 1]], axis=1
    ).astype(F32)
    silu_low = jax.nn.silu(cond_all.astype(F32)).astype(BF)
    silu_own = lax.dynamic_slice_in_dim(silu_low, fi * geo.R, geo.R, 1)
    mod_part = jnp.einsum("bd,dcj->bcj", silu_own, mod_weight, preferred_element_type=F32)
    mod_part += jnp.where(fi == 0, mod_bias.astype(F32), 0.0)
    mod_part = mod_part.reshape(geo.P, 1, T, 6, cols)
    mod_part = jnp.broadcast_to(mod_part, (geo.P, 2, T, 6, cols)).reshape(F * T, 6, cols)
    mod_part = lax.all_to_all(mod_part, BOTH, 0, 0, tiled=True)
    mod = mod_part.reshape(F, T, 6, cols).sum(axis=0).transpose(1, 0, 2).reshape(6, width)

    w_attn = Gathered(attn_halves, geo, scal)
    w_up = Gathered(up_halves, geo, scal)
    w_down = Gathered(down_halves, geo, scal)
    bias_rows = branch_bias.astype(F32)

    h1, q, kv = in_proj(scal, x, mod, w_attn, triple_bias, geo)
    kvo = flip_core(kv, geo)
    h1o = flip_core(h1, geo)
    mixed, lse = attn_fwd(q, kv, kvo)
    mixed_o = flip_core(mixed, geo)
    attn, resid, h2 = out_proj(scal, mixed, x, mod, bias_rows[0:1], w_attn, geo)
    h2o = flip_core(h2, geo)
    hidden, gp = up_proj(scal, h2, unit_bias, w_up, geo)
    hidden_o = flip_core(hidden, geo)
    ffn_grad = (cot.astype(F32) * mod[5]).astype(BF)
    ffn_sum = jnp.sum(ffn_grad.astype(F32), axis=0)
    ffn_o = flip_core(ffn_grad, geo)
    block_rows, ffn_sums = down_proj(scal, hidden, resid, cot, mod, bias_rows[1:2], w_down, geo)
    block_out = from_chip(block_rows)

    down_grad = scatter_grad(
        weight_grad(scal, ffn_grad, ffn_o, [(hidden[:, None], hidden_o[:, None])], geo, "w_down"),
        geo,
    )
    pre, unit_sum = pre_back(scal, ffn_grad, gp, w_down, geo)
    pre_o = flip_core(pre, geo)
    up_grad = scatter_grad(
        weight_grad(scal, h2, h2o, [(pre[:, None], pre_o[:, None])], geo, "w_up"), geo
    )
    rg, ag, mid_sums = second_back(scal, pre, resid, attn, cot, mod, w_up, geo)
    ag_o = flip_core(ag, geo)
    out_grad = scatter_grad(
        weight_grad(scal, ag, ag_o, [(mixed[:, None], mixed_o[:, None])], geo, "w_out"), geo
    )
    mg = mixed_back(scal, ag, w_attn, geo)
    dq, dkv, dkv_send, tri_sums = attn_bwd(q, kv, kvo, mixed, mg, lse)
    dq_o = flip_core(dq, geo)
    dkv = (dkv.astype(F32) + flip_core(dkv_send, geo).astype(F32)).astype(BF)
    dkv_o = flip_core(dkv, geo)
    in_grad = scatter_grad(
        weight_grad(scal, h1, h1o, [(dq[:, None], dq_o[:, None]), (dkv, dkv_o)], geo, "w_in"), geo
    )
    latent_rows, first_sums = first_back(scal, dq, dkv, x, rg, mod, w_attn, geo)
    latent_grad = from_chip(latent_rows)

    mine = [i ^ ti for i in range(T)]
    bias_pack = jnp.concatenate(
        [
            mid_sums[3].sum(axis=0),
            ffn_sum,
            reorder(unit_sum, mine).reshape(-1),
            reorder(tri_sums, mine).reshape(-1),
        ]
    )
    bias_total = lax.psum(bias_pack, BOTH)
    branch_grad = bias_total[: 2 * width].reshape(2, width)
    unit_grad = lax.dynamic_index_in_dim(
        bias_total[2 * width : 2 * width + T * units].reshape(T, units), ti, 0, keepdims=False
    )
    pair_grad = lax.dynamic_index_in_dim(
        bias_total[2 * width + T * units :].reshape(T, 2, cols), ti, 0, keepdims=False
    )

    rows = jnp.concatenate(
        [first_sums.sum(axis=1), mid_sums[:3].sum(axis=1), ffn_sums.sum(axis=0, keepdims=True)]
    )
    rows = lax.all_gather(rows, BOTH, axis=0)
    rows = rows.reshape(geo.P, 2, T, 6, width).sum(axis=1).reshape(F * images, 6, width)
    mine_rows = lax.dynamic_slice_in_dim(rows, ti * cols, cols, 2)
    mod_weight_grad = jnp.einsum(
        "bd,bcj->dcj", silu_own.astype(F32), mine_rows, precision=highest
    )
    mod_bias_grad = mine_rows.sum(axis=0)
    cond_part = jnp.einsum("bcj,dcj->bd", mine_rows, mod_weight.astype(F32), precision=highest)
    cond_all_parts = lax.all_gather(cond_part, BOTH, axis=0).reshape(F, T, F * images, geo.R)
    cond_mine = lax.dynamic_slice_in_dim(cond_all_parts.sum(axis=1), fi * images, images, 1)
    silu_grad = cond_mine.transpose(1, 0, 2).reshape(images, width)
    cond_f = conditioning.astype(F32)
    sig = jax.nn.sigmoid(cond_f)
    cond_grad = silu_grad * (sig * (1.0 + cond_f * (1.0 - sig)))

    return (
        block_out,
        latent_grad,
        cond_grad,
        mod_weight_grad,
        mod_bias_grad,
        in_grad,
        pair_grad,
        out_grad[0].T,
        branch_grad,
        up_grad[0],
        unit_grad,
        down_grad[0].T,
    )


def solution(mesh):
    in_specs = (
        P("fsdp", "tensor", None),
        P("fsdp", None),
        P("fsdp", None, "tensor"),
        P(None, "tensor"),
        P(None, "fsdp", "tensor"),
        P(None, "tensor"),
        P("tensor", "fsdp"),
        P(),
        P("fsdp", "tensor"),
        P("tensor"),
        P("tensor", "fsdp"),
        P("fsdp", "tensor", None),
    )
    out_specs = (
        P("fsdp", "tensor", None),
        P("fsdp", "tensor", None),
        P("fsdp", None),
        P("fsdp", None, "tensor"),
        P(None, "tensor"),
        P(None, "fsdp", "tensor"),
        P(None, "tensor"),
        P("tensor", "fsdp"),
        P(),
        P("fsdp", "tensor"),
        P("tensor"),
        P("tensor", "fsdp"),
    )
    return jax.shard_map(body, mesh=mesh, in_specs=in_specs, out_specs=out_specs, check_vma=False)
```

time: 1840 us -> 1110 us (0.60)
  waiting for transfers between devices: 1270 us -> 446 us
  matrix products: 252 us -> 3.45 us
  Pallas kernels: 0 us -> 240 us
  starting transfers between devices: 3.46 us -> 111 us
  other arithmetic: 115 us -> 39 us
  blocking collectives: 110 us -> 183 us
    all_gather x24 -> x0, waiting for transfers between devices: 748 us -> none  [the longest x4 149 us: fetch(): lax.all_gather(shards[4], 'fsdp', axis=0, tiled=True)]
    reduce_scatter x10 -> x0, waiting for transfers between devices: 463 us -> none  [the longest x2 94.1 us: one_image(): lax.psum_scatter(jnp.dot(piece, down_w, preferred_element_type=jnp.float3...]
    ppermute x0 -> x76, waiting for transfers between devices: none -> 315 us  [the longest x17 150 us: flip_tensor(): return lax.ppermute(x, 'tensor', [(i, i ^ k) for i in range(geo.T)])]
    dot_general x40 -> x3, matrix products: 252 us -> 3.45 us  [the longest x1 2.6 us: body(): jnp.einsum('bd,bcj->dcj', silu_own.astype(F32), mine_rows, precision=high...]
    pallas_call x0 -> x14, Pallas kernels: none -> 240 us  [the longest x4 51.4 us: weight_grad(): pl.pallas_call(kernel, grid_spec=pltpu.PrefetchScalarGridSpec(num_scalar_...]
    ppermute x0 -> x76, starting transfers between devices: none -> 107 us  [the longest x28 36 us: flip_pair(): return lax.ppermute(x, 'fsdp', [(i, i ^ 2 * bit) for i in range(geo.F)])]
    all_gather x6 -> x2, blocking collectives: 73 us -> 143 us  [the longest x1 71.9 us: body(): lax.all_gather(cond_part, BOTH, axis=0).reshape(F, T, F * images, geo.R)]
    unnamed x8 -> x2, waiting for transfers between devices: 53.3 us -> 122 us
  transfers between devices with their start and end apart: 39 -> 78, of which waited for: 34 -> 33; matrix products, arithmetic and copies ran while one was open for 13% -> 9% of each run, Pallas kernels for 0% -> 21%
where the time goes in v1:
time: 1110 us; the launch traced here: 1100 us
  waiting for transfers between devices  446 us (40%)
  Pallas kernels  240 us (22%)
  blocking collectives  183 us (16%)
  starting transfers between devices  111 us (10%)
  local copies, waits for them, and re-layouts  57.2 us (5%)
  other arithmetic  39 us (4%)
  between operations  15.4 us (1%)
    ppermute x17, waiting for transfers between devices, flip_tensor(): return lax.ppermute(x, 'tensor', [(i, i ^ k) for i in range(geo.T)])  150 us
    ppermute x28, waiting for transfers between devices, flip_pair(): return lax.ppermute(x, 'fsdp', [(i, i ^ 2 * bit) for i in range(geo.F)])  142 us
    unnamed x2, waiting for transfers between devices  122 us
    all_gather x1, blocking collectives, body(): lax.all_gather(cond_part, BOTH, axis=0).reshape(F, T, F * images, geo.R)  71.9 us
    all_gather x1, blocking collectives, body(): rows = lax.all_gather(rows, BOTH, axis=0)  71.2 us
    pallas_call x4, Pallas kernels, weight_grad(): pl.pallas_call(kernel, grid_spec=pltpu.PrefetchScalarGridSpec(num_scalar_...  51.4 us
    psum x1, blocking collectives, body(): bias_total = lax.psum(bias_pack, BOTH)  40.2 us
    ppermute x28, starting transfers between devices, flip_pair(): return lax.ppermute(x, 'fsdp', [(i, i ^ 2 * bit) for i in range(geo.F)])  36 us
  transfers between devices with their start and end apart: 78, of which 33 were waited for; matrix products, arithmetic and copies ran while one was open for 9% of the time, Pallas kernels for 21%

profile of v1, /device:TPU:10, one launch (start us, length us, event | category | flops | bytes accessed | tf_op | source)
XLA Modules:
  0.0 1095.8 jit_solution(897861764114080228)
XLA Ops:
  22.3 19.3 %collective-permute-done.8 = bf16[4,144,288]{2,1,0:T(8,128)(2,1)S(1)} collective-permute-done((bf16[4,144,288]{2,1,0:T(8,128)(2,1)S(1)}, bf16[4,144,288]{2,1,0:T(8,128)(2,1)S(1)}, u32[]{:S(2)}, u32[]{:S(2)}) %collective-permute-start.8) | collective-permute-done | bytes 331808 | tf_op jit(solution)/shard_map/ppermute | solution.py:57
  51.9 20.1 %collective-permute-done.9 = bf16[1,2,4,144,288]{4,3,2,1,0:T(8,128)(2,1)S(1)} collective-permute-done((bf16[1,2,4,144,288]{4,3,2,1,0:T(8,128)(2,1)S(1)}, bf16[1,2,4,144,288]{4,3,2,1,0:T(8,128)(2,1)S(1)}, u32[]{:S(2)}, u32[]{:S(2)}) %collective-permute-start.9) | collective-permute-done | bytes 663584 | tf_op jit(solution)/shard_map/ppermute | solution.py:49
  89.3 122.5 %all-reduce.3.cloned.1.call-done = bf16[129024]{0:T(1024)(128)(2,1)} async-done(((bf16[129024]{0:T(1024)(128)(2,1)}), bf16[129024]{0:T(1024)(128)(2,1)}) %all-reduce.3.cloned.1.call-update) | async-done | bytes 258064
  249.5 20.2 %in_proj.1 = (bf16[512,1152]{1,0:T(8,128)(2,1)}, bf16[4,512,288]{2,1,0:T(8,128)(2,1)}, bf16[4,2,512,288]{3,2,1,0:T(8,128)(2,1)}) custom-call(s32[3]{0:T(128)} %pad_add_fusion.s, bf16[512,1152]{1,0:T(8,128)(2,1)} %copy-done.2, f32[6,1152]{1,0:T(8,128)} %reshape.255.m_ref, f32[4,3,1,288]{3,2,1,0:T(1,128)} %maximum_convert_fusion.b_ref, ...), custom_call_target="tpu_custom_call" | custom-call | flops 4076863488 | bytes 12681216 | tf_op jit(solution)/shard_map/in_proj/pallas_call | solution.py:215
  324.3 15.6 %collective-permute-done.26 = bf16[256,1152]{1,0:T(8,128)(2,1)S(1)} collective-permute-done((bf16[256,1152]{1,0:T(8,128)(2,1)S(1)}, bf16[256,1152]{1,0:T(8,128)(2,1)S(1)}, u32[]{:S(2)}, u32[]{:S(2)}) %collective-permute-start.26) | collective-permute-done | bytes 589856 | tf_op jit(solution)/shard_map/ppermute | solution.py:825
  359.1 19.3 %collective-permute-done.29 = bf16[2,2,1,144,1152]{4,3,1,2,0:T(8,128)(2,1)} collective-permute-done((bf16[2,2,1,144,1152]{4,3,1,2,0:T(8,128)(2,1)}, bf16[2,2,1,144,1152]{4,3,1,2,0:T(8,128)(2,1)}, u32[]{:S(2)}, u32[]{:S(2)}) %collective-permute-start.29) | collective-permute-done | bytes 1327136 | tf_op jit(solution)/shard_map/ppermute | solution.py:49
  384.2 17.7 %attn_fwd.1 = (bf16[4,512,288]{2,1,0:T(8,128)(2,1)}, f32[4,4,512]{2,1,0:T(4,128)}) custom-call(bf16[4,512,288]{2,1,0:T(8,128)(2,1)} %get-tuple-element.51.q_ref, bf16[4,2,512,288]{3,2,1,0:T(8,128)(2,1)} %get-tuple-element.52.kv_ref, bf16[4,2,512,288]{3,2,1,0:T(8,128)(2,1)} %copy.292.kvo_ref), custom_call_target="tpu_custom_call" | custom-call | flops 30000001024 | bytes 8257536 | tf_op jit(solution)/shard_map/attn_fwd/pallas_call | solution.py:270
  404.3 16.5 %out_proj.1 = (f32[512,1152]{1,0:T(8,128)}, f32[512,1152]{1,0:T(8,128)}, bf16[512,1152]{1,0:T(8,128)(2,1)}) custom-call(s32[3]{0:T(128)} %pad_add_fusion.s, bf16[4,512,288]{2,1,0:T(8,128)(2,1)} %get-tuple-element.53.y_ref.o_ref, bf16[512,1152]{1,0:T(8,128)(2,1)} %copy-done.2, f32[6,1152]{1,0:T(8,128)} %reshape.255.m_ref, ...), custom_call_target="tpu_custom_call" | custom-call | flops 1358954496 | bytes 10911744 | tf_op jit(solution)/shard_map/out_proj/pallas_call | solution.py:373
  421.9 18.8 %up_proj.1 = (bf16[4,512,1152]{2,1,0:T(8,128)(2,1)}, bf16[4,512,1152]{2,1,0:T(8,128)(2,1)}) custom-call(s32[3]{0:T(128)} %pad_add_fusion.s, bf16[512,1152]{1,0:T(8,128)(2,1)} %get-tuple-element.54.h_ref.a_ref, f32[4,1,1152]{2,1,0:T(1,128)} %fusion.20.b_ref, bf16[2,2,1,144,1152]{4,3,2,1,0:T(8,128)(2,1)} %get-tuple-element.97.refs_0_, ...), custom_call_target="tpu_custom_call" | custom-call | flops 5435817984 | bytes 20054016 | tf_op jit(solution)/shard_map/up_proj/pallas_call | solution.py:420
  441.8 14.5 %pre_back.1 = (bf16[4,512,1152]{2,1,0:T(8,128)(2,1)}, f32[4,1,1152]{2,1,0:T(1,128)}) custom-call(s32[3]{0:T(128)} %pad_add_fusion.s, bf16[512,1152]{1,0:T(8,128)(2,1)} %get-tuple-element.91.g_ref.a_ref, bf16[4,512,1152]{2,1,0:T(8,128)(2,1)} %get-tuple-element.58.gp_ref, bf16[2,2,1,144,1152]{4,3,2,1,0:T(8,128)(2,1)} %get-tuple-element.95.refs_0_, ...), custom_call_target="tpu_custom_call" | custom-call | flops 5435817984 | bytes 20054016 | tf_op jit(solution)/shard_map/pre_back/pallas_call | solution.py:509
  456.9 26.3 %second_back.1 = (f32[512,1152]{1,0:T(8,128)}, bf16[512,1152]{1,0:T(8,128)(2,1)}, f32[4,8,1152]{2,1,0:T(8,128)}) custom-call(s32[3]{0:T(128)} %pad_add_fusion.s, bf16[4,512,1152]{2,1,0:T(8,128)(2,1)} %get-tuple-element.59.y_ref, f32[512,1152]{1,0:T(8,128)} %get-tuple-element.56.r_ref, f32[512,1152]{1,0:T(8,128)} %get-tuple-element.60.a_ref, ...), custom_call_target="tpu_custom_call" | custom-call | flops 5435817984 | bytes 25952256 | tf_op jit(solution)/shard_map/second_back/pallas_call | solution.py:564
  491.0 25.7 %attn_bwd.1 = (bf16[4,512,288]{2,1,0:T(8,128)(2,1)}, bf16[4,2,512,288]{3,2,1,0:T(8,128)(2,1)}, bf16[4,2,512,288]{3,2,1,0:T(8,128)(2,1)}, f32[4,2,288]{2,1,0:T(2,128)}) custom-call(bf16[4,512,288]{2,1,0:T(8,128)(2,1)} %get-tuple-element.51.q_ref, bf16[4,2,512,288]{3,2,1,0:T(8,128)(2,1)} %get-tuple-element.52.kv_ref, bf16[4,2,512,288]{3,2,1,0:T(8,128)(2,1)} %copy.292.kvo_ref, ...), custom_call_target="tpu_custom_call" | custom-call | flops 49999998976 | bytes 14155776 | tf_op jit(solution)/shard_map/attn_bwd/pallas_call | solution.py:325
  521.6 16.0 %down_proj.1 = (bf16[512,1152]{1,0:T(8,128)(2,1)}, f32[8,1152]{1,0:T(8,128)}) custom-call(s32[3]{0:T(128)} %pad_add_fusion.s, bf16[4,512,1152]{2,1,0:T(8,128)(2,1)} %get-tuple-element.55.y_ref, f32[512,1152]{1,0:T(8,128)} %get-tuple-element.56.r_ref, bf16[512,1152]{1,0:T(8,128)(2,1)} %copy-done.3, f32[6,1152]{1,0:T(8,128)} %reshape.255.m_ref, ...), custom_call_target="tpu_custom_call" | custom-call | flops 5435817984 | bytes 20054016 | tf_op jit(solution)/shard_map/down_proj/pallas_call | solution.py:469
  541.5 40.2 %psum.7 = f32[9216]{0:T(1024)S(1)} all-reduce(f32[9216]{0:T(1024)S(1)} %pad_maximum_fusion.9), channel_id=1, replica_groups=mesh['fsdp'=8,'tensor'=4] {'fsdp','tensor'}, use_global_device_ids=true, to_apply=%region_9.10 | all-reduce | flops 9216 | bytes 73728 | tf_op jit(solution)/shard_map/psum | solution.py:913
  658.1 25.2 %first_back.1 = (bf16[512,1152]{1,0:T(8,128)(2,1)}, f32[2,8,1152]{2,1,0:T(8,128)}) custom-call(s32[3]{0:T(128)} %pad_add_fusion.s, bf16[4,512,288]{2,1,0:T(8,128)(2,1)} %get-tuple-element.63.q_ref, bf16[4,2,512,288]{3,2,1,0:T(8,128)(2,1)} %add_convert_fusion.kv_ref.refs_2_, bf16[512,1152]{1,0:T(8,128)(2,1)} %copy-done.2, ...), custom_call_target="tpu_custom_call" | custom-call | flops 4076863488 | bytes 17399808 | tf_op jit(solution)/shard_map/first_back/pallas_call | solution.py:651
  692.5 71.2 %all-gather.3 = f32[32,6,1152]{2,1,0:T(8,128)S(1)} all-gather(f32[1,6,1152]{2,1,0:T(8,128)S(1)} %maximum_bitcast_fusion.6), channel_id=3, replica_groups=mesh['fsdp'=8,'tensor'=4] {'fsdp','tensor'}, dimensions={0}, use_global_device_ids=true | all-gather | bytes 912384 | tf_op jit(solution)/shard_map/all_gather | solution.py:925
  770.3 71.9 %all-gather.2 = f32[512,144]{1,0:T(8,128)S(1)} all-gather(f32[16,144]{1,0:T(8,128)S(1)} %convolution_bitcast_fusion), channel_id=4, replica_groups=mesh['fsdp'=8,'tensor'=4] {'fsdp','tensor'}, dimensions={0}, use_global_device_ids=true | all-gather | bytes 304128 | tf_op jit(solution)/shard_map/all_gather | solution.py:933
  856.8 16.3 %w_in.1 = (bf16[2,2,3,144,288]{4,3,2,1,0:T(8,128)(2,1)}, bf16[2,2,3,144,288]{4,3,2,1,0:T(8,128)(2,1)}, bf16[2,2,3,144,288]{4,3,2,1,0:T(8,128)(2,1)}, bf16[2,2,3,144,288]{4,3,2,1,0:T(8,128)(2,1)}) custom-call(s32[3]{0:T(128)} %pad_add_fusion.s, bf16[512,1152]{1,0:T(8,128)(2,1)} %get-tuple-element.71.a_ref, bf16[512,1152]{1,0:T(8,128)(2,1)} %collective-permute-done.43.ao_ref, ...), custom_call_target="tpu_custom_call" | custom-call | flops 4076863488 | bytes 11059200 | tf_op jit(solution)/shard_map/w_in/pallas_call | solution.py:752
  897.1 13.6 %w_down.1 = (bf16[2,2,1,144,1152]{4,3,2,1,0:T(8,128)(2,1)}, bf16[2,2,1,144,1152]{4,3,2,1,0:T(8,128)(2,1)}, bf16[2,2,1,144,1152]{4,3,2,1,0:T(8,128)(2,1)}, bf16[2,2,1,144,1152]{4,3,2,1,0:T(8,128)(2,1)}) custom-call(s32[3]{0:T(128)} %pad_add_fusion.s, bf16[512,1152]{1,0:T(8,128)(2,1)} %get-tuple-element.91.g_ref.a_ref, ...), custom_call_target="tpu_custom_call" | custom-call | flops 5435817984 | bytes 14745600 | tf_op jit(solution)/shard_map/w_down/pallas_call | solution.py:752
  915.2 24.1 %collective-permute-done.64 = bf16[2,2,1,144,1152]{4,3,2,1,0:T(8,128)(2,1)S(1)} collective-permute-done((bf16[2,2,1,144,1152]{4,3,2,1,0:T(8,128)(2,1)}, bf16[2,2,1,144,1152]{4,3,2,1,0:T(8,128)(2,1)S(1)}, u32[]{:S(2)}, u32[]{:S(2)}) %collective-permute-start.64) | collective-permute-done | bytes 1327136 | tf_op jit(solution)/shard_map/ppermute | solution.py:49
  943.5 24.3 %collective-permute-done.72 = bf16[2,2,1,144,1152]{4,3,2,1,0:T(8,128)(2,1)S(1)} collective-permute-done((bf16[2,2,1,144,1152]{4,3,2,1,0:T(8,128)(2,1)}, bf16[2,2,1,144,1152]{4,3,2,1,0:T(8,128)(2,1)S(1)}, u32[]{:S(2)}, u32[]{:S(2)}) %collective-permute-start.72) | collective-permute-done | bytes 1327136 | tf_op jit(solution)/shard_map/ppermute | solution.py:49
  969.9 14.1 %collective-permute-done.49 = bf16[1,2,3,144,288]{4,3,2,1,0:T(8,128)(2,1)S(1)} collective-permute-done((bf16[1,2,3,144,288]{4,3,2,1,0:T(8,128)(2,1)S(1)}, bf16[1,2,3,144,288]{4,3,2,1,0:T(8,128)(2,1)S(1)}, u32[]{:S(2)}, u32[]{:S(2)}) %collective-permute-start.49) | collective-permute-done | bytes 497696 | tf_op jit(solution)/shard_map/ppermute | solution.py:49
  986.6 25.8 %collective-permute-done.50 = bf16[2,3,144,288]{3,2,1,0:T(8,128)(2,1)S(1)} collective-permute-done((bf16[2,3,144,288]{3,2,1,0:T(8,128)(2,1)S(1)}, bf16[2,3,144,288]{3,2,1,0:T(8,128)(2,1)S(1)}, u32[]{:S(2)}, u32[]{:S(2)}) %collective-permute-start.50) | collective-permute-done | bytes 497696 | tf_op jit(solution)/shard_map/ppermute | solution.py:57
  1029.2 31.1 %collective-permute-done.66 = bf16[2,1,144,1152]{3,2,0,1:T(8,128)(2,1)S(1)} collective-permute-done((bf16[2,1,144,1152]{3,2,0,1:T(8,128)(2,1)S(1)}, bf16[2,1,144,1152]{3,2,0,1:T(8,128)(2,1)S(1)}, u32[]{:S(2)}, u32[]{:S(2)}) %collective-permute-start.66) | collective-permute-done | bytes 663584 | tf_op jit(solution)/shard_map/ppermute | solution.py:57
  (347 shorter events, 369.8 us)
Async XLA Ops:
  7.2 204.6 %all-reduce.3.cloned.1.call-start = ((), (), s32[]{:S(2)}) async-start(), calls=%async_computation.1 | async-start | bytes 516096
  51.3 162.5 %collective-permute-start.4 = (bf16[2,2,4,144,288]{4,3,2,1,0:T(8,128)(2,1)S(1)}, bf16[2,2,4,144,288]{4,3,2,1,0:T(8,128)(2,1)}, u32[]{:S(2)}, u32[]{:S(2)}) collective-permute-start(bf16[2,2,4,144,288]{4,3,2,1,0:T(8,128)(2,1)S(1)} %pad_maximum_fusion.refs_0_), channel_id=1, source_target_pairs={{0,16},{4,20},{8,24},{12,28},{16,0},{20,4},{24,8},{28,12},{1,17},{... | collective-permute-start | bytes 3981320 | tf_op jit(solution)/shard_map/ppermute | solution.py:49
  73.7 140.2 %collective-permute-start.10 = (bf16[2,2,4,144,288]{4,3,2,1,0:T(8,128)(2,1)}, bf16[2,2,4,144,288]{4,3,2,1,0:T(8,128)(2,1)}, u32[]{:S(2)}, u32[]{:S(2)}) collective-permute-start(bf16[2,2,4,144,288]{4,3,2,1,0:T(8,128)(2,1)} %pad_maximum_fusion.1.refs_4_), channel_id=1, source_target_pairs={{0,8},{4,12},{8,0},{12,4},{16,24},{20,28},{24,16},{28,20},{1,9},{5... | collective-permute-start | bytes 3981320 | tf_op jit(solution)/shard_map/ppermute | solution.py:49
  76.6 143.0 %collective-permute-start = (bf16[256,1152]{1,0:T(8,128)(2,1)}, bf16[256,1152]{1,0:T(8,128)(2,1)}, u32[]{:S(2)}, u32[]{:S(2)}) collective-permute-start(bf16[256,1152]{1,0:T(8,128)(2,1)} %get-tuple-element.109), channel_id=1, source_target_pairs={{0,0},{1,1},{2,4},{3,5},{4,2},{5,3},{6,6},{7,7},{8,8},{9,9},{10,12... | collective-permute-start | bytes 1769480 | tf_op jit(solution)/shard_map/ppermute | solution.py:825
  83.9 129.4 %collective-permute-start.14 = (bf16[1,144,1152]{2,1,0:T(8,128)(2,1)S(1)}, bf16[1,144,1152]{2,1,0:T(8,128)(2,1)S(1)}, u32[]{:S(2)}, u32[]{:S(2)}) collective-permute-start(bf16[1,144,1152]{2,1,0:T(8,128)(2,1)S(1)} %bitcast.191), channel_id=1, source_target_pairs={{0,1},{1,0},{2,3},{3,2},{4,5},{5,4},{6,7},{7,6},{8,9},{9,8},{10,11... | collective-permute-start | bytes 995336 | tf_op jit(solution)/shard_map/ppermute | solution.py:57
  286.1 63.3 %collective-permute-start.13 = (bf16[4,2,512,288]{2,3,1,0:T(8,128)(2,1)}, bf16[4,2,512,288]{2,3,1,0:T(8,128)(2,1)}, u32[]{:S(2)}, u32[]{:S(2)}) collective-permute-start(bf16[4,2,512,288]{2,3,1,0:T(8,128)(2,1)} %copy.291), channel_id=1, source_target_pairs={{0,4},{4,0},{8,12},{12,8},{16,20},{20,16},{24,28},{28,24},{1,5},{5... | collective-permute-start | bytes 7077896 | tf_op jit(solution)/shard_map/ppermute | solution.py:53
  357.6 83.2 %collective-permute-start.30 = (bf16[2,2,1,144,1152]{4,3,1,2,0:T(8,128)(2,1)}, bf16[2,2,1,144,1152]{4,3,1,2,0:T(8,128)(2,1)S(1)}, u32[]{:S(2)}, u32[]{:S(2)}) collective-permute-start(bf16[2,2,1,144,1152]{4,3,1,2,0:T(8,128)(2,1)} %get-tuple-element.94), channel_id=1, source_target_pairs={{0,4},{4,0},{8,12},{12,8},{16,20},{20,16},{24,28},{28,24},{1,5},{5... | collective-permute-start | bytes 3981320 | tf_op jit(solution)/shard_map/ppermute | solution.py:53
  359.1 81.7 %collective-permute-start.36 = (bf16[2,2,1,144,1152]{4,3,2,1,0:T(8,128)(2,1)}, bf16[2,2,1,144,1152]{4,3,2,1,0:T(8,128)(2,1)}, u32[]{:S(2)}, u32[]{:S(2)}) collective-permute-start(bf16[2,2,1,144,1152]{4,3,2,1,0:T(8,128)(2,1)} %pad_maximum_fusion.5.refs_4_), channel_id=1, source_target_pairs={{0,4},{4,0},{8,12},{12,8},{16,20},{20,16},{24,28},{28,24},{1,5},{5... | collective-permute-start | bytes 3981320 | tf_op jit(solution)/shard_map/ppermute | solution.py:53
  381.3 59.5 %collective-permute-start.31 = (bf16[2,2,1,144,1152]{4,3,1,2,0:T(8,128)(2,1)}, bf16[2,2,1,144,1152]{4,3,1,2,0:T(8,128)(2,1)}, u32[]{:S(2)}, u32[]{:S(2)}) collective-permute-start(bf16[2,2,1,144,1152]{4,3,1,2,0:T(8,128)(2,1)} %collective-permute-done.29), channel_id=1, source_target_pairs={{0,4},{4,0},{8,12},{12,8},{16,20},{20,16},{24,28},{28,24},{1,5},{5... | collective-permute-start | bytes 3981320 | tf_op jit(solution)/shard_map/ppermute | solution.py:53
  384.2 56.6 %collective-permute-start.37 = (bf16[2,2,1,144,1152]{4,3,2,1,0:T(8,128)(2,1)}, bf16[2,2,1,144,1152]{4,3,2,1,0:T(8,128)(2,1)}, u32[]{:S(2)}, u32[]{:S(2)}) collective-permute-start(bf16[2,2,1,144,1152]{4,3,2,1,0:T(8,128)(2,1)} %collective-permute-done.35.refs_5_), channel_id=1, source_target_pairs={{0,4},{4,0},{8,12},{12,8},{16,20},{20,16},{24,28},{28,24},{1,5},{5... | collective-permute-start | bytes 3981320 | tf_op jit(solution)/shard_map/ppermute | solution.py:53
  456.3 426.1 %collective-permute-start.61 = (bf16[4,512,1152]{2,1,0:T(8,128)(2,1)}, bf16[4,512,1152]{2,1,0:T(8,128)(2,1)}, u32[]{:S(2)}, u32[]{:S(2)}) collective-permute-start(bf16[4,512,1152]{2,1,0:T(8,128)(2,1)} %get-tuple-element.59.y_ref), channel_id=1, source_target_pairs={{0,4},{4,0},{8,12},{12,8},{16,20},{20,16},{24,28},{28,24},{1,5},{5... | collective-permute-start | bytes 14155784 | tf_op jit(solution)/shard_map/ppermute | solution.py:53
  483.2 101.2 %collective-permute-start.52 = (bf16[512,1152]{1,0:T(8,128)(2,1)}, bf16[512,1152]{1,0:T(8,128)(2,1)}, u32[]{:S(2)}, u32[]{:S(2)}) collective-permute-start(bf16[512,1152]{1,0:T(8,128)(2,1)} %get-tuple-element.61.g_ref.a_ref), channel_id=1, source_target_pairs={{0,4},{4,0},{8,12},{12,8},{16,20},{20,16},{24,28},{28,24},{1,5},{5... | collective-permute-start | bytes 3538952 | tf_op jit(solution)/shard_map/ppermute | solution.py:53
  521.1 117.6 %collective-permute-start.40 = (bf16[4,2,512,288]{2,3,1,0:T(8,128)(2,1)}, bf16[4,2,512,288]{2,3,1,0:T(8,128)(2,1)}, u32[]{:S(2)}, u32[]{:S(2)}) collective-permute-start(bf16[4,2,512,288]{2,3,1,0:T(8,128)(2,1)} %copy.313), channel_id=1, source_target_pairs={{0,4},{4,0},{8,12},{12,8},{16,20},{20,16},{24,28},{28,24},{1,5},{5... | collective-permute-start | bytes 7077896 | tf_op jit(solution)/shard_map/ppermute | solution.py:53
  521.6 375.5 %collective-permute-start.69 = (bf16[4,512,1152]{2,1,0:T(8,128)(2,1)}, bf16[4,512,1152]{2,1,0:T(8,128)(2,1)}, u32[]{:S(2)}, u32[]{:S(2)}) collective-permute-start(bf16[4,512,1152]{2,1,0:T(8,128)(2,1)} %get-tuple-element.55.y_ref), channel_id=1, source_target_pairs={{0,4},{4,0},{8,12},{12,8},{16,20},{20,16},{24,28},{28,24},{1,5},{5... | collective-permute-start | bytes 14155784 | tf_op jit(solution)/shard_map/ppermute | solution.py:53
  632.8 53.0 %collective-permute-start.39 = (bf16[256,1152]{1,0:T(8,128)(2,1)}, bf16[256,1152]{1,0:T(8,128)(2,1)S(1)}, u32[]{:S(2)}, u32[]{:S(2)}) collective-permute-start(bf16[256,1152]{1,0:T(8,128)(2,1)} %get-tuple-element.104), channel_id=1, source_target_pairs={{1,0},{0,1},{5,2},{4,3},{3,4},{2,5},{7,6},{6,7},{9,8},{8,9},{13,10... | collective-permute-start | bytes 1769480 | tf_op jit(solution)/shard_map/ppermute | solution.py:832
  635.4 129.9 %collective-permute-start.38 = (bf16[256,1152]{1,0:T(8,128)(2,1)}, bf16[256,1152]{1,0:T(8,128)(2,1)S(1)}, u32[]{:S(2)}, u32[]{:S(2)}) collective-permute-start(bf16[256,1152]{1,0:T(8,128)(2,1)} %get-tuple-element.105), channel_id=1, source_target_pairs={{0,0},{1,1},{4,2},{5,3},{2,4},{3,5},{6,6},{7,7},{8,8},{9,9},{12,10... | collective-permute-start | bytes 1769480 | tf_op jit(solution)/shard_map/ppermute | solution.py:832
  653.1 197.3 %collective-permute-start.45 = (bf16[4,2,512,288]{2,3,1,0:T(8,128)(2,1)}, bf16[4,2,512,288]{2,3,1,0:T(8,128)(2,1)}, u32[]{:S(2)}, u32[]{:S(2)}) collective-permute-start(bf16[4,2,512,288]{2,3,1,0:T(8,128)(2,1)} %copy.319), channel_id=1, source_target_pairs={{0,4},{4,0},{8,12},{12,8},{16,20},{20,16},{24,28},{28,24},{1,5},{5... | collective-permute-start | bytes 7077896 | tf_op jit(solution)/shard_map/ppermute | solution.py:53
  686.6 155.7 %collective-permute-start.41 = (bf16[256,1152]{1,0:T(8,128)(2,1)}, bf16[256,1152]{1,0:T(8,128)(2,1)}, u32[]{:S(2)}, u32[]{:S(2)}) collective-permute-start(bf16[256,1152]{1,0:T(8,128)(2,1)} %get-tuple-element.101), channel_id=1, source_target_pairs={{0,0},{1,1},{4,2},{5,3},{2,4},{3,5},{6,6},{7,7},{8,8},{9,9},{12,10... | collective-permute-start | bytes 1769480 | tf_op jit(solution)/shard_map/ppermute | solution.py:832
  765.3 80.2 %collective-permute-start.42 = (bf16[256,1152]{1,0:T(8,128)(2,1)}, bf16[256,1152]{1,0:T(8,128)(2,1)}, u32[]{:S(2)}, u32[]{:S(2)}) collective-permute-start(bf16[256,1152]{1,0:T(8,128)(2,1)} %get-tuple-element.100), channel_id=1, source_target_pairs={{1,0},{0,1},{5,2},{4,3},{3,4},{2,5},{7,6},{6,7},{9,8},{8,9},{13,10... | collective-permute-start | bytes 1769480 | tf_op jit(solution)/shard_map/ppermute | solution.py:832
  910.7 57.1 %collective-permute-start.72 = (bf16[2,2,1,144,1152]{4,3,2,1,0:T(8,128)(2,1)}, bf16[2,2,1,144,1152]{4,3,2,1,0:T(8,128)(2,1)S(1)}, u32[]{:S(2)}, u32[]{:S(2)}) collective-permute-start(bf16[2,2,1,144,1152]{4,3,2,1,0:T(8,128)(2,1)} %get-tuple-element.89), channel_id=1, source_target_pairs={{0,8},{4,12},{8,0},{12,4},{16,24},{20,28},{24,16},{28,20},{1,9},{5... | collective-permute-start | bytes 3981320 | tf_op jit(solution)/shard_map/ppermute | solution.py:49
  912.7 73.3 %collective-permute-start.70 = (bf16[2,2,1,144,1152]{4,3,2,1,0:T(8,128)(2,1)}, bf16[2,2,1,144,1152]{4,3,2,1,0:T(8,128)(2,1)S(1)}, u32[]{:S(2)}, u32[]{:S(2)}) collective-permute-start(bf16[2,2,1,144,1152]{4,3,2,1,0:T(8,128)(2,1)} %get-tuple-element.87), channel_id=1, source_target_pairs={{0,16},{4,20},{8,24},{12,28},{16,0},{20,4},{24,8},{28,12},{1,17},{... | collective-permute-start | bytes 3981320 | tf_op jit(solution)/shard_map/ppermute | solution.py:49
  914.7 69.4 %collective-permute-start.49 = (bf16[1,2,3,144,288]{4,3,2,1,0:T(8,128)(2,1)S(1)}, bf16[1,2,3,144,288]{4,3,2,1,0:T(8,128)(2,1)S(1)}, u32[]{:S(2)}, u32[]{:S(2)}) collective-permute-start(bf16[1,2,3,144,288]{4,3,2,1,0:T(8,128)(2,1)S(1)} %add_convert_fusion.14), channel_id=1, source_target_pairs={{0,16},{4,20},{8,24},{12,28},{16,0},{20,4},{24,8},{28,12},{1,17},{... | collective-permute-start | bytes 1493000 | tf_op jit(solution)/shard_map/ppermute | solution.py:49
  941.5 74.7 %collective-permute-start.65 = (bf16[1,2,1,144,1152]{4,3,2,1,0:T(8,128)(2,1)S(1)}, bf16[1,2,1,144,1152]{4,3,2,1,0:T(8,128)(2,1)S(1)}, u32[]{:S(2)}, u32[]{:S(2)}) collective-permute-start(bf16[1,2,1,144,1152]{4,3,2,1,0:T(8,128)(2,1)S(1)} %add_convert_fusion.8), channel_id=1, source_target_pairs={{0,16},{4,20},{8,24},{12,28},{16,0},{20,4},{24,8},{28,12},{1,17},{... | collective-permute-start | bytes 1990664 | tf_op jit(solution)/shard_map/ppermute | solution.py:49
  1016.8 56.6 %collective-permute-start.74 = (bf16[2,1,144,1152]{3,2,0,1:T(8,128)(2,1)S(1)}, bf16[2,1,144,1152]{3,2,0,1:T(8,128)(2,1)S(1)}, u32[]{:S(2)}, u32[]{:S(2)}) collective-permute-start(bf16[2,1,144,1152]{3,2,0,1:T(8,128)(2,1)S(1)} %fusion.2), channel_id=1, source_target_pairs={{0,2},{1,3},{2,0},{3,1},{4,6},{5,7},{6,4},{7,5},{8,10},{9,11},{10,... | collective-permute-start | bytes 1990664 | tf_op jit(solution)/shard_map/ppermute | solution.py:57
  (95 other events, 2544.0 us)
Sparse Core Ops, SparseCore 0:
  84.0 127.7 all-reduce.2

commit v2 on v1

v2 whole, which is shorter than its diff:
```python
import functools

import jax
import jax.numpy as jnp
from jax import lax
from jax.experimental import pallas as pl
from jax.experimental.pallas import tpu as pltpu
from jax.sharding import PartitionSpec as P

HEAD_DIM = 72
EPS = 1e-06
TANH_C = 0.7978845608028654
CUBIC = 0.044715
LOG2E = 1.4426950408889634
VMEM_BYTES = 56 << 20
ROWS = 16
BF = jnp.bfloat16
F32 = jnp.float32
BOTH = ("fsdp", "tensor")


def dotg(a, b, ca, cb):
    return lax.dot_general(a, b, (((ca,), (cb,)), ((), ())), preferred_element_type=F32)


class Geo:
    def __init__(self, fsdp, tensor, dim):
        self.F, self.T, self.P = fsdp, tensor, fsdp // 2
        self.Th = tensor // 2
        self.D = dim
        self.R = dim // fsdp
        self.bits = [1 << b for b in range((self.P - 1).bit_length())]
        self.order = (self.orders(self.bits[::-1]), self.orders(self.bits))
        self.direct = self.R % 16 == 0

    @staticmethod
    def orders(msb_first):
        vals = [0]
        for bit in reversed(msb_first):
            vals = vals + [v | bit for v in vals]
        return vals


def reorder(x, index, axis=0):
    return jnp.stack([lax.dynamic_index_in_dim(x, i, axis, keepdims=False) for i in index], axis)


def flip_pair(x, bit, geo):
    return lax.ppermute(x, "fsdp", [(i, i ^ (2 * bit)) for i in range(geo.F)])


def flip_core(x, geo):
    return lax.ppermute(x, "fsdp", [(i, i ^ 1) for i in range(geo.F)])


def flip_tensor(x, k, geo):
    return lax.ppermute(x, "tensor", [(i, i ^ k) for i in range(geo.T)])


def after(value, *done):
    return lax.optimization_barrier((value, done))[0] if done else value


class Chain:
    def __init__(self, steps):
        self.steps = steps
        self.flight = next(steps)
        self.result = None

    def advance(self, *done):
        if self.result is not None:
            return []
        try:
            self.flight = self.steps.send(after(self.flight, *done))
        except StopIteration as end:
            self.flight, self.result = [], end.value
        return self.flight

    def finish(self, *done):
        while self.result is None:
            self.advance(*done)
        return self.result


def gather_steps(shard, geo):
    got = yield [flip_tensor(shard, k, geo) for k in range(1, geo.T)]
    parts = [shard] + got
    bufs = [jnp.stack(parts[h * geo.Th : (h + 1) * geo.Th])[None] for h in range(2)]
    for at in range(len(geo.bits)):
        bits = (geo.bits[at], geo.bits[-1 - at])
        got = yield [flip_pair(bufs[h], bits[h], geo) for h in range(2)]
        bufs = [jnp.concatenate(pair) for pair in zip(bufs, got)]
    got = yield [flip_core(b, geo) for b in bufs]
    return [[bufs[h], got[h]] for h in range(2)]


class Gathered:
    def __init__(self, halves, geo, scal):
        self.geo = geo
        if not geo.direct:
            fixed = []
            for half, arrays in enumerate(halves):
                at = [geo.order[half].index(rel) for rel in range(geo.P)]
                lookup = jnp.array(at, jnp.int32)
                blocks = jnp.concatenate(arrays)
                blocks = reorder(
                    blocks,
                    [
                        lookup[(f // 2) ^ scal[0]] + geo.P * ((f % 2) ^ scal[1])
                        for f in range(geo.F)
                    ],
                )
                _, th, r, w = blocks.shape
                fixed.append([blocks.transpose(1, 0, 2, 3).reshape(1, th, geo.D, w)])
            halves = fixed
        self.halves = halves
        self.arrays = halves[0] + halves[1]
        self.n = len(halves[0])
        self.width = self.arrays[0].shape[-1]

    def specs(self, half=None):
        th = self.geo.Th
        out = []
        for idx, a in enumerate(self.arrays if half is None else self.halves[half]):
            block = (a.shape[0], 1, a.shape[2], a.shape[3])
            if half is not None:
                out.append(pl.BlockSpec(block, lambda j, s: (0, j, 0, 0)))
            elif idx < self.n:
                out.append(pl.BlockSpec(block, lambda j, s: (0, jnp.minimum(j, th - 1), 0, 0)))
            else:
                out.append(pl.BlockSpec(block, lambda j, s: (0, jnp.maximum(j - th, 0), 0, 0)))
        return out

    def place(self, half, s_ref, refs, dst):
        geo = self.geo
        for at, ref in enumerate(refs):
            n, _, rows, _ = ref.shape
            for i in range(n):
                if geo.direct:
                    rel = geo.order[half][i]
                    row = 2 * (s_ref[0] ^ rel) + (s_ref[1] ^ at)
                    row = pl.multiple_of(row * rows, rows)
                else:
                    row = 0
                dst[pl.ds(row, rows), :] = ref[i, 0]

    def assemble(self, j, s_ref, refs, dst):
        for half in range(2):

            @pl.when((j < self.geo.Th) if half == 0 else (j >= self.geo.Th))
            def _():
                self.place(half, s_ref, refs[half * self.n : (half + 1) * self.n], dst)


def scatter_steps(pieces, geo):
    def add(a, b):
        return a.astype(F32) + b.astype(F32)

    keeps, sends = [pieces[0], pieces[2]], [pieces[1], pieces[3]]
    for at in range(len(geo.bits)):
        bits = (geo.bits[-1 - at], geo.bits[at])
        got = yield [flip_pair(sends[h], bits[h], geo) for h in range(2)]
        m = max(1, keeps[0].shape[0] // 2)
        if at < len(geo.bits) - 1:
            sends = [add(keeps[h][m:], got[h][m:]).astype(BF) for h in range(2)]
        keeps = [add(keeps[h][:m], got[h][:m]).astype(BF) for h in range(2)]
    units = [keep[0, k] for keep in keeps for k in range(geo.Th)]
    got = yield [flip_tensor(units[k], k, geo) for k in range(1, geo.T)]
    total = units[0].astype(F32)
    for part in got:
        total = total + part.astype(F32)
    return total


def params():
    return pltpu.CompilerParams(vmem_limit_bytes=VMEM_BYTES)


def cost(flops, size):
    return pl.CostEstimate(flops=int(flops), bytes_accessed=int(size), transcendentals=0)


def whole(shape):
    zeros = (0,) * len(shape)
    return pl.BlockSpec(shape, lambda j, s: zeros)


def padded(w):
    return -(-w // 128) * 128


def chunked(total, want):
    return want if total % want == 0 else total


def norm_of(v):
    centre = v - jnp.mean(v, axis=-1, keepdims=True)
    inv = lax.rsqrt(jnp.mean(centre * centre, axis=-1, keepdims=True) + EPS)
    return centre * inv, inv


def norm_back(norm, inv, g):
    return (
        g
        - jnp.mean(g, axis=-1, keepdims=True)
        - norm * jnp.mean(g * norm, axis=-1, keepdims=True)
    ) * inv


def fold_rows(v):
    return v.reshape(v.shape[0] // 8, 8, v.shape[1]).sum(axis=0)


def two_halves(block, th, tail):
    return [
        pl.BlockSpec(block, lambda j, s: (jnp.minimum(j, th - 1),) + tail),
        pl.BlockSpec(block, lambda j, s: (jnp.maximum(j - th, 0),) + tail),
    ]


def norm_mod(x, mod):
    n, d = x.shape

    def kernel(x_ref, m_ref, h_ref):
        @pl.loop(0, n // ROWS, unroll=4)
        def _(i):
            at = pl.ds(pl.multiple_of(i * ROWS, ROWS), ROWS)
            norm, _ = norm_of(x_ref[at, :].astype(F32))
            h_ref[at, :] = (norm * (1.0 + m_ref[1:2, :]) + m_ref[0:1, :]).astype(BF)

    return pl.pallas_call(
        kernel,
        out_shape=jax.ShapeDtypeStruct((n, d), BF),
        compiler_params=params(),
        cost_estimate=cost(20 * n * d, 4 * n * d),
        name="norm_mod",
    )(x, mod)


def in_proj(scal, h, wt, bias, w, half, geo):
    n, d = h.shape
    wp = padded(w)
    nw = wt.n

    def kernel(s, h_ref, b_ref, *refs):
        w_refs, (q_ref, kv_ref, wbuf) = refs[:nw], refs[nw:]
        wt.place(half, s, w_refs, wbuf)
        y = dotg(h_ref[...], wbuf[:, : 3 * w], 1, 0) + b_ref[0]
        y = y.astype(BF)
        q_ref[0, :, :w] = y[:, :w]
        kv_ref[0, 0, :, :w] = y[:, w : 2 * w]
        kv_ref[0, 1, :, :w] = y[:, 2 * w :]

    first = half * geo.Th
    return pl.pallas_call(
        kernel,
        grid_spec=pltpu.PrefetchScalarGridSpec(
            num_scalar_prefetch=1,
            grid=(geo.Th,),
            in_specs=[
                whole((n, d)),
                pl.BlockSpec((1, 1, 3 * w), lambda j, s: (s[2] ^ (j + first), 0, 0)),
                *wt.specs(half),
            ],
            out_specs=[
                pl.BlockSpec((1, n, wp), lambda j, s: (j, 0, 0)),
                pl.BlockSpec((1, 2, n, wp), lambda j, s: (j, 0, 0, 0)),
            ],
            scratch_shapes=[pltpu.VMEM((d, wt.width), BF)],
        ),
        out_shape=[
            jax.ShapeDtypeStruct((geo.Th, n, wp), BF),
            jax.ShapeDtypeStruct((geo.Th, 2, n, wp), BF),
        ],
        compiler_params=params(),
        cost_estimate=cost(6 * n * d * w * geo.Th, 8 * d * w * geo.Th + 8 * n * d),
        name="in_proj",
    )(scal, h, bias, *wt.halves[half])


def attn_fwd(q, kv, kvo, heads):
    z, n, w = q.shape
    used = heads * HEAD_DIM
    c = HEAD_DIM**-0.5 * LOG2E

    def kernel(q_ref, kv_ref, kvo_ref, o_ref, lse_ref):
        outs = []
        for h in range(heads):
            sl = slice(h * HEAD_DIM, (h + 1) * HEAD_DIM)
            qh = q_ref[0, :, sl]
            sa = dotg(kv_ref[0, 0, :, sl], qh, 1, 1) * c
            sb = dotg(kvo_ref[0, 0, :, sl], qh, 1, 1) * c
            top = jnp.maximum(
                jnp.max(sa, axis=0, keepdims=True), jnp.max(sb, axis=0, keepdims=True)
            )
            pa, pb = jnp.exp2(sa - top), jnp.exp2(sb - top)
            total = jnp.sum(pa, axis=0, keepdims=True) + jnp.sum(pb, axis=0, keepdims=True)
            o = dotg(kv_ref[0, 1, :, sl], pa.astype(BF), 0, 0)
            o = o + dotg(kvo_ref[0, 1, :, sl], pb.astype(BF), 0, 0)
            outs.append(o / total)
            lse_ref[0, h : h + 1, :] = top + jnp.log2(total)
        o_ref[0, :, :used] = jnp.concatenate(outs, axis=0).T.astype(BF)

    s3 = pl.BlockSpec((1, n, w), lambda j: (j, 0, 0))
    s4 = pl.BlockSpec((1, 2, n, w), lambda j: (j, 0, 0, 0))
    sl = pl.BlockSpec((1, heads, n), lambda j: (j, 0, 0))
    return pl.pallas_call(
        kernel,
        grid=(z,),
        in_specs=[s3, s4, s4],
        out_specs=[s3, sl],
        out_shape=[
            jax.ShapeDtypeStruct((z, n, w), BF),
            jax.ShapeDtypeStruct((z, heads, n), F32),
        ],
        compiler_params=params(),
        cost_estimate=cost(3e9 * z, 14 * z * n * w),
        name="attn_fwd",
    )(q, kv, kvo)


def attn_bwd(q, kv, kvo, o, do, lse, first):
    z, n, w = q.shape
    heads = lse.shape[1]
    used = heads * HEAD_DIM
    scale = HEAD_DIM**-0.5
    c = scale * LOG2E

    def kernel(q_ref, kv_ref, kvo_ref, o_ref, do_ref, lse_ref, dq_ref, dkv_ref, dkvo_ref, sum_ref):
        both = (do_ref[0, :, :used].astype(F32) * o_ref[0, :, :used].astype(F32)).T
        dqs, parts = [], [[[], []], [[], []]]
        for h in range(heads):
            sl = slice(h * HEAD_DIM, (h + 1) * HEAD_DIM)
            qh, doh = q_ref[0, :, sl], do_ref[0, :, sl]
            delta = jnp.sum(both[sl], axis=0, keepdims=True)
            lse_h = lse_ref[0, h : h + 1, :]
            dq = None
            for i, ref in enumerate((kv_ref, kvo_ref)):
                k, v = ref[0, 0, :, sl], ref[0, 1, :, sl]
                p = jnp.exp2(dotg(k, qh, 1, 1) * c - lse_h)
                ds = (p * (dotg(v, doh, 1, 1) - delta)).astype(BF)
                parts[i][1].append(dotg(doh, p.astype(BF), 0, 1))
                parts[i][0].append(dotg(qh, ds, 0, 1) * scale)
                got = dotg(k, ds, 0, 0)
                dq = got if dq is None else dq + got
            dqs.append(dq * scale)
        dq = jnp.concatenate(dqs, axis=0).T
        dq_ref[0, :, :used] = dq.astype(BF)
        sum_ref[0, 0:1, :] = jnp.sum(dq, axis=0, keepdims=True)
        dv_sum = None
        for i, ref in enumerate((dkv_ref, dkvo_ref)):
            for at in range(2):
                full = jnp.concatenate(parts[i][at], axis=0).T
                ref[0, at, :, :used] = full.astype(BF)
                if at == 1:
                    now = jnp.sum(full, axis=0, keepdims=True)
                    dv_sum = now if dv_sum is None else dv_sum + now
        sum_ref[0, 1:2, :] = dv_sum

    s3 = pl.BlockSpec((1, n, w), lambda j: (j, 0, 0))
    s4 = pl.BlockSpec((1, 2, n, w), lambda j: (j, 0, 0, 0))
    sl = pl.BlockSpec((1, heads, n), lambda j: (j, 0, 0))
    return pl.pallas_call(
        kernel,
        grid=(z,),
        in_specs=[s3, s4, s4, s3, pl.BlockSpec((1, n, w), lambda j: (j + first, 0, 0)), sl],
        out_specs=[s3, s4, s4, pl.BlockSpec((1, 2, used), lambda j: (j, 0, 0))],
        out_shape=[
            jax.ShapeDtypeStruct((z, n, w), BF),
            jax.ShapeDtypeStruct((z, 2, n, w), BF),
            jax.ShapeDtypeStruct((z, 2, n, w), BF),
            jax.ShapeDtypeStruct((z, 2, used), F32),
        ],
        compiler_params=params(),
        cost_estimate=cost(5e9 * z, 24 * z * n * w),
        name="attn_bwd",
    )(q, kv, kvo, o, do, lse)


def out_proj(scal, mixed, x, mod, bias, wt, geo):
    _, n, wp = mixed[0].shape
    w = wt.width // 4
    d = geo.D
    nw = len(wt.arrays)
    th = geo.Th

    def kernel(s, ya_ref, yb_ref, x_ref, m_ref, b_ref, *refs):
        w_refs, (attn_ref, resid_ref, h_ref, wbuf) = refs[:nw], refs[nw:]
        j = pl.program_id(0)
        wt.assemble(j, s, w_refs, wbuf)
        y = jnp.where(j < th, ya_ref[0, :, :w], yb_ref[0, :, :w])
        part = dotg(y, wbuf[:, 3 * w :], 1, 1)

        @pl.when(j == 0)
        def _():
            attn_ref[...] = part

        @pl.when(j > 0)
        def _():
            attn_ref[...] += part

        @pl.when(j == geo.T - 1)
        def _():
            @pl.loop(0, n // ROWS, unroll=4)
            def _(i):
                at = pl.ds(pl.multiple_of(i * ROWS, ROWS), ROWS)
                attn = attn_ref[at, :] + b_ref[...]
                attn_ref[at, :] = attn
                resid = x_ref[at, :].astype(F32) + m_ref[2:3, :] * attn
                resid_ref[at, :] = resid
                norm, _ = norm_of(resid)
                h_ref[at, :] = (norm * (1.0 + m_ref[4:5, :]) + m_ref[3:4, :]).astype(BF)

    return pl.pallas_call(
        kernel,
        grid_spec=pltpu.PrefetchScalarGridSpec(
            num_scalar_prefetch=1,
            grid=(geo.T,),
            in_specs=[
                *two_halves((1, n, wp), th, (0, 0)),
                whole((n, d)),
                whole(mod.shape),
                whole((1, d)),
                *wt.specs(),
            ],
            out_specs=[whole((n, d))] * 3,
            scratch_shapes=[pltpu.VMEM((d, wt.width), BF)],
        ),
        out_shape=[
            jax.ShapeDtypeStruct((n, d), F32),
            jax.ShapeDtypeStruct((n, d), F32),
            jax.ShapeDtypeStruct((n, d), BF),
        ],
        compiler_params=params(),
        cost_estimate=cost(2 * n * d * d, 8 * d * d + 14 * n * d),
        name="out_proj",
    )(scal, *mixed, x, mod, bias, *wt.arrays)


def up_proj(scal, h, bias, wt, geo):
    n, d = h.shape
    w = wt.width
    nw = len(wt.arrays)
    step = chunked(w, 384)

    def kernel(s, h_ref, b_ref, *refs):
        w_refs, (hid_ref, gp_ref, wbuf) = refs[:nw], refs[nw:]
        j = pl.program_id(0)
        wt.assemble(j, s, w_refs, wbuf)
        for at in range(0, w, step):
            cols = slice(at, at + step)
            u = dotg(h_ref[...], wbuf[:, cols], 1, 0) + b_ref[0, :, cols]
            sq = u * u
            t = jnp.tanh(TANH_C * (u + CUBIC * sq * u))
            half = 0.5 * (1.0 + t)
            hid_ref[0, :, cols] = (u * half).astype(BF)
            slope = TANH_C * (1.0 + 3.0 * CUBIC * sq)
            gp_ref[0, :, cols] = (half + 0.5 * u * (1.0 - t * t) * slope).astype(BF)

    out = pl.BlockSpec((1, n, w), lambda j, s: (j, 0, 0))
    return pl.pallas_call(
        kernel,
        grid_spec=pltpu.PrefetchScalarGridSpec(
            num_scalar_prefetch=1,
            grid=(geo.T,),
            in_specs=[
                whole((n, d)),
                pl.BlockSpec((1, 1, w), lambda j, s: (s[2] ^ j, 0, 0)),
                *wt.specs(),
            ],
            out_specs=[out, out],
            scratch_shapes=[pltpu.VMEM((d, w), BF)],
        ),
        out_shape=[jax.ShapeDtypeStruct((geo.T, n, w), BF)] * 2,
        compiler_params=params(),
        cost_estimate=cost(2 * n * d * w * geo.T, 2 * geo.T * w * (d + 2 * n)),
        name="up_proj",
    )(scal, h, bias, *wt.arrays)


def down_proj(scal, hidden, resid, cot, mod, bias, wt, geo):
    _, n, w = hidden.shape
    d = geo.D
    nw = len(wt.arrays)

    def kernel(s, y_ref, r_ref, c_ref, m_ref, b_ref, *refs):
        w_refs, (out_ref, sum_ref, wbuf, acc) = refs[:nw], refs[nw:]
        j = pl.program_id(0)
        wt.assemble(j, s, w_refs, wbuf)
        part = dotg(y_ref[0], wbuf[...], 1, 1)

        @pl.when(j == 0)
        def _():
            acc[...] = part
            sum_ref[...] = jnp.zeros_like(sum_ref)

        @pl.when(j > 0)
        def _():
            acc[...] += part

        @pl.when(j == geo.T - 1)
        def _():
            @pl.loop(0, n // ROWS, unroll=4)
            def _(i):
                at = pl.ds(pl.multiple_of(i * ROWS, ROWS), ROWS)
                ffn = acc[at, :] + b_ref[...]
                out_ref[at, :] = (r_ref[at, :] + m_ref[5:6, :] * ffn).astype(BF)
                sum_ref[...] += fold_rows(c_ref[at, :].astype(F32) * ffn)

    return pl.pallas_call(
        kernel,
        grid_spec=pltpu.PrefetchScalarGridSpec(
            num_scalar_prefetch=1,
            grid=(geo.T,),
            in_specs=[
                pl.BlockSpec((1, n, w), lambda j, s: (j, 0, 0)),
                whole((n, d)),
                whole((n, d)),
                whole(mod.shape),
                whole((1, d)),
                *wt.specs(),
            ],
            out_specs=[whole((n, d)), whole((8, d))],
            scratch_shapes=[pltpu.VMEM((d, w), BF), pltpu.VMEM((n, d), F32)],
        ),
        out_shape=[jax.ShapeDtypeStruct((n, d), BF), jax.ShapeDtypeStruct((8, d), F32)],
        compiler_params=params(),
        cost_estimate=cost(2 * n * d * w * geo.T, 2 * geo.T * w * (d + n) + 8 * n * d),
        name="down_proj",
    )(scal, hidden, resid, cot, mod, bias, *wt.arrays)


def pre_back(scal, g, gp, wt, geo):
    n, d = g.shape
    w = wt.width
    nw = len(wt.arrays)
    step = chunked(w, 384)

    def kernel(s, g_ref, gp_ref, *refs):
        w_refs, (out_ref, sum_ref, wbuf) = refs[:nw], refs[nw:]
        j = pl.program_id(0)
        wt.assemble(j, s, w_refs, wbuf)
        for at in range(0, w, step):
            cols = slice(at, at + step)
            y = dotg(g_ref[...], wbuf[:, cols], 1, 0) * gp_ref[0, :, cols].astype(F32)
            out_ref[0, :, cols] = y.astype(BF)
            sum_ref[0, :, cols] = jnp.sum(y, axis=0, keepdims=True)

    out = pl.BlockSpec((1, n, w), lambda j, s: (j, 0, 0))
    return pl.pallas_call(
        kernel,
        grid_spec=pltpu.PrefetchScalarGridSpec(
            num_scalar_prefetch=1,
            grid=(geo.T,),
            in_specs=[whole((n, d)), out, *wt.specs()],
            out_specs=[out, pl.BlockSpec((1, 1, w), lambda j, s: (j, 0, 0))],
            scratch_shapes=[pltpu.VMEM((d, w), BF)],
        ),
        out_shape=[
            jax.ShapeDtypeStruct((geo.T, n, w), BF),
            jax.ShapeDtypeStruct((geo.T, 1, w), F32),
        ],
        compiler_params=params(),
        cost_estimate=cost(2 * n * d * w * geo.T, 2 * geo.T * w * (d + 2 * n)),
        name="pre_back",
    )(scal, g, gp, *wt.arrays)


def second_back(scal, pre, resid, attn, cot, mod, wt, geo):
    _, n, w = pre.shape
    d = geo.D
    nw = len(wt.arrays)

    def kernel(s, y_ref, r_ref, a_ref, c_ref, m_ref, *refs):
        w_refs, (rg_ref, ag_ref, sum_ref, wbuf, acc) = refs[:nw], refs[nw:]
        j = pl.program_id(0)
        wt.assemble(j, s, w_refs, wbuf)
        part = dotg(y_ref[0], wbuf[...], 1, 1)

        @pl.when(j == 0)
        def _():
            acc[...] = part
            sum_ref[...] = jnp.zeros_like(sum_ref)

        @pl.when(j > 0)
        def _():
            acc[...] += part

        @pl.when(j == geo.T - 1)
        def _():
            @pl.loop(0, n // ROWS, unroll=4)
            def _(i):
                at = pl.ds(pl.multiple_of(i * ROWS, ROWS), ROWS)
                g = acc[at, :]
                norm, inv = norm_of(r_ref[at, :])
                rg = c_ref[at, :].astype(F32) + norm_back(norm, inv, g * (1.0 + m_ref[4:5, :]))
                rg_ref[at, :] = rg
                ag = rg * m_ref[2:3, :]
                ag_ref[at, :] = ag.astype(BF)
                sum_ref[0] += fold_rows(rg * a_ref[at, :])
                sum_ref[1] += fold_rows(g)
                sum_ref[2] += fold_rows(g * norm)
                sum_ref[3] += fold_rows(ag)

    return pl.pallas_call(
        kernel,
        grid_spec=pltpu.PrefetchScalarGridSpec(
            num_scalar_prefetch=1,
            grid=(geo.T,),
            in_specs=[
                pl.BlockSpec((1, n, w), lambda j, s: (j, 0, 0)),
                whole((n, d)),
                whole((n, d)),
                whole((n, d)),
                whole(mod.shape),
                *wt.specs(),
            ],
            out_specs=[whole((n, d)), whole((n, d)), whole((4, 8, d))],
            scratch_shapes=[pltpu.VMEM((d, w), BF), pltpu.VMEM((n, d), F32)],
        ),
        out_shape=[
            jax.ShapeDtypeStruct((n, d), F32),
            jax.ShapeDtypeStruct((n, d), BF),
            jax.ShapeDtypeStruct((4, 8, d), F32),
        ],
        compiler_params=params(),
        cost_estimate=cost(2 * n * d * w * geo.T, 2 * geo.T * w * (d + n) + 18 * n * d),
        name="second_back",
    )(scal, pre, resid, attn, cot, mod, *wt.arrays)


def mixed_back(scal, g, wt, geo):
    n, d = g.shape
    w = wt.width // 4
    nw = len(wt.arrays)

    def kernel(s, g_ref, *refs):
        w_refs, (out_ref, wbuf) = refs[:nw], refs[nw:]
        wt.assemble(pl.program_id(0), s, w_refs, wbuf)
        out_ref[0, :, :w] = dotg(g_ref[...], wbuf[:, 3 * w :], 1, 0).astype(BF)

    return pl.pallas_call(
        kernel,
        grid_spec=pltpu.PrefetchScalarGridSpec(
            num_scalar_prefetch=1,
            grid=(geo.T,),
            in_specs=[whole((n, d)), *wt.specs()],
            out_specs=pl.BlockSpec((1, n, padded(w)), lambda j, s: (j, 0, 0)),
            scratch_shapes=[pltpu.VMEM((d, wt.width), BF)],
        ),
        out_shape=jax.ShapeDtypeStruct((geo.T, n, padded(w)), BF),
        compiler_params=params(),
        cost_estimate=cost(2 * n * d * d, 8 * d * d + 4 * n * d),
        name="mixed_back",
    )(scal, g, *wt.arrays)


def first_back(scal, dq, dkv, got, x, rg, mod, wt, geo):
    _, n, wp = dq[0].shape
    w = wt.width // 4
    d = geo.D
    nw = len(wt.arrays)
    th = geo.Th

    def kernel(s, qa, qb, kva, kvb, ga, gb, x_ref, r_ref, m_ref, *refs):
        w_refs, (out_ref, sum_ref, wbuf, lhs, acc) = refs[:nw], refs[nw:]
        j = pl.program_id(0)
        wt.assemble(j, s, w_refs, wbuf)
        for half, (q, kv, g) in enumerate(((qa, kva, ga), (qb, kvb, gb))):

            @pl.when((j < th) if half == 0 else (j >= th))
            def _():
                lhs[:, :w] = q[0, :, :w]
                for at in range(2):
                    both = kv[0, at, :, :w].astype(F32) + g[0, at, :, :w].astype(F32)
                    lhs[:, (at + 1) * w : (at + 2) * w] = both.astype(BF)

        part = dotg(lhs[...], wbuf[:, : 3 * w], 1, 1)

        @pl.when(j == 0)
        def _():
            acc[...] = part
            sum_ref[...] = jnp.zeros_like(sum_ref)

        @pl.when(j > 0)
        def _():
            acc[...] += part

        @pl.when(j == geo.T - 1)
        def _():
            @pl.loop(0, n // ROWS, unroll=4)
            def _(i):
                at = pl.ds(pl.multiple_of(i * ROWS, ROWS), ROWS)
                g = acc[at, :]
                norm, inv = norm_of(x_ref[at, :].astype(F32))
                back = norm_back(norm, inv, g * (1.0 + m_ref[1:2, :]))
                out_ref[at, :] = (r_ref[at, :] + back).astype(BF)
                sum_ref[0] += fold_rows(g)
                sum_ref[1] += fold_rows(g * norm)

    return pl.pallas_call(
        kernel,
        grid_spec=pltpu.PrefetchScalarGridSpec(
            num_scalar_prefetch=1,
            grid=(geo.T,),
            in_specs=[
                *two_halves((1, n, wp), th, (0, 0)),
                *two_halves((1, 2, n, wp), th, (0, 0, 0)),
                *two_halves((1, 2, n, wp), th, (0, 0, 0)),
                whole((n, d)),
                whole((n, d)),
                whole(mod.shape),
                *wt.specs(),
            ],
            out_specs=[whole((n, d)), whole((2, 8, d))],
            scratch_shapes=[
                pltpu.VMEM((d, wt.width), BF),
                pltpu.VMEM((n, 3 * w), BF),
                pltpu.VMEM((n, d), F32),
            ],
        ),
        out_shape=[jax.ShapeDtypeStruct((n, d), BF), jax.ShapeDtypeStruct((2, 8, d), F32)],
        compiler_params=params(),
        cost_estimate=cost(6 * n * d * d, 8 * d * d + 16 * n * d),
        name="first_back",
    )(scal, *dq, *dkv, *got, x, rg, mod, *wt.arrays)


def weight_grad(scal, terms, w, mine, geo, name, partial=None):
    n = terms[0][0].shape[0]
    pr = geo.P * geo.R
    th = geo.Th
    half_n = geo.P // 2
    want = scal[1] if mine else 1 - scal[1]
    lefts = [term[0] for term in terms]
    if not geo.direct:

        def pick(a):
            cols = a.reshape(n, geo.P, 2, geo.R)
            cols = jnp.where(want == 0, cols[:, :, 0], cols[:, :, 1])
            return cols.reshape(n, pr).T

        lefts = [pick(a) for a in lefts]
    ops, op_specs, counts = [], [], []
    for _, operands, _, _ in terms:
        counts.append(len(operands))
        for pair in operands:
            if isinstance(pair, tuple):
                tail = (0,) * (pair[0].ndim - 1)
                op_specs += two_halves((1,) + pair[0].shape[1:], th, tail)
                ops += pair
            else:
                op_specs.append(pl.BlockSpec((1,) + pair.shape[1:], lambda j, s: (j, 0, 0)))
                ops.append(pair)
    na, nb = len(lefts), len(ops)

    def kernel(s, *refs):
        a_refs, b_refs = refs[:na], refs[na : na + nb]
        rest = refs[na + nb :]
        got_ref = None
        if mine:
            got_ref, rest = rest[0], rest[1:]
        n_out = 4 if (mine and geo.direct) else 1
        outs, ats = rest[:n_out], rest[n_out:]
        j = pl.program_id(0)
        if geo.direct:

            @pl.when(j == 0)
            def _():
                pick_odd = (s[1] == 1) if mine else (s[1] == 0)
                for ref, at in zip(a_refs, ats):
                    flip = ref[...].T
                    for p in range(geo.P):
                        even = flip[2 * p * geo.R : (2 * p + 1) * geo.R]
                        odd = flip[(2 * p + 1) * geo.R : (2 * p + 2) * geo.R]
                        at[p * geo.R : (p + 1) * geo.R, :] = jnp.where(pick_odd, odd, even)
        else:
            ats = a_refs

        def store(half):
            at_op, parts = 0, []
            for at, (_, operands, build, _) in zip(ats, terms):
                blocks = []
                for pair in operands:
                    if isinstance(pair, tuple):
                        blocks.append(b_refs[at_op + half])
                        at_op += 2
                    else:
                        blocks.append(b_refs[at_op])
                        at_op += 1
                parts.append(dotg(at[...], build(*blocks), 1, 0))
            full = parts[0] if len(parts) == 1 else jnp.concatenate(parts, axis=1)
            if not geo.direct:
                if mine:
                    full = full + got_ref[0, 0].astype(F32)
                outs[0][0, 0] = full.astype(BF)
                return
            for p in range(geo.P):
                part = full[p * geo.R : (p + 1) * geo.R]
                rel = s[0] ^ p
                if not mine:
                    outs[0][0, rel] = part.astype(BF)
                    continue
                part = (part + got_ref[0, rel].astype(F32)).astype(BF)
                for i, here in enumerate(geo.order[half]):

                    @pl.when(rel == here)
                    def _():
                        outs[2 * half + i // half_n][i % half_n, 0] = part

        for half in range(2):

            @pl.when((j < th) if half == 0 else (j >= th))
            def _():
                store(half)

    in_specs = [whole(a.shape) for a in lefts] + op_specs
    rel_block = (1, geo.P, geo.R, w) if geo.direct else (1, 1, pr, w)
    rel_spec = pl.BlockSpec(rel_block, lambda j, s: (j, 0, 0, 0))
    rel_shape = jax.ShapeDtypeStruct((geo.T,) + rel_block[1:], BF)
    args = [*lefts, *ops]
    out_specs, shapes = [rel_spec], [rel_shape]
    if mine:
        in_specs.append(rel_spec)
        args.append(partial)
        if geo.direct:
            block = (half_n, 1, geo.R, w)
            first = pl.BlockSpec(block, lambda j, s: (0, jnp.minimum(j, th - 1), 0, 0))
            second = pl.BlockSpec(block, lambda j, s: (0, jnp.maximum(j - th, 0), 0, 0))
            out_specs = [first, first, second, second]
            shapes = [jax.ShapeDtypeStruct((half_n, th, geo.R, w), BF)] * 4
    got = pl.pallas_call(
        kernel,
        grid_spec=pltpu.PrefetchScalarGridSpec(
            num_scalar_prefetch=1,
            grid=(geo.T,),
            in_specs=in_specs,
            out_specs=out_specs,
            scratch_shapes=[pltpu.VMEM((pr, n), BF)] * (na if geo.direct else 0),
        ),
        out_shape=shapes,
        compiler_params=params(),
        cost_estimate=cost(2 * pr * n * w * geo.T, 2 * geo.T * w * (2 * pr + n)),
        name=name,
    )(scal, *args)
    if not mine:
        return got[0]
    if geo.direct:
        return got
    blocks = got[0].reshape(geo.T, geo.P, geo.R, w)
    out = []
    for half in range(2):
        part = blocks[half * th : (half + 1) * th]
        part = reorder(part, [scal[0] ^ rel for rel in geo.order[half]], 1)
        part = part.transpose(1, 0, 2, 3)
        out += [part[:half_n], part[half_n:]]
    return out


def body(
    latents,
    conditioning,
    mod_weight,
    mod_bias,
    in_weight,
    query_value_bias,
    out_weight,
    branch_bias,
    up_weight,
    up_bias,
    down_weight,
    cotangent,
):
    images, row_count, width = latents.shape
    geo = Geo(lax.axis_size("fsdp"), lax.axis_size("tensor"), width)
    F, T = geo.F, geo.T
    assert 2 * images == T
    highest = lax.Precision.HIGHEST
    fi = lax.axis_index("fsdp")
    ti = lax.axis_index("tensor")
    pair, core = fi // 2, fi % 2
    scal = jnp.stack([pair, core, ti]).astype(jnp.int32)
    cols = in_weight.shape[2]
    units = up_weight.shape[1]

    def places(k):
        return [
            ((2 * p + c) * T + t, (2 * p + t // images) * T + c * images + (t % images + k) % images)
            for p in range(geo.P)
            for c in range(2)
            for t in range(T)
        ]

    def to_chip(arr):
        got = []
        for k in range(images):
            item = lax.dynamic_index_in_dim(arr, (ti + k) % images, 0, keepdims=False)
            got.append(lax.ppermute(item, BOTH, places(k)))
        return got

    def from_chip(arr):
        got = []
        for k in range(images):
            back = [(dst, src) for src, dst in places(k)]
            got.append(lax.ppermute(arr[k * row_count : (k + 1) * row_count], BOTH, back))
        return got

    def home(parts):
        return reorder(jnp.stack(parts), [(i - ti) % images for i in range(images)])

    def share(arr):
        sent = jnp.broadcast_to(arr[None], (F * T,) + arr.shape)
        return lax.all_to_all(sent, BOTH, 0, 0, tiled=True)

    now, opened = (), []

    def tie(value):
        return after(value, *now)

    def start(*chains):
        for way in chains:
            opened.extend(way.advance(*now))

    def begin(shard, make):
        way = Chain(make(tie(shard), geo))
        opened.extend(way.flight)
        return way

    def across(value):
        got = flip_core(tie(value), geo)
        opened.append(got)
        return got

    def close(*made):
        nonlocal now
        now = (*opened, *made)
        opened.clear()

    heads = cols // HEAD_DIM
    attn_shard = jnp.concatenate([in_weight[0], in_weight[1], in_weight[2], out_weight.T], axis=1)
    attn_way = begin(attn_shard, gather_steps)
    info = jnp.concatenate([conditioning.reshape(-1), query_value_bias.reshape(-1), up_bias])
    info = share(info)
    close(info)
    start(attn_way)
    x_parts = to_chip(tie(latents))
    opened.extend(x_parts)
    info = info.reshape(F, T, -1)
    cond_all = info[:, 0, : images * width].reshape(F * images, width)
    qv_bias = info[0, :, images * width : images * width + 2 * cols].reshape(T, 2, 1, cols)
    unit_bias = info[0, :, images * width + 2 * cols :].reshape(T, 1, units).astype(F32)
    triple_bias = jnp.concatenate(
        [qv_bias[:, 0], jnp.zeros_like(qv_bias[:, 0]), qv_bias[:, 1]], axis=2
    ).astype(F32)
    silu_low = jax.nn.silu(cond_all.astype(F32)).astype(BF)
    silu_own = lax.dynamic_slice_in_dim(silu_low, fi * geo.R, geo.R, 1)
    mod_part = jnp.einsum("bd,dcj->bcj", silu_own, mod_weight, preferred_element_type=F32)
    mod_part += jnp.where(fi == 0, mod_bias.astype(F32), 0.0)
    mod_part = mod_part.reshape(geo.P, 1, T, 6, cols)
    mod_part = jnp.broadcast_to(mod_part, (geo.P, 2, T, 6, cols)).reshape(F * T, 6, cols)
    mod_part = lax.all_to_all(mod_part, BOTH, 0, 0, tiled=True)
    mod = mod_part.reshape(F, T, 6, cols).sum(axis=0).transpose(1, 0, 2).reshape(6, width)
    bias_rows = branch_bias.astype(F32)
    close(mod)
    x = jnp.concatenate(x_parts)
    start(attn_way)
    up_way = begin(up_weight, gather_steps)
    close()
    start(attn_way, up_way)
    h1 = norm_mod(tie(x), mod)
    close(h1)
    start(attn_way)
    w_attn = Gathered(attn_way.finish(*now), geo, scal)

    start(up_way)
    down_way = begin(down_weight.T, gather_steps)
    q, kv, kvo = [None] * 2, [None] * 2, [None] * 2
    mixed, lse = [None] * 2, [None] * 2
    for half in range(2):
        q[half], kv[half] = in_proj(tie(scal), h1, w_attn, triple_bias, cols, half, geo)
    close(q[0], q[1])
    kvo = [across(kv[0]), across(kv[1])]
    start(up_way)
    close()
    start(down_way, up_way)
    cot_parts = to_chip(tie(cotangent))
    opened.extend(cot_parts)
    w_up = Gathered(up_way.finish(*now), geo, scal)
    for half in range(2):
        mixed[half], lse[half] = attn_fwd(tie(q[half]), kv[half], kvo[half], heads)
    close(lse[0], lse[1])
    start(down_way)
    cot = jnp.concatenate(cot_parts)
    attn, resid, h2 = out_proj(tie(scal), mixed, x, mod, bias_rows[0:1], w_attn, geo)
    hidden, gp = up_proj(tie(scal), h2, unit_bias, w_up, geo)
    ffn_grad = (cot.astype(F32) * mod[5]).astype(BF)
    ffn_sum = jnp.sum(ffn_grad.astype(F32), axis=0)
    close(hidden)
    start(down_way)
    down_terms = [(ffn_grad, [hidden], lambda ref: ref[0], units)]
    down_half = weight_grad(tie(scal), down_terms, units, False, geo, "w_down_send")
    close(down_half)
    start(down_way)
    w_down = Gathered(down_way.finish(*now), geo, scal)
    down_got = across(down_half)
    block_rows, ffn_sums = down_proj(
        tie(scal), hidden, resid, cot, mod, bias_rows[1:2], w_down, geo
    )
    close(ffn_sums)

    down_parts = weight_grad(tie(scal), down_terms, units, True, geo, "w_down", down_got)
    close(*down_parts)
    down_back = begin(down_parts, scatter_steps)
    block_back = from_chip(tie(block_rows))
    opened.extend(block_back)
    pre, unit_sum = pre_back(tie(scal), ffn_grad, gp, w_down, geo)
    up_terms = [(h2, [pre], lambda ref: ref[0], units)]
    up_half = weight_grad(tie(scal), up_terms, units, False, geo, "w_up_send")
    close(up_half)
    start(down_back)
    up_got = across(up_half)
    rg, ag, mid_sums = second_back(tie(scal), pre, resid, attn, cot, mod, w_up, geo)
    close(ag)
    start(down_back)
    up_parts = weight_grad(tie(scal), up_terms, units, True, geo, "w_up", up_got)
    mg = mixed_back(tie(scal), ag, w_attn, geo)
    close(mg, *up_parts)
    start(down_back)
    up_back = begin(up_parts, scatter_steps)
    dq, dkv, dkv_got, tri_sums = [None] * 2, [None] * 2, [None] * 2, [None] * 2
    dkv_send = [None] * 2
    for half in range(2):
        dq[half], dkv[half], dkv_send[half], tri_sums[half] = attn_bwd(
            tie(q[half]), kv[half], kvo[half], mixed[half], mg, lse[half], half * geo.Th
        )
    dkv_got[0] = across(dkv_send[0])
    close(*tri_sums)
    dkv_got[1] = across(dkv_send[1])
    tri_sums = jnp.concatenate(tri_sums)
    close()
    start(up_back)

    def triple(q_ref, kv_ref, got_ref):
        parts = [q_ref[0, :, :cols]]
        for at in range(2):
            both = kv_ref[0, at, :, :cols].astype(F32) + got_ref[0, at, :, :cols].astype(F32)
            parts.append(both.astype(BF))
        return jnp.concatenate(parts, axis=1)

    attn_terms = [
        (h1, [tuple(dq), tuple(dkv), tuple(dkv_got)], triple, 3 * cols),
        (ag, [tuple(mixed)], lambda ref: ref[0, :, :cols], cols),
    ]
    attn_half = weight_grad(tie(scal), attn_terms, 4 * cols, False, geo, "w_attn_send")
    close(attn_half)
    start(up_back)
    attn_got = across(attn_half)
    latent_rows, first_sums = first_back(tie(scal), dq, dkv, dkv_got, x, rg, mod, w_attn, geo)
    close(first_sums)
    attn_parts = weight_grad(tie(scal), attn_terms, 4 * cols, True, geo, "w_attn", attn_got)
    close(*attn_parts)
    start(up_back)
    attn_back = begin(attn_parts, scatter_steps)
    latent_back = from_chip(tie(latent_rows))
    opened.extend(latent_back)
    close()
    start(attn_back)
    close()
    start(attn_back)
    close()
    start(attn_back)
    block_out, latent_grad = home(block_back), home(latent_back)
    down_grad, up_grad = down_back.finish(*now), up_back.finish(*now)
    attn_grad = attn_back.finish(*now)
    in_grad = attn_grad[:, : 3 * cols].reshape(geo.R, 3, cols).transpose(1, 0, 2)

    mine = [i ^ ti for i in range(T)]
    branch_sums = jnp.stack([mid_sums[3].sum(axis=0), ffn_sum]).reshape(1, 2 * width)
    bias_pack = jnp.concatenate(
        [
            jnp.broadcast_to(branch_sums, (T, 2 * width)),
            reorder(unit_sum, mine).reshape(T, units),
            reorder(tri_sums, mine).reshape(T, 2 * cols),
        ],
        axis=1,
    )
    bias_pack = jnp.broadcast_to(bias_pack[None], (F,) + bias_pack.shape).reshape(F * T, -1)
    bias_total = lax.all_to_all(bias_pack, BOTH, 0, 0, tiled=True).sum(axis=0)
    branch_grad = bias_total[: 2 * width].reshape(2, width)
    unit_grad = bias_total[2 * width : 2 * width + units]
    pair_grad = bias_total[2 * width + units :].reshape(2, cols)

    rows = jnp.concatenate(
        [first_sums.sum(axis=1), mid_sums[:3].sum(axis=1), ffn_sums.sum(axis=0, keepdims=True)]
    )
    rows = rows.reshape(6, T, cols).transpose(1, 0, 2)
    rows = jnp.broadcast_to(rows[None], (F, T, 6, cols)).reshape(F * T, 6, cols)
    rows = lax.all_to_all(rows, BOTH, 0, 0, tiled=True)
    mine_rows = rows.reshape(geo.P, 2, T, 6, cols).sum(axis=1).reshape(F * images, 6, cols)
    mod_weight_grad = jnp.einsum(
        "bd,bcj->dcj", silu_own.astype(F32), mine_rows, precision=highest
    )
    mod_bias_grad = mine_rows.sum(axis=0)
    cond_part = jnp.einsum("bcj,dcj->bd", mine_rows, mod_weight.astype(F32), precision=highest)
    cond_part = cond_part.reshape(F, 1, images, geo.R)
    cond_part = jnp.broadcast_to(cond_part, (F, T, images, geo.R)).reshape(F * T, images, geo.R)
    cond_part = lax.all_to_all(cond_part, BOTH, 0, 0, tiled=True)
    cond_mine = cond_part.reshape(F, T, images, geo.R).sum(axis=1)
    silu_grad = cond_mine.transpose(1, 0, 2).reshape(images, width)
    cond_f = conditioning.astype(F32)
    sig = jax.nn.sigmoid(cond_f)
    cond_grad = silu_grad * (sig * (1.0 + cond_f * (1.0 - sig)))

    return (
        block_out,
        latent_grad,
        cond_grad,
        mod_weight_grad,
        mod_bias_grad,
        in_grad,
        pair_grad,
        attn_grad[:, 3 * cols :].T,
        branch_grad,
        up_grad,
        unit_grad,
        down_grad.T,
    )


def solution(mesh):
    in_specs = (
        P("fsdp", "tensor", None),
        P("fsdp", None),
        P("fsdp", None, "tensor"),
        P(None, "tensor"),
        P(None, "fsdp", "tensor"),
        P(None, "tensor"),
        P("tensor", "fsdp"),
        P(),
        P("fsdp", "tensor"),
        P("tensor"),
        P("tensor", "fsdp"),
        P("fsdp", "tensor", None),
    )
    out_specs = (
        P("fsdp", "tensor", None),
        P("fsdp", "tensor", None),
        P("fsdp", None),
        P("fsdp", None, "tensor"),
        P(None, "tensor"),
        P(None, "fsdp", "tensor"),
        P(None, "tensor"),
        P("tensor", "fsdp"),
        P(),
        P("fsdp", "tensor"),
        P("tensor"),
        P("tensor", "fsdp"),
    )
    return jax.shard_map(body, mesh=mesh, in_specs=in_specs, out_specs=out_specs, check_vma=False)
```

time: 1110 us -> 668 us (0.60)
  waiting for transfers between devices: 446 us -> 192 us
  blocking collectives: 183 us -> 24.8 us
  other arithmetic: 39 us -> 61.2 us
  local copies, waits for them, and re-layouts: 57.2 us -> 36.2 us
  starting transfers between devices: 111 us -> 95.4 us
  between operations: 15.4 us -> 2.48 us
    all_gather x2 -> x0, blocking collectives: 143 us -> none  [the longest x1 71.9 us: body(): lax.all_gather(cond_part, BOTH, axis=0).reshape(F, T, F * images, geo.R)]
    unnamed x2 -> x0, waiting for transfers between devices: 122 us -> none
    ppermute x28 -> x24, waiting for transfers between devices: 142 us -> 45.5 us  [flip_pair(): return lax.ppermute(x, 'fsdp', [(i, i ^ 2 * bit) for i in range(geo.F)])]
    ppermute x17 -> x18, waiting for transfers between devices: 150 us -> 104 us  [flip_tensor(): return lax.ppermute(x, 'tensor', [(i, i ^ k) for i in range(geo.T)])]
    psum x1 -> x0, blocking collectives: 40.2 us -> none  [body(): bias_total = lax.psum(bias_pack, BOTH)]
    all_to_all x0 -> x1, blocking collectives: none -> 24.8 us  [body(): mod_part = lax.all_to_all(mod_part, BOTH, 0, 0, tiled=True)]
    ppermute x4, waiting for transfers between devices: 22.8 us -> 0.01 us  [to_chip(): got.append(lax.ppermute(item, BOTH, places(k)))]
    all_to_all x1 -> x4, waiting for transfers between devices: 9.02 us -> 28.6 us  [the longest x1 22 us: body(): rows = lax.all_to_all(rows, BOTH, 0, 0, tiled=True)]
  transfers between devices with their start and end apart: 78 -> 67, of which waited for: 33 -> 27; matrix products, arithmetic and copies ran while one was open for 9% -> 10% of each run, Pallas kernels for 21% -> 33%
where the time goes in v2:
time: 668 us; the launch traced here: 659 us
  Pallas kernels  244 us (37%)
  waiting for transfers between devices  192 us (29%)
  starting transfers between devices  95.4 us (14%)
  other arithmetic  61.2 us (9%)
  local copies, waits for them, and re-layouts  36.2 us (5%)
  blocking collectives  24.8 us (4%)
    ppermute x18, waiting for transfers between devices, flip_tensor(): return lax.ppermute(x, 'tensor', [(i, i ^ k) for i in range(geo.T)])  104 us
    pallas_call x6, Pallas kernels, weight_grad(): pl.pallas_call(kernel, grid_spec=pltpu.PrefetchScalarGridSpec(num_scalar_...  65.1 us
    ppermute x24, waiting for transfers between devices, flip_pair(): return lax.ppermute(x, 'fsdp', [(i, i ^ 2 * bit) for i in range(geo.F)])  45.5 us
    pallas_call x2, Pallas kernels, attn_bwd(): pl.pallas_call(kernel, grid=(z,), in_specs=[s3, s4, s4, s3, pl.BlockSpec(...  28.7 us
    ppermute x24, starting transfers between devices, flip_pair(): return lax.ppermute(x, 'fsdp', [(i, i ^ 2 * bit) for i in range(geo.F)])  25 us
    ppermute x18, starting transfers between devices, flip_tensor(): return lax.ppermute(x, 'tensor', [(i, i ^ k) for i in range(geo.T)])  24.8 us
    all_to_all x1, blocking collectives, body(): mod_part = lax.all_to_all(mod_part, BOTH, 0, 0, tiled=True)  24.8 us
    all_to_all x1, waiting for transfers between devices, body(): rows = lax.all_to_all(rows, BOTH, 0, 0, tiled=True)  22 us
  transfers between devices with their start and end apart: 67, of which 27 were waited for; matrix products, arithmetic and copies ran while one was open for 10% of the time, Pallas kernels for 33%

profile of v2, /device:TPU:10, one launch (start us, length us, event | category | flops | bytes accessed | tf_op | source)
XLA Modules:
  0.0 659.2 jit_solution(10579502062606226493)
XLA Ops:
  32.1 9.1 %collective-permute-done.1 = bf16[144,1152]{1,0:T(8,128)(2,1)} collective-permute-done((bf16[144,1152]{1,0:T(8,128)(2,1)S(1)}, bf16[144,1152]{1,0:T(8,128)(2,1)}, u32[]{:S(2)}, u32[]{:S(2)}) %collective-permute-start.1) | collective-permute-done | bytes 331808 | tf_op jit(solution)/shard_map/ppermute | solution.py:57
  41.2 8.9 %collective-permute-done.2 = bf16[144,1152]{1,0:T(8,128)(2,1)} collective-permute-done((bf16[144,1152]{1,0:T(8,128)(2,1)S(1)}, bf16[144,1152]{1,0:T(8,128)(2,1)}, u32[]{:S(2)}, u32[]{:S(2)}) %collective-permute-start.2) | collective-permute-done | bytes 331808 | tf_op jit(solution)/shard_map/ppermute | solution.py:57
  64.9 24.8 %all_to_all.33 = f32[32,6,288]{2,1,0:T(8,128)} all-to-all(f32[32,6,288]{2,1,0:T(8,128)S(1)} %bitcast.133), channel_id=1, replica_groups=mesh['fsdp'=8,'tensor'=4] {'fsdp','tensor'}, dimensions={0} | all-to-all | bytes 442368 | tf_op jit(solution)/shard_map/all_to_all | solution.py:961
  98.4 18.0 %collective-permute-done.10 = bf16[144,1152]{1,0:T(8,128)(2,1)S(1)} collective-permute-done((bf16[144,1152]{1,0:T(8,128)(2,1)S(1)}, bf16[144,1152]{1,0:T(8,128)(2,1)S(1)}, u32[]{:S(2)}, u32[]{:S(2)}) %collective-permute-start.10) | collective-permute-done | bytes 331808 | tf_op jit(solution)/shard_map/ppermute | solution.py:57
  116.4 8.8 %collective-permute-done.11 = bf16[144,1152]{1,0:T(8,128)(2,1)S(1)} collective-permute-done((bf16[144,1152]{1,0:T(8,128)(2,1)S(1)}, bf16[144,1152]{1,0:T(8,128)(2,1)S(1)}, u32[]{:S(2)}, u32[]{:S(2)}) %collective-permute-start.11) | collective-permute-done | bytes 331808 | tf_op jit(solution)/shard_map/ppermute | solution.py:57
  210.8 9.9 %attn_fwd.3 = (bf16[2,512,384]{2,1,0:T(8,128)(2,1)}, f32[2,4,512]{2,1,0:T(4,128)}) custom-call(bf16[2,512,384]{2,1,0:T(8,128)(2,1)} %get-tuple-element.226.q_ref, bf16[2,2,512,384]{3,2,1,0:T(8,128)(2,1)} %get-tuple-element.167.kv_ref, bf16[2,2,512,384]{3,2,1,0:T(8,128)(2,1)} %copy-done.66), custom_call_target="tpu_custom_call" | custom-call | flops 6000000000 | bytes 5505024 | tf_op jit(solution)/shard_map/attn_fwd/pallas_call | solution.py:307
  220.8 10.0 %attn_fwd.2 = (bf16[2,512,384]{2,1,0:T(8,128)(2,1)}, f32[2,4,512]{2,1,0:T(4,128)}) custom-call(bf16[2,512,384]{2,1,0:T(8,128)(2,1)} %get-tuple-element.228.q_ref, bf16[2,2,512,384]{3,2,1,0:T(8,128)(2,1)} %get-tuple-element.165.kv_ref, bf16[2,2,512,384]{3,2,1,0:T(8,128)(2,1)} %copy-done.67), custom_call_target="tpu_custom_call" | custom-call | flops 6000000000 | bytes 5505024 | tf_op jit(solution)/shard_map/attn_fwd/pallas_call | solution.py:307
  236.6 14.3 %out_proj.1 = (f32[512,1152]{1,0:T(8,128)}, f32[512,1152]{1,0:T(8,128)}, bf16[512,1152]{1,0:T(8,128)(2,1)}) custom-call(s32[3]{0:T(128)} %pad_add_fusion.s, bf16[2,512,384]{2,1,0:T(8,128)(2,1)} %get-tuple-element.181.ya_ref.o_ref.refs_8_, bf16[2,512,384]{2,1,0:T(8,128)(2,1)} %get-tuple-element.182.yb_ref.o_ref.refs_9_, bf16[512,1152]{1,0:T(8,128)(2,1)} %copy-done.3, ...), custom_call_target="tpu_custom_call" | custom-call | flops 1358954496 | bytes 18874368 | tf_op jit(solution)/shard_map/out_proj/pallas_call | solution.py:414
  250.9 18.9 %up_proj.1 = (bf16[4,512,1152]{2,1,0:T(8,128)(2,1)}, bf16[4,512,1152]{2,1,0:T(8,128)(2,1)}) custom-call(s32[3]{0:T(128)} %pad_add_fusion.s, bf16[512,1152]{1,0:T(8,128)(2,1)} %get-tuple-element.183.h_ref.refs_0_, f32[4,1,1152]{2,1,0:T(1,128)} %fusion.14.b_ref, bf16[4,2,144,1152]{3,2,1,0:T(8,128)(2,1)} %copy-done.6, bf16[4,2,144,1152]{3,2,1,0:T(8,128)(2,1)} %copy-done.17, ...), custom_call_target="tpu_custom_call" | custom-call | flops 5435817984 | bytes 20054016 | tf_op jit(solution)/shard_map/up_proj/pallas_call | solution.py:461
  290.3 15.7 %down_proj.1 = (bf16[512,1152]{1,0:T(8,128)(2,1)}, f32[8,1152]{1,0:T(8,128)}) custom-call(s32[3]{0:T(128)} %pad_add_fusion.s, bf16[4,512,1152]{2,1,0:T(8,128)(2,1)} %get-tuple-element.186.refs_1_.y_ref, f32[512,1152]{1,0:T(8,128)} %get-tuple-element.191.r_ref, bf16[512,1152]{1,0:T(8,128)(2,1)} %copy-done.7, f32[6,1152]{1,0:T(8,128)} %reshape.188.m_ref, ...), custom_call_target="tpu_custom_call" | custom-call | flops 5435817984 | bytes 20054016 | tf_op jit(solution)/shard_map/down_proj/pallas_call | solution.py:510
  308.4 11.8 %w_down.1 = (bf16[2,2,144,1152]{3,2,1,0:T(8,128)(2,1)}, bf16[2,2,144,1152]{3,2,1,0:T(8,128)(2,1)}, bf16[2,2,144,1152]{3,2,1,0:T(8,128)(2,1)}, bf16[2,2,144,1152]{3,2,1,0:T(8,128)(2,1)}) custom-call(s32[3]{0:T(128)} %pad_add_fusion.s, bf16[512,1152]{1,0:T(8,128)(2,1)} %get-tuple-element.347.refs_0_.g_ref, ...), custom_call_target="tpu_custom_call" | custom-call | flops 2717908992 | bytes 15335424 | tf_op jit(solution)/shard_map/w_down/pallas_call | solution.py:832
  324.6 14.5 %pre_back.1 = (bf16[4,512,1152]{2,1,0:T(8,128)(2,1)}, f32[4,1,1152]{2,1,0:T(1,128)}) custom-call(s32[3]{0:T(128)} %pad_add_fusion.s, bf16[512,1152]{1,0:T(8,128)(2,1)} %get-tuple-element.347.refs_0_.g_ref, bf16[4,512,1152]{2,1,0:T(8,128)(2,1)} %get-tuple-element.207.gp_ref, bf16[4,2,144,1152]{3,2,1,0:T(8,128)(2,1)} %pad_maximum_fusion.4.refs_0_, ...), custom_call_target="tpu_custom_call" | custom-call | flops 5435817984 | bytes 20054016 | tf_op jit(solution)/shard_map/pre_back/pallas_call | solution.py:550
  361.3 19.6 %second_back.1 = (f32[512,1152]{1,0:T(8,128)}, bf16[512,1152]{1,0:T(8,128)(2,1)}, f32[4,8,1152]{2,1,0:T(8,128)}) custom-call(s32[3]{0:T(128)} %pad_add_fusion.s, bf16[4,512,1152]{2,1,0:T(8,128)(2,1)} %get-tuple-element.208.refs_1_.y_ref, f32[512,1152]{1,0:T(8,128)} %get-tuple-element.191.r_ref, f32[512,1152]{1,0:T(8,128)} %get-tuple-element.214.a_ref, ...), custom_call_target="tpu_custom_call" | custom-call | flops 5435817984 | bytes 25952256 | tf_op jit(solution)/shard_map/second_back/pallas_call | solution.py:605
  390.8 9.6 %mixed_back.1.do_ref = bf16[4,512,384]{2,1,0:T(8,128)(2,1)} custom-call(s32[3]{0:T(128)} %pad_add_fusion.s, bf16[512,1152]{1,0:T(8,128)(2,1)} %get-tuple-element.215.g_ref.refs_1_, bf16[4,2,144,1152]{3,2,1,0:T(8,128)(2,1)} %copy-done.2, bf16[4,2,144,1152]{3,2,1,0:T(8,128)(2,1)} %collective-permute-done.12.refs_1_, bf16[4,2,144,1152]{3,2,1,0:T(8,128)(2,1)} %copy-done.1, ...), custom_call_target="tpu_custom_call" | custom-call | flops 1358954496 | bytes 12976128 | tf_op jit(solution)/shard_map/mixed_back/pallas_call | solution.py:642
  400.4 11.4 %w_up.1 = (bf16[2,2,144,1152]{3,2,1,0:T(8,128)(2,1)}, bf16[2,2,144,1152]{3,2,1,0:T(8,128)(2,1)}, bf16[2,2,144,1152]{3,2,1,0:T(8,128)(2,1)}, bf16[2,2,144,1152]{3,2,1,0:T(8,128)(2,1)}) custom-call(s32[3]{0:T(128)} %pad_add_fusion.s, bf16[512,1152]{1,0:T(8,128)(2,1)} %get-tuple-element.183.h_ref.refs_0_, ...), custom_call_target="tpu_custom_call" | custom-call | flops 2717908992 | bytes 15335424 | tf_op jit(solution)/shard_map/w_up/pallas_call | solution.py:832
  415.2 14.3 %attn_bwd.3 = (bf16[2,512,384]{2,1,0:T(8,128)(2,1)}, bf16[2,2,512,384]{3,2,1,0:T(8,128)(2,1)}, bf16[2,2,512,384]{3,2,1,0:T(8,128)(2,1)}, f32[2,2,288]{2,1,0:T(2,128)}) custom-call(bf16[2,512,384]{2,1,0:T(8,128)(2,1)} %get-tuple-element.228.q_ref, bf16[2,2,512,384]{3,2,1,0:T(8,128)(2,1)} %get-tuple-element.165.kv_ref, bf16[2,2,512,384]{3,2,1,0:T(8,128)(2,1)} %copy-done.67, ...), custom_call_target="tpu_custom_call" | custom-call | flops 10000000000 | bytes 9437184 | tf_op jit(solution)/shard_map/attn_bwd/pallas_call | solution.py:363
  431.7 14.4 %attn_bwd.2 = (bf16[2,512,384]{2,1,0:T(8,128)(2,1)}, bf16[2,2,512,384]{3,2,1,0:T(8,128)(2,1)}, bf16[2,2,512,384]{3,2,1,0:T(8,128)(2,1)}, f32[2,2,288]{2,1,0:T(2,128)}) custom-call(bf16[2,512,384]{2,1,0:T(8,128)(2,1)} %get-tuple-element.226.q_ref, bf16[2,2,512,384]{3,2,1,0:T(8,128)(2,1)} %get-tuple-element.167.kv_ref, bf16[2,2,512,384]{3,2,1,0:T(8,128)(2,1)} %copy-done.66, ...), custom_call_target="tpu_custom_call" | custom-call | flops 10000000000 | bytes 9437184 | tf_op jit(solution)/shard_map/attn_bwd/pallas_call | solution.py:363
  446.1 15.3 %collective-permute-done.44 = bf16[2,2,144,1152]{3,2,1,0:T(8,128)(2,1)S(1)} collective-permute-done((bf16[2,2,144,1152]{3,2,1,0:T(8,128)(2,1)}, bf16[2,2,144,1152]{3,2,1,0:T(8,128)(2,1)S(1)}, u32[]{:S(2)}, u32[]{:S(2)}) %collective-permute-start.44) | collective-permute-done | bytes 1327136 | tf_op jit(solution)/shard_map/ppermute | solution.py:49
  471.5 11.5 %w_attn_send.1 = bf16[4,4,144,1152]{3,2,1,0:T(8,128)(2,1)} custom-call(s32[3]{0:T(128)} %pad_add_fusion.s, bf16[512,1152]{1,0:T(8,128)(2,1)} %norm_mod.1.h_ref.refs_0_, bf16[512,1152]{1,0:T(8,128)(2,1)} %get-tuple-element.215.g_ref.refs_1_, bf16[2,512,384]{2,1,0:T(8,128)(2,1)} %get-tuple-element.238.refs_2_.qa, ...), custom_call_target="tpu_custom_call" | custom-call | flops 2717908992 | bytes 15335424 | tf_op jit(solution)/shard_map/w_attn_send/pallas_call | solution.py:832
  504.1 18.5 %first_back.1 = (bf16[512,1152]{1,0:T(8,128)(2,1)}, f32[2,8,1152]{2,1,0:T(8,128)}) custom-call(s32[3]{0:T(128)} %pad_add_fusion.s, bf16[2,512,384]{2,1,0:T(8,128)(2,1)} %get-tuple-element.238.refs_2_.qa, bf16[2,512,384]{2,1,0:T(8,128)(2,1)} %get-tuple-element.239.refs_3_.qb, bf16[2,2,512,384]{3,2,1,0:T(8,128)(2,1)} %get-tuple-element.240.refs_4_.kva, ...), custom_call_target="tpu_custom_call" | custom-call | flops 4076863488 | bytes 20054016 | tf_op jit(solution)/shard_map/first_back/pallas_call | solution.py:701
  537.8 13.5 %w_attn.1 = (bf16[2,2,144,1152]{3,2,1,0:T(8,128)(2,1)}, bf16[2,2,144,1152]{3,2,1,0:T(8,128)(2,1)}, bf16[2,2,144,1152]{3,2,1,0:T(8,128)(2,1)}, bf16[2,2,144,1152]{3,2,1,0:T(8,128)(2,1)}) custom-call(s32[3]{0:T(128)} %pad_add_fusion.s, bf16[512,1152]{1,0:T(8,128)(2,1)} %norm_mod.1.h_ref.refs_0_, bf16[512,1152]{1,0:T(8,128)(2,1)} %get-tuple-element.215.g_ref.refs_1_, ...), custom_call_target="tpu_custom_call" | custom-call | flops 2717908992 | bytes 15335424 | tf_op jit(solution)/shard_map/w_attn/pallas_call | solution.py:832
  570.8 22.0 %all-to-all-done.2 = f32[32,6,288]{2,1,0:T(8,128)S(1)} async-done(((f32[32,6,288]{2,1,0:T(8,128)}), f32[32,6,288]{2,1,0:T(8,128)S(1)}, u32[]{:S(2)}, u32[]{:S(2)}) %all-to-all-start.2) | async-done | bytes 221216 | tf_op jit(solution)/shard_map/all_to_all | solution.py:1098
  611.8 10.6 %collective-permute-done.59 = bf16[1,2,144,1152]{3,2,1,0:T(8,128)(2,1)S(1)} collective-permute-done((bf16[1,2,144,1152]{3,2,1,0:T(8,128)(2,1)S(1)}, bf16[1,2,144,1152]{3,2,1,0:T(8,128)(2,1)S(1)}, u32[]{:S(2)}, u32[]{:S(2)}) %collective-permute-start.59) | collective-permute-done | bytes 663584 | tf_op jit(solution)/shard_map/ppermute | solution.py:49
  634.6 13.5 %collective-permute-done.61 = bf16[144,1152]{1,0:T(8,128)(2,1)S(1)} collective-permute-done((bf16[144,1152]{1,0:T(8,128)(2,1)S(1)}, bf16[144,1152]{1,0:T(8,128)(2,1)S(1)}, u32[]{:S(2)}, u32[]{:S(2)}) %collective-permute-start.61) | collective-permute-done | bytes 331808 | tf_op jit(solution)/shard_map/ppermute | solution.py:57
  (404 shorter events, 317.9 us)
Async XLA Ops:
  16.7 33.4 %collective-permute-start.2 = (bf16[144,1152]{1,0:T(8,128)(2,1)S(1)}, bf16[144,1152]{1,0:T(8,128)(2,1)}, u32[]{:S(2)}, u32[]{:S(2)}) collective-permute-start(bf16[144,1152]{1,0:T(8,128)(2,1)S(1)} %concatenate.85), channel_id=1, source_target_pairs={{0,3},{1,2},{2,1},{3,0},{4,7},{5,6},{6,5},{7,4},{8,11},{9,10},{10,... | collective-permute-start | bytes 995336 | tf_op jit(solution)/shard_map/ppermute | solution.py:57
  51.2 40.2 %collective-permute-start.5 = (bf16[256,1152]{1,0:T(8,128)(2,1)}, bf16[256,1152]{1,0:T(8,128)(2,1)}, u32[]{:S(2)}, u32[]{:S(2)}) collective-permute-start(bf16[256,1152]{1,0:T(8,128)(2,1)} %get-tuple-element.359), channel_id=1, source_target_pairs={{0,0},{1,1},{2,4},{3,5},{4,2},{5,3},{6,6},{7,7},{8,8},{9,9},{10,12... | collective-permute-start | bytes 1769480 | tf_op jit(solution)/shard_map/ppermute | solution.py:898
  57.2 34.3 %collective-permute-start.6 = (bf16[256,1152]{1,0:T(8,128)(2,1)}, bf16[256,1152]{1,0:T(8,128)(2,1)}, u32[]{:S(2)}, u32[]{:S(2)}) collective-permute-start(bf16[256,1152]{1,0:T(8,128)(2,1)} %get-tuple-element.358), channel_id=1, source_target_pairs={{0,1},{1,0},{2,5},{3,4},{4,3},{5,2},{6,7},{7,6},{8,9},{9,8},{10,13... | collective-permute-start | bytes 1769480 | tf_op jit(solution)/shard_map/ppermute | solution.py:898
  58.4 33.1 %collective-permute-start.4 = (bf16[1,2,144,1152]{3,2,1,0:T(8,128)(2,1)S(1)}, bf16[1,2,144,1152]{3,2,1,0:T(8,128)(2,1)S(1)}, u32[]{:S(2)}, u32[]{:S(2)}) collective-permute-start(bf16[1,2,144,1152]{3,2,1,0:T(8,128)(2,1)S(1)} %maximum_bitcast_fusion.1), channel_id=1, source_target_pairs={{0,16},{4,20},{8,24},{12,28},{16,0},{20,4},{24,8},{28,12},{1,17},{... | collective-permute-start | bytes 1990664 | tf_op jit(solution)/shard_map/ppermute | solution.py:49
  91.7 33.5 %collective-permute-start.8 = (bf16[2,2,144,1152]{3,2,1,0:T(8,128)(2,1)S(1)}, bf16[2,2,144,1152]{3,2,1,0:T(8,128)(2,1)S(1)}, u32[]{:S(2)}, u32[]{:S(2)}) collective-permute-start(bf16[2,2,144,1152]{3,2,1,0:T(8,128)(2,1)S(1)} %pad_maximum_fusion.7), channel_id=1, source_target_pairs={{0,8},{4,12},{8,0},{12,4},{16,24},{20,28},{24,16},{28,20},{1,9},{5... | collective-permute-start | bytes 3981320 | tf_op jit(solution)/shard_map/ppermute | solution.py:49
  92.8 32.3 %collective-permute-start.7 = (bf16[2,2,144,1152]{3,2,1,0:T(8,128)(2,1)S(1)}, bf16[2,2,144,1152]{3,2,1,0:T(8,128)(2,1)S(1)}, u32[]{:S(2)}, u32[]{:S(2)}) collective-permute-start(bf16[2,2,144,1152]{3,2,1,0:T(8,128)(2,1)S(1)} %pad_maximum_fusion.6), channel_id=1, source_target_pairs={{0,16},{4,20},{8,24},{12,28},{16,0},{20,4},{24,8},{28,12},{1,17},{... | collective-permute-start | bytes 3981320 | tf_op jit(solution)/shard_map/ppermute | solution.py:49
  147.5 38.0 %collective-permute-start.20 = (bf16[2,2,144,1152]{3,2,1,0:T(8,128)(2,1)S(1)}, bf16[2,2,144,1152]{3,2,1,0:T(8,128)(2,1)}, u32[]{:S(2)}, u32[]{:S(2)}) collective-permute-start(bf16[2,2,144,1152]{3,2,1,0:T(8,128)(2,1)S(1)} %pad_maximum_fusion.9), channel_id=1, source_target_pairs={{0,8},{4,12},{8,0},{12,4},{16,24},{20,28},{24,16},{28,20},{1,9},{5... | collective-permute-start | bytes 3981320 | tf_op jit(solution)/shard_map/ppermute | solution.py:49
  151.4 34.1 %collective-permute-start.19 = (bf16[2,2,144,1152]{3,2,1,0:T(8,128)(2,1)}, bf16[2,2,144,1152]{3,2,1,0:T(8,128)(2,1)}, u32[]{:S(2)}, u32[]{:S(2)}) collective-permute-start(bf16[2,2,144,1152]{3,2,1,0:T(8,128)(2,1)} %pad_maximum_fusion.8), channel_id=1, source_target_pairs={{0,16},{4,20},{8,24},{12,28},{16,0},{20,4},{24,8},{28,12},{1,17},{... | collective-permute-start | bytes 3981320 | tf_op jit(solution)/shard_map/ppermute | solution.py:49
  232.3 37.5 %collective-permute-start.30 = (bf16[2,2,144,1152]{3,2,1,0:T(8,128)(2,1)S(1)}, bf16[2,2,144,1152]{3,2,1,0:T(8,128)(2,1)S(1)}, u32[]{:S(2)}, u32[]{:S(2)}) collective-permute-start(bf16[2,2,144,1152]{3,2,1,0:T(8,128)(2,1)S(1)} %pad_maximum_fusion.11), channel_id=1, source_target_pairs={{0,8},{4,12},{8,0},{12,4},{16,24},{20,28},{24,16},{28,20},{1,9},{5... | collective-permute-start | bytes 3981320 | tf_op jit(solution)/shard_map/ppermute | solution.py:49
  233.9 35.9 %collective-permute-start.29 = (bf16[2,2,144,1152]{3,2,1,0:T(8,128)(2,1)S(1)}, bf16[2,2,144,1152]{3,2,1,0:T(8,128)(2,1)S(1)}, u32[]{:S(2)}, u32[]{:S(2)}) collective-permute-start(bf16[2,2,144,1152]{3,2,1,0:T(8,128)(2,1)S(1)} %pad_maximum_fusion.10), channel_id=1, source_target_pairs={{0,16},{4,20},{8,24},{12,28},{16,0},{20,4},{24,8},{28,12},{1,17},{... | collective-permute-start | bytes 3981320 | tf_op jit(solution)/shard_map/ppermute | solution.py:49
  320.1 31.7 %collective-permute-start.36 = (bf16[2,2,144,1152]{3,2,1,0:T(8,128)(2,1)}, bf16[2,2,144,1152]{3,2,1,0:T(8,128)(2,1)S(1)}, u32[]{:S(2)}, u32[]{:S(2)}) collective-permute-start(bf16[2,2,144,1152]{3,2,1,0:T(8,128)(2,1)} %get-tuple-element.204), channel_id=1, source_target_pairs={{0,16},{4,20},{8,24},{12,28},{16,0},{20,4},{24,8},{28,12},{1,17},{... | collective-permute-start | bytes 3981320 | tf_op jit(solution)/shard_map/ppermute | solution.py:49
  321.3 31.6 %collective-permute-start.37 = (bf16[2,2,144,1152]{3,2,1,0:T(8,128)(2,1)}, bf16[2,2,144,1152]{3,2,1,0:T(8,128)(2,1)}, u32[]{:S(2)}, u32[]{:S(2)}) collective-permute-start(bf16[2,2,144,1152]{3,2,1,0:T(8,128)(2,1)} %get-tuple-element.205), channel_id=1, source_target_pairs={{0,8},{4,12},{8,0},{12,4},{16,24},{20,28},{24,16},{28,20},{1,9},{5... | collective-permute-start | bytes 3981320 | tf_op jit(solution)/shard_map/ppermute | solution.py:49
  429.5 32.9 %collective-permute-start.46 = (bf16[2,2,512,384]{3,2,1,0:T(8,128)(2,1)}, bf16[2,2,512,384]{3,2,1,0:T(8,128)(2,1)S(1)}, u32[]{:S(2)}, u32[]{:S(2)}) collective-permute-start(bf16[2,2,512,384]{3,2,1,0:T(8,128)(2,1)} %get-tuple-element.230), channel_id=1, source_target_pairs={{0,4},{4,0},{8,12},{12,8},{16,20},{20,16},{24,28},{28,24},{1,5},{5... | collective-permute-start | bytes 4718600 | tf_op jit(solution)/shard_map/ppermute | solution.py:53
  429.6 31.8 %collective-permute-start.44 = (bf16[2,2,144,1152]{3,2,1,0:T(8,128)(2,1)}, bf16[2,2,144,1152]{3,2,1,0:T(8,128)(2,1)S(1)}, u32[]{:S(2)}, u32[]{:S(2)}) collective-permute-start(bf16[2,2,144,1152]{3,2,1,0:T(8,128)(2,1)} %get-tuple-element.224), channel_id=1, source_target_pairs={{0,16},{4,20},{8,24},{12,28},{16,0},{20,4},{24,8},{28,12},{1,17},{... | collective-permute-start | bytes 3981320 | tf_op jit(solution)/shard_map/ppermute | solution.py:49
  431.0 31.5 %collective-permute-start.45 = (bf16[2,2,144,1152]{3,2,1,0:T(8,128)(2,1)}, bf16[2,2,144,1152]{3,2,1,0:T(8,128)(2,1)}, u32[]{:S(2)}, u32[]{:S(2)}) collective-permute-start(bf16[2,2,144,1152]{3,2,1,0:T(8,128)(2,1)} %get-tuple-element.225), channel_id=1, source_target_pairs={{0,8},{4,12},{8,0},{12,4},{16,24},{20,28},{24,16},{28,20},{1,9},{5... | collective-permute-start | bytes 3981320 | tf_op jit(solution)/shard_map/ppermute | solution.py:49
  487.1 50.7 %collective-permute-start.53 = (bf16[4,4,144,1152]{3,2,1,0:T(8,128)(2,1)}, bf16[4,4,144,1152]{3,2,1,0:T(8,128)(2,1)}, u32[]{:S(2)}, u32[]{:S(2)}) collective-permute-start(bf16[4,4,144,1152]{3,2,1,0:T(8,128)(2,1)} %w_attn_send.1), channel_id=1, source_target_pairs={{0,4},{4,0},{8,12},{12,8},{16,20},{20,16},{24,28},{28,24},{1,5},{5... | collective-permute-start | bytes 15925256 | tf_op jit(solution)/shard_map/ppermute | solution.py:53
  490.9 69.5 %all-to-all-start.4 = ((f32[32,1,4032]{2,1,0:T(1,128)}), f32[32,1,4032]{2,1,0:T(1,128)S(1)}, u32[]{:S(2)}, u32[]{:S(2)}) async-start(f32[32,1,4032]{2,1,0:T(1,128)} %all_to_all.26), calls=%async_computation.4 | async-start | bytes 1048576 | tf_op jit(solution)/shard_map/all_to_all | solution.py:1088
  500.6 37.1 %collective-permute-start.52 = (bf16[144,1152]{1,0:T(8,128)(2,1)S(1)}, bf16[144,1152]{1,0:T(8,128)(2,1)}, u32[]{:S(2)}, u32[]{:S(2)}) collective-permute-start(bf16[144,1152]{1,0:T(8,128)(2,1)S(1)} %get-tuple-element.362), channel_id=1, source_target_pairs={{0,3},{1,2},{2,1},{3,0},{4,7},{5,6},{6,5},{7,4},{8,11},{9,10},{10,... | collective-permute-start | bytes 995336 | tf_op jit(solution)/shard_map/ppermute | solution.py:57
  502.1 35.7 %collective-permute-start.50 = (bf16[144,1152]{1,0:T(8,128)(2,1)S(1)}, bf16[144,1152]{1,0:T(8,128)(2,1)}, u32[]{:S(2)}, u32[]{:S(2)}) collective-permute-start(bf16[144,1152]{1,0:T(8,128)(2,1)S(1)} %slice_bitcast_fusion.8), channel_id=1, source_target_pairs={{0,1},{1,0},{2,3},{3,2},{4,5},{5,4},{6,7},{7,6},{8,9},{9,8},{10,11... | collective-permute-start | bytes 995336 | tf_op jit(solution)/shard_map/ppermute | solution.py:57
  551.3 52.7 %collective-permute-start.56 = (bf16[2,2,144,1152]{3,2,1,0:T(8,128)(2,1)}, bf16[2,2,144,1152]{3,2,1,0:T(8,128)(2,1)}, u32[]{:S(2)}, u32[]{:S(2)}) collective-permute-start(bf16[2,2,144,1152]{3,2,1,0:T(8,128)(2,1)} %get-tuple-element.257), channel_id=1, source_target_pairs={{0,16},{4,20},{8,24},{12,28},{16,0},{20,4},{24,8},{28,12},{1,17},{... | collective-permute-start | bytes 3981320 | tf_op jit(solution)/shard_map/ppermute | solution.py:49
  552.8 51.1 %collective-permute-start.57 = (bf16[2,2,144,1152]{3,2,1,0:T(8,128)(2,1)}, bf16[2,2,144,1152]{3,2,1,0:T(8,128)(2,1)}, u32[]{:S(2)}, u32[]{:S(2)}) collective-permute-start(bf16[2,2,144,1152]{3,2,1,0:T(8,128)(2,1)} %get-tuple-element.258), channel_id=1, source_target_pairs={{0,8},{4,12},{8,0},{12,4},{16,24},{20,28},{24,16},{28,20},{1,9},{5... | collective-permute-start | bytes 3981320 | tf_op jit(solution)/shard_map/ppermute | solution.py:49
  554.5 49.4 %collective-permute-start.54 = (bf16[256,1152]{1,0:T(8,128)(2,1)}, bf16[256,1152]{1,0:T(8,128)(2,1)}, u32[]{:S(2)}, u32[]{:S(2)}) collective-permute-start(bf16[256,1152]{1,0:T(8,128)(2,1)} %get-tuple-element.351), channel_id=1, source_target_pairs={{0,0},{1,1},{4,2},{5,3},{2,4},{3,5},{6,6},{7,7},{8,8},{9,9},{12,10... | collective-permute-start | bytes 1769480 | tf_op jit(solution)/shard_map/ppermute | solution.py:905
  560.4 43.5 %collective-permute-start.55 = (bf16[256,1152]{1,0:T(8,128)(2,1)}, bf16[256,1152]{1,0:T(8,128)(2,1)}, u32[]{:S(2)}, u32[]{:S(2)}) collective-permute-start(bf16[256,1152]{1,0:T(8,128)(2,1)} %get-tuple-element.350), channel_id=1, source_target_pairs={{1,0},{0,1},{5,2},{4,3},{3,4},{2,5},{7,6},{6,7},{9,8},{8,9},{13,10... | collective-permute-start | bytes 1769480 | tf_op jit(solution)/shard_map/ppermute | solution.py:905
  561.2 31.5 %all-to-all-start.2 = ((f32[32,6,288]{2,1,0:T(8,128)}), f32[32,6,288]{2,1,0:T(8,128)S(1)}, u32[]{:S(2)}, u32[]{:S(2)}) async-start(f32[32,6,288]{2,1,0:T(8,128)} %bitcast.49), calls=%async_computation.2 | async-start | bytes 786432 | tf_op jit(solution)/shard_map/all_to_all | solution.py:1098
  (111 other events, 1712.1 us)

commit v3 on v2

--- a/solution.py
+++ b/solution.py
@@ -33,6 +33,16 @@
         self.order = (self.orders(self.bits[::-1]), self.orders(self.bits))
         self.direct = self.R % 16 == 0
 
+    def windows(self, w):
+        self.w = w
+        self.n3 = min(padded(3 * w), 4 * w)
+        self.kbase = w // 128 * 128
+        self.koff = w - self.kbase
+        self.kvw = self.n3 - self.kbase
+        self.base = 3 * w // 128 * 128
+        self.off = 3 * w - self.base
+        self.win = 4 * w - self.base
+
     @staticmethod
     def orders(msb_first):
         vals = [0]
@@ -82,16 +92,25 @@
         return self.result
 
 
-def gather_steps(shard, geo):
-    got = yield [flip_tensor(shard, k, geo) for k in range(1, geo.T)]
-    parts = [shard] + got
+def gather_steps(shard, geo, parted=True, joined=False):
+    if parted:
+        far = yield [flip_tensor(shard, k, geo) for k in range(geo.Th + 1, geo.T)]
+        near = yield [flip_tensor(shard, k, geo) for k in range(1, geo.Th)]
+        mid = yield [flip_tensor(shard, geo.Th, geo)]
+        parts = [shard] + near + mid + far
+    else:
+        got = yield [flip_tensor(shard, k, geo) for k in range(1, geo.T)]
+        parts = [shard] + got
     bufs = [jnp.stack(parts[h * geo.Th : (h + 1) * geo.Th])[None] for h in range(2)]
     for at in range(len(geo.bits)):
         bits = (geo.bits[at], geo.bits[-1 - at])
         got = yield [flip_pair(bufs[h], bits[h], geo) for h in range(2)]
-        bufs = [jnp.concatenate(pair) for pair in zip(bufs, got)]
-    got = yield [flip_core(b, geo) for b in bufs]
-    return [[bufs[h], got[h]] for h in range(2)]
+        if joined or at < len(geo.bits) - 1:
+            bufs = [jnp.concatenate(pair) for pair in zip(bufs, got)]
+    owns = [[buf] for buf in bufs] if joined else [list(pair) for pair in zip(bufs, got)]
+    count = len(owns[0])
+    others = yield [flip_core(a, geo) for own in owns for a in own]
+    return [owns[h] + others[h * count : (h + 1) * count] for h in range(2)]
 
 
 class Gathered:
@@ -118,41 +137,74 @@
         self.n = len(halves[0])
         self.width = self.arrays[0].shape[-1]
 
+    def operands(self, half=None):
+        return self.arrays if half is None else self.halves[half]
+
     def specs(self, half=None):
-        th = self.geo.Th
-        out = []
-        for idx, a in enumerate(self.arrays if half is None else self.halves[half]):
-            block = (a.shape[0], 1, a.shape[2], a.shape[3])
-            if half is not None:
-                out.append(pl.BlockSpec(block, lambda j, s: (0, j, 0, 0)))
-            elif idx < self.n:
-                out.append(pl.BlockSpec(block, lambda j, s: (0, jnp.minimum(j, th - 1), 0, 0)))
-            else:
-                out.append(pl.BlockSpec(block, lambda j, s: (0, jnp.maximum(j - th, 0), 0, 0)))
-        return out
-
-    def place(self, half, s_ref, refs, dst):
-        geo = self.geo
+        return [pl.BlockSpec(memory_space=pl.ANY)] * len(self.operands(half))
+
+    def scratch(self, lo=0, hi=None):
+        hi = self.width if hi is None else hi
+        if lo % 128 or hi % 128:
+            lo, hi = 0, self.width
+        self.lo, self.hi = lo, hi
+        count = self.n * self.arrays[0].shape[0]
+        return [
+            pltpu.VMEM((2, self.geo.D, hi - lo), BF),
+            pltpu.SemaphoreType.DMA((2, count)),
+        ]
+
+    def copies(self, group, slot, half, s_ref, refs, buf, sem):
+        geo, out = self.geo, []
         for at, ref in enumerate(refs):
             n, _, rows, _ = ref.shape
             for i in range(n):
+                row = 0
                 if geo.direct:
-                    rel = geo.order[half][i]
-                    row = 2 * (s_ref[0] ^ rel) + (s_ref[1] ^ at)
+                    place = at * n + i
+                    rel = geo.order[half][place % geo.P]
+                    row = 2 * (s_ref[0] ^ rel) + (s_ref[1] ^ (place // geo.P))
                     row = pl.multiple_of(row * rows, rows)
-                else:
-                    row = 0
-                dst[pl.ds(row, rows), :] = ref[i, 0]
-
-    def assemble(self, j, s_ref, refs, dst):
-        for half in range(2):
-
-            @pl.when((j < self.geo.Th) if half == 0 else (j >= self.geo.Th))
-            def _():
-                self.place(half, s_ref, refs[half * self.n : (half + 1) * self.n], dst)
-
-
-def scatter_steps(pieces, geo):
+                out.append(
+                    pltpu.make_async_copy(
+                        ref.at[i, group, :, pl.ds(self.lo, self.hi - self.lo)],
+                        buf.at[slot, pl.ds(row, rows), :],
+                        sem.at[slot, at * n + i],
+                    )
+                )
+        return out
+
+    def stream(self, j, s_ref, refs, buf, sem, half=None):
+        th = self.geo.Th
+
+        def each(step, act):
+            if half is not None:
+                for copy in self.copies(step, step % 2, half, s_ref, refs, buf, sem):
+                    act(copy)
+                return
+            for part in range(2):
+
+                @pl.when((step < th) if part == 0 else (step >= th))
+                def _():
+                    mine = refs[part * self.n : (part + 1) * self.n]
+                    for copy in self.copies(
+                        step - part * th, step % 2, part, s_ref, mine, buf, sem
+                    ):
+                        act(copy)
+
+        @pl.when(j == 0)
+        def _():
+            each(j, lambda copy: copy.start())
+
+        @pl.when(j + 1 < (self.geo.T if half is None else th))
+        def _():
+            each(j + 1, lambda copy: copy.start())
+
+        each(j, lambda copy: copy.wait())
+        return buf.at[j % 2]
+
+
+def scatter_steps(pieces, geo, parted=True):
     def add(a, b):
         return a.astype(F32) + b.astype(F32)
 
@@ -165,7 +217,12 @@
             sends = [add(keeps[h][m:], got[h][m:]).astype(BF) for h in range(2)]
         keeps = [add(keeps[h][:m], got[h][:m]).astype(BF) for h in range(2)]
     units = [keep[0, k] for keep in keeps for k in range(geo.Th)]
-    got = yield [flip_tensor(units[k], k, geo) for k in range(1, geo.T)]
+    if parted:
+        rest = [k for k in range(1, geo.T) if k != geo.Th]
+        got = yield [flip_tensor(units[k], k, geo) for k in rest]
+        got += yield [flip_tensor(units[geo.Th], geo.Th, geo)]
+    else:
+        got = yield [flip_tensor(units[k], k, geo) for k in range(1, geo.T)]
     total = units[0].astype(F32)
     for part in got:
         total = total + part.astype(F32)
@@ -237,19 +294,18 @@
     )(x, mod)
 
 
-def in_proj(scal, h, wt, bias, w, half, geo):
+def in_proj(scal, h, wt, bias, half, geo):
     n, d = h.shape
-    wp = padded(w)
+    n3, wp = geo.n3, padded(geo.w)
     nw = wt.n
 
     def kernel(s, h_ref, b_ref, *refs):
-        w_refs, (q_ref, kv_ref, wbuf) = refs[:nw], refs[nw:]
-        wt.place(half, s, w_refs, wbuf)
-        y = dotg(h_ref[...], wbuf[:, : 3 * w], 1, 0) + b_ref[0]
+        w_refs, (q_ref, kv_ref, wbuf, sem) = refs[:nw], refs[nw:]
+        now = wt.stream(pl.program_id(0), s, w_refs, wbuf, sem, half)
+        y = dotg(h_ref[...], now[:, :n3], 1, 0) + b_ref[0]
         y = y.astype(BF)
-        q_ref[0, :, :w] = y[:, :w]
-        kv_ref[0, 0, :, :w] = y[:, w : 2 * w]
-        kv_ref[0, 1, :, :w] = y[:, 2 * w :]
+        q_ref[0] = y[:, :wp]
+        kv_ref[0] = y[:, geo.kbase :]
 
     first = half * geo.Th
     return pl.pallas_call(
@@ -259,84 +315,91 @@
             grid=(geo.Th,),
             in_specs=[
                 whole((n, d)),
-                pl.BlockSpec((1, 1, 3 * w), lambda j, s: (s[2] ^ (j + first), 0, 0)),
+                pl.BlockSpec((1, 1, n3), lambda j, s: (s[2] ^ (j + first), 0, 0)),
                 *wt.specs(half),
             ],
             out_specs=[
                 pl.BlockSpec((1, n, wp), lambda j, s: (j, 0, 0)),
-                pl.BlockSpec((1, 2, n, wp), lambda j, s: (j, 0, 0, 0)),
+                pl.BlockSpec((1, n, geo.kvw), lambda j, s: (j, 0, 0)),
             ],
-            scratch_shapes=[pltpu.VMEM((d, wt.width), BF)],
+            scratch_shapes=wt.scratch(0, n3),
         ),
         out_shape=[
             jax.ShapeDtypeStruct((geo.Th, n, wp), BF),
-            jax.ShapeDtypeStruct((geo.Th, 2, n, wp), BF),
+            jax.ShapeDtypeStruct((geo.Th, n, geo.kvw), BF),
         ],
         compiler_params=params(),
-        cost_estimate=cost(6 * n * d * w * geo.Th, 8 * d * w * geo.Th + 8 * n * d),
+        cost_estimate=cost(2 * n * d * n3 * geo.Th, 8 * d * geo.w * geo.Th + 8 * n * d),
         name="in_proj",
-    )(scal, h, bias, *wt.halves[half])
-
-
-def attn_fwd(q, kv, kvo, heads):
-    z, n, w = q.shape
-    used = heads * HEAD_DIM
+    )(scal, h, bias, *wt.operands(half))
+
+
+def head_lanes(geo, h):
+    at = h * HEAD_DIM
+    return [
+        slice(start + at, start + at + HEAD_DIM)
+        for start in (0, geo.koff, geo.koff + geo.w, geo.off)
+    ]
+
+
+def attn_fwd(q, kv, kvo, geo):
+    z, n, wp = q.shape
+    heads = geo.w // HEAD_DIM
     c = HEAD_DIM**-0.5 * LOG2E
 
     def kernel(q_ref, kv_ref, kvo_ref, o_ref, lse_ref):
-        outs = []
+        outs = [jnp.zeros((geo.off, n), F32)] if geo.off else []
         for h in range(heads):
-            sl = slice(h * HEAD_DIM, (h + 1) * HEAD_DIM)
-            qh = q_ref[0, :, sl]
-            sa = dotg(kv_ref[0, 0, :, sl], qh, 1, 1) * c
-            sb = dotg(kvo_ref[0, 0, :, sl], qh, 1, 1) * c
+            lq, lk, lv, _ = head_lanes(geo, h)
+            qh = q_ref[0, :, lq]
+            sa = dotg(kv_ref[0, :, lk], qh, 1, 1) * c
+            sb = dotg(kvo_ref[0, :, lk], qh, 1, 1) * c
             top = jnp.maximum(
                 jnp.max(sa, axis=0, keepdims=True), jnp.max(sb, axis=0, keepdims=True)
             )
             pa, pb = jnp.exp2(sa - top), jnp.exp2(sb - top)
             total = jnp.sum(pa, axis=0, keepdims=True) + jnp.sum(pb, axis=0, keepdims=True)
-            o = dotg(kv_ref[0, 1, :, sl], pa.astype(BF), 0, 0)
-            o = o + dotg(kvo_ref[0, 1, :, sl], pb.astype(BF), 0, 0)
+            o = dotg(kv_ref[0, :, lv], pa.astype(BF), 0, 0)
+            o = o + dotg(kvo_ref[0, :, lv], pb.astype(BF), 0, 0)
             outs.append(o / total)
             lse_ref[0, h : h + 1, :] = top + jnp.log2(total)
-        o_ref[0, :, :used] = jnp.concatenate(outs, axis=0).T.astype(BF)
-
-    s3 = pl.BlockSpec((1, n, w), lambda j: (j, 0, 0))
-    s4 = pl.BlockSpec((1, 2, n, w), lambda j: (j, 0, 0, 0))
-    sl = pl.BlockSpec((1, heads, n), lambda j: (j, 0, 0))
+        o_ref[0] = jnp.concatenate(outs, axis=0).T.astype(BF)
+
+    def spec(width):
+        return pl.BlockSpec((1, n, width), lambda j: (j, 0, 0))
+
     return pl.pallas_call(
         kernel,
         grid=(z,),
-        in_specs=[s3, s4, s4],
-        out_specs=[s3, sl],
+        in_specs=[spec(wp), spec(geo.kvw), spec(geo.kvw)],
+        out_specs=[spec(geo.win), pl.BlockSpec((1, heads, n), lambda j: (j, 0, 0))],
         out_shape=[
-            jax.ShapeDtypeStruct((z, n, w), BF),
+            jax.ShapeDtypeStruct((z, n, geo.win), BF),
             jax.ShapeDtypeStruct((z, heads, n), F32),
         ],
         compiler_params=params(),
-        cost_estimate=cost(3e9 * z, 14 * z * n * w),
+        cost_estimate=cost(3e9 * z, 10 * z * n * wp),
         name="attn_fwd",
     )(q, kv, kvo)
 
 
-def attn_bwd(q, kv, kvo, o, do, lse, first):
-    z, n, w = q.shape
+def attn_bwd(q, kv, kvo, o, do, lse, first, geo):
+    z, n, wp = q.shape
     heads = lse.shape[1]
-    used = heads * HEAD_DIM
     scale = HEAD_DIM**-0.5
     c = scale * LOG2E
 
-    def kernel(q_ref, kv_ref, kvo_ref, o_ref, do_ref, lse_ref, dq_ref, dkv_ref, dkvo_ref, sum_ref):
-        both = (do_ref[0, :, :used].astype(F32) * o_ref[0, :, :used].astype(F32)).T
+    def kernel(q_ref, kv_ref, kvo_ref, o_ref, do_ref, lse_ref, tri_ref, send_ref, ts_ref, ss_ref):
+        both = (do_ref[0].astype(F32) * o_ref[0].astype(F32)).T
         dqs, parts = [], [[[], []], [[], []]]
         for h in range(heads):
-            sl = slice(h * HEAD_DIM, (h + 1) * HEAD_DIM)
-            qh, doh = q_ref[0, :, sl], do_ref[0, :, sl]
-            delta = jnp.sum(both[sl], axis=0, keepdims=True)
+            lq, lk, lv, lm = head_lanes(geo, h)
+            qh, doh = q_ref[0, :, lq], do_ref[0, :, lm]
+            delta = jnp.sum(both[lm], axis=0, keepdims=True)
             lse_h = lse_ref[0, h : h + 1, :]
             dq = None
             for i, ref in enumerate((kv_ref, kvo_ref)):
-                k, v = ref[0, 0, :, sl], ref[0, 1, :, sl]
+                k, v = ref[0, :, lk], ref[0, :, lv]
                 p = jnp.exp2(dotg(k, qh, 1, 1) * c - lse_h)
                 ds = (p * (dotg(v, doh, 1, 1) - delta)).astype(BF)
                 parts[i][1].append(dotg(doh, p.astype(BF), 0, 1))
@@ -344,52 +407,64 @@
                 got = dotg(k, ds, 0, 0)
                 dq = got if dq is None else dq + got
             dqs.append(dq * scale)
-        dq = jnp.concatenate(dqs, axis=0).T
-        dq_ref[0, :, :used] = dq.astype(BF)
-        sum_ref[0, 0:1, :] = jnp.sum(dq, axis=0, keepdims=True)
-        dv_sum = None
-        for i, ref in enumerate((dkv_ref, dkvo_ref)):
-            for at in range(2):
-                full = jnp.concatenate(parts[i][at], axis=0).T
-                ref[0, at, :, :used] = full.astype(BF)
-                if at == 1:
-                    now = jnp.sum(full, axis=0, keepdims=True)
-                    dv_sum = now if dv_sum is None else dv_sum + now
-        sum_ref[0, 1:2, :] = dv_sum
-
-    s3 = pl.BlockSpec((1, n, w), lambda j: (j, 0, 0))
-    s4 = pl.BlockSpec((1, 2, n, w), lambda j: (j, 0, 0, 0))
-    sl = pl.BlockSpec((1, heads, n), lambda j: (j, 0, 0))
+
+        def rows(count):
+            return [jnp.zeros((count, n), F32)] if count else []
+
+        pad = rows(geo.n3 - 3 * geo.w)
+        own = jnp.concatenate(dqs + parts[0][0] + parts[0][1] + pad, axis=0).T
+        other = jnp.concatenate(rows(geo.koff) + parts[1][0] + parts[1][1] + pad, axis=0).T
+        tri_ref[0] = own.astype(BF)
+        send_ref[0] = other.astype(BF)
+        ts_ref[0] = jnp.sum(own, axis=0, keepdims=True)
+        ss_ref[0] = jnp.sum(other, axis=0, keepdims=True)
+
+    def spec(width, at=0, count=n):
+        return pl.BlockSpec((1, count, width), lambda j: (j + at, 0, 0))
+
     return pl.pallas_call(
         kernel,
         grid=(z,),
-        in_specs=[s3, s4, s4, s3, pl.BlockSpec((1, n, w), lambda j: (j + first, 0, 0)), sl],
-        out_specs=[s3, s4, s4, pl.BlockSpec((1, 2, used), lambda j: (j, 0, 0))],
+        in_specs=[
+            spec(wp),
+            spec(geo.kvw),
+            spec(geo.kvw),
+            spec(geo.win),
+            spec(geo.win, first),
+            spec(n, 0, heads),
+        ],
+        out_specs=[spec(geo.n3), spec(geo.kvw), spec(geo.n3, 0, 1), spec(geo.kvw, 0, 1)],
         out_shape=[
-            jax.ShapeDtypeStruct((z, n, w), BF),
-            jax.ShapeDtypeStruct((z, 2, n, w), BF),
-            jax.ShapeDtypeStruct((z, 2, n, w), BF),
-            jax.ShapeDtypeStruct((z, 2, used), F32),
+            jax.ShapeDtypeStruct((z, n, geo.n3), BF),
+            jax.ShapeDtypeStruct((z, n, geo.kvw), BF),
+            jax.ShapeDtypeStruct((z, 1, geo.n3), F32),
+            jax.ShapeDtypeStruct((z, 1, geo.kvw), F32),
         ],
         compiler_params=params(),
-        cost_estimate=cost(5e9 * z, 24 * z * n * w),
+        cost_estimate=cost(5e9 * z, 16 * z * n * wp),
         name="attn_bwd",
     )(q, kv, kvo, o, do, lse)
 
 
+def triple_grad(tri_ref, got_ref, geo):
+    late = tri_ref[0, :, geo.kbase :].astype(F32) + got_ref[0].astype(F32)
+    if not geo.kbase:
+        return late.astype(BF)
+    return jnp.concatenate([tri_ref[0, :, : geo.kbase], late.astype(BF)], axis=1)
+
+
 def out_proj(scal, mixed, x, mod, bias, wt, geo):
-    _, n, wp = mixed[0].shape
-    w = wt.width // 4
+    _, n, win = mixed[0].shape
     d = geo.D
     nw = len(wt.arrays)
     th = geo.Th
 
     def kernel(s, ya_ref, yb_ref, x_ref, m_ref, b_ref, *refs):
-        w_refs, (attn_ref, resid_ref, h_ref, wbuf) = refs[:nw], refs[nw:]
+        w_refs, (attn_ref, resid_ref, h_ref, wbuf, sem) = refs[:nw], refs[nw:]
         j = pl.program_id(0)
-        wt.assemble(j, s, w_refs, wbuf)
-        y = jnp.where(j < th, ya_ref[0, :, :w], yb_ref[0, :, :w])
-        part = dotg(y, wbuf[:, 3 * w :], 1, 1)
+        now = wt.stream(j, s, w_refs, wbuf, sem)
+        y = jnp.where(j < th, ya_ref[0], yb_ref[0])
+        part = dotg(y, now[:, -win:], 1, 1)
 
         @pl.when(j == 0)
         def _():
@@ -417,14 +492,14 @@
             num_scalar_prefetch=1,
             grid=(geo.T,),
             in_specs=[
-                *two_halves((1, n, wp), th, (0, 0)),
+                *two_halves((1, n, win), th, (0, 0)),
                 whole((n, d)),
                 whole(mod.shape),
                 whole((1, d)),
                 *wt.specs(),
             ],
             out_specs=[whole((n, d))] * 3,
-            scratch_shapes=[pltpu.VMEM((d, wt.width), BF)],
+            scratch_shapes=wt.scratch(geo.base, 4 * geo.w),
         ),
         out_shape=[
             jax.ShapeDtypeStruct((n, d), F32),
@@ -444,12 +519,12 @@
     step = chunked(w, 384)
 
     def kernel(s, h_ref, b_ref, *refs):
-        w_refs, (hid_ref, gp_ref, wbuf) = refs[:nw], refs[nw:]
+        w_refs, (hid_ref, gp_ref, wbuf, sem) = refs[:nw], refs[nw:]
         j = pl.program_id(0)
-        wt.assemble(j, s, w_refs, wbuf)
+        now = wt.stream(j, s, w_refs, wbuf, sem)
         for at in range(0, w, step):
             cols = slice(at, at + step)
-            u = dotg(h_ref[...], wbuf[:, cols], 1, 0) + b_ref[0, :, cols]
+            u = dotg(h_ref[...], now[:, cols], 1, 0) + b_ref[0, :, cols]
             sq = u * u
             t = jnp.tanh(TANH_C * (u + CUBIC * sq * u))
             half = 0.5 * (1.0 + t)
@@ -469,7 +544,7 @@
                 *wt.specs(),
             ],
             out_specs=[out, out],
-            scratch_shapes=[pltpu.VMEM((d, w), BF)],
+            scratch_shapes=wt.scratch(),
         ),
         out_shape=[jax.ShapeDtypeStruct((geo.T, n, w), BF)] * 2,
         compiler_params=params(),
@@ -484,10 +559,10 @@
     nw = len(wt.arrays)
 
     def kernel(s, y_ref, r_ref, c_ref, m_ref, b_ref, *refs):
-        w_refs, (out_ref, sum_ref, wbuf, acc) = refs[:nw], refs[nw:]
+        w_refs, (out_ref, sum_ref, wbuf, sem, acc) = refs[:nw], refs[nw:]
         j = pl.program_id(0)
-        wt.assemble(j, s, w_refs, wbuf)
-        part = dotg(y_ref[0], wbuf[...], 1, 1)
+        now = wt.stream(j, s, w_refs, wbuf, sem)
+        part = dotg(y_ref[0], now[...], 1, 1)
 
         @pl.when(j == 0)
         def _():
@@ -521,7 +596,7 @@
                 *wt.specs(),
             ],
             out_specs=[whole((n, d)), whole((8, d))],
-            scratch_shapes=[pltpu.VMEM((d, w), BF), pltpu.VMEM((n, d), F32)],
+            scratch_shapes=[*wt.scratch(), pltpu.VMEM((n, d), F32)],
         ),
         out_shape=[jax.ShapeDtypeStruct((n, d), BF), jax.ShapeDtypeStruct((8, d), F32)],
         compiler_params=params(),
@@ -537,12 +612,12 @@
     step = chunked(w, 384)
 
     def kernel(s, g_ref, gp_ref, *refs):
-        w_refs, (out_ref, sum_ref, wbuf) = refs[:nw], refs[nw:]
+        w_refs, (out_ref, sum_ref, wbuf, sem) = refs[:nw], refs[nw:]
         j = pl.program_id(0)
-        wt.assemble(j, s, w_refs, wbuf)
+        now = wt.stream(j, s, w_refs, wbuf, sem)
         for at in range(0, w, step):
             cols = slice(at, at + step)
-            y = dotg(g_ref[...], wbuf[:, cols], 1, 0) * gp_ref[0, :, cols].astype(F32)
+            y = dotg(g_ref[...], now[:, cols], 1, 0) * gp_ref[0, :, cols].astype(F32)
             out_ref[0, :, cols] = y.astype(BF)
             sum_ref[0, :, cols] = jnp.sum(y, axis=0, keepdims=True)
 
@@ -554,7 +629,7 @@
             grid=(geo.T,),
             in_specs=[whole((n, d)), out, *wt.specs()],
             out_specs=[out, pl.BlockSpec((1, 1, w), lambda j, s: (j, 0, 0))],
-            scratch_shapes=[pltpu.VMEM((d, w), BF)],
+            scratch_shapes=wt.scratch(),
         ),
         out_shape=[
             jax.ShapeDtypeStruct((geo.T, n, w), BF),
@@ -572,10 +647,10 @@
     nw = len(wt.arrays)
 
     def kernel(s, y_ref, r_ref, a_ref, c_ref, m_ref, *refs):
-        w_refs, (rg_ref, ag_ref, sum_ref, wbuf, acc) = refs[:nw], refs[nw:]
+        w_refs, (rg_ref, ag_ref, sum_ref, wbuf, sem, acc) = refs[:nw], refs[nw:]
         j = pl.program_id(0)
-        wt.assemble(j, s, w_refs, wbuf)
-        part = dotg(y_ref[0], wbuf[...], 1, 1)
+        now = wt.stream(j, s, w_refs, wbuf, sem)
+        part = dotg(y_ref[0], now[...], 1, 1)
 
         @pl.when(j == 0)
         def _():
@@ -616,7 +691,7 @@
                 *wt.specs(),
             ],
             out_specs=[whole((n, d)), whole((n, d)), whole((4, 8, d))],
-            scratch_shapes=[pltpu.VMEM((d, w), BF), pltpu.VMEM((n, d), F32)],
+            scratch_shapes=[*wt.scratch(), pltpu.VMEM((n, d), F32)],
         ),
         out_shape=[
             jax.ShapeDtypeStruct((n, d), F32),
@@ -631,13 +706,13 @@
 
 def mixed_back(scal, g, wt, geo):
     n, d = g.shape
-    w = wt.width // 4
+    win = geo.win
     nw = len(wt.arrays)
 
     def kernel(s, g_ref, *refs):
-        w_refs, (out_ref, wbuf) = refs[:nw], refs[nw:]
-        wt.assemble(pl.program_id(0), s, w_refs, wbuf)
-        out_ref[0, :, :w] = dotg(g_ref[...], wbuf[:, 3 * w :], 1, 0).astype(BF)
+        w_refs, (out_ref, wbuf, sem) = refs[:nw], refs[nw:]
+        now = wt.stream(pl.program_id(0), s, w_refs, wbuf, sem)
+        out_ref[0] = dotg(g_ref[...], now[:, -win:], 1, 0).astype(BF)
 
     return pl.pallas_call(
         kernel,
@@ -645,37 +720,33 @@
             num_scalar_prefetch=1,
             grid=(geo.T,),
             in_specs=[whole((n, d)), *wt.specs()],
-            out_specs=pl.BlockSpec((1, n, padded(w)), lambda j, s: (j, 0, 0)),
-            scratch_shapes=[pltpu.VMEM((d, wt.width), BF)],
+            out_specs=pl.BlockSpec((1, n, win), lambda j, s: (j, 0, 0)),
+            scratch_shapes=wt.scratch(geo.base, 4 * geo.w),
         ),
-        out_shape=jax.ShapeDtypeStruct((geo.T, n, padded(w)), BF),
+        out_shape=jax.ShapeDtypeStruct((geo.T, n, win), BF),
         compiler_params=params(),
         cost_estimate=cost(2 * n * d * d, 8 * d * d + 4 * n * d),
         name="mixed_back",
     )(scal, g, *wt.arrays)
 
 
-def first_back(scal, dq, dkv, got, x, rg, mod, wt, geo):
-    _, n, wp = dq[0].shape
-    w = wt.width // 4
+def first_back(scal, tri, got, x, rg, mod, wt, geo):
+    _, n, n3 = tri[0].shape
     d = geo.D
     nw = len(wt.arrays)
     th = geo.Th
 
-    def kernel(s, qa, qb, kva, kvb, ga, gb, x_ref, r_ref, m_ref, *refs):
-        w_refs, (out_ref, sum_ref, wbuf, lhs, acc) = refs[:nw], refs[nw:]
+    def kernel(s, ta, tb, ga, gb, x_ref, r_ref, m_ref, *refs):
+        w_refs, (out_ref, sum_ref, wbuf, sem, lhs, acc) = refs[:nw], refs[nw:]
         j = pl.program_id(0)
-        wt.assemble(j, s, w_refs, wbuf)
-        for half, (q, kv, g) in enumerate(((qa, kva, ga), (qb, kvb, gb))):
+        now = wt.stream(j, s, w_refs, wbuf, sem)
+        for half, (tri_ref, got_ref) in enumerate(((ta, ga), (tb, gb))):
 
             @pl.when((j < th) if half == 0 else (j >= th))
             def _():
-                lhs[:, :w] = q[0, :, :w]
-                for at in range(2):
-                    both = kv[0, at, :, :w].astype(F32) + g[0, at, :, :w].astype(F32)
-                    lhs[:, (at + 1) * w : (at + 2) * w] = both.astype(BF)
-
-        part = dotg(lhs[...], wbuf[:, : 3 * w], 1, 1)
+                lhs[...] = triple_grad(tri_ref, got_ref, geo)
+
+        part = dotg(lhs[...], now[:, :n3], 1, 1)
 
         @pl.when(j == 0)
         def _():
@@ -704,9 +775,8 @@
             num_scalar_prefetch=1,
             grid=(geo.T,),
             in_specs=[
-                *two_halves((1, n, wp), th, (0, 0)),
-                *two_halves((1, 2, n, wp), th, (0, 0, 0)),
-                *two_halves((1, 2, n, wp), th, (0, 0, 0)),
+                *two_halves((1, n, n3), th, (0, 0)),
+                *two_halves((1, n, geo.kvw), th, (0, 0)),
                 whole((n, d)),
                 whole((n, d)),
                 whole(mod.shape),
@@ -714,8 +784,8 @@
             ],
             out_specs=[whole((n, d)), whole((2, 8, d))],
             scratch_shapes=[
-                pltpu.VMEM((d, wt.width), BF),
-                pltpu.VMEM((n, 3 * w), BF),
+                *wt.scratch(0, n3),
+                pltpu.VMEM((n, n3), BF),
                 pltpu.VMEM((n, d), F32),
             ],
         ),
@@ -723,10 +793,10 @@
         compiler_params=params(),
         cost_estimate=cost(6 * n * d * d, 8 * d * d + 16 * n * d),
         name="first_back",
-    )(scal, *dq, *dkv, *got, x, rg, mod, *wt.arrays)
-
-
-def weight_grad(scal, terms, w, mine, geo, name, partial=None):
+    )(scal, *tri, *got, x, rg, mod, *wt.arrays)
+
+
+def weight_grad(scal, terms, join, w, mine, geo, name, partial=None):
     n = terms[0][0].shape[0]
     pr = geo.P * geo.R
     th = geo.Th
@@ -742,7 +812,7 @@
 
         lefts = [pick(a) for a in lefts]
     ops, op_specs, counts = [], [], []
-    for _, operands, _, _ in terms:
+    for _, operands, _ in terms:
         counts.append(len(operands))
         for pair in operands:
             if isinstance(pair, tuple):
@@ -779,7 +849,7 @@
 
         def store(half):
             at_op, parts = 0, []
-            for at, (_, operands, build, _) in zip(ats, terms):
+            for at, (_, operands, build) in zip(ats, terms):
                 blocks = []
                 for pair in operands:
                     if isinstance(pair, tuple):
@@ -789,7 +859,7 @@
                         blocks.append(b_refs[at_op])
                         at_op += 1
                 parts.append(dotg(at[...], build(*blocks), 1, 0))
-            full = parts[0] if len(parts) == 1 else jnp.concatenate(parts, axis=1)
+            full = join(*parts)
             if not geo.direct:
                 if mine:
                     full = full + got_ref[0, 0].astype(F32)
@@ -882,6 +952,7 @@
     scal = jnp.stack([pair, core, ti]).astype(jnp.int32)
     cols = in_weight.shape[2]
     units = up_weight.shape[1]
+    geo.windows(cols)
 
     def places(k):
         return [
@@ -921,8 +992,8 @@
         for way in chains:
             opened.extend(way.advance(*now))
 
-    def begin(shard, make):
-        way = Chain(make(tie(shard), geo))
+    def begin(shard, make, *how):
+        way = Chain(make(tie(shard), geo, *how))
         opened.extend(way.flight)
         return way
 
@@ -938,19 +1009,26 @@
 
     heads = cols // HEAD_DIM
     attn_shard = jnp.concatenate([in_weight[0], in_weight[1], in_weight[2], out_weight.T], axis=1)
-    attn_way = begin(attn_shard, gather_steps)
+    attn_way = begin(attn_shard, gather_steps, False)
     info = jnp.concatenate([conditioning.reshape(-1), query_value_bias.reshape(-1), up_bias])
+    count = info.shape[0]
+    info = jnp.pad(info, (0, -count % 2048)).reshape(-1, 128)
     info = share(info)
-    close(info)
+    close()
     start(attn_way)
-    x_parts = to_chip(tie(latents))
-    opened.extend(x_parts)
-    info = info.reshape(F, T, -1)
+    up_way = begin(up_weight, gather_steps, True, True)
+    info = info.reshape(F, T, -1)[:, :, :count]
     cond_all = info[:, 0, : images * width].reshape(F * images, width)
     qv_bias = info[0, :, images * width : images * width + 2 * cols].reshape(T, 2, 1, cols)
     unit_bias = info[0, :, images * width + 2 * cols :].reshape(T, 1, units).astype(F32)
     triple_bias = jnp.concatenate(
-        [qv_bias[:, 0], jnp.zeros_like(qv_bias[:, 0]), qv_bias[:, 1]], axis=2
+        [
+            qv_bias[:, 0],
+            jnp.zeros_like(qv_bias[:, 0]),
+            qv_bias[:, 1],
+            jnp.zeros((T, 1, geo.n3 - 3 * cols), BF),
+        ],
+        axis=2,
     ).astype(F32)
     silu_low = jax.nn.silu(cond_all.astype(F32)).astype(BF)
     silu_own = lax.dynamic_slice_in_dim(silu_low, fi * geo.R, geo.R, 1)
@@ -958,49 +1036,58 @@
     mod_part += jnp.where(fi == 0, mod_bias.astype(F32), 0.0)
     mod_part = mod_part.reshape(geo.P, 1, T, 6, cols)
     mod_part = jnp.broadcast_to(mod_part, (geo.P, 2, T, 6, cols)).reshape(F * T, 6, cols)
-    mod_part = lax.all_to_all(mod_part, BOTH, 0, 0, tiled=True)
+    mod_part = lax.all_to_all(after(mod_part, *up_way.flight), BOTH, 0, 0, tiled=True)
     mod = mod_part.reshape(F, T, 6, cols).sum(axis=0).transpose(1, 0, 2).reshape(6, width)
     bias_rows = branch_bias.astype(F32)
     close(mod)
+    start(attn_way)
+    start(up_way)
+    x_parts = to_chip(tie(latents))
+    opened.extend(x_parts)
+    close()
     x = jnp.concatenate(x_parts)
-    start(attn_way)
-    up_way = begin(up_weight, gather_steps)
-    close()
     start(attn_way, up_way)
     h1 = norm_mod(tie(x), mod)
     close(h1)
-    start(attn_way)
     w_attn = Gathered(attn_way.finish(*now), geo, scal)
-
     start(up_way)
-    down_way = begin(down_weight.T, gather_steps)
+
     q, kv, kvo = [None] * 2, [None] * 2, [None] * 2
     mixed, lse = [None] * 2, [None] * 2
+    down_way = begin(down_weight.T, gather_steps)
     for half in range(2):
-        q[half], kv[half] = in_proj(tie(scal), h1, w_attn, triple_bias, cols, half, geo)
+        q[half], kv[half] = in_proj(tie(scal), h1, w_attn, triple_bias, half, geo)
     close(q[0], q[1])
     kvo = [across(kv[0]), across(kv[1])]
-    start(up_way)
+    start(down_way)
     close()
-    start(down_way, up_way)
+    start(up_way, down_way)
+    for half in range(2):
+        mixed[half], lse[half] = attn_fwd(tie(q[half]), kv[half], kvo[half], geo)
+    attn, resid, h2 = out_proj(tie(scal), mixed, x, mod, bias_rows[0:1], w_attn, geo)
+    close(h2)
+    start(up_way, down_way)
+    close()
+    w_up = Gathered(up_way.finish(*now), geo, scal)
+    start(down_way)
     cot_parts = to_chip(tie(cotangent))
     opened.extend(cot_parts)
-    w_up = Gathered(up_way.finish(*now), geo, scal)
-    for half in range(2):
-        mixed[half], lse[half] = attn_fwd(tie(q[half]), kv[half], kvo[half], heads)
-    close(lse[0], lse[1])
+    hidden, gp = up_proj(tie(scal), h2, unit_bias, w_up, geo)
+    close(hidden)
     start(down_way)
     cot = jnp.concatenate(cot_parts)
-    attn, resid, h2 = out_proj(tie(scal), mixed, x, mod, bias_rows[0:1], w_attn, geo)
-    hidden, gp = up_proj(tie(scal), h2, unit_bias, w_up, geo)
     ffn_grad = (cot.astype(F32) * mod[5]).astype(BF)
     ffn_sum = jnp.sum(ffn_grad.astype(F32), axis=0)
-    close(hidden)
-    start(down_way)
-    down_terms = [(ffn_grad, [hidden], lambda ref: ref[0], units)]
-    down_half = weight_grad(tie(scal), down_terms, units, False, geo, "w_down_send")
+
+    def block(ref):
+        return ref[0]
+
+    def alone(part):
+        return part
+
+    down_terms = [(ffn_grad, [hidden], block)]
+    down_half = weight_grad(tie(scal), down_terms, alone, units, False, geo, "w_down_send")
     close(down_half)
-    start(down_way)
     w_down = Gathered(down_way.finish(*now), geo, scal)
     down_got = across(down_half)
     block_rows, ffn_sums = down_proj(
@@ -1008,63 +1095,93 @@
     )
     close(ffn_sums)
 
-    down_parts = weight_grad(tie(scal), down_terms, units, True, geo, "w_down", down_got)
+    down_parts = weight_grad(tie(scal), down_terms, alone, units, True, geo, "w_down", down_got)
     close(*down_parts)
     down_back = begin(down_parts, scatter_steps)
     block_back = from_chip(tie(block_rows))
     opened.extend(block_back)
     pre, unit_sum = pre_back(tie(scal), ffn_grad, gp, w_down, geo)
-    up_terms = [(h2, [pre], lambda ref: ref[0], units)]
-    up_half = weight_grad(tie(scal), up_terms, units, False, geo, "w_up_send")
+    up_terms = [(h2, [pre], block)]
+    up_half = weight_grad(tie(scal), up_terms, alone, units, False, geo, "w_up_send")
     close(up_half)
     start(down_back)
     up_got = across(up_half)
     rg, ag, mid_sums = second_back(tie(scal), pre, resid, attn, cot, mod, w_up, geo)
     close(ag)
     start(down_back)
-    up_parts = weight_grad(tie(scal), up_terms, units, True, geo, "w_up", up_got)
+    up_parts = weight_grad(tie(scal), up_terms, alone, units, True, geo, "w_up", up_got)
     mg = mixed_back(tie(scal), ag, w_attn, geo)
     close(mg, *up_parts)
     start(down_back)
-    up_back = begin(up_parts, scatter_steps)
-    dq, dkv, dkv_got, tri_sums = [None] * 2, [None] * 2, [None] * 2, [None] * 2
-    dkv_send = [None] * 2
+    up_back = begin(up_parts, scatter_steps, False)
+    tri, tri_send, tri_sums, send_sums = [None] * 2, [None] * 2, [None] * 2, [None] * 2
     for half in range(2):
-        dq[half], dkv[half], dkv_send[half], tri_sums[half] = attn_bwd(
-            tie(q[half]), kv[half], kvo[half], mixed[half], mg, lse[half], half * geo.Th
+        tri[half], tri_send[half], tri_sums[half], send_sums[half] = attn_bwd(
+            tie(q[half]), kv[half], kvo[half], mixed[half], mg, lse[half], half * geo.Th, geo
         )
-    dkv_got[0] = across(dkv_send[0])
     close(*tri_sums)
-    dkv_got[1] = across(dkv_send[1])
-    tri_sums = jnp.concatenate(tri_sums)
+    tri_got = [across(tri_send[0]), across(tri_send[1])]
+    tri_sum, send_sum = jnp.concatenate(tri_sums), jnp.concatenate(send_sums)
+    pair_sums = jnp.concatenate(
+        [
+            tri_sum[:, :, :cols],
+            tri_sum[:, :, 2 * cols : 3 * cols]
+            + send_sum[:, :, geo.koff + cols : geo.koff + 2 * cols],
+        ],
+        axis=1,
+    )
     close()
     start(up_back)
-
-    def triple(q_ref, kv_ref, got_ref):
-        parts = [q_ref[0, :, :cols]]
-        for at in range(2):
-            both = kv_ref[0, at, :, :cols].astype(F32) + got_ref[0, at, :, :cols].astype(F32)
-            parts.append(both.astype(BF))
-        return jnp.concatenate(parts, axis=1)
+    down_back.finish(*now)
+
+    def beside(first, second):
+        shared = geo.n3 - geo.base
+        middle = first[:, geo.base :] + second[:, :shared]
+        return jnp.concatenate([first[:, : geo.base], middle, second[:, shared:]], axis=1)
 
     attn_terms = [
-        (h1, [tuple(dq), tuple(dkv), tuple(dkv_got)], triple, 3 * cols),
-        (ag, [tuple(mixed)], lambda ref: ref[0, :, :cols], cols),
+        (h1, [tuple(tri), tuple(tri_got)], lambda a, b: triple_grad(a, b, geo)),
+        (ag, [tuple(mixed)], block),
     ]
-    attn_half = weight_grad(tie(scal), attn_terms, 4 * cols, False, geo, "w_attn_send")
+    attn_half = weight_grad(tie(scal), attn_terms, beside, 4 * cols, False, geo, "w_attn_send")
     close(attn_half)
     start(up_back)
     attn_got = across(attn_half)
-    latent_rows, first_sums = first_back(tie(scal), dq, dkv, dkv_got, x, rg, mod, w_attn, geo)
+    latent_rows, first_sums = first_back(tie(scal), tri, tri_got, x, rg, mod, w_attn, geo)
     close(first_sums)
-    attn_parts = weight_grad(tie(scal), attn_terms, 4 * cols, True, geo, "w_attn", attn_got)
-    close(*attn_parts)
-    start(up_back)
-    attn_back = begin(attn_parts, scatter_steps)
+    mine = [i ^ ti for i in range(T)]
+    rows = jnp.concatenate(
+        [first_sums.sum(axis=1), mid_sums[:3].sum(axis=1), ffn_sums.sum(axis=0, keepdims=True)]
+    )
+    rows = rows.reshape(6, T, cols).transpose(1, 0, 2).reshape(T, 6 * cols)
+    branch_sums = jnp.stack([mid_sums[3].sum(axis=0), ffn_sum]).reshape(1, 2 * width)
+    rows = tie(rows)
+    pack = jnp.concatenate(
+        [
+            rows,
+            jnp.broadcast_to(branch_sums, (T, 2 * width)),
+            reorder(unit_sum, mine).reshape(T, units),
+            reorder(pair_sums, mine).reshape(T, 2 * cols),
+        ],
+        axis=1,
+    )
+    pack = jnp.pad(pack, ((0, 0), (0, -pack.shape[1] % 1024)))
+    pack = jnp.broadcast_to(pack[None], (F,) + pack.shape).reshape(F * T, -1, 128)
+    pack = lax.all_to_all(pack, BOTH, 0, 0, tiled=True)
+    attn_parts = weight_grad(
+        tie(scal), attn_terms, beside, 4 * cols, True, geo, "w_attn", attn_got
+    )
+    close(pack, *attn_parts)
+    attn_back = begin(attn_parts, scatter_steps, False)
+    pack = tie(pack).reshape(F, T, -1)
+    mine_rows = pack[:, :, : 6 * cols].reshape(geo.P, 2, T, 6, cols).sum(axis=1)
+    mine_rows = mine_rows.reshape(F * images, 6, cols)
+    cond_part = jnp.einsum("bcj,dcj->bd", mine_rows, mod_weight.astype(F32), precision=highest)
+    cond_part = cond_part.reshape(F, 1, images, geo.R)
+    cond_part = jnp.broadcast_to(cond_part, (F, T, images, geo.R)).reshape(F * T, images, geo.R)
+    cond_part = lax.all_to_all(cond_part, BOTH, 0, 0, tiled=True)
     latent_back = from_chip(tie(latent_rows))
     opened.extend(latent_back)
-    close()
-    start(attn_back)
     close()
     start(attn_back)
     close()
@@ -1074,37 +1191,12 @@
     attn_grad = attn_back.finish(*now)
     in_grad = attn_grad[:, : 3 * cols].reshape(geo.R, 3, cols).transpose(1, 0, 2)
 
-    mine = [i ^ ti for i in range(T)]
-    branch_sums = jnp.stack([mid_sums[3].sum(axis=0), ffn_sum]).reshape(1, 2 * width)
-    bias_pack = jnp.concatenate(
-        [
-            jnp.broadcast_to(branch_sums, (T, 2 * width)),
-            reorder(unit_sum, mine).reshape(T, units),
-            reorder(tri_sums, mine).reshape(T, 2 * cols),
-        ],
-        axis=1,
-    )
-    bias_pack = jnp.broadcast_to(bias_pack[None], (F,) + bias_pack.shape).reshape(F * T, -1)
-    bias_total = lax.all_to_all(bias_pack, BOTH, 0, 0, tiled=True).sum(axis=0)
+    bias_total = pack[:, :, 6 * cols :].sum(axis=(0, 1))
     branch_grad = bias_total[: 2 * width].reshape(2, width)
     unit_grad = bias_total[2 * width : 2 * width + units]
-    pair_grad = bias_total[2 * width + units :].reshape(2, cols)
-
-    rows = jnp.concatenate(
-        [first_sums.sum(axis=1), mid_sums[:3].sum(axis=1), ffn_sums.sum(axis=0, keepdims=True)]
-    )
-    rows = rows.reshape(6, T, cols).transpose(1, 0, 2)
-    rows = jnp.broadcast_to(rows[None], (F, T, 6, cols)).reshape(F * T, 6, cols)
-    rows = lax.all_to_all(rows, BOTH, 0, 0, tiled=True)
-    mine_rows = rows.reshape(geo.P, 2, T, 6, cols).sum(axis=1).reshape(F * images, 6, cols)
-    mod_weight_grad = jnp.einsum(
-        "bd,bcj->dcj", silu_own.astype(F32), mine_rows, precision=highest
-    )
+    pair_grad = bias_total[2 * width + units :][: 2 * cols].reshape(2, cols)
+    mod_weight_grad = jnp.einsum("bd,bcj->dcj", silu_own.astype(F32), mine_rows, precision=highest)
     mod_bias_grad = mine_rows.sum(axis=0)
-    cond_part = jnp.einsum("bcj,dcj->bd", mine_rows, mod_weight.astype(F32), precision=highest)
-    cond_part = cond_part.reshape(F, 1, images, geo.R)
-    cond_part = jnp.broadcast_to(cond_part, (F, T, images, geo.R)).reshape(F * T, images, geo.R)
-    cond_part = lax.all_to_all(cond_part, BOTH, 0, 0, tiled=True)
     cond_mine = cond_part.reshape(F, T, images, geo.R).sum(axis=1)
     silu_grad = cond_mine.transpose(1, 0, 2).reshape(images, width)
     cond_f = conditioning.astype(F32)

time: 668 us -> 602 us (0.901)
  waiting for transfers between devices: 192 us -> 172 us
  other arithmetic: 61.2 us -> 42.9 us
  starting transfers between devices: 95.4 us -> 83.8 us
  blocking collectives: 24.8 us -> 16.2 us
    all_to_all x2 -> x1, waiting for transfers between devices: 22 us -> 2.13 us  [body(): pack = lax.all_to_all(pack, BOTH, 0, 0, tiled=True)]
    all_to_all x1, waiting for transfers between devices: 1.79 us -> 16.4 us  [body(): cond_part = lax.all_to_all(cond_part, BOTH, 0, 0, tiled=True)]
    ppermute x4, starting transfers between devices: 12.2 us -> 2.51 us  [to_chip(): got.append(lax.ppermute(item, BOTH, places(k)))]
    concatenate x12 -> x8, other arithmetic: 15 us -> 6.11 us  [gather_steps(): bufs = [jnp.concatenate(pair) for pair in zip(bufs, got)]]
    ppermute x13 -> x17, waiting for transfers between devices: 13.5 us -> 4.65 us  [flip_core(): return lax.ppermute(x, 'fsdp', [(i, i ^ 1) for i in range(geo.F)])]
    all_to_all x1, blocking collectives: 24.8 us -> 16.2 us  [body(): lax.all_to_all(after(mod_part, *up_way.flight), BOTH, 0, 0, tiled=True)]
    unnamed x144 -> x158, local copies, waits for them, and re-layouts: 12.5 us -> 16.8 us
  transfers between devices with their start and end apart: 67 -> 70, of which waited for: 27 -> 24; matrix products, arithmetic and copies ran while one was open for 10% -> 9% of each run, Pallas kernels for 33% -> 38%
where the time goes in v3:
time: 602 us; the launch traced here: 595 us
  Pallas kernels  238 us (40%)
  waiting for transfers between devices  172 us (29%)
  starting transfers between devices  83.8 us (14%)
  other arithmetic  42.9 us (7%)
  local copies, waits for them, and re-layouts  36.6 us (6%)
  blocking collectives  16.2 us (3%)
    ppermute x18, waiting for transfers between devices, flip_tensor(): return lax.ppermute(x, 'tensor', [(i, i ^ k) for i in range(geo.T)])  104 us
    pallas_call x6, Pallas kernels, weight_grad(): pl.pallas_call(kernel, grid_spec=pltpu.PrefetchScalarGridSpec(num_scalar_...  63.5 us
    ppermute x24, waiting for transfers between devices, flip_pair(): return lax.ppermute(x, 'fsdp', [(i, i ^ 2 * bit) for i in range(geo.F)])  45.2 us
    pallas_call x2, Pallas kernels, attn_bwd(): pl.pallas_call(kernel, grid=(z,), in_specs=[spec(wp), spec(geo.kvw), spec...  29.4 us
    ppermute x18, starting transfers between devices, flip_tensor(): return lax.ppermute(x, 'tensor', [(i, i ^ k) for i in range(geo.T)])  26.2 us
    ppermute x24, starting transfers between devices, flip_pair(): return lax.ppermute(x, 'fsdp', [(i, i ^ 2 * bit) for i in range(geo.F)])  25.8 us
    pallas_call x2, Pallas kernels, attn_fwd(): pl.pallas_call(kernel, grid=(z,), in_specs=[spec(wp), spec(geo.kvw), spec...  19.6 us
    pallas_call x1, Pallas kernels, second_back(): pl.pallas_call(kernel, grid_spec=pltpu.PrefetchScalarGridSpec(num_scalar_...  19.3 us
  transfers between devices with their start and end apart: 70, of which 24 were waited for; matrix products, arithmetic and copies ran while one was open for 9% of the time, Pallas kernels for 38%

profile of v3, /device:TPU:10, one launch (start us, length us, event | category | flops | bytes accessed | tf_op | source)
XLA Modules:
  0.0 595.3 jit_solution(6035279780904029236)
XLA Ops:
  17.6 17.4 %collective-permute-done.1 = bf16[144,1152]{1,0:T(8,128)(2,1)S(1)} collective-permute-done((bf16[144,1152]{1,0:T(8,128)(2,1)S(1)}, bf16[144,1152]{1,0:T(8,128)(2,1)S(1)}, u32[]{:S(2)}, u32[]{:S(2)}) %collective-permute-start.1) | collective-permute-done | bytes 331808 | tf_op jit(solution)/shard_map/ppermute | solution.py:67
  35.0 11.5 %collective-permute-done.2 = bf16[144,1152]{1,0:T(8,128)(2,1)S(1)} collective-permute-done((bf16[144,1152]{1,0:T(8,128)(2,1)S(1)}, bf16[144,1152]{1,0:T(8,128)(2,1)S(1)}, u32[]{:S(2)}, u32[]{:S(2)}) %collective-permute-start.2) | collective-permute-done | bytes 331808 | tf_op jit(solution)/shard_map/ppermute | solution.py:67
  55.7 16.2 %all_to_all.20 = f32[32,6,288]{2,1,0:T(8,128)S(1)} all-to-all(f32[32,6,288]{2,1,0:T(8,128)S(1)} %bitcast.140), channel_id=1, replica_groups=mesh['fsdp'=8,'tensor'=4] {'fsdp','tensor'}, dimensions={0} | all-to-all | bytes 442368 | tf_op jit(solution)/shard_map/all_to_all | solution.py:1039
  81.7 25.8 %collective-permute-done.9 = bf16[144,1152]{1,0:T(8,128)(2,1)S(1)} collective-permute-done((bf16[144,1152]{1,0:T(8,128)(2,1)S(1)}, bf16[144,1152]{1,0:T(8,128)(2,1)S(1)}, u32[]{:S(2)}, u32[]{:S(2)}) %collective-permute-start.9) | collective-permute-done | bytes 331808 | tf_op jit(solution)/shard_map/ppermute | solution.py:67
  167.8 9.8 %attn_fwd.3 = (bf16[2,512,384]{2,1,0:T(8,128)(2,1)}, f32[2,4,512]{2,1,0:T(4,128)}) custom-call(bf16[2,512,384]{2,1,0:T(8,128)(2,1)} %get-tuple-element.242.q_ref, bf16[2,512,640]{2,1,0:T(8,128)(2,1)} %get-tuple-element.176.kv_ref, bf16[2,512,640]{2,1,0:T(8,128)(2,1)} %copy-done.74), custom_call_target="tpu_custom_call" | custom-call | flops 6000000000 | bytes 3932160 | tf_op jit(solution)/shard_map/attn_fwd/pallas_call | solution.py:371
  177.6 9.8 %attn_fwd.2 = (bf16[2,512,384]{2,1,0:T(8,128)(2,1)}, f32[2,4,512]{2,1,0:T(4,128)}) custom-call(bf16[2,512,384]{2,1,0:T(8,128)(2,1)} %get-tuple-element.238.q_ref, bf16[2,512,640]{2,1,0:T(8,128)(2,1)} %get-tuple-element.174.kv_ref, bf16[2,512,640]{2,1,0:T(8,128)(2,1)} %copy-done.73), custom_call_target="tpu_custom_call" | custom-call | flops 6000000000 | bytes 3932160 | tf_op jit(solution)/shard_map/attn_fwd/pallas_call | solution.py:371
  187.4 13.1 %out_proj.1 = (f32[512,1152]{1,0:T(8,128)}, f32[512,1152]{1,0:T(8,128)}, bf16[512,1152]{1,0:T(8,128)(2,1)}) custom-call(s32[3]{0:T(128)} %pad_add_fusion.s, bf16[2,512,384]{2,1,0:T(8,128)(2,1)} %get-tuple-element.182.ya_ref.o_ref.refs_6_, bf16[2,512,384]{2,1,0:T(8,128)(2,1)} %get-tuple-element.184.yb_ref.o_ref.refs_7_, bf16[512,1152]{1,0:T(8,128)(2,1)} %copy-done.3, ...), custom_call_target="tpu_custom_call" | custom-call | flops 1358954496 | bytes 18874368 | tf_op jit(solution)/shard_map/out_proj/pallas_call | solution.py:489
  206.9 14.2 %collective-permute-done.22 = bf16[1,2,144,1152]{3,2,1,0:T(8,128)(2,1)S(1)} collective-permute-done((bf16[1,2,144,1152]{3,2,1,0:T(8,128)(2,1)S(1)}, bf16[1,2,144,1152]{3,2,1,0:T(8,128)(2,1)S(1)}, u32[]{:S(2)}, u32[]{:S(2)}) %collective-permute-start.22) | collective-permute-done | bytes 663584 | tf_op jit(solution)/shard_map/ppermute | solution.py:59
  231.5 18.1 %up_proj.1 = (bf16[4,512,1152]{2,1,0:T(8,128)(2,1)}, bf16[4,512,1152]{2,1,0:T(8,128)(2,1)}) custom-call(s32[3]{0:T(128)} %pad_add_fusion.s, bf16[512,1152]{1,0:T(8,128)(2,1)} %get-tuple-element.185.h_ref.refs_0_, f32[4,1,1152]{2,1,0:T(1,128)} %fusion.14.b_ref, bf16[4,2,144,1152]{3,2,1,0:T(8,128)(2,1)} %copy-done.7, bf16[4,2,144,1152]{3,2,1,0:T(8,128)(2,1)} %copy-done.12, ...), custom_call_target="tpu_custom_call" | custom-call | flops 5435817984 | bytes 20054016 | tf_op jit(solution)/shard_map/up_proj/pallas_call | solution.py:536
  261.8 8.5 %w_down_send.1 = bf16[4,4,144,1152]{3,2,1,0:T(8,128)(2,1)} custom-call(s32[3]{0:T(128)} %pad_add_fusion.s, bf16[512,1152]{1,0:T(8,128)(2,1)} %get-tuple-element.375.refs_0_.g_ref, bf16[4,512,1152]{2,1,0:T(8,128)(2,1)} %get-tuple-element.196.refs_1_.y_ref), custom_call_target="tpu_custom_call" | custom-call | flops 2717908992 | bytes 15335424 | tf_op jit(solution)/shard_map/w_down_send/pallas_call | solution.py:902
  270.8 15.4 %down_proj.1 = (bf16[512,1152]{1,0:T(8,128)(2,1)}, f32[8,1152]{1,0:T(8,128)}) custom-call(s32[3]{0:T(128)} %pad_add_fusion.s, bf16[4,512,1152]{2,1,0:T(8,128)(2,1)} %get-tuple-element.196.refs_1_.y_ref, f32[512,1152]{1,0:T(8,128)} %get-tuple-element.201.r_ref, bf16[512,1152]{1,0:T(8,128)(2,1)} %copy-done.8, f32[6,1152]{1,0:T(8,128)} %reshape.184.m_ref, ...), custom_call_target="tpu_custom_call" | custom-call | flops 5435817984 | bytes 20054016 | tf_op jit(solution)/shard_map/down_proj/pallas_call | solution.py:585
  288.6 11.3 %w_down.1 = (bf16[2,2,144,1152]{3,2,1,0:T(8,128)(2,1)}, bf16[2,2,144,1152]{3,2,1,0:T(8,128)(2,1)}, bf16[2,2,144,1152]{3,2,1,0:T(8,128)(2,1)}, bf16[2,2,144,1152]{3,2,1,0:T(8,128)(2,1)}) custom-call(s32[3]{0:T(128)} %pad_add_fusion.s, bf16[512,1152]{1,0:T(8,128)(2,1)} %get-tuple-element.375.refs_0_.g_ref, ...), custom_call_target="tpu_custom_call" | custom-call | flops 2717908992 | bytes 15335424 | tf_op jit(solution)/shard_map/w_down/pallas_call | solution.py:902
  304.2 14.4 %pre_back.1 = (bf16[4,512,1152]{2,1,0:T(8,128)(2,1)}, f32[4,1,1152]{2,1,0:T(1,128)}) custom-call(s32[3]{0:T(128)} %pad_add_fusion.s, bf16[512,1152]{1,0:T(8,128)(2,1)} %get-tuple-element.375.refs_0_.g_ref, bf16[4,512,1152]{2,1,0:T(8,128)(2,1)} %get-tuple-element.219.gp_ref, bf16[2,2,144,1152]{3,2,1,0:T(8,128)(2,1)} %pad_maximum_fusion.6.refs_0_, ...), custom_call_target="tpu_custom_call" | custom-call | flops 5435817984 | bytes 20054016 | tf_op jit(solution)/shard_map/pre_back/pallas_call | solution.py:625
  318.6 8.4 %w_up_send.1 = bf16[4,4,144,1152]{3,2,1,0:T(8,128)(2,1)} custom-call(s32[3]{0:T(128)} %pad_add_fusion.s, bf16[512,1152]{1,0:T(8,128)(2,1)} %get-tuple-element.185.h_ref.refs_0_, bf16[4,512,1152]{2,1,0:T(8,128)(2,1)} %get-tuple-element.220.refs_1_.y_ref), custom_call_target="tpu_custom_call" | custom-call | flops 2717908992 | bytes 15335424 | tf_op jit(solution)/shard_map/w_up_send/pallas_call | solution.py:902
  339.3 19.3 %second_back.1 = (f32[512,1152]{1,0:T(8,128)}, bf16[512,1152]{1,0:T(8,128)(2,1)}, f32[4,8,1152]{2,1,0:T(8,128)}) custom-call(s32[3]{0:T(128)} %pad_add_fusion.s, bf16[4,512,1152]{2,1,0:T(8,128)(2,1)} %get-tuple-element.220.refs_1_.y_ref, f32[512,1152]{1,0:T(8,128)} %get-tuple-element.201.r_ref, f32[512,1152]{1,0:T(8,128)} %get-tuple-element.226.a_ref, ...), custom_call_target="tpu_custom_call" | custom-call | flops 5435817984 | bytes 25952256 | tf_op jit(solution)/shard_map/second_back/pallas_call | solution.py:680
  374.5 11.3 %w_up.1 = (bf16[2,2,144,1152]{3,2,1,0:T(8,128)(2,1)}, bf16[2,2,144,1152]{3,2,1,0:T(8,128)(2,1)}, bf16[2,2,144,1152]{3,2,1,0:T(8,128)(2,1)}, bf16[2,2,144,1152]{3,2,1,0:T(8,128)(2,1)}) custom-call(s32[3]{0:T(128)} %pad_add_fusion.s, bf16[512,1152]{1,0:T(8,128)(2,1)} %get-tuple-element.185.h_ref.refs_0_, ...), custom_call_target="tpu_custom_call" | custom-call | flops 2717908992 | bytes 15335424 | tf_op jit(solution)/shard_map/w_up/pallas_call | solution.py:902
  388.2 14.7 %attn_bwd.3 = (bf16[2,512,896]{2,1,0:T(8,128)(2,1)}, bf16[2,512,640]{2,1,0:T(8,128)(2,1)}, f32[2,1,896]{2,1,0:T(1,128)}, f32[2,1,640]{2,1,0:T(1,128)}) custom-call(bf16[2,512,384]{2,1,0:T(8,128)(2,1)} %get-tuple-element.242.q_ref, bf16[2,512,640]{2,1,0:T(8,128)(2,1)} %get-tuple-element.176.kv_ref, bf16[2,512,640]{2,1,0:T(8,128)(2,1)} %copy-done.74, ...), custom_call_target="tpu_custom_call" | custom-call | flops 10000000000 | bytes 6291456 | tf_op jit(solution)/shard_map/attn_bwd/pallas_call | solution.py:425
  403.0 14.7 %attn_bwd.2 = (bf16[2,512,896]{2,1,0:T(8,128)(2,1)}, bf16[2,512,640]{2,1,0:T(8,128)(2,1)}, f32[2,1,896]{2,1,0:T(1,128)}, f32[2,1,640]{2,1,0:T(1,128)}) custom-call(bf16[2,512,384]{2,1,0:T(8,128)(2,1)} %get-tuple-element.238.q_ref, bf16[2,512,640]{2,1,0:T(8,128)(2,1)} %get-tuple-element.174.kv_ref, bf16[2,512,640]{2,1,0:T(8,128)(2,1)} %copy-done.73, ...), custom_call_target="tpu_custom_call" | custom-call | flops 10000000000 | bytes 6291456 | tf_op jit(solution)/shard_map/attn_bwd/pallas_call | solution.py:425
  426.8 11.2 %w_attn_send.1 = bf16[4,4,144,1152]{3,2,1,0:T(8,128)(2,1)} custom-call(s32[3]{0:T(128)} %pad_add_fusion.s, bf16[512,1152]{1,0:T(8,128)(2,1)} %norm_mod.1.h_ref.refs_0_, bf16[512,1152]{1,0:T(8,128)(2,1)} %get-tuple-element.227.g_ref.refs_1_, bf16[2,512,896]{2,1,0:T(8,128)(2,1)} %get-tuple-element.252.refs_2_.ta, ...), custom_call_target="tpu_custom_call" | custom-call | flops 2717908992 | bytes 15335424 | tf_op jit(solution)/shard_map/w_attn_send/pallas_call | solution.py:902
  452.7 17.0 %first_back.1 = (bf16[512,1152]{1,0:T(8,128)(2,1)}, f32[2,8,1152]{2,1,0:T(8,128)}) custom-call(s32[3]{0:T(128)} %pad_add_fusion.s, bf16[2,512,896]{2,1,0:T(8,128)(2,1)} %get-tuple-element.252.refs_2_.ta, bf16[2,512,896]{2,1,0:T(8,128)(2,1)} %get-tuple-element.253.refs_3_.tb, bf16[2,512,640]{2,1,0:T(8,128)(2,1)} %copy-done.5, bf16[2,512,640]{2,1,0:T(8,128)(2,1)} %copy-done.4, ...), custom_call_target="tpu_custom_call" | custom-call | flops 4076863488 | bytes 20054016 | tf_op jit(solution)/shard_map/first_back/pallas_call | solution.py:772
  488.5 12.9 %w_attn.1 = (bf16[2,2,144,1152]{3,2,1,0:T(8,128)(2,1)}, bf16[2,2,144,1152]{3,2,1,0:T(8,128)(2,1)}, bf16[2,2,144,1152]{3,2,1,0:T(8,128)(2,1)}, bf16[2,2,144,1152]{3,2,1,0:T(8,128)(2,1)}) custom-call(s32[3]{0:T(128)} %pad_add_fusion.s, bf16[512,1152]{1,0:T(8,128)(2,1)} %norm_mod.1.h_ref.refs_0_, bf16[512,1152]{1,0:T(8,128)(2,1)} %get-tuple-element.227.g_ref.refs_1_, ...), custom_call_target="tpu_custom_call" | custom-call | flops 2717908992 | bytes 15335424 | tf_op jit(solution)/shard_map/w_attn/pallas_call | solution.py:902
  524.1 16.4 %all-to-all-done.3 = f32[32,2,144]{2,1,0:T(2,128)S(1)} async-done(((f32[32,2,144]{2,1,0:T(2,128)}), f32[32,2,144]{2,1,0:T(2,128)S(1)}, u32[]{:S(2)}, u32[]{:S(2)}) %all-to-all-start.3) | async-done | bytes 36896 | tf_op jit(solution)/shard_map/all_to_all | solution.py:1182
  548.9 9.8 %collective-permute-done.63 = bf16[1,2,144,1152]{3,2,1,0:T(8,128)(2,1)S(1)} collective-permute-done((bf16[1,2,144,1152]{3,2,1,0:T(8,128)(2,1)S(1)}, bf16[1,2,144,1152]{3,2,1,0:T(8,128)(2,1)S(1)}, u32[]{:S(2)}, u32[]{:S(2)}) %collective-permute-start.63) | collective-permute-done | bytes 663584 | tf_op jit(solution)/shard_map/ppermute | solution.py:59
  570.1 14.5 %collective-permute-done.65 = bf16[144,1152]{1,0:T(8,128)(2,1)S(1)} collective-permute-done((bf16[144,1152]{1,0:T(8,128)(2,1)S(1)}, bf16[144,1152]{1,0:T(8,128)(2,1)S(1)}, u32[]{:S(2)}, u32[]{:S(2)}) %collective-permute-start.65) | collective-permute-done | bytes 331808 | tf_op jit(solution)/shard_map/ppermute | solution.py:67
  (426 shorter events, 257.3 us)
Async XLA Ops:
  3.5 31.5 %collective-permute-start.1 = (bf16[144,1152]{1,0:T(8,128)(2,1)S(1)}, bf16[144,1152]{1,0:T(8,128)(2,1)S(1)}, u32[]{:S(2)}, u32[]{:S(2)}) collective-permute-start(bf16[144,1152]{1,0:T(8,128)(2,1)S(1)} %concatenate.75), channel_id=1, source_target_pairs={{0,2},{1,3},{2,0},{3,1},{4,6},{5,7},{6,4},{7,5},{8,10},{9,11},{10,... | collective-permute-start | bytes 995336 | tf_op jit(solution)/shard_map/ppermute | solution.py:67
  6.1 40.4 %collective-permute-start.2 = (bf16[144,1152]{1,0:T(8,128)(2,1)S(1)}, bf16[144,1152]{1,0:T(8,128)(2,1)S(1)}, u32[]{:S(2)}, u32[]{:S(2)}) collective-permute-start(bf16[144,1152]{1,0:T(8,128)(2,1)S(1)} %concatenate.75), channel_id=1, source_target_pairs={{0,3},{1,2},{2,1},{3,0},{4,7},{5,6},{6,5},{7,4},{8,11},{9,10},{10,... | collective-permute-start | bytes 995336 | tf_op jit(solution)/shard_map/ppermute | solution.py:67
  7.5 44.9 %all-to-all-start = ((bf16[32,32,128]{2,1,0:T(8,128)(2,1)}), bf16[32,32,128]{2,1,0:T(8,128)(2,1)S(1)}, u32[]{:S(2)}, u32[]{:S(2)}) async-start(bf16[32,32,128]{2,1,0:T(8,128)(2,1)} %broadcast_in_dim.65), calls=%async_computation | async-start | bytes 524288 | tf_op jit(solution)/shard_map/all_to_all | solution.py:984
  74.0 35.3 %collective-permute-start.8 = (bf16[2,2,144,1152]{3,2,1,0:T(8,128)(2,1)S(1)}, bf16[2,2,144,1152]{3,2,1,0:T(8,128)(2,1)}, u32[]{:S(2)}, u32[]{:S(2)}) collective-permute-start(bf16[2,2,144,1152]{3,2,1,0:T(8,128)(2,1)S(1)} %pad_maximum_fusion.3.refs_0_.refs_4_), channel_id=1, source_target_pairs={{0,8},{4,12},{8,0},{12,4},{16,24},{20,28},{24,16},{28,20},{1,9},{5... | collective-permute-start | bytes 3981320 | tf_op jit(solution)/shard_map/ppermute | solution.py:59
  76.9 32.4 %collective-permute-start.7 = (bf16[2,2,144,1152]{3,2,1,0:T(8,128)(2,1)S(1)}, bf16[2,2,144,1152]{3,2,1,0:T(8,128)(2,1)}, u32[]{:S(2)}, u32[]{:S(2)}) collective-permute-start(bf16[2,2,144,1152]{3,2,1,0:T(8,128)(2,1)S(1)} %pad_maximum_fusion.2.refs_0_), channel_id=1, source_target_pairs={{0,16},{4,20},{8,24},{12,28},{16,0},{20,4},{24,8},{28,12},{1,17},{... | collective-permute-start | bytes 3981320 | tf_op jit(solution)/shard_map/ppermute | solution.py:59
  78.9 30.3 %collective-permute-start.10 = (bf16[256,1152]{1,0:T(8,128)(2,1)S(1)}, bf16[256,1152]{1,0:T(8,128)(2,1)S(1)}, u32[]{:S(2)}, u32[]{:S(2)}) collective-permute-start(bf16[256,1152]{1,0:T(8,128)(2,1)S(1)} %get-tuple-element.387), channel_id=1, source_target_pairs={{0,0},{1,1},{2,4},{3,5},{4,2},{5,3},{6,6},{7,7},{8,8},{9,9},{10,12... | collective-permute-start | bytes 1769480 | tf_op jit(solution)/shard_map/ppermute | solution.py:969
  79.6 29.7 %collective-permute-start.11 = (bf16[256,1152]{1,0:T(8,128)(2,1)S(1)}, bf16[256,1152]{1,0:T(8,128)(2,1)S(1)}, u32[]{:S(2)}, u32[]{:S(2)}) collective-permute-start(bf16[256,1152]{1,0:T(8,128)(2,1)S(1)} %get-tuple-element.386), channel_id=1, source_target_pairs={{0,1},{1,0},{2,5},{3,4},{4,3},{5,2},{6,7},{7,6},{8,9},{9,8},{10,13... | collective-permute-start | bytes 1769480 | tf_op jit(solution)/shard_map/ppermute | solution.py:969
  161.4 39.1 %collective-permute-start.25 = (bf16[2,2,144,1152]{3,2,1,0:T(8,128)(2,1)S(1)}, bf16[2,2,144,1152]{3,2,1,0:T(8,128)(2,1)}, u32[]{:S(2)}, u32[]{:S(2)}) collective-permute-start(bf16[2,2,144,1152]{3,2,1,0:T(8,128)(2,1)S(1)} %pad_maximum_fusion.5), channel_id=1, source_target_pairs={{0,8},{4,12},{8,0},{12,4},{16,24},{20,28},{24,16},{28,20},{1,9},{5... | collective-permute-start | bytes 3981320 | tf_op jit(solution)/shard_map/ppermute | solution.py:59
  162.9 37.5 %collective-permute-start.24 = (bf16[2,2,144,1152]{3,2,1,0:T(8,128)(2,1)S(1)}, bf16[2,2,144,1152]{3,2,1,0:T(8,128)(2,1)S(1)}, u32[]{:S(2)}, u32[]{:S(2)}) collective-permute-start(bf16[2,2,144,1152]{3,2,1,0:T(8,128)(2,1)S(1)} %pad_maximum_fusion.4), channel_id=1, source_target_pairs={{0,16},{4,20},{8,24},{12,28},{16,0},{20,4},{24,8},{28,12},{1,17},{... | collective-permute-start | bytes 3981320 | tf_op jit(solution)/shard_map/ppermute | solution.py:59
  164.3 36.1 %collective-permute-start.23 = (bf16[144,1152]{1,0:T(8,128)(2,1)S(1)}, bf16[144,1152]{1,0:T(8,128)(2,1)}, u32[]{:S(2)}, u32[]{:S(2)}) collective-permute-start(bf16[144,1152]{1,0:T(8,128)(2,1)S(1)} %bitcast.150), channel_id=1, source_target_pairs={{0,2},{1,3},{2,0},{3,1},{4,6},{5,7},{6,4},{7,5},{8,10},{9,11},{10,... | collective-permute-start | bytes 995336 | tf_op jit(solution)/shard_map/ppermute | solution.py:67
  224.7 30.5 %collective-permute-start.31 = (bf16[2,2,144,1152]{3,2,1,0:T(8,128)(2,1)S(1)}, bf16[2,2,144,1152]{3,2,1,0:T(8,128)(2,1)}, u32[]{:S(2)}, u32[]{:S(2)}) collective-permute-start(bf16[2,2,144,1152]{3,2,1,0:T(8,128)(2,1)S(1)} %pad_maximum_fusion.7.refs_4_), channel_id=1, source_target_pairs={{0,8},{4,12},{8,0},{12,4},{16,24},{20,28},{24,16},{28,20},{1,9},{5... | collective-permute-start | bytes 3981320 | tf_op jit(solution)/shard_map/ppermute | solution.py:59
  226.8 30.5 %collective-permute-start.30 = (bf16[2,2,144,1152]{3,2,1,0:T(8,128)(2,1)}, bf16[2,2,144,1152]{3,2,1,0:T(8,128)(2,1)}, u32[]{:S(2)}, u32[]{:S(2)}) collective-permute-start(bf16[2,2,144,1152]{3,2,1,0:T(8,128)(2,1)} %pad_maximum_fusion.6.refs_0_), channel_id=1, source_target_pairs={{0,16},{4,20},{8,24},{12,28},{16,0},{20,4},{24,8},{28,12},{1,17},{... | collective-permute-start | bytes 3981320 | tf_op jit(solution)/shard_map/ppermute | solution.py:59
  230.2 40.1 %collective-permute-start.35 = (bf16[2,2,144,1152]{3,2,1,0:T(8,128)(2,1)S(1)}, bf16[2,2,144,1152]{3,2,1,0:T(8,128)(2,1)}, u32[]{:S(2)}, u32[]{:S(2)}) collective-permute-start(bf16[2,2,144,1152]{3,2,1,0:T(8,128)(2,1)S(1)} %pad_maximum_fusion.7.refs_4_), channel_id=1, source_target_pairs={{0,4},{4,0},{8,12},{12,8},{16,20},{20,16},{24,28},{28,24},{1,5},{5... | collective-permute-start | bytes 3981320 | tf_op jit(solution)/shard_map/ppermute | solution.py:63
  299.9 31.3 %collective-permute-start.40 = (bf16[2,2,144,1152]{3,2,1,0:T(8,128)(2,1)}, bf16[2,2,144,1152]{3,2,1,0:T(8,128)(2,1)S(1)}, u32[]{:S(2)}, u32[]{:S(2)}) collective-permute-start(bf16[2,2,144,1152]{3,2,1,0:T(8,128)(2,1)} %get-tuple-element.216), channel_id=1, source_target_pairs={{0,16},{4,20},{8,24},{12,28},{16,0},{20,4},{24,8},{28,12},{1,17},{... | collective-permute-start | bytes 3981320 | tf_op jit(solution)/shard_map/ppermute | solution.py:59
  301.0 31.1 %collective-permute-start.41 = (bf16[2,2,144,1152]{3,2,1,0:T(8,128)(2,1)}, bf16[2,2,144,1152]{3,2,1,0:T(8,128)(2,1)}, u32[]{:S(2)}, u32[]{:S(2)}) collective-permute-start(bf16[2,2,144,1152]{3,2,1,0:T(8,128)(2,1)} %get-tuple-element.217), channel_id=1, source_target_pairs={{0,8},{4,12},{8,0},{12,4},{16,24},{20,28},{24,16},{28,20},{1,9},{5... | collective-permute-start | bytes 3981320 | tf_op jit(solution)/shard_map/ppermute | solution.py:59
  365.0 52.7 %collective-permute-start.49 = (bf16[144,1152]{1,0:T(8,128)(2,1)S(1)}, bf16[144,1152]{1,0:T(8,128)(2,1)}, u32[]{:S(2)}, u32[]{:S(2)}) collective-permute-start(bf16[144,1152]{1,0:T(8,128)(2,1)S(1)} %get-tuple-element.394), channel_id=1, source_target_pairs={{0,2},{1,3},{2,0},{3,1},{4,6},{5,7},{6,4},{7,5},{8,10},{9,11},{10,... | collective-permute-start | bytes 995336 | tf_op jit(solution)/shard_map/ppermute | solution.py:67
  385.9 31.8 %collective-permute-start.47 = (bf16[2,2,144,1152]{3,2,1,0:T(8,128)(2,1)}, bf16[2,2,144,1152]{3,2,1,0:T(8,128)(2,1)S(1)}, u32[]{:S(2)}, u32[]{:S(2)}) collective-permute-start(bf16[2,2,144,1152]{3,2,1,0:T(8,128)(2,1)} %get-tuple-element.236), channel_id=1, source_target_pairs={{0,16},{4,20},{8,24},{12,28},{16,0},{20,4},{24,8},{28,12},{1,17},{... | collective-permute-start | bytes 3981320 | tf_op jit(solution)/shard_map/ppermute | solution.py:59
  387.1 30.6 %collective-permute-start.48 = (bf16[2,2,144,1152]{3,2,1,0:T(8,128)(2,1)}, bf16[2,2,144,1152]{3,2,1,0:T(8,128)(2,1)}, u32[]{:S(2)}, u32[]{:S(2)}) collective-permute-start(bf16[2,2,144,1152]{3,2,1,0:T(8,128)(2,1)} %get-tuple-element.237), channel_id=1, source_target_pairs={{0,8},{4,12},{8,0},{12,4},{16,24},{20,28},{24,16},{28,20},{1,9},{5... | collective-permute-start | bytes 3981320 | tf_op jit(solution)/shard_map/ppermute | solution.py:59
  442.7 35.1 %collective-permute-start.57 = (bf16[4,4,144,1152]{3,2,1,0:T(8,128)(2,1)}, bf16[4,4,144,1152]{3,2,1,0:T(8,128)(2,1)}, u32[]{:S(2)}, u32[]{:S(2)}) collective-permute-start(bf16[4,4,144,1152]{3,2,1,0:T(8,128)(2,1)} %w_attn_send.1), channel_id=1, source_target_pairs={{0,4},{4,0},{8,12},{12,8},{16,20},{20,16},{24,28},{28,24},{1,5},{5... | collective-permute-start | bytes 15925256 | tf_op jit(solution)/shard_map/ppermute | solution.py:63
  447.3 30.5 %collective-permute-start.56 = (bf16[144,1152]{1,0:T(8,128)(2,1)S(1)}, bf16[144,1152]{1,0:T(8,128)(2,1)}, u32[]{:S(2)}, u32[]{:S(2)}) collective-permute-start(bf16[144,1152]{1,0:T(8,128)(2,1)S(1)} %get-tuple-element.392), channel_id=1, source_target_pairs={{0,3},{1,2},{2,1},{3,0},{4,7},{5,6},{6,5},{7,4},{8,11},{9,10},{10,... | collective-permute-start | bytes 995336 | tf_op jit(solution)/shard_map/ppermute | solution.py:67
  503.5 37.2 %collective-permute-start.60 = (bf16[2,2,144,1152]{3,2,1,0:T(8,128)(2,1)}, bf16[2,2,144,1152]{3,2,1,0:T(8,128)(2,1)}, u32[]{:S(2)}, u32[]{:S(2)}) collective-permute-start(bf16[2,2,144,1152]{3,2,1,0:T(8,128)(2,1)} %get-tuple-element.274), channel_id=1, source_target_pairs={{0,16},{4,20},{8,24},{12,28},{16,0},{20,4},{24,8},{28,12},{1,17},{... | collective-permute-start | bytes 3981320 | tf_op jit(solution)/shard_map/ppermute | solution.py:59
  505.0 35.7 %collective-permute-start.61 = (bf16[2,2,144,1152]{3,2,1,0:T(8,128)(2,1)}, bf16[2,2,144,1152]{3,2,1,0:T(8,128)(2,1)}, u32[]{:S(2)}, u32[]{:S(2)}) collective-permute-start(bf16[2,2,144,1152]{3,2,1,0:T(8,128)(2,1)} %get-tuple-element.275), channel_id=1, source_target_pairs={{0,8},{4,12},{8,0},{12,4},{16,24},{20,28},{24,16},{28,20},{1,9},{5... | collective-permute-start | bytes 3981320 | tf_op jit(solution)/shard_map/ppermute | solution.py:59
  507.6 33.1 %collective-permute-start.58 = (bf16[256,1152]{1,0:T(8,128)(2,1)}, bf16[256,1152]{1,0:T(8,128)(2,1)S(1)}, u32[]{:S(2)}, u32[]{:S(2)}) collective-permute-start(bf16[256,1152]{1,0:T(8,128)(2,1)} %get-tuple-element.379), channel_id=1, source_target_pairs={{0,0},{1,1},{4,2},{5,3},{2,4},{3,5},{6,6},{7,7},{8,8},{9,9},{12,10... | collective-permute-start | bytes 1769480 | tf_op jit(solution)/shard_map/ppermute | solution.py:976
  509.3 31.4 %collective-permute-start.59 = (bf16[256,1152]{1,0:T(8,128)(2,1)}, bf16[256,1152]{1,0:T(8,128)(2,1)}, u32[]{:S(2)}, u32[]{:S(2)}) collective-permute-start(bf16[256,1152]{1,0:T(8,128)(2,1)} %get-tuple-element.378), channel_id=1, source_target_pairs={{1,0},{0,1},{5,2},{4,3},{3,4},{2,5},{7,6},{6,7},{9,8},{8,9},{13,10... | collective-permute-start | bytes 1769480 | tf_op jit(solution)/shard_map/ppermute | solution.py:976
  (122 other events, 1575.1 us)

commit v4 on v3

--- a/solution.py
+++ b/solution.py
@@ -13,7 +13,7 @@
 CUBIC = 0.044715
 LOG2E = 1.4426950408889634
 VMEM_BYTES = 56 << 20
-ROWS = 16
+ROWS = 32
 BF = jnp.bfloat16
 F32 = jnp.float32
 BOTH = ("fsdp", "tensor")
@@ -92,15 +92,18 @@
         return self.result
 
 
-def gather_steps(shard, geo, parted=True, joined=False):
+def gather_steps(shard, geo, parted=True, joined=False, extras=None):
     if parted:
-        far = yield [flip_tensor(shard, k, geo) for k in range(geo.Th + 1, geo.T)]
-        near = yield [flip_tensor(shard, k, geo) for k in range(1, geo.Th)]
+        most = [k for k in range(1, geo.T) if k != geo.Th]
+        got = yield [flip_tensor(shard, k, geo) for k in most]
         mid = yield [flip_tensor(shard, geo.Th, geo)]
-        parts = [shard] + near + mid + far
+        parts = [shard] + got[: geo.Th - 1] + mid + got[geo.Th - 1 :]
     else:
         got = yield [flip_tensor(shard, k, geo) for k in range(1, geo.T)]
         parts = [shard] + got
+    if extras is not None:
+        extras += [part[geo.R :] for part in parts]
+        parts = [part[: geo.R] for part in parts]
     bufs = [jnp.stack(parts[h * geo.Th : (h + 1) * geo.Th])[None] for h in range(2)]
     for at in range(len(geo.bits)):
         bits = (geo.bits[at], geo.bits[-1 - at])
@@ -194,11 +197,11 @@
 
         @pl.when(j == 0)
         def _():
-            each(j, lambda copy: copy.start())
+            each(j, lambda copy: copy.start(priority=1))
 
         @pl.when(j + 1 < (self.geo.T if half is None else th))
         def _():
-            each(j + 1, lambda copy: copy.start())
+            each(j + 1, lambda copy: copy.start(priority=1))
 
         each(j, lambda copy: copy.wait())
         return buf.at[j % 2]
@@ -229,8 +232,8 @@
     return total
 
 
-def params():
-    return pltpu.CompilerParams(vmem_limit_bytes=VMEM_BYTES)
+def params(size=VMEM_BYTES):
+    return pltpu.CompilerParams(vmem_limit_bytes=size)
 
 
 def cost(flops, size):
@@ -268,6 +271,31 @@
     return v.reshape(v.shape[0] // 8, 8, v.shape[1]).sum(axis=0)
 
 
+class Late:
+    def __init__(self, *arrays):
+        self.arrays = arrays
+        self.specs = [pl.BlockSpec(memory_space=pl.ANY)] * len(arrays)
+        self.scratch = [pltpu.VMEM(a.shape, a.dtype) for a in arrays]
+        self.scratch.append(pltpu.SemaphoreType.DMA((len(arrays),)))
+
+    def copies(self, refs, scratch):
+        sem = scratch[-1]
+        return [
+            pltpu.make_async_copy(ref, scratch[i], sem.at[i]) for i, ref in enumerate(refs)
+        ]
+
+    def start(self, j, refs, scratch):
+        @pl.when(j == 0)
+        def _():
+            for copy in self.copies(refs, scratch):
+                copy.start(priority=1)
+
+    def wait(self, refs, scratch):
+        for copy in self.copies(refs, scratch):
+            copy.wait()
+        return scratch[:-1]
+
+
 def two_halves(block, th, tail):
     return [
         pl.BlockSpec(block, lambda j, s: (jnp.minimum(j, th - 1),) + tail),
@@ -276,7 +304,7 @@
 
 
 def norm_mod(x, mod):
-    n, d = x.shape
+    n, d = x.shape[0] - ROWS, x.shape[1]
 
     def kernel(x_ref, m_ref, h_ref):
         @pl.loop(0, n // ROWS, unroll=4)
@@ -459,9 +487,13 @@
     nw = len(wt.arrays)
     th = geo.Th
 
-    def kernel(s, ya_ref, yb_ref, x_ref, m_ref, b_ref, *refs):
-        w_refs, (attn_ref, resid_ref, h_ref, wbuf, sem) = refs[:nw], refs[nw:]
+    late = Late(x)
+
+    def kernel(s, ya_ref, yb_ref, m_ref, b_ref, *refs):
+        late_in, refs = refs[:1], refs[1:]
+        w_refs, (attn_out, resid_ref, h_ref, wbuf, sem, attn_ref, *late_buf) = refs[:nw], refs[nw:]
         j = pl.program_id(0)
+        late.start(j, late_in, late_buf)
         now = wt.stream(j, s, w_refs, wbuf, sem)
         y = jnp.where(j < th, ya_ref[0], yb_ref[0])
         part = dotg(y, now[:, -win:], 1, 1)
@@ -476,11 +508,13 @@
 
         @pl.when(j == geo.T - 1)
         def _():
+            (x_ref,) = late.wait(late_in, late_buf)
+
             @pl.loop(0, n // ROWS, unroll=4)
             def _(i):
                 at = pl.ds(pl.multiple_of(i * ROWS, ROWS), ROWS)
                 attn = attn_ref[at, :] + b_ref[...]
-                attn_ref[at, :] = attn
+                attn_out[at, :] = attn.astype(BF)
                 resid = x_ref[at, :].astype(F32) + m_ref[2:3, :] * attn
                 resid_ref[at, :] = resid
                 norm, _ = norm_of(resid)
@@ -493,27 +527,31 @@
             grid=(geo.T,),
             in_specs=[
                 *two_halves((1, n, win), th, (0, 0)),
-                whole((n, d)),
                 whole(mod.shape),
                 whole((1, d)),
+                *late.specs,
                 *wt.specs(),
             ],
             out_specs=[whole((n, d))] * 3,
-            scratch_shapes=wt.scratch(geo.base, 4 * geo.w),
+            scratch_shapes=[
+                *wt.scratch(geo.base, 4 * geo.w),
+                pltpu.VMEM((n, d), F32),
+                *late.scratch,
+            ],
         ),
         out_shape=[
+            jax.ShapeDtypeStruct((n + ROWS, d), BF),
             jax.ShapeDtypeStruct((n, d), F32),
-            jax.ShapeDtypeStruct((n, d), F32),
-            jax.ShapeDtypeStruct((n, d), BF),
+            jax.ShapeDtypeStruct((n + ROWS, d), BF),
         ],
         compiler_params=params(),
         cost_estimate=cost(2 * n * d * d, 8 * d * d + 14 * n * d),
         name="out_proj",
-    )(scal, *mixed, x, mod, bias, *wt.arrays)
+    )(scal, *mixed, mod, bias, *late.arrays, *wt.arrays)
 
 
 def up_proj(scal, h, bias, wt, geo):
-    n, d = h.shape
+    n, d = h.shape[0] - ROWS, h.shape[1]
     w = wt.width
     nw = len(wt.arrays)
     step = chunked(w, 384)
@@ -540,7 +578,7 @@
             grid=(geo.T,),
             in_specs=[
                 whole((n, d)),
-                pl.BlockSpec((1, 1, w), lambda j, s: (s[2] ^ j, 0, 0)),
+                pl.BlockSpec((1, 1, w), lambda j, s: (j, 0, 0)),
                 *wt.specs(),
             ],
             out_specs=[out, out],
@@ -558,9 +596,13 @@
     d = geo.D
     nw = len(wt.arrays)
 
-    def kernel(s, y_ref, r_ref, c_ref, m_ref, b_ref, *refs):
-        w_refs, (out_ref, sum_ref, wbuf, sem, acc) = refs[:nw], refs[nw:]
+    late = Late(resid, cot)
+
+    def kernel(s, y_ref, m_ref, b_ref, *refs):
+        late_in, refs = refs[:2], refs[2:]
+        w_refs, (out_ref, sum_ref, wbuf, sem, acc, *late_buf) = refs[:nw], refs[nw:]
         j = pl.program_id(0)
+        late.start(j, late_in, late_buf)
         now = wt.stream(j, s, w_refs, wbuf, sem)
         part = dotg(y_ref[0], now[...], 1, 1)
 
@@ -575,6 +617,8 @@
 
         @pl.when(j == geo.T - 1)
         def _():
+            r_ref, c_ref = late.wait(late_in, late_buf)
+
             @pl.loop(0, n // ROWS, unroll=4)
             def _(i):
                 at = pl.ds(pl.multiple_of(i * ROWS, ROWS), ROWS)
@@ -589,20 +633,19 @@
             grid=(geo.T,),
             in_specs=[
                 pl.BlockSpec((1, n, w), lambda j, s: (j, 0, 0)),
-                whole((n, d)),
-                whole((n, d)),
                 whole(mod.shape),
                 whole((1, d)),
+                *late.specs,
                 *wt.specs(),
             ],
             out_specs=[whole((n, d)), whole((8, d))],
-            scratch_shapes=[*wt.scratch(), pltpu.VMEM((n, d), F32)],
+            scratch_shapes=[*wt.scratch(), pltpu.VMEM((n, d), F32), *late.scratch],
         ),
         out_shape=[jax.ShapeDtypeStruct((n, d), BF), jax.ShapeDtypeStruct((8, d), F32)],
         compiler_params=params(),
         cost_estimate=cost(2 * n * d * w * geo.T, 2 * geo.T * w * (d + n) + 8 * n * d),
         name="down_proj",
-    )(scal, hidden, resid, cot, mod, bias, *wt.arrays)
+    )(scal, hidden, mod, bias, *late.arrays, *wt.arrays)
 
 
 def pre_back(scal, g, gp, wt, geo):
@@ -646,9 +689,13 @@
     d = geo.D
     nw = len(wt.arrays)
 
-    def kernel(s, y_ref, r_ref, a_ref, c_ref, m_ref, *refs):
-        w_refs, (rg_ref, ag_ref, sum_ref, wbuf, sem, acc) = refs[:nw], refs[nw:]
+    late = Late(resid, attn, cot)
+
+    def kernel(s, y_ref, m_ref, *refs):
+        late_in, refs = refs[:3], refs[3:]
+        w_refs, (rg_ref, ag_ref, sum_ref, wbuf, sem, acc, *late_buf) = refs[:nw], refs[nw:]
         j = pl.program_id(0)
+        late.start(j, late_in, late_buf)
         now = wt.stream(j, s, w_refs, wbuf, sem)
         part = dotg(y_ref[0], now[...], 1, 1)
 
@@ -663,6 +710,8 @@
 
         @pl.when(j == geo.T - 1)
         def _():
+            r_ref, a_ref, c_ref = late.wait(late_in, late_buf)
+
             @pl.loop(0, n // ROWS, unroll=4)
             def _(i):
                 at = pl.ds(pl.multiple_of(i * ROWS, ROWS), ROWS)
@@ -672,7 +721,7 @@
                 rg_ref[at, :] = rg
                 ag = rg * m_ref[2:3, :]
                 ag_ref[at, :] = ag.astype(BF)
-                sum_ref[0] += fold_rows(rg * a_ref[at, :])
+                sum_ref[0] += fold_rows(rg * a_ref[at, :].astype(F32))
                 sum_ref[1] += fold_rows(g)
                 sum_ref[2] += fold_rows(g * norm)
                 sum_ref[3] += fold_rows(ag)
@@ -684,14 +733,12 @@
             grid=(geo.T,),
             in_specs=[
                 pl.BlockSpec((1, n, w), lambda j, s: (j, 0, 0)),
-                whole((n, d)),
-                whole((n, d)),
-                whole((n, d)),
                 whole(mod.shape),
+                *late.specs,
                 *wt.specs(),
             ],
             out_specs=[whole((n, d)), whole((n, d)), whole((4, 8, d))],
-            scratch_shapes=[*wt.scratch(), pltpu.VMEM((n, d), F32)],
+            scratch_shapes=[*wt.scratch(), pltpu.VMEM((n, d), F32), *late.scratch],
         ),
         out_shape=[
             jax.ShapeDtypeStruct((n, d), F32),
@@ -701,7 +748,7 @@
         compiler_params=params(),
         cost_estimate=cost(2 * n * d * w * geo.T, 2 * geo.T * w * (d + n) + 18 * n * d),
         name="second_back",
-    )(scal, pre, resid, attn, cot, mod, *wt.arrays)
+    )(scal, pre, mod, *late.arrays, *wt.arrays)
 
 
 def mixed_back(scal, g, wt, geo):
@@ -736,9 +783,13 @@
     nw = len(wt.arrays)
     th = geo.Th
 
-    def kernel(s, ta, tb, ga, gb, x_ref, r_ref, m_ref, *refs):
-        w_refs, (out_ref, sum_ref, wbuf, sem, lhs, acc) = refs[:nw], refs[nw:]
+    late = Late(x, rg)
+
+    def kernel(s, ta, tb, ga, gb, m_ref, *refs):
+        late_in, refs = refs[:2], refs[2:]
+        w_refs, (out_ref, sum_ref, wbuf, sem, lhs, acc, *late_buf) = refs[:nw], refs[nw:]
         j = pl.program_id(0)
+        late.start(j, late_in, late_buf)
         now = wt.stream(j, s, w_refs, wbuf, sem)
         for half, (tri_ref, got_ref) in enumerate(((ta, ga), (tb, gb))):
 
@@ -759,6 +810,8 @@
 
         @pl.when(j == geo.T - 1)
         def _():
+            x_ref, r_ref = late.wait(late_in, late_buf)
+
             @pl.loop(0, n // ROWS, unroll=4)
             def _(i):
                 at = pl.ds(pl.multiple_of(i * ROWS, ROWS), ROWS)
@@ -777,9 +830,8 @@
             in_specs=[
                 *two_halves((1, n, n3), th, (0, 0)),
                 *two_halves((1, n, geo.kvw), th, (0, 0)),
-                whole((n, d)),
-                whole((n, d)),
                 whole(mod.shape),
+                *late.specs,
                 *wt.specs(),
             ],
             out_specs=[whole((n, d)), whole((2, 8, d))],
@@ -787,22 +839,25 @@
                 *wt.scratch(0, n3),
                 pltpu.VMEM((n, n3), BF),
                 pltpu.VMEM((n, d), F32),
+                *late.scratch,
             ],
         ),
         out_shape=[jax.ShapeDtypeStruct((n, d), BF), jax.ShapeDtypeStruct((2, 8, d), F32)],
         compiler_params=params(),
         cost_estimate=cost(6 * n * d * d, 8 * d * d + 16 * n * d),
         name="first_back",
-    )(scal, *tri, *got, x, rg, mod, *wt.arrays)
+    )(scal, *tri, *got, mod, *late.arrays, *wt.arrays)
 
 
 def weight_grad(scal, terms, join, w, mine, geo, name, partial=None):
-    n = terms[0][0].shape[0]
+    n = terms[0][1][0].shape[-2] if not isinstance(terms[0][1][0], tuple) else terms[0][1][0][0].shape[-2]
     pr = geo.P * geo.R
     th = geo.Th
     half_n = geo.P // 2
     want = scal[1] if mine else 1 - scal[1]
     lefts = [term[0] for term in terms]
+    if not geo.direct:
+        lefts = [a[:n] for a in lefts]
     if not geo.direct:
 
         def pick(a):
@@ -832,6 +887,8 @@
             got_ref, rest = rest[0], rest[1:]
         n_out = 4 if (mine and geo.direct) else 1
         outs, ats = rest[:n_out], rest[n_out:]
+        if mine and geo.direct:
+            total, ats = ats[-1], ats[:-1]
         j = pl.program_id(0)
         if geo.direct:
 
@@ -865,18 +922,15 @@
                     full = full + got_ref[0, 0].astype(F32)
                 outs[0][0, 0] = full.astype(BF)
                 return
-            for p in range(geo.P):
-                part = full[p * geo.R : (p + 1) * geo.R]
-                rel = s[0] ^ p
-                if not mine:
-                    outs[0][0, rel] = part.astype(BF)
-                    continue
-                part = (part + got_ref[0, rel].astype(F32)).astype(BF)
-                for i, here in enumerate(geo.order[half]):
-
-                    @pl.when(rel == here)
-                    def _():
-                        outs[2 * half + i // half_n][i % half_n, 0] = part
+            if not mine:
+                for p in range(geo.P):
+                    outs[0][0, s[0] ^ p] = full[p * geo.R : (p + 1) * geo.R].astype(BF)
+                return
+            total[...] = full
+            for i, here in enumerate(geo.order[half]):
+                row = pl.multiple_of((s[0] ^ here) * geo.R, geo.R)
+                part = total[pl.ds(row, geo.R), :] + got_ref[0, here].astype(F32)
+                outs[2 * half + i // half_n][i % half_n, 0] = part.astype(BF)
 
         for half in range(2):
 
@@ -884,7 +938,7 @@
             def _():
                 store(half)
 
-    in_specs = [whole(a.shape) for a in lefts] + op_specs
+    in_specs = [whole((n, a.shape[1])) if geo.direct else whole(a.shape) for a in lefts] + op_specs
     rel_block = (1, geo.P, geo.R, w) if geo.direct else (1, 1, pr, w)
     rel_spec = pl.BlockSpec(rel_block, lambda j, s: (j, 0, 0, 0))
     rel_shape = jax.ShapeDtypeStruct((geo.T,) + rel_block[1:], BF)
@@ -899,6 +953,9 @@
             second = pl.BlockSpec(block, lambda j, s: (0, jnp.maximum(j - th, 0), 0, 0))
             out_specs = [first, first, second, second]
             shapes = [jax.ShapeDtypeStruct((half_n, th, geo.R, w), BF)] * 4
+    scratch = [pltpu.VMEM((pr, n), BF)] * na if geo.direct else []
+    if mine and geo.direct:
+        scratch.append(pltpu.VMEM((pr, w), F32))
     got = pl.pallas_call(
         kernel,
         grid_spec=pltpu.PrefetchScalarGridSpec(
@@ -906,10 +963,10 @@
             grid=(geo.T,),
             in_specs=in_specs,
             out_specs=out_specs,
-            scratch_shapes=[pltpu.VMEM((pr, n), BF)] * (na if geo.direct else 0),
+            scratch_shapes=scratch,
         ),
         out_shape=shapes,
-        compiler_params=params(),
+        compiler_params=params(62 << 20),
         cost_estimate=cost(2 * pr * n * w * geo.T, 2 * geo.T * w * (2 * pr + n)),
         name=name,
     )(scal, *args)
@@ -1010,42 +1067,44 @@
     heads = cols // HEAD_DIM
     attn_shard = jnp.concatenate([in_weight[0], in_weight[1], in_weight[2], out_weight.T], axis=1)
     attn_way = begin(attn_shard, gather_steps, False)
-    info = jnp.concatenate([conditioning.reshape(-1), query_value_bias.reshape(-1), up_bias])
-    count = info.shape[0]
-    info = jnp.pad(info, (0, -count % 2048)).reshape(-1, 128)
-    info = share(info)
+    cond_all = conditioning[None]
+    bit = 1
+    while bit < F:
+        got = lax.ppermute(cond_all, "fsdp", [(i, i ^ bit) for i in range(F)])
+        cond_all = jnp.concatenate([cond_all, got])
+        bit *= 2
+    cond_all = reorder(cond_all, [fi ^ f for f in range(F)]).reshape(F * images, width)
+    silu_low = jax.nn.silu(cond_all.astype(F32)).astype(BF)
+    silu_own = lax.dynamic_slice_in_dim(silu_low, fi * geo.R, geo.R, 1)
+    mod_part = jnp.einsum("bd,dcj->bcj", silu_own, mod_weight, preferred_element_type=F32)
+    bias_rows = jnp.concatenate([mod_bias, query_value_bias]).astype(F32)
+    bias_rows = jnp.where(fi == 0, bias_rows, 0.0)
+    mod_part = jnp.pad(mod_part, ((0, 0), (0, 2), (0, 0))) + bias_rows
+    mod_part = mod_part.reshape(geo.P, 1, T, 8, cols)
+    mod_part = jnp.broadcast_to(mod_part, (geo.P, 2, T, 8, cols)).reshape(F * T, 8, cols)
     close()
     start(attn_way)
     up_way = begin(up_weight, gather_steps, True, True)
-    info = info.reshape(F, T, -1)[:, :, :count]
-    cond_all = info[:, 0, : images * width].reshape(F * images, width)
-    qv_bias = info[0, :, images * width : images * width + 2 * cols].reshape(T, 2, 1, cols)
-    unit_bias = info[0, :, images * width + 2 * cols :].reshape(T, 1, units).astype(F32)
+    mod_part = lax.all_to_all(mod_part, BOTH, 0, 0, tiled=True)
+    mod_part = mod_part.reshape(F, T, 8, cols).sum(axis=0)
+    mod = mod_part[:, :6].transpose(1, 0, 2).reshape(6, width)
+    qv_bias = mod_part[:, 6:]
     triple_bias = jnp.concatenate(
         [
-            qv_bias[:, 0],
-            jnp.zeros_like(qv_bias[:, 0]),
-            qv_bias[:, 1],
-            jnp.zeros((T, 1, geo.n3 - 3 * cols), BF),
+            qv_bias[:, :1],
+            jnp.zeros_like(qv_bias[:, :1]),
+            qv_bias[:, 1:],
+            jnp.zeros((T, 1, geo.n3 - 3 * cols), F32),
         ],
         axis=2,
-    ).astype(F32)
-    silu_low = jax.nn.silu(cond_all.astype(F32)).astype(BF)
-    silu_own = lax.dynamic_slice_in_dim(silu_low, fi * geo.R, geo.R, 1)
-    mod_part = jnp.einsum("bd,dcj->bcj", silu_own, mod_weight, preferred_element_type=F32)
-    mod_part += jnp.where(fi == 0, mod_bias.astype(F32), 0.0)
-    mod_part = mod_part.reshape(geo.P, 1, T, 6, cols)
-    mod_part = jnp.broadcast_to(mod_part, (geo.P, 2, T, 6, cols)).reshape(F * T, 6, cols)
-    mod_part = lax.all_to_all(after(mod_part, *up_way.flight), BOTH, 0, 0, tiled=True)
-    mod = mod_part.reshape(F, T, 6, cols).sum(axis=0).transpose(1, 0, 2).reshape(6, width)
+    )
     bias_rows = branch_bias.astype(F32)
     close(mod)
     start(attn_way)
-    start(up_way)
     x_parts = to_chip(tie(latents))
     opened.extend(x_parts)
     close()
-    x = jnp.concatenate(x_parts)
+    x = jnp.concatenate([*x_parts, jnp.zeros((ROWS, width), BF)])
     start(attn_way, up_way)
     h1 = norm_mod(tie(x), mod)
     close(h1)
@@ -1054,12 +1113,15 @@
 
     q, kv, kvo = [None] * 2, [None] * 2, [None] * 2
     mixed, lse = [None] * 2, [None] * 2
-    down_way = begin(down_weight.T, gather_steps)
+    extras = []
+    down_shard = jnp.concatenate(
+        [down_weight.T, jnp.broadcast_to(up_bias, (16, units))]
+    )
+    down_way = begin(down_shard, gather_steps, True, False, extras)
     for half in range(2):
         q[half], kv[half] = in_proj(tie(scal), h1, w_attn, triple_bias, half, geo)
     close(q[0], q[1])
     kvo = [across(kv[0]), across(kv[1])]
-    start(down_way)
     close()
     start(up_way, down_way)
     for half in range(2):
@@ -1072,6 +1134,7 @@
     start(down_way)
     cot_parts = to_chip(tie(cotangent))
     opened.extend(cot_parts)
+    unit_bias = jnp.stack([part[:1] for part in extras]).astype(F32)
     hidden, gp = up_proj(tie(scal), h2, unit_bias, w_up, geo)
     close(hidden)
     start(down_way)
@@ -1113,7 +1176,7 @@
     mg = mixed_back(tie(scal), ag, w_attn, geo)
     close(mg, *up_parts)
     start(down_back)
-    up_back = begin(up_parts, scatter_steps, False)
+    up_back = begin(up_parts, scatter_steps)
     tri, tri_send, tri_sums, send_sums = [None] * 2, [None] * 2, [None] * 2, [None] * 2
     for half in range(2):
         tri[half], tri_send[half], tri_sums[half], send_sums[half] = attn_bwd(
@@ -1149,40 +1212,40 @@
     attn_got = across(attn_half)
     latent_rows, first_sums = first_back(tie(scal), tri, tri_got, x, rg, mod, w_attn, geo)
     close(first_sums)
+    start(up_back)
     mine = [i ^ ti for i in range(T)]
     rows = jnp.concatenate(
         [first_sums.sum(axis=1), mid_sums[:3].sum(axis=1), ffn_sums.sum(axis=0, keepdims=True)]
     )
-    rows = rows.reshape(6, T, cols).transpose(1, 0, 2).reshape(T, 6 * cols)
-    branch_sums = jnp.stack([mid_sums[3].sum(axis=0), ffn_sum]).reshape(1, 2 * width)
-    rows = tie(rows)
-    pack = jnp.concatenate(
-        [
-            rows,
-            jnp.broadcast_to(branch_sums, (T, 2 * width)),
-            reorder(unit_sum, mine).reshape(T, units),
-            reorder(pair_sums, mine).reshape(T, 2 * cols),
-        ],
-        axis=1,
-    )
-    pack = jnp.pad(pack, ((0, 0), (0, -pack.shape[1] % 1024)))
-    pack = jnp.broadcast_to(pack[None], (F,) + pack.shape).reshape(F * T, -1, 128)
+    rows = tie(rows).reshape(6, T, cols).transpose(1, 0, 2).reshape(T, 6 * cols)
+    branch_sums = jnp.stack([mid_sums[3].sum(axis=0), ffn_sum]).reshape(F, T, -1)
+    unit_sums = reorder(unit_sum, mine).reshape(T, F, units // F).transpose(1, 0, 2)
+    pair_sums = reorder(pair_sums, mine).reshape(T, F, 2 * cols // F).transpose(1, 0, 2)
+    rows = jnp.broadcast_to(rows[None], (F,) + rows.shape)
+    pack = jnp.concatenate([rows, branch_sums, unit_sums, pair_sums], axis=2)
+    count = pack.shape[2]
+    pack = jnp.pad(pack, ((0, 0), (0, 0), (0, -count % 1024))).reshape(F * T, -1, 128)
     pack = lax.all_to_all(pack, BOTH, 0, 0, tiled=True)
     attn_parts = weight_grad(
         tie(scal), attn_terms, beside, 4 * cols, True, geo, "w_attn", attn_got
     )
     close(pack, *attn_parts)
     attn_back = begin(attn_parts, scatter_steps, False)
-    pack = tie(pack).reshape(F, T, -1)
-    mine_rows = pack[:, :, : 6 * cols].reshape(geo.P, 2, T, 6, cols).sum(axis=1)
-    mine_rows = mine_rows.reshape(F * images, 6, cols)
-    cond_part = jnp.einsum("bcj,dcj->bd", mine_rows, mod_weight.astype(F32), precision=highest)
-    cond_part = cond_part.reshape(F, 1, images, geo.R)
-    cond_part = jnp.broadcast_to(cond_part, (F, T, images, geo.R)).reshape(F * T, images, geo.R)
-    cond_part = lax.all_to_all(cond_part, BOTH, 0, 0, tiled=True)
     latent_back = from_chip(tie(latent_rows))
     opened.extend(latent_back)
-    close()
+    pack = tie(pack)
+    slices = pack.sum(axis=0).reshape(-1)[6 * cols : count]
+    tiles = -(-6 * cols // 128)
+    mine_rows = pack[:, :tiles].reshape(geo.P, 2, T, tiles, 128).sum(axis=1)
+    mine_rows = mine_rows.reshape(F * images, -1)[:, : 6 * cols].reshape(F * images, 6, cols)
+    cond_part = jnp.einsum("bcj,dcj->bd", mine_rows, mod_weight.astype(F32), precision=highest)
+    cond_part = cond_part.reshape(F, 1, images * geo.R)
+    cond_part = jnp.broadcast_to(cond_part, (F, T, images * geo.R))
+    kept = jnp.broadcast_to(slices[None, None], (F, T) + slices.shape)
+    final = jnp.concatenate([cond_part, kept], axis=2).reshape(F * T, -1)
+    final = jnp.pad(final, ((0, 0), (0, -final.shape[1] % 1024))).reshape(F * T, -1, 128)
+    final = lax.all_to_all(final, BOTH, 0, 0, tiled=True)
+    close(final)
     start(attn_back)
     close()
     start(attn_back)
@@ -1191,13 +1254,18 @@
     attn_grad = attn_back.finish(*now)
     in_grad = attn_grad[:, : 3 * cols].reshape(geo.R, 3, cols).transpose(1, 0, 2)
 
-    bias_total = pack[:, :, 6 * cols :].sum(axis=(0, 1))
-    branch_grad = bias_total[: 2 * width].reshape(2, width)
-    unit_grad = bias_total[2 * width : 2 * width + units]
-    pair_grad = bias_total[2 * width + units :][: 2 * cols].reshape(2, cols)
+    final = final.reshape(F, T, -1)
+    at = images * geo.R
+    cond_mine = final[:, :, :at].sum(axis=1).reshape(F, images, geo.R)
+    step = 2 * width // (F * T)
+    branch_grad = final[:, :, at : at + step].reshape(2, width)
+    own = lax.dynamic_index_in_dim(final, ti, 1, keepdims=False)
+    at += step
+    unit_grad = own[:, at : at + units // F].reshape(units)
+    at += units // F
+    pair_grad = own[:, at : at + 2 * cols // F].reshape(2, cols)
     mod_weight_grad = jnp.einsum("bd,bcj->dcj", silu_own.astype(F32), mine_rows, precision=highest)
     mod_bias_grad = mine_rows.sum(axis=0)
-    cond_mine = cond_part.reshape(F, T, images, geo.R).sum(axis=1)
     silu_grad = cond_mine.transpose(1, 0, 2).reshape(images, width)
     cond_f = conditioning.astype(F32)
     sig = jax.nn.sigmoid(cond_f)

time: 602 us -> 573 us (0.952)
  waiting for transfers between devices: 172 us -> 136 us
  starting transfers between devices: 83.8 us -> 116 us
  blocking collectives: 16.2 us -> 0 us
  local copies, waits for them, and re-layouts: 36.6 us -> 25.8 us
  Pallas kernels: 238 us -> 229 us
    ppermute x18, waiting for transfers between devices: 104 us -> 64 us  [flip_tensor(): return lax.ppermute(x, 'tensor', [(i, i ^ k) for i in range(geo.T)])]
    ppermute x17, starting transfers between devices: 8.31 us -> 27.6 us  [flip_core(): return lax.ppermute(x, 'fsdp', [(i, i ^ 1) for i in range(geo.F)])]
    all_to_all x1 -> x0, blocking collectives: 16.2 us -> none  [body(): lax.all_to_all(after(mod_part, *up_way.flight), BOTH, 0, 0, tiled=True)]
    unnamed x158 -> x126, local copies, waits for them, and re-layouts: 16.8 us -> 7.04 us
    ppermute x4, starting transfers between devices: 2.53 us -> 8.9 us  [from_chip(): got.append(lax.ppermute(arr[k * row_count:(k + 1) * row_count], BOTH, back))]
  transfers between devices with their start and end apart: 70 -> 73, of which waited for: 24 -> 29; matrix products, arithmetic and copies ran while one was open for 9% -> 10% of each run, Pallas kernels for 38% -> 39%
where the time goes in v4:
time: 573 us; the launch traced here: 562 us
  Pallas kernels  229 us (40%)
  waiting for transfers between devices  136 us (24%)
  starting transfers between devices  116 us (20%)
  other arithmetic  48.6 us (8%)
  local copies, waits for them, and re-layouts  25.8 us (5%)
    ppermute x18, waiting for transfers between devices, flip_tensor(): return lax.ppermute(x, 'tensor', [(i, i ^ k) for i in range(geo.T)])  64 us
    pallas_call x6, Pallas kernels, weight_grad(): pl.pallas_call(kernel, grid_spec=pltpu.PrefetchScalarGridSpec(num_scalar_...  62.9 us
    ppermute x24, waiting for transfers between devices, flip_pair(): return lax.ppermute(x, 'fsdp', [(i, i ^ 2 * bit) for i in range(geo.F)])  42.1 us
    ppermute x18, starting transfers between devices, flip_tensor(): return lax.ppermute(x, 'tensor', [(i, i ^ k) for i in range(geo.T)])  30.3 us
    pallas_call x2, Pallas kernels, attn_bwd(): pl.pallas_call(kernel, grid=(z,), in_specs=[spec(wp), spec(geo.kvw), spec...  29.3 us
    ppermute x24, starting transfers between devices, flip_pair(): return lax.ppermute(x, 'fsdp', [(i, i ^ 2 * bit) for i in range(geo.F)])  27.8 us
    ppermute x17, starting transfers between devices, flip_core(): return lax.ppermute(x, 'fsdp', [(i, i ^ 1) for i in range(geo.F)])  27.6 us
    pallas_call x2, Pallas kernels, attn_fwd(): pl.pallas_call(kernel, grid=(z,), in_specs=[spec(wp), spec(geo.kvw), spec...  19.6 us
  transfers between devices with their start and end apart: 73, of which 29 were waited for; matrix products, arithmetic and copies ran while one was open for 10% of the time, Pallas kernels for 39%

profile of v4, /device:TPU:10, one launch (start us, length us, event | category | flops | bytes accessed | tf_op | source)
XLA Modules:
  0.0 561.7 jit_solution(65757592981308331)
XLA Ops:
  21.5 13.8 %collective-permute-done.1 = bf16[144,1152]{1,0:T(8,128)(2,1)S(1)} collective-permute-done((bf16[144,1152]{1,0:T(8,128)(2,1)S(1)}, bf16[144,1152]{1,0:T(8,128)(2,1)S(1)}, u32[]{:S(2)}, u32[]{:S(2)}) %collective-permute-start.1) | collective-permute-done | bytes 331808 | tf_op jit(solution)/shard_map/ppermute | solution.py:67
  35.3 8.2 %collective-permute-done.2 = bf16[144,1152]{1,0:T(8,128)(2,1)S(1)} collective-permute-done((bf16[144,1152]{1,0:T(8,128)(2,1)S(1)}, bf16[144,1152]{1,0:T(8,128)(2,1)S(1)}, u32[]{:S(2)}, u32[]{:S(2)}) %collective-permute-start.2) | collective-permute-done | bytes 331808 | tf_op jit(solution)/shard_map/ppermute | solution.py:67
  71.6 11.1 %collective-permute-start.10 = (bf16[2,2,144,1152]{3,2,1,0:T(8,128)(2,1)S(1)}, bf16[2,2,144,1152]{3,2,1,0:T(8,128)(2,1)}, u32[]{:S(2)}, u32[]{:S(2)}) collective-permute-start(bf16[2,2,144,1152]{3,2,1,0:T(8,128)(2,1)S(1)} %pad_maximum_fusion.2.refs_0_.refs_1_.refs_2_), channel_id=1, source_target_pairs={{0,4},{4,0},{8,12},{12,8},{16,20},{20,16},{24,28},{28,24},{1,5},{5... | collective-permute-start | bytes 3981320 | tf_op jit(solution)/shard_map/ppermute | solution.py:63
  150.6 9.8 %attn_fwd.3 = (bf16[2,512,384]{2,1,0:T(8,128)(2,1)}, f32[2,4,512]{2,1,0:T(4,128)}) custom-call(bf16[2,512,384]{2,1,0:T(8,128)(2,1)} %get-tuple-element.240.q_ref, bf16[2,512,640]{2,1,0:T(8,128)(2,1)} %get-tuple-element.174.kv_ref, bf16[2,512,640]{2,1,0:T(8,128)(2,1)} %copy-done.55), custom_call_target="tpu_custom_call" | custom-call | flops 6000000000 | bytes 3932160 | tf_op jit(solution)/shard_map/attn_fwd/pallas_call | solution.py:399
  160.4 9.8 %attn_fwd.2 = (bf16[2,512,384]{2,1,0:T(8,128)(2,1)}, f32[2,4,512]{2,1,0:T(4,128)}) custom-call(bf16[2,512,384]{2,1,0:T(8,128)(2,1)} %get-tuple-element.236.q_ref, bf16[2,512,640]{2,1,0:T(8,128)(2,1)} %get-tuple-element.172.kv_ref, bf16[2,512,640]{2,1,0:T(8,128)(2,1)} %copy-done.54), custom_call_target="tpu_custom_call" | custom-call | flops 6000000000 | bytes 3932160 | tf_op jit(solution)/shard_map/attn_fwd/pallas_call | solution.py:399
  170.2 11.6 %out_proj.1 = (bf16[544,1152]{1,0:T(8,128)(2,1)}, f32[512,1152]{1,0:T(8,128)}, bf16[544,1152]{1,0:T(8,128)(2,1)}) custom-call(s32[3]{0:T(128)} %pad_add_fusion.1.s, bf16[2,512,384]{2,1,0:T(8,128)(2,1)} %get-tuple-element.180.ya_ref.o_ref.refs_6_, bf16[2,512,384]{2,1,0:T(8,128)(2,1)} %get-tuple-element.182.yb_ref.o_ref.refs_7_, f32[6,1152]{1,0:T(8,128)} %reshape.191.m_ref, ...), custom_call_target="tpu_custom_call" | custom-call | flops 1358954496 | bytes 18874368 | tf_op jit(solution)/shard_map/out_proj/pallas_call | solution.py:523
  188.1 14.6 %collective-permute-done.25 = bf16[1,2,144,1152]{3,2,1,0:T(8,128)(2,1)S(1)} collective-permute-done((bf16[1,2,144,1152]{3,2,1,0:T(8,128)(2,1)S(1)}, bf16[1,2,144,1152]{3,2,1,0:T(8,128)(2,1)S(1)}, u32[]{:S(2)}, u32[]{:S(2)}) %collective-permute-start.25) | collective-permute-done | bytes 663584 | tf_op jit(solution)/shard_map/ppermute | solution.py:59
  213.7 18.1 %up_proj.1 = (bf16[4,512,1152]{2,1,0:T(8,128)(2,1)}, bf16[4,512,1152]{2,1,0:T(8,128)(2,1)}) custom-call(s32[3]{0:T(128)} %pad_add_fusion.1.s, bf16[544,1152]{1,0:T(8,128)(2,1)} %get-tuple-element.183.h_ref.refs_0_, f32[4,1,1152]{2,1,0:T(1,128)} %maximum_convert_fusion.b_ref, bf16[4,2,144,1152]{3,2,1,0:T(8,128)(2,1)} %copy-done.5, ...), custom_call_target="tpu_custom_call" | custom-call | flops 5435817984 | bytes 20054016 | tf_op jit(solution)/shard_map/up_proj/pallas_call | solution.py:574
  240.4 8.4 %w_down_send.1 = bf16[4,4,144,1152]{3,2,1,0:T(8,128)(2,1)} custom-call(s32[3]{0:T(128)} %pad_add_fusion.1.s, bf16[512,1152]{1,0:T(8,128)(2,1)} %get-tuple-element.349.refs_0_.g_ref, bf16[4,512,1152]{2,1,0:T(8,128)(2,1)} %get-tuple-element.194.refs_1_.y_ref), custom_call_target="tpu_custom_call" | custom-call | flops 2717908992 | bytes 15335424 | tf_op jit(solution)/shard_map/w_down_send/pallas_call | solution.py:959
  249.3 14.2 %down_proj.1 = (bf16[512,1152]{1,0:T(8,128)(2,1)}, f32[8,1152]{1,0:T(8,128)}) custom-call(s32[3]{0:T(128)} %pad_add_fusion.1.s, bf16[4,512,1152]{2,1,0:T(8,128)(2,1)} %get-tuple-element.194.refs_1_.y_ref, f32[6,1152]{1,0:T(8,128)} %reshape.191.m_ref, f32[1,1152]{1,0:T(1,128)} %get-tuple-element.385.b_ref, f32[512,1152]{1,0:T(8,128)} %get-tuple-element.199.refs_0_, ...), custom_call_target="tpu_custom_call" | custom-call | flops 5435817984 | bytes 20054016 | tf_op jit(solution)/shard_map/down_proj/pallas_call | solution.py:629
  263.6 11.1 %w_down.1 = (bf16[2,2,144,1152]{3,2,1,0:T(8,128)(2,1)}, bf16[2,2,144,1152]{3,2,1,0:T(8,128)(2,1)}, bf16[2,2,144,1152]{3,2,1,0:T(8,128)(2,1)}, bf16[2,2,144,1152]{3,2,1,0:T(8,128)(2,1)}) custom-call(s32[3]{0:T(128)} %pad_add_fusion.1.s, bf16[512,1152]{1,0:T(8,128)(2,1)} %get-tuple-element.349.refs_0_.g_ref, ...), custom_call_target="tpu_custom_call" | custom-call | flops 2717908992 | bytes 15335424 | tf_op jit(solution)/shard_map/w_down/pallas_call | solution.py:959
  285.9 14.3 %pre_back.1 = (bf16[4,512,1152]{2,1,0:T(8,128)(2,1)}, f32[4,1,1152]{2,1,0:T(1,128)}) custom-call(s32[3]{0:T(128)} %pad_add_fusion.1.s, bf16[512,1152]{1,0:T(8,128)(2,1)} %get-tuple-element.349.refs_0_.g_ref, bf16[4,512,1152]{2,1,0:T(8,128)(2,1)} %get-tuple-element.217.gp_ref, bf16[2,2,144,1152]{3,2,1,0:T(8,128)(2,1)} %pad_maximum_fusion.6.refs_2_.refs_0_, ...), custom_call_target="tpu_custom_call" | custom-call | flops 5435817984 | bytes 20054016 | tf_op jit(solution)/shard_map/pre_back/pallas_call | solution.py:668
  300.2 8.4 %w_up_send.1 = bf16[4,4,144,1152]{3,2,1,0:T(8,128)(2,1)} custom-call(s32[3]{0:T(128)} %pad_add_fusion.1.s, bf16[544,1152]{1,0:T(8,128)(2,1)} %get-tuple-element.183.h_ref.refs_0_, bf16[4,512,1152]{2,1,0:T(8,128)(2,1)} %get-tuple-element.218.refs_1_.y_ref), custom_call_target="tpu_custom_call" | custom-call | flops 2717908992 | bytes 15335424 | tf_op jit(solution)/shard_map/w_up_send/pallas_call | solution.py:959
  313.9 16.9 %second_back.1 = (f32[512,1152]{1,0:T(8,128)}, bf16[512,1152]{1,0:T(8,128)(2,1)}, f32[4,8,1152]{2,1,0:T(8,128)}) custom-call(s32[3]{0:T(128)} %pad_add_fusion.1.s, bf16[4,512,1152]{2,1,0:T(8,128)(2,1)} %get-tuple-element.218.refs_1_.y_ref, f32[6,1152]{1,0:T(8,128)} %reshape.191.m_ref, f32[512,1152]{1,0:T(8,128)} %get-tuple-element.199.refs_0_, ...), custom_call_target="tpu_custom_call" | custom-call | flops 5435817984 | bytes 25952256 | tf_op jit(solution)/shard_map/second_back/pallas_call | solution.py:729
  344.8 11.2 %w_up.1 = (bf16[2,2,144,1152]{3,2,1,0:T(8,128)(2,1)}, bf16[2,2,144,1152]{3,2,1,0:T(8,128)(2,1)}, bf16[2,2,144,1152]{3,2,1,0:T(8,128)(2,1)}, bf16[2,2,144,1152]{3,2,1,0:T(8,128)(2,1)}) custom-call(s32[3]{0:T(128)} %pad_add_fusion.1.s, bf16[544,1152]{1,0:T(8,128)(2,1)} %get-tuple-element.183.h_ref.refs_0_, ...), custom_call_target="tpu_custom_call" | custom-call | flops 2717908992 | bytes 15335424 | tf_op jit(solution)/shard_map/w_up/pallas_call | solution.py:959
  358.8 14.7 %attn_bwd.3 = (bf16[2,512,896]{2,1,0:T(8,128)(2,1)}, bf16[2,512,640]{2,1,0:T(8,128)(2,1)}, f32[2,1,896]{2,1,0:T(1,128)}, f32[2,1,640]{2,1,0:T(1,128)}) custom-call(bf16[2,512,384]{2,1,0:T(8,128)(2,1)} %get-tuple-element.240.q_ref, bf16[2,512,640]{2,1,0:T(8,128)(2,1)} %get-tuple-element.174.kv_ref, bf16[2,512,640]{2,1,0:T(8,128)(2,1)} %copy-done.55, ...), custom_call_target="tpu_custom_call" | custom-call | flops 10000000000 | bytes 6291456 | tf_op jit(solution)/shard_map/attn_bwd/pallas_call | solution.py:453
  373.5 14.6 %attn_bwd.2 = (bf16[2,512,896]{2,1,0:T(8,128)(2,1)}, bf16[2,512,640]{2,1,0:T(8,128)(2,1)}, f32[2,1,896]{2,1,0:T(1,128)}, f32[2,1,640]{2,1,0:T(1,128)}) custom-call(bf16[2,512,384]{2,1,0:T(8,128)(2,1)} %get-tuple-element.236.q_ref, bf16[2,512,640]{2,1,0:T(8,128)(2,1)} %get-tuple-element.172.kv_ref, bf16[2,512,640]{2,1,0:T(8,128)(2,1)} %copy-done.54, ...), custom_call_target="tpu_custom_call" | custom-call | flops 10000000000 | bytes 6291456 | tf_op jit(solution)/shard_map/attn_bwd/pallas_call | solution.py:453
  399.1 11.0 %w_attn_send.1 = bf16[4,4,144,1152]{3,2,1,0:T(8,128)(2,1)} custom-call(s32[3]{0:T(128)} %pad_add_fusion.1.s, bf16[512,1152]{1,0:T(8,128)(2,1)} %norm_mod.1.h_ref.refs_0_, bf16[512,1152]{1,0:T(8,128)(2,1)} %get-tuple-element.225.g_ref.refs_1_, bf16[2,512,896]{2,1,0:T(8,128)(2,1)} %get-tuple-element.250.refs_2_.ta, ...), custom_call_target="tpu_custom_call" | custom-call | flops 2717908992 | bytes 15335424 | tf_op jit(solution)/shard_map/w_attn_send/pallas_call | solution.py:959
  427.5 15.2 %first_back.1 = (bf16[512,1152]{1,0:T(8,128)(2,1)}, f32[2,8,1152]{2,1,0:T(8,128)}) custom-call(s32[3]{0:T(128)} %pad_add_fusion.1.s, bf16[2,512,896]{2,1,0:T(8,128)(2,1)} %get-tuple-element.250.refs_2_.ta, bf16[2,512,896]{2,1,0:T(8,128)(2,1)} %get-tuple-element.251.refs_3_.tb, bf16[2,512,640]{2,1,0:T(8,128)(2,1)} %collective-permute-done.53.refs_4_.ga, ...), custom_call_target="tpu_custom_call" | custom-call | flops 4076863488 | bytes 20054016 | tf_op jit(solution)/shard_map/first_back/pallas_call | solution.py:825
  454.3 12.7 %w_attn.1 = (bf16[2,2,144,1152]{3,2,1,0:T(8,128)(2,1)}, bf16[2,2,144,1152]{3,2,1,0:T(8,128)(2,1)}, bf16[2,2,144,1152]{3,2,1,0:T(8,128)(2,1)}, bf16[2,2,144,1152]{3,2,1,0:T(8,128)(2,1)}) custom-call(s32[3]{0:T(128)} %pad_add_fusion.1.s, bf16[512,1152]{1,0:T(8,128)(2,1)} %norm_mod.1.h_ref.refs_0_, bf16[512,1152]{1,0:T(8,128)(2,1)} %get-tuple-element.225.g_ref.refs_1_, ...), custom_call_target="tpu_custom_call" | custom-call | flops 2717908992 | bytes 15335424 | tf_op jit(solution)/shard_map/w_attn/pallas_call | solution.py:959
  484.5 16.8 %all-to-all-done.2 = f32[32,8,128]{2,1,0:T(8,128)S(1)} async-done(((f32[32,8,128]{2,1,0:T(8,128)}), f32[32,8,128]{2,1,0:T(8,128)S(1)}, u32[]{:S(2)}, u32[]{:S(2)}) %all-to-all-start.2) | async-done | bytes 131104 | tf_op jit(solution)/shard_map/all_to_all | solution.py:1247
  520.9 8.2 %collective-permute-start.68 = (bf16[144,1152]{1,0:T(8,128)(2,1)S(1)}, bf16[144,1152]{1,0:T(8,128)(2,1)S(1)}, u32[]{:S(2)}, u32[]{:S(2)}) collective-permute-start(bf16[144,1152]{1,0:T(8,128)(2,1)S(1)} %get-tuple-element.363), channel_id=1, source_target_pairs={{0,2},{1,3},{2,0},{3,1},{4,6},{5,7},{6,4},{7,5},{8,10},{9,11},{10,... | collective-permute-start | bytes 995336 | tf_op jit(solution)/shard_map/ppermute | solution.py:67
  535.3 14.8 %collective-permute-done.68 = bf16[144,1152]{1,0:T(8,128)(2,1)S(1)} collective-permute-done((bf16[144,1152]{1,0:T(8,128)(2,1)S(1)}, bf16[144,1152]{1,0:T(8,128)(2,1)S(1)}, u32[]{:S(2)}, u32[]{:S(2)}) %collective-permute-start.68) | collective-permute-done | bytes 331808 | tf_op jit(solution)/shard_map/ppermute | solution.py:67
  550.1 9.0 %collective-permute-done.69 = bf16[144,1152]{1,0:T(8,128)(2,1)S(1)} collective-permute-done((bf16[144,1152]{1,0:T(8,128)(2,1)S(1)}, bf16[144,1152]{1,0:T(8,128)(2,1)S(1)}, u32[]{:S(2)}, u32[]{:S(2)}) %collective-permute-start.69) | collective-permute-done | bytes 331808 | tf_op jit(solution)/shard_map/ppermute | solution.py:67
  (407 shorter events, 260.7 us)
Async XLA Ops:
  5.7 29.6 %collective-permute-start.1 = (bf16[144,1152]{1,0:T(8,128)(2,1)S(1)}, bf16[144,1152]{1,0:T(8,128)(2,1)S(1)}, u32[]{:S(2)}, u32[]{:S(2)}) collective-permute-start(bf16[144,1152]{1,0:T(8,128)(2,1)S(1)} %concatenate.86), channel_id=1, source_target_pairs={{0,2},{1,3},{2,0},{3,1},{4,6},{5,7},{6,4},{7,5},{8,10},{9,11},{10,... | collective-permute-start | bytes 995336 | tf_op jit(solution)/shard_map/ppermute | solution.py:67
  8.7 34.7 %collective-permute-start.2 = (bf16[144,1152]{1,0:T(8,128)(2,1)S(1)}, bf16[144,1152]{1,0:T(8,128)(2,1)S(1)}, u32[]{:S(2)}, u32[]{:S(2)}) collective-permute-start(bf16[144,1152]{1,0:T(8,128)(2,1)S(1)} %concatenate.86), channel_id=1, source_target_pairs={{0,3},{1,2},{2,1},{3,0},{4,7},{5,6},{6,5},{7,4},{8,11},{9,10},{10,... | collective-permute-start | bytes 995336 | tf_op jit(solution)/shard_map/ppermute | solution.py:67
  14.5 34.0 %all-to-all-start = ((f32[32,8,288]{2,1,0:T(8,128)}), f32[32,8,288]{2,1,0:T(8,128)S(1)}, u32[]{:S(2)}, u32[]{:S(2)}) async-start(f32[32,8,288]{2,1,0:T(8,128)} %bitcast.17), calls=%async_computation | async-start | bytes 786432 | tf_op jit(solution)/shard_map/all_to_all | solution.py:1088
  61.3 28.0 %collective-permute-start.12 = (bf16[2,2,144,1152]{3,2,1,0:T(8,128)(2,1)S(1)}, bf16[2,2,144,1152]{3,2,1,0:T(8,128)(2,1)}, u32[]{:S(2)}, u32[]{:S(2)}) collective-permute-start(bf16[2,2,144,1152]{3,2,1,0:T(8,128)(2,1)S(1)} %pad_maximum_fusion.3.refs_0_.refs_5_.refs_4_.refs_6_), channel_id=1, source_target_pairs={{0,8},{4,12},{8,0},{12,4},{16,24},{20,28},{24,16},{28,20},{1,9},{5... | collective-permute-start | bytes 3981320 | tf_op jit(solution)/shard_map/ppermute | solution.py:59
  64.1 27.3 %collective-permute-start.11 = (bf16[2,2,144,1152]{3,2,1,0:T(8,128)(2,1)S(1)}, bf16[2,2,144,1152]{3,2,1,0:T(8,128)(2,1)}, u32[]{:S(2)}, u32[]{:S(2)}) collective-permute-start(bf16[2,2,144,1152]{3,2,1,0:T(8,128)(2,1)S(1)} %pad_maximum_fusion.2.refs_0_.refs_1_.refs_2_), channel_id=1, source_target_pairs={{0,16},{4,20},{8,24},{12,28},{16,0},{20,4},{24,8},{28,12},{1,17},{... | collective-permute-start | bytes 3981320 | tf_op jit(solution)/shard_map/ppermute | solution.py:59
  69.4 46.9 %collective-permute-start.16 = (bf16[2,2,144,1152]{3,2,1,0:T(8,128)(2,1)S(1)}, bf16[2,2,144,1152]{3,2,1,0:T(8,128)(2,1)}, u32[]{:S(2)}, u32[]{:S(2)}) collective-permute-start(bf16[2,2,144,1152]{3,2,1,0:T(8,128)(2,1)S(1)} %pad_maximum_fusion.3.refs_0_.refs_5_.refs_4_.refs_6_), channel_id=1, source_target_pairs={{0,4},{4,0},{8,12},{12,8},{16,20},{20,16},{24,28},{28,24},{1,5},{5... | collective-permute-start | bytes 3981320 | tf_op jit(solution)/shard_map/ppermute | solution.py:63
  71.6 44.7 %collective-permute-start.10 = (bf16[2,2,144,1152]{3,2,1,0:T(8,128)(2,1)S(1)}, bf16[2,2,144,1152]{3,2,1,0:T(8,128)(2,1)}, u32[]{:S(2)}, u32[]{:S(2)}) collective-permute-start(bf16[2,2,144,1152]{3,2,1,0:T(8,128)(2,1)S(1)} %pad_maximum_fusion.2.refs_0_.refs_1_.refs_2_), channel_id=1, source_target_pairs={{0,4},{4,0},{8,12},{12,8},{16,20},{20,16},{24,28},{28,24},{1,5},{5... | collective-permute-start | bytes 3981320 | tf_op jit(solution)/shard_map/ppermute | solution.py:63
  147.2 34.6 %collective-permute-start.28 = (bf16[2,2,144,1152]{3,2,1,0:T(8,128)(2,1)S(1)}, bf16[2,2,144,1152]{3,2,1,0:T(8,128)(2,1)}, u32[]{:S(2)}, u32[]{:S(2)}) collective-permute-start(bf16[2,2,144,1152]{3,2,1,0:T(8,128)(2,1)S(1)} %pad_maximum_fusion.5), channel_id=1, source_target_pairs={{0,8},{4,12},{8,0},{12,4},{16,24},{20,28},{24,16},{28,20},{1,9},{5... | collective-permute-start | bytes 3981320 | tf_op jit(solution)/shard_map/ppermute | solution.py:59
  148.1 33.7 %collective-permute-start.27 = (bf16[2,2,144,1152]{3,2,1,0:T(8,128)(2,1)S(1)}, bf16[2,2,144,1152]{3,2,1,0:T(8,128)(2,1)S(1)}, u32[]{:S(2)}, u32[]{:S(2)}) collective-permute-start(bf16[2,2,144,1152]{3,2,1,0:T(8,128)(2,1)S(1)} %pad_maximum_fusion.4), channel_id=1, source_target_pairs={{0,16},{4,20},{8,24},{12,28},{16,0},{20,4},{24,8},{28,12},{1,17},{... | collective-permute-start | bytes 3981320 | tf_op jit(solution)/shard_map/ppermute | solution.py:59
  149.6 32.2 %collective-permute-start.26 = (bf16[160,1152]{1,0:T(8,128)(2,1)S(1)}, bf16[160,1152]{1,0:T(8,128)(2,1)S(1)}, u32[]{:S(2)}, u32[]{:S(2)}) collective-permute-start(bf16[160,1152]{1,0:T(8,128)(2,1)S(1)} %pad_maximum_fusion.10), channel_id=1, source_target_pairs={{0,2},{1,3},{2,0},{3,1},{4,6},{5,7},{6,4},{7,5},{8,10},{9,11},{10,... | collective-permute-start | bytes 1105928 | tf_op jit(solution)/shard_map/ppermute | solution.py:67
  205.7 30.7 %collective-permute-start.34 = (bf16[2,2,144,1152]{3,2,1,0:T(8,128)(2,1)}, bf16[2,2,144,1152]{3,2,1,0:T(8,128)(2,1)}, u32[]{:S(2)}, u32[]{:S(2)}) collective-permute-start(bf16[2,2,144,1152]{3,2,1,0:T(8,128)(2,1)} %pad_maximum_fusion.7.refs_6_.refs_4_), channel_id=1, source_target_pairs={{0,8},{4,12},{8,0},{12,4},{16,24},{20,28},{24,16},{28,20},{1,9},{5... | collective-permute-start | bytes 3981320 | tf_op jit(solution)/shard_map/ppermute | solution.py:59
  207.8 30.2 %collective-permute-start.33 = (bf16[2,2,144,1152]{3,2,1,0:T(8,128)(2,1)}, bf16[2,2,144,1152]{3,2,1,0:T(8,128)(2,1)}, u32[]{:S(2)}, u32[]{:S(2)}) collective-permute-start(bf16[2,2,144,1152]{3,2,1,0:T(8,128)(2,1)} %pad_maximum_fusion.6.refs_2_.refs_0_), channel_id=1, source_target_pairs={{0,16},{4,20},{8,24},{12,28},{16,0},{20,4},{24,8},{28,12},{1,17},{... | collective-permute-start | bytes 3981320 | tf_op jit(solution)/shard_map/ppermute | solution.py:59
  211.2 37.6 %collective-permute-start.38 = (bf16[2,2,144,1152]{3,2,1,0:T(8,128)(2,1)}, bf16[2,2,144,1152]{3,2,1,0:T(8,128)(2,1)}, u32[]{:S(2)}, u32[]{:S(2)}) collective-permute-start(bf16[2,2,144,1152]{3,2,1,0:T(8,128)(2,1)} %pad_maximum_fusion.7.refs_6_.refs_4_), channel_id=1, source_target_pairs={{0,4},{4,0},{8,12},{12,8},{16,20},{20,16},{24,28},{28,24},{1,5},{5... | collective-permute-start | bytes 3981320 | tf_op jit(solution)/shard_map/ppermute | solution.py:63
  274.7 33.9 %collective-permute-start.43 = (bf16[2,2,144,1152]{3,2,1,0:T(8,128)(2,1)}, bf16[2,2,144,1152]{3,2,1,0:T(8,128)(2,1)S(1)}, u32[]{:S(2)}, u32[]{:S(2)}) collective-permute-start(bf16[2,2,144,1152]{3,2,1,0:T(8,128)(2,1)} %get-tuple-element.214), channel_id=1, source_target_pairs={{0,16},{4,20},{8,24},{12,28},{16,0},{20,4},{24,8},{28,12},{1,17},{... | collective-permute-start | bytes 3981320 | tf_op jit(solution)/shard_map/ppermute | solution.py:59
  275.6 33.1 %collective-permute-start.44 = (bf16[2,2,144,1152]{3,2,1,0:T(8,128)(2,1)}, bf16[2,2,144,1152]{3,2,1,0:T(8,128)(2,1)}, u32[]{:S(2)}, u32[]{:S(2)}) collective-permute-start(bf16[2,2,144,1152]{3,2,1,0:T(8,128)(2,1)} %get-tuple-element.215), channel_id=1, source_target_pairs={{0,8},{4,12},{8,0},{12,4},{16,24},{20,28},{24,16},{28,20},{1,9},{5... | collective-permute-start | bytes 3981320 | tf_op jit(solution)/shard_map/ppermute | solution.py:59
  279.2 29.4 %collective-permute-start.41 = (bf16[256,1152]{1,0:T(8,128)(2,1)}, bf16[256,1152]{1,0:T(8,128)(2,1)}, u32[]{:S(2)}, u32[]{:S(2)}) collective-permute-start(bf16[256,1152]{1,0:T(8,128)(2,1)} %get-tuple-element.357), channel_id=1, source_target_pairs={{0,0},{1,1},{4,2},{5,3},{2,4},{3,5},{6,6},{7,7},{8,8},{9,9},{12,10... | collective-permute-start | bytes 1769480 | tf_op jit(solution)/shard_map/ppermute | solution.py:1033
  336.2 52.0 %collective-permute-start.52 = (bf16[144,1152]{1,0:T(8,128)(2,1)S(1)}, bf16[144,1152]{1,0:T(8,128)(2,1)}, u32[]{:S(2)}, u32[]{:S(2)}) collective-permute-start(bf16[144,1152]{1,0:T(8,128)(2,1)S(1)} %get-tuple-element.366), channel_id=1, source_target_pairs={{0,2},{1,3},{2,0},{3,1},{4,6},{5,7},{6,4},{7,5},{8,10},{9,11},{10,... | collective-permute-start | bytes 995336 | tf_op jit(solution)/shard_map/ppermute | solution.py:67
  356.1 32.1 %collective-permute-start.50 = (bf16[2,2,144,1152]{3,2,1,0:T(8,128)(2,1)}, bf16[2,2,144,1152]{3,2,1,0:T(8,128)(2,1)S(1)}, u32[]{:S(2)}, u32[]{:S(2)}) collective-permute-start(bf16[2,2,144,1152]{3,2,1,0:T(8,128)(2,1)} %get-tuple-element.234), channel_id=1, source_target_pairs={{0,16},{4,20},{8,24},{12,28},{16,0},{20,4},{24,8},{28,12},{1,17},{... | collective-permute-start | bytes 3981320 | tf_op jit(solution)/shard_map/ppermute | solution.py:59
  357.2 31.0 %collective-permute-start.51 = (bf16[2,2,144,1152]{3,2,1,0:T(8,128)(2,1)}, bf16[2,2,144,1152]{3,2,1,0:T(8,128)(2,1)S(1)}, u32[]{:S(2)}, u32[]{:S(2)}) collective-permute-start(bf16[2,2,144,1152]{3,2,1,0:T(8,128)(2,1)} %get-tuple-element.235), channel_id=1, source_target_pairs={{0,8},{4,12},{8,0},{12,4},{16,24},{20,28},{24,16},{28,20},{1,9},{5... | collective-permute-start | bytes 3981320 | tf_op jit(solution)/shard_map/ppermute | solution.py:59
  415.4 29.5 %collective-permute-start.60 = (bf16[4,4,144,1152]{3,2,1,0:T(8,128)(2,1)}, bf16[4,4,144,1152]{3,2,1,0:T(8,128)(2,1)}, u32[]{:S(2)}, u32[]{:S(2)}) collective-permute-start(bf16[4,4,144,1152]{3,2,1,0:T(8,128)(2,1)} %w_attn_send.1), channel_id=1, source_target_pairs={{0,4},{4,0},{8,12},{12,8},{16,20},{20,16},{24,28},{28,24},{1,5},{5... | collective-permute-start | bytes 15925256 | tf_op jit(solution)/shard_map/ppermute | solution.py:63
  467.6 34.7 %collective-permute-start.63 = (bf16[2,2,144,1152]{3,2,1,0:T(8,128)(2,1)}, bf16[2,2,144,1152]{3,2,1,0:T(8,128)(2,1)}, u32[]{:S(2)}, u32[]{:S(2)}) collective-permute-start(bf16[2,2,144,1152]{3,2,1,0:T(8,128)(2,1)} %get-tuple-element.272), channel_id=1, source_target_pairs={{0,16},{4,20},{8,24},{12,28},{16,0},{20,4},{24,8},{28,12},{1,17},{... | collective-permute-start | bytes 3981320 | tf_op jit(solution)/shard_map/ppermute | solution.py:59
  468.6 33.7 %collective-permute-start.64 = (bf16[2,2,144,1152]{3,2,1,0:T(8,128)(2,1)}, bf16[2,2,144,1152]{3,2,1,0:T(8,128)(2,1)}, u32[]{:S(2)}, u32[]{:S(2)}) collective-permute-start(bf16[2,2,144,1152]{3,2,1,0:T(8,128)(2,1)} %get-tuple-element.273), channel_id=1, source_target_pairs={{0,8},{4,12},{8,0},{12,4},{16,24},{20,28},{24,16},{28,20},{1,9},{5... | collective-permute-start | bytes 3981320 | tf_op jit(solution)/shard_map/ppermute | solution.py:59
  520.9 29.2 %collective-permute-start.68 = (bf16[144,1152]{1,0:T(8,128)(2,1)S(1)}, bf16[144,1152]{1,0:T(8,128)(2,1)S(1)}, u32[]{:S(2)}, u32[]{:S(2)}) collective-permute-start(bf16[144,1152]{1,0:T(8,128)(2,1)S(1)} %get-tuple-element.363), channel_id=1, source_target_pairs={{0,2},{1,3},{2,0},{3,1},{4,6},{5,7},{6,4},{7,5},{8,10},{9,11},{10,... | collective-permute-start | bytes 995336 | tf_op jit(solution)/shard_map/ppermute | solution.py:67
  529.1 30.0 %collective-permute-start.69 = (bf16[144,1152]{1,0:T(8,128)(2,1)S(1)}, bf16[144,1152]{1,0:T(8,128)(2,1)S(1)}, u32[]{:S(2)}, u32[]{:S(2)}) collective-permute-start(bf16[144,1152]{1,0:T(8,128)(2,1)S(1)} %get-tuple-element.362), channel_id=1, source_target_pairs={{0,3},{1,2},{2,1},{3,0},{4,7},{5,6},{6,5},{7,4},{8,11},{9,10},{10,... | collective-permute-start | bytes 995336 | tf_op jit(solution)/shard_map/ppermute | solution.py:67
  (105 other events, 1260.7 us)

commit v5 on v4

--- a/solution.py
+++ b/solution.py
@@ -94,10 +94,11 @@
 
 def gather_steps(shard, geo, parted=True, joined=False, extras=None):
     if parted:
-        most = [k for k in range(1, geo.T) if k != geo.Th]
-        got = yield [flip_tensor(shard, k, geo) for k in most]
-        mid = yield [flip_tensor(shard, geo.Th, geo)]
-        parts = [shard] + got[: geo.Th - 1] + mid + got[geo.Th - 1 :]
+        late = [geo.Th] if extras is None else list(range(1, geo.Th + 1))
+        most = [k for k in range(1, geo.T) if k not in late]
+        got = dict(zip(most, (yield [flip_tensor(shard, k, geo) for k in most])))
+        got.update(zip(late, (yield [flip_tensor(shard, k, geo) for k in late])))
+        parts = [shard] + [got[k] for k in range(1, geo.T)]
     else:
         got = yield [flip_tensor(shard, k, geo) for k in range(1, geo.T)]
         parts = [shard] + got
@@ -887,8 +888,6 @@
             got_ref, rest = rest[0], rest[1:]
         n_out = 4 if (mine and geo.direct) else 1
         outs, ats = rest[:n_out], rest[n_out:]
-        if mine and geo.direct:
-            total, ats = ats[-1], ats[:-1]
         j = pl.program_id(0)
         if geo.direct:
 
@@ -900,7 +899,8 @@
                     for p in range(geo.P):
                         even = flip[2 * p * geo.R : (2 * p + 1) * geo.R]
                         odd = flip[(2 * p + 1) * geo.R : (2 * p + 2) * geo.R]
-                        at[p * geo.R : (p + 1) * geo.R, :] = jnp.where(pick_odd, odd, even)
+                        row = pl.multiple_of((s[0] ^ p) * geo.R, geo.R)
+                        at[pl.ds(row, geo.R), :] = jnp.where(pick_odd, odd, even)
         else:
             ats = a_refs
 
@@ -923,13 +923,11 @@
                 outs[0][0, 0] = full.astype(BF)
                 return
             if not mine:
-                for p in range(geo.P):
-                    outs[0][0, s[0] ^ p] = full[p * geo.R : (p + 1) * geo.R].astype(BF)
+                for rel in range(geo.P):
+                    outs[0][0, rel] = full[rel * geo.R : (rel + 1) * geo.R].astype(BF)
                 return
-            total[...] = full
-            for i, here in enumerate(geo.order[half]):
-                row = pl.multiple_of((s[0] ^ here) * geo.R, geo.R)
-                part = total[pl.ds(row, geo.R), :] + got_ref[0, here].astype(F32)
+            for i, rel in enumerate(geo.order[half]):
+                part = full[rel * geo.R : (rel + 1) * geo.R] + got_ref[0, rel].astype(F32)
                 outs[2 * half + i // half_n][i % half_n, 0] = part.astype(BF)
 
         for half in range(2):
@@ -954,8 +952,6 @@
             out_specs = [first, first, second, second]
             shapes = [jax.ShapeDtypeStruct((half_n, th, geo.R, w), BF)] * 4
     scratch = [pltpu.VMEM((pr, n), BF)] * na if geo.direct else []
-    if mine and geo.direct:
-        scratch.append(pltpu.VMEM((pr, w), F32))
     got = pl.pallas_call(
         kernel,
         grid_spec=pltpu.PrefetchScalarGridSpec(
@@ -1067,7 +1063,7 @@
     heads = cols // HEAD_DIM
     attn_shard = jnp.concatenate([in_weight[0], in_weight[1], in_weight[2], out_weight.T], axis=1)
     attn_way = begin(attn_shard, gather_steps, False)
-    cond_all = conditioning[None]
+    cond_all = after(conditioning, attn_shard)[None]
     bit = 1
     while bit < F:
         got = lax.ppermute(cond_all, "fsdp", [(i, i ^ bit) for i in range(F)])
@@ -1126,10 +1122,10 @@
     start(up_way, down_way)
     for half in range(2):
         mixed[half], lse[half] = attn_fwd(tie(q[half]), kv[half], kvo[half], geo)
+    close(lse[0], lse[1])
+    start(up_way, down_way)
     attn, resid, h2 = out_proj(tie(scal), mixed, x, mod, bias_rows[0:1], w_attn, geo)
     close(h2)
-    start(up_way, down_way)
-    close()
     w_up = Gathered(up_way.finish(*now), geo, scal)
     start(down_way)
     cot_parts = to_chip(tie(cotangent))

time: 573 us -> 562 us (0.981)
  waiting for transfers between devices: 136 us -> 128 us
    ppermute x24, waiting for transfers between devices: 42.1 us -> 33.5 us  [flip_pair(): return lax.ppermute(x, 'fsdp', [(i, i ^ 2 * bit) for i in range(geo.F)])]
  transfers between devices with their start and end apart: 73 -> 73, of which waited for: 29 -> 32; matrix products, arithmetic and copies ran while one was open for 10% -> 10% of each run, Pallas kernels for 39% -> 39%
where the time goes in v5:
time: 562 us; the launch traced here: 556 us
  Pallas kernels  226 us (40%)
  waiting for transfers between devices  128 us (23%)
  starting transfers between devices  119 us (21%)
  other arithmetic  48.5 us (9%)
  local copies, waits for them, and re-layouts  28.6 us (5%)
    ppermute x18, waiting for transfers between devices, flip_tensor(): return lax.ppermute(x, 'tensor', [(i, i ^ k) for i in range(geo.T)])  61.3 us
    pallas_call x6, Pallas kernels, weight_grad(): pl.pallas_call(kernel, grid_spec=pltpu.PrefetchScalarGridSpec(num_scalar_...  59.4 us
    ppermute x24, waiting for transfers between devices, flip_pair(): return lax.ppermute(x, 'fsdp', [(i, i ^ 2 * bit) for i in range(geo.F)])  33.5 us
    ppermute x17, starting transfers between devices, flip_core(): return lax.ppermute(x, 'fsdp', [(i, i ^ 1) for i in range(geo.F)])  31.1 us
    ppermute x18, starting transfers between devices, flip_tensor(): return lax.ppermute(x, 'tensor', [(i, i ^ k) for i in range(geo.T)])  31 us
    pallas_call x2, Pallas kernels, attn_bwd(): pl.pallas_call(kernel, grid=(z,), in_specs=[spec(wp), spec(geo.kvw), spec...  29.3 us
    ppermute x24, starting transfers between devices, flip_pair(): return lax.ppermute(x, 'fsdp', [(i, i ^ 2 * bit) for i in range(geo.F)])  27.6 us
    pallas_call x2, Pallas kernels, attn_fwd(): pl.pallas_call(kernel, grid=(z,), in_specs=[spec(wp), spec(geo.kvw), spec...  20.1 us
  transfers between devices with their start and end apart: 73, of which 32 were waited for; matrix products, arithmetic and copies ran while one was open for 10% of the time, Pallas kernels for 39%

profile of v5, /device:TPU:10, one launch (start us, length us, event | category | flops | bytes accessed | tf_op | source)
XLA Modules:
  0.0 555.9 jit_solution(2681804620914063632)
XLA Ops:
  20.6 13.8 %collective-permute-done.1 = bf16[144,1152]{1,0:T(8,128)(2,1)S(1)} collective-permute-done((bf16[144,1152]{1,0:T(8,128)(2,1)S(1)}, bf16[144,1152]{1,0:T(8,128)(2,1)S(1)}, u32[]{:S(2)}, u32[]{:S(2)}) %collective-permute-start.1) | collective-permute-done | bytes 331808 | tf_op jit(solution)/shard_map/ppermute | solution.py:67
  34.4 8.2 %collective-permute-done.2 = bf16[144,1152]{1,0:T(8,128)(2,1)S(1)} collective-permute-done((bf16[144,1152]{1,0:T(8,128)(2,1)S(1)}, bf16[144,1152]{1,0:T(8,128)(2,1)S(1)}, u32[]{:S(2)}, u32[]{:S(2)}) %collective-permute-start.2) | collective-permute-done | bytes 331808 | tf_op jit(solution)/shard_map/ppermute | solution.py:67
  48.4 7.9 %collective-permute-done.5 = bf16[144,1152]{1,0:T(8,128)(2,1)} collective-permute-done((bf16[144,1152]{1,0:T(8,128)(2,1)}, bf16[144,1152]{1,0:T(8,128)(2,1)}, u32[]{:S(2)}, u32[]{:S(2)}) %collective-permute-start.5) | collective-permute-done | bytes 331808 | tf_op jit(solution)/shard_map/ppermute | solution.py:67
  70.7 11.1 %collective-permute-start.10 = (bf16[2,2,144,1152]{3,2,1,0:T(8,128)(2,1)S(1)}, bf16[2,2,144,1152]{3,2,1,0:T(8,128)(2,1)}, u32[]{:S(2)}, u32[]{:S(2)}) collective-permute-start(bf16[2,2,144,1152]{3,2,1,0:T(8,128)(2,1)S(1)} %pad_maximum_fusion.2.refs_0_.refs_1_.refs_2_), channel_id=1, source_target_pairs={{0,4},{4,0},{8,12},{12,8},{16,20},{20,16},{24,28},{28,24},{1,5},{5... | collective-permute-start | bytes 3981320 | tf_op jit(solution)/shard_map/ppermute | solution.py:63
  128.3 7.8 %in_proj.2 = (bf16[2,512,384]{2,1,0:T(8,128)(2,1)}, bf16[2,512,640]{2,1,0:T(8,128)(2,1)}) custom-call(s32[3]{0:T(128)} %pad_add_fusion.1.s, bf16[512,1152]{1,0:T(8,128)(2,1)} %norm_mod.1.h_ref.refs_0_, f32[4,1,896]{2,1,0:T(1,128)} %maximum_maximum_fusion.1.b_ref, bf16[2,2,144,1152]{3,2,1,0:T(8,128)(2,1)} %copy-done.2, ...), custom_call_target="tpu_custom_call" | custom-call | flops 2113929216 | bytes 10027008 | tf_op jit(solution)/shard_map/in_proj/pallas_call | solution.py:340
  149.4 9.8 %attn_fwd.3 = (bf16[2,512,384]{2,1,0:T(8,128)(2,1)}, f32[2,4,512]{2,1,0:T(4,128)}) custom-call(bf16[2,512,384]{2,1,0:T(8,128)(2,1)} %get-tuple-element.243.q_ref, bf16[2,512,640]{2,1,0:T(8,128)(2,1)} %get-tuple-element.176.kv_ref, bf16[2,512,640]{2,1,0:T(8,128)(2,1)} %copy-done.57), custom_call_target="tpu_custom_call" | custom-call | flops 6000000000 | bytes 3932160 | tf_op jit(solution)/shard_map/attn_fwd/pallas_call | solution.py:400
  159.2 10.3 %attn_fwd.2 = (bf16[2,512,384]{2,1,0:T(8,128)(2,1)}, f32[2,4,512]{2,1,0:T(4,128)}) custom-call(bf16[2,512,384]{2,1,0:T(8,128)(2,1)} %get-tuple-element.240.q_ref, bf16[2,512,640]{2,1,0:T(8,128)(2,1)} %get-tuple-element.174.kv_ref, bf16[2,512,640]{2,1,0:T(8,128)(2,1)} %copy-done.56), custom_call_target="tpu_custom_call" | custom-call | flops 6000000000 | bytes 3932160 | tf_op jit(solution)/shard_map/attn_fwd/pallas_call | solution.py:400
  183.0 11.2 %out_proj.1 = (bf16[544,1152]{1,0:T(8,128)(2,1)}, f32[512,1152]{1,0:T(8,128)}, bf16[544,1152]{1,0:T(8,128)(2,1)}) custom-call(s32[3]{0:T(128)} %pad_add_fusion.1.s, bf16[2,512,384]{2,1,0:T(8,128)(2,1)} %get-tuple-element.189.ya_ref.o_ref.refs_6_, bf16[2,512,384]{2,1,0:T(8,128)(2,1)} %get-tuple-element.190.yb_ref.o_ref.refs_7_, f32[6,1152]{1,0:T(8,128)} %reshape.191.m_ref, ...), custom_call_target="tpu_custom_call" | custom-call | flops 1358954496 | bytes 18874368 | tf_op jit(solution)/shard_map/out_proj/pallas_call | solution.py:524
  213.0 18.1 %up_proj.1 = (bf16[4,512,1152]{2,1,0:T(8,128)(2,1)}, bf16[4,512,1152]{2,1,0:T(8,128)(2,1)}) custom-call(s32[3]{0:T(128)} %pad_add_fusion.1.s, bf16[544,1152]{1,0:T(8,128)(2,1)} %get-tuple-element.191.h_ref.refs_0_, f32[4,1,1152]{2,1,0:T(1,128)} %maximum_convert_fusion.b_ref, bf16[4,2,144,1152]{3,2,1,0:T(8,128)(2,1)} %copy-done.5, ...), custom_call_target="tpu_custom_call" | custom-call | flops 5435817984 | bytes 20054016 | tf_op jit(solution)/shard_map/up_proj/pallas_call | solution.py:575
  239.4 8.4 %w_down_send.1 = bf16[4,4,144,1152]{3,2,1,0:T(8,128)(2,1)} custom-call(s32[3]{0:T(128)} %pad_add_fusion.1.s, bf16[512,1152]{1,0:T(8,128)(2,1)} %get-tuple-element.351.refs_0_.g_ref, bf16[4,512,1152]{2,1,0:T(8,128)(2,1)} %get-tuple-element.198.refs_1_.y_ref), custom_call_target="tpu_custom_call" | custom-call | flops 2717908992 | bytes 15335424 | tf_op jit(solution)/shard_map/w_down_send/pallas_call | solution.py:955
  248.3 14.2 %down_proj.1 = (bf16[512,1152]{1,0:T(8,128)(2,1)}, f32[8,1152]{1,0:T(8,128)}) custom-call(s32[3]{0:T(128)} %pad_add_fusion.1.s, bf16[4,512,1152]{2,1,0:T(8,128)(2,1)} %get-tuple-element.198.refs_1_.y_ref, f32[6,1152]{1,0:T(8,128)} %reshape.191.m_ref, f32[1,1152]{1,0:T(1,128)} %get-tuple-element.387.b_ref, f32[512,1152]{1,0:T(8,128)} %get-tuple-element.203.refs_0_, ...), custom_call_target="tpu_custom_call" | custom-call | flops 5435817984 | bytes 20054016 | tf_op jit(solution)/shard_map/down_proj/pallas_call | solution.py:630
  262.6 10.0 %w_down.1 = (bf16[2,2,144,1152]{3,2,1,0:T(8,128)(2,1)}, bf16[2,2,144,1152]{3,2,1,0:T(8,128)(2,1)}, bf16[2,2,144,1152]{3,2,1,0:T(8,128)(2,1)}, bf16[2,2,144,1152]{3,2,1,0:T(8,128)(2,1)}) custom-call(s32[3]{0:T(128)} %pad_add_fusion.1.s, bf16[512,1152]{1,0:T(8,128)(2,1)} %get-tuple-element.351.refs_0_.g_ref, ...), custom_call_target="tpu_custom_call" | custom-call | flops 2717908992 | bytes 15335424 | tf_op jit(solution)/shard_map/w_down/pallas_call | solution.py:955
  282.4 14.3 %pre_back.1 = (bf16[4,512,1152]{2,1,0:T(8,128)(2,1)}, f32[4,1,1152]{2,1,0:T(1,128)}) custom-call(s32[3]{0:T(128)} %pad_add_fusion.1.s, bf16[512,1152]{1,0:T(8,128)(2,1)} %get-tuple-element.351.refs_0_.g_ref, bf16[4,512,1152]{2,1,0:T(8,128)(2,1)} %get-tuple-element.221.gp_ref, bf16[2,2,144,1152]{3,2,1,0:T(8,128)(2,1)} %pad_maximum_fusion.6.refs_2_.refs_0_, ...), custom_call_target="tpu_custom_call" | custom-call | flops 5435817984 | bytes 20054016 | tf_op jit(solution)/shard_map/pre_back/pallas_call | solution.py:669
  296.8 8.4 %w_up_send.1 = bf16[4,4,144,1152]{3,2,1,0:T(8,128)(2,1)} custom-call(s32[3]{0:T(128)} %pad_add_fusion.1.s, bf16[544,1152]{1,0:T(8,128)(2,1)} %get-tuple-element.191.h_ref.refs_0_, bf16[4,512,1152]{2,1,0:T(8,128)(2,1)} %get-tuple-element.222.refs_1_.y_ref), custom_call_target="tpu_custom_call" | custom-call | flops 2717908992 | bytes 15335424 | tf_op jit(solution)/shard_map/w_up_send/pallas_call | solution.py:955
  311.7 16.9 %second_back.1 = (f32[512,1152]{1,0:T(8,128)}, bf16[512,1152]{1,0:T(8,128)(2,1)}, f32[4,8,1152]{2,1,0:T(8,128)}) custom-call(s32[3]{0:T(128)} %pad_add_fusion.1.s, bf16[4,512,1152]{2,1,0:T(8,128)(2,1)} %get-tuple-element.222.refs_1_.y_ref, f32[6,1152]{1,0:T(8,128)} %reshape.191.m_ref, f32[512,1152]{1,0:T(8,128)} %get-tuple-element.203.refs_0_, ...), custom_call_target="tpu_custom_call" | custom-call | flops 5435817984 | bytes 25952256 | tf_op jit(solution)/shard_map/second_back/pallas_call | solution.py:730
  334.6 8.0 %mixed_back.1.do_ref = bf16[4,512,384]{2,1,0:T(8,128)(2,1)} custom-call(s32[3]{0:T(128)} %pad_add_fusion.1.s, bf16[512,1152]{1,0:T(8,128)(2,1)} %get-tuple-element.229.g_ref.refs_1_, bf16[2,2,144,1152]{3,2,1,0:T(8,128)(2,1)} %copy-done.2, bf16[2,2,144,1152]{3,2,1,0:T(8,128)(2,1)} %collective-permute-done.11.refs_1_.refs_2_.refs_3_, ...), custom_call_target="tpu_custom_call" | custom-call | flops 1358954496 | bytes 12976128 | tf_op jit(solution)/shard_map/mixed_back/pallas_call | solution.py:765
  342.6 10.0 %w_up.1 = (bf16[2,2,144,1152]{3,2,1,0:T(8,128)(2,1)}, bf16[2,2,144,1152]{3,2,1,0:T(8,128)(2,1)}, bf16[2,2,144,1152]{3,2,1,0:T(8,128)(2,1)}, bf16[2,2,144,1152]{3,2,1,0:T(8,128)(2,1)}) custom-call(s32[3]{0:T(128)} %pad_add_fusion.1.s, bf16[544,1152]{1,0:T(8,128)(2,1)} %get-tuple-element.191.h_ref.refs_0_, ...), custom_call_target="tpu_custom_call" | custom-call | flops 2717908992 | bytes 15335424 | tf_op jit(solution)/shard_map/w_up/pallas_call | solution.py:955
  354.3 14.7 %attn_bwd.3 = (bf16[2,512,896]{2,1,0:T(8,128)(2,1)}, bf16[2,512,640]{2,1,0:T(8,128)(2,1)}, f32[2,1,896]{2,1,0:T(1,128)}, f32[2,1,640]{2,1,0:T(1,128)}) custom-call(bf16[2,512,384]{2,1,0:T(8,128)(2,1)} %get-tuple-element.243.q_ref, bf16[2,512,640]{2,1,0:T(8,128)(2,1)} %get-tuple-element.176.kv_ref, bf16[2,512,640]{2,1,0:T(8,128)(2,1)} %copy-done.57, ...), custom_call_target="tpu_custom_call" | custom-call | flops 10000000000 | bytes 6291456 | tf_op jit(solution)/shard_map/attn_bwd/pallas_call | solution.py:454
  369.0 14.7 %attn_bwd.2 = (bf16[2,512,896]{2,1,0:T(8,128)(2,1)}, bf16[2,512,640]{2,1,0:T(8,128)(2,1)}, f32[2,1,896]{2,1,0:T(1,128)}, f32[2,1,640]{2,1,0:T(1,128)}) custom-call(bf16[2,512,384]{2,1,0:T(8,128)(2,1)} %get-tuple-element.240.q_ref, bf16[2,512,640]{2,1,0:T(8,128)(2,1)} %get-tuple-element.174.kv_ref, bf16[2,512,640]{2,1,0:T(8,128)(2,1)} %copy-done.56, ...), custom_call_target="tpu_custom_call" | custom-call | flops 10000000000 | bytes 6291456 | tf_op jit(solution)/shard_map/attn_bwd/pallas_call | solution.py:454
  395.7 11.0 %w_attn_send.1 = bf16[4,4,144,1152]{3,2,1,0:T(8,128)(2,1)} custom-call(s32[3]{0:T(128)} %pad_add_fusion.1.s, bf16[512,1152]{1,0:T(8,128)(2,1)} %norm_mod.1.h_ref.refs_0_, bf16[512,1152]{1,0:T(8,128)(2,1)} %get-tuple-element.229.g_ref.refs_1_, bf16[2,512,896]{2,1,0:T(8,128)(2,1)} %get-tuple-element.252.refs_2_.ta, ...), custom_call_target="tpu_custom_call" | custom-call | flops 2717908992 | bytes 15335424 | tf_op jit(solution)/shard_map/w_attn_send/pallas_call | solution.py:955
  422.4 15.2 %first_back.1 = (bf16[512,1152]{1,0:T(8,128)(2,1)}, f32[2,8,1152]{2,1,0:T(8,128)}) custom-call(s32[3]{0:T(128)} %pad_add_fusion.1.s, bf16[2,512,896]{2,1,0:T(8,128)(2,1)} %get-tuple-element.252.refs_2_.ta, bf16[2,512,896]{2,1,0:T(8,128)(2,1)} %get-tuple-element.253.refs_3_.tb, bf16[2,512,640]{2,1,0:T(8,128)(2,1)} %collective-permute-done.53.refs_4_.ga, ...), custom_call_target="tpu_custom_call" | custom-call | flops 4076863488 | bytes 20054016 | tf_op jit(solution)/shard_map/first_back/pallas_call | solution.py:826
  448.0 11.6 %w_attn.1 = (bf16[2,2,144,1152]{3,2,1,0:T(8,128)(2,1)}, bf16[2,2,144,1152]{3,2,1,0:T(8,128)(2,1)}, bf16[2,2,144,1152]{3,2,1,0:T(8,128)(2,1)}, bf16[2,2,144,1152]{3,2,1,0:T(8,128)(2,1)}) custom-call(s32[3]{0:T(128)} %pad_add_fusion.1.s, bf16[512,1152]{1,0:T(8,128)(2,1)} %norm_mod.1.h_ref.refs_0_, bf16[512,1152]{1,0:T(8,128)(2,1)} %get-tuple-element.229.g_ref.refs_1_, ...), custom_call_target="tpu_custom_call" | custom-call | flops 2717908992 | bytes 15335424 | tf_op jit(solution)/shard_map/w_attn/pallas_call | solution.py:955
  479.8 16.4 %all-to-all-done.2 = f32[32,8,128]{2,1,0:T(8,128)S(1)} async-done(((f32[32,8,128]{2,1,0:T(8,128)}), f32[32,8,128]{2,1,0:T(8,128)S(1)}, u32[]{:S(2)}, u32[]{:S(2)}) %all-to-all-start.2) | async-done | bytes 131104 | tf_op jit(solution)/shard_map/all_to_all | solution.py:1243
  530.6 15.2 %collective-permute-done.68 = bf16[144,1152]{1,0:T(8,128)(2,1)S(1)} collective-permute-done((bf16[144,1152]{1,0:T(8,128)(2,1)S(1)}, bf16[144,1152]{1,0:T(8,128)(2,1)S(1)}, u32[]{:S(2)}, u32[]{:S(2)}) %collective-permute-start.68) | collective-permute-done | bytes 331808 | tf_op jit(solution)/shard_map/ppermute | solution.py:67
  (411 shorter events, 266.6 us)
Async XLA Ops:
  4.8 29.6 %collective-permute-start.1 = (bf16[144,1152]{1,0:T(8,128)(2,1)S(1)}, bf16[144,1152]{1,0:T(8,128)(2,1)S(1)}, u32[]{:S(2)}, u32[]{:S(2)}) collective-permute-start(bf16[144,1152]{1,0:T(8,128)(2,1)S(1)} %concatenate.86), channel_id=1, source_target_pairs={{0,2},{1,3},{2,0},{3,1},{4,6},{5,7},{6,4},{7,5},{8,10},{9,11},{10,... | collective-permute-start | bytes 995336 | tf_op jit(solution)/shard_map/ppermute | solution.py:67
  7.9 34.7 %collective-permute-start.2 = (bf16[144,1152]{1,0:T(8,128)(2,1)S(1)}, bf16[144,1152]{1,0:T(8,128)(2,1)S(1)}, u32[]{:S(2)}, u32[]{:S(2)}) collective-permute-start(bf16[144,1152]{1,0:T(8,128)(2,1)S(1)} %concatenate.86), channel_id=1, source_target_pairs={{0,3},{1,2},{2,1},{3,0},{4,7},{5,6},{6,5},{7,4},{8,11},{9,10},{10,... | collective-permute-start | bytes 995336 | tf_op jit(solution)/shard_map/ppermute | solution.py:67
  13.6 34.0 %all-to-all-start = ((f32[32,8,288]{2,1,0:T(8,128)}), f32[32,8,288]{2,1,0:T(8,128)S(1)}, u32[]{:S(2)}, u32[]{:S(2)}) async-start(f32[32,8,288]{2,1,0:T(8,128)} %bitcast.17), calls=%async_computation | async-start | bytes 786432 | tf_op jit(solution)/shard_map/all_to_all | solution.py:1084
  60.4 28.0 %collective-permute-start.12 = (bf16[2,2,144,1152]{3,2,1,0:T(8,128)(2,1)S(1)}, bf16[2,2,144,1152]{3,2,1,0:T(8,128)(2,1)}, u32[]{:S(2)}, u32[]{:S(2)}) collective-permute-start(bf16[2,2,144,1152]{3,2,1,0:T(8,128)(2,1)S(1)} %pad_maximum_fusion.3.refs_0_.refs_5_.refs_4_.refs_6_), channel_id=1, source_target_pairs={{0,8},{4,12},{8,0},{12,4},{16,24},{20,28},{24,16},{28,20},{1,9},{5... | collective-permute-start | bytes 3981320 | tf_op jit(solution)/shard_map/ppermute | solution.py:59
  63.2 27.3 %collective-permute-start.11 = (bf16[2,2,144,1152]{3,2,1,0:T(8,128)(2,1)S(1)}, bf16[2,2,144,1152]{3,2,1,0:T(8,128)(2,1)}, u32[]{:S(2)}, u32[]{:S(2)}) collective-permute-start(bf16[2,2,144,1152]{3,2,1,0:T(8,128)(2,1)S(1)} %pad_maximum_fusion.2.refs_0_.refs_1_.refs_2_), channel_id=1, source_target_pairs={{0,16},{4,20},{8,24},{12,28},{16,0},{20,4},{24,8},{28,12},{1,17},{... | collective-permute-start | bytes 3981320 | tf_op jit(solution)/shard_map/ppermute | solution.py:59
  68.5 46.9 %collective-permute-start.16 = (bf16[2,2,144,1152]{3,2,1,0:T(8,128)(2,1)S(1)}, bf16[2,2,144,1152]{3,2,1,0:T(8,128)(2,1)}, u32[]{:S(2)}, u32[]{:S(2)}) collective-permute-start(bf16[2,2,144,1152]{3,2,1,0:T(8,128)(2,1)S(1)} %pad_maximum_fusion.3.refs_0_.refs_5_.refs_4_.refs_6_), channel_id=1, source_target_pairs={{0,4},{4,0},{8,12},{12,8},{16,20},{20,16},{24,28},{28,24},{1,5},{5... | collective-permute-start | bytes 3981320 | tf_op jit(solution)/shard_map/ppermute | solution.py:63
  70.7 44.6 %collective-permute-start.10 = (bf16[2,2,144,1152]{3,2,1,0:T(8,128)(2,1)S(1)}, bf16[2,2,144,1152]{3,2,1,0:T(8,128)(2,1)}, u32[]{:S(2)}, u32[]{:S(2)}) collective-permute-start(bf16[2,2,144,1152]{3,2,1,0:T(8,128)(2,1)S(1)} %pad_maximum_fusion.2.refs_0_.refs_1_.refs_2_), channel_id=1, source_target_pairs={{0,4},{4,0},{8,12},{12,8},{16,20},{20,16},{24,28},{28,24},{1,5},{5... | collective-permute-start | bytes 3981320 | tf_op jit(solution)/shard_map/ppermute | solution.py:63
  143.3 31.2 %collective-permute-start.27 = (bf16[2,2,144,1152]{3,2,1,0:T(8,128)(2,1)S(1)}, bf16[2,2,144,1152]{3,2,1,0:T(8,128)(2,1)S(1)}, u32[]{:S(2)}, u32[]{:S(2)}) collective-permute-start(bf16[2,2,144,1152]{3,2,1,0:T(8,128)(2,1)S(1)} %pad_maximum_fusion.5), channel_id=1, source_target_pairs={{0,8},{4,12},{8,0},{12,4},{16,24},{20,28},{24,16},{28,20},{1,9},{5... | collective-permute-start | bytes 3981320 | tf_op jit(solution)/shard_map/ppermute | solution.py:59
  144.1 31.0 %collective-permute-start.26 = (bf16[2,2,144,1152]{3,2,1,0:T(8,128)(2,1)S(1)}, bf16[2,2,144,1152]{3,2,1,0:T(8,128)(2,1)S(1)}, u32[]{:S(2)}, u32[]{:S(2)}) collective-permute-start(bf16[2,2,144,1152]{3,2,1,0:T(8,128)(2,1)S(1)} %pad_maximum_fusion.4), channel_id=1, source_target_pairs={{0,16},{4,20},{8,24},{12,28},{16,0},{20,4},{24,8},{28,12},{1,17},{... | collective-permute-start | bytes 3981320 | tf_op jit(solution)/shard_map/ppermute | solution.py:59
  201.0 30.4 %collective-permute-start.34 = (bf16[2,2,144,1152]{3,2,1,0:T(8,128)(2,1)}, bf16[2,2,144,1152]{3,2,1,0:T(8,128)(2,1)}, u32[]{:S(2)}, u32[]{:S(2)}) collective-permute-start(bf16[2,2,144,1152]{3,2,1,0:T(8,128)(2,1)} %pad_maximum_fusion.7.refs_6_.refs_4_), channel_id=1, source_target_pairs={{0,8},{4,12},{8,0},{12,4},{16,24},{20,28},{24,16},{28,20},{1,9},{5... | collective-permute-start | bytes 3981320 | tf_op jit(solution)/shard_map/ppermute | solution.py:59
  204.5 30.2 %collective-permute-start.33 = (bf16[2,2,144,1152]{3,2,1,0:T(8,128)(2,1)}, bf16[2,2,144,1152]{3,2,1,0:T(8,128)(2,1)}, u32[]{:S(2)}, u32[]{:S(2)}) collective-permute-start(bf16[2,2,144,1152]{3,2,1,0:T(8,128)(2,1)} %pad_maximum_fusion.6.refs_2_.refs_0_), channel_id=1, source_target_pairs={{0,16},{4,20},{8,24},{12,28},{16,0},{20,4},{24,8},{28,12},{1,17},{... | collective-permute-start | bytes 3981320 | tf_op jit(solution)/shard_map/ppermute | solution.py:59
  209.6 38.2 %collective-permute-start.38 = (bf16[2,2,144,1152]{3,2,1,0:T(8,128)(2,1)}, bf16[2,2,144,1152]{3,2,1,0:T(8,128)(2,1)}, u32[]{:S(2)}, u32[]{:S(2)}) collective-permute-start(bf16[2,2,144,1152]{3,2,1,0:T(8,128)(2,1)} %pad_maximum_fusion.7.refs_6_.refs_4_), channel_id=1, source_target_pairs={{0,4},{4,0},{8,12},{12,8},{16,20},{20,16},{24,28},{28,24},{1,5},{5... | collective-permute-start | bytes 3981320 | tf_op jit(solution)/shard_map/ppermute | solution.py:63
  272.5 32.6 %collective-permute-start.43 = (bf16[2,2,144,1152]{3,2,1,0:T(8,128)(2,1)}, bf16[2,2,144,1152]{3,2,1,0:T(8,128)(2,1)S(1)}, u32[]{:S(2)}, u32[]{:S(2)}) collective-permute-start(bf16[2,2,144,1152]{3,2,1,0:T(8,128)(2,1)} %get-tuple-element.218), channel_id=1, source_target_pairs={{0,16},{4,20},{8,24},{12,28},{16,0},{20,4},{24,8},{28,12},{1,17},{... | collective-permute-start | bytes 3981320 | tf_op jit(solution)/shard_map/ppermute | solution.py:59
  273.3 31.9 %collective-permute-start.44 = (bf16[2,2,144,1152]{3,2,1,0:T(8,128)(2,1)}, bf16[2,2,144,1152]{3,2,1,0:T(8,128)(2,1)}, u32[]{:S(2)}, u32[]{:S(2)}) collective-permute-start(bf16[2,2,144,1152]{3,2,1,0:T(8,128)(2,1)} %get-tuple-element.219), channel_id=1, source_target_pairs={{0,8},{4,12},{8,0},{12,4},{16,24},{20,28},{24,16},{28,20},{1,9},{5... | collective-permute-start | bytes 3981320 | tf_op jit(solution)/shard_map/ppermute | solution.py:59
  276.5 28.7 %collective-permute-start.41 = (bf16[256,1152]{1,0:T(8,128)(2,1)}, bf16[256,1152]{1,0:T(8,128)(2,1)}, u32[]{:S(2)}, u32[]{:S(2)}) collective-permute-start(bf16[256,1152]{1,0:T(8,128)(2,1)} %get-tuple-element.359), channel_id=1, source_target_pairs={{0,0},{1,1},{4,2},{5,3},{2,4},{3,5},{6,6},{7,7},{8,8},{9,9},{12,10... | collective-permute-start | bytes 1769480 | tf_op jit(solution)/shard_map/ppermute | solution.py:1029
  333.9 49.8 %collective-permute-start.52 = (bf16[144,1152]{1,0:T(8,128)(2,1)S(1)}, bf16[144,1152]{1,0:T(8,128)(2,1)}, u32[]{:S(2)}, u32[]{:S(2)}) collective-permute-start(bf16[144,1152]{1,0:T(8,128)(2,1)S(1)} %get-tuple-element.368), channel_id=1, source_target_pairs={{0,2},{1,3},{2,0},{3,1},{4,6},{5,7},{6,4},{7,5},{8,10},{9,11},{10,... | collective-permute-start | bytes 995336 | tf_op jit(solution)/shard_map/ppermute | solution.py:67
  352.7 31.0 %collective-permute-start.50 = (bf16[2,2,144,1152]{3,2,1,0:T(8,128)(2,1)}, bf16[2,2,144,1152]{3,2,1,0:T(8,128)(2,1)S(1)}, u32[]{:S(2)}, u32[]{:S(2)}) collective-permute-start(bf16[2,2,144,1152]{3,2,1,0:T(8,128)(2,1)} %get-tuple-element.238), channel_id=1, source_target_pairs={{0,16},{4,20},{8,24},{12,28},{16,0},{20,4},{24,8},{28,12},{1,17},{... | collective-permute-start | bytes 3981320 | tf_op jit(solution)/shard_map/ppermute | solution.py:59
  353.5 30.2 %collective-permute-start.51 = (bf16[2,2,144,1152]{3,2,1,0:T(8,128)(2,1)}, bf16[2,2,144,1152]{3,2,1,0:T(8,128)(2,1)S(1)}, u32[]{:S(2)}, u32[]{:S(2)}) collective-permute-start(bf16[2,2,144,1152]{3,2,1,0:T(8,128)(2,1)} %get-tuple-element.239), channel_id=1, source_target_pairs={{0,8},{4,12},{8,0},{12,4},{16,24},{20,28},{24,16},{28,20},{1,9},{5... | collective-permute-start | bytes 3981320 | tf_op jit(solution)/shard_map/ppermute | solution.py:59
  411.4 28.9 %collective-permute-start.60 = (bf16[4,4,144,1152]{3,2,1,0:T(8,128)(2,1)}, bf16[4,4,144,1152]{3,2,1,0:T(8,128)(2,1)}, u32[]{:S(2)}, u32[]{:S(2)}) collective-permute-start(bf16[4,4,144,1152]{3,2,1,0:T(8,128)(2,1)} %w_attn_send.1), channel_id=1, source_target_pairs={{0,4},{4,0},{8,12},{12,8},{16,20},{20,16},{24,28},{28,24},{1,5},{5... | collective-permute-start | bytes 15925256 | tf_op jit(solution)/shard_map/ppermute | solution.py:63
  462.9 34.2 %collective-permute-start.63 = (bf16[2,2,144,1152]{3,2,1,0:T(8,128)(2,1)}, bf16[2,2,144,1152]{3,2,1,0:T(8,128)(2,1)}, u32[]{:S(2)}, u32[]{:S(2)}) collective-permute-start(bf16[2,2,144,1152]{3,2,1,0:T(8,128)(2,1)} %get-tuple-element.274), channel_id=1, source_target_pairs={{0,16},{4,20},{8,24},{12,28},{16,0},{20,4},{24,8},{28,12},{1,17},{... | collective-permute-start | bytes 3981320 | tf_op jit(solution)/shard_map/ppermute | solution.py:59
  463.8 33.3 %collective-permute-start.64 = (bf16[2,2,144,1152]{3,2,1,0:T(8,128)(2,1)}, bf16[2,2,144,1152]{3,2,1,0:T(8,128)(2,1)}, u32[]{:S(2)}, u32[]{:S(2)}) collective-permute-start(bf16[2,2,144,1152]{3,2,1,0:T(8,128)(2,1)} %get-tuple-element.275), channel_id=1, source_target_pairs={{0,8},{4,12},{8,0},{12,4},{16,24},{20,28},{24,16},{28,20},{1,9},{5... | collective-permute-start | bytes 3981320 | tf_op jit(solution)/shard_map/ppermute | solution.py:59
  468.9 27.3 %all-to-all-start.2 = ((f32[32,8,128]{2,1,0:T(8,128)}), f32[32,8,128]{2,1,0:T(8,128)S(1)}, u32[]{:S(2)}, u32[]{:S(2)}) async-start(f32[32,8,128]{2,1,0:T(8,128)} %bitcast.74), calls=%async_computation.2 | async-start | bytes 262144 | tf_op jit(solution)/shard_map/all_to_all | solution.py:1243
  515.8 30.0 %collective-permute-start.68 = (bf16[144,1152]{1,0:T(8,128)(2,1)S(1)}, bf16[144,1152]{1,0:T(8,128)(2,1)S(1)}, u32[]{:S(2)}, u32[]{:S(2)}) collective-permute-start(bf16[144,1152]{1,0:T(8,128)(2,1)S(1)} %get-tuple-element.365), channel_id=1, source_target_pairs={{0,2},{1,3},{2,0},{3,1},{4,6},{5,7},{6,4},{7,5},{8,10},{9,11},{10,... | collective-permute-start | bytes 995336 | tf_op jit(solution)/shard_map/ppermute | solution.py:67
  523.3 30.0 %collective-permute-start.69 = (bf16[144,1152]{1,0:T(8,128)(2,1)S(1)}, bf16[144,1152]{1,0:T(8,128)(2,1)S(1)}, u32[]{:S(2)}, u32[]{:S(2)}) collective-permute-start(bf16[144,1152]{1,0:T(8,128)(2,1)S(1)} %get-tuple-element.364), channel_id=1, source_target_pairs={{0,3},{1,2},{2,1},{3,0},{4,7},{5,6},{6,5},{7,4},{8,11},{9,10},{10,... | collective-permute-start | bytes 995336 | tf_op jit(solution)/shard_map/ppermute | solution.py:67
  (107 other events, 1251.9 us)

commit v6 on v5

--- a/solution.py
+++ b/solution.py
@@ -250,8 +250,9 @@
     return -(-w // 128) * 128
 
 
-def chunked(total, want):
-    return want if total % want == 0 else total
+def pieces(total):
+    step = 512 if total % 128 == 0 else total
+    return [slice(at, min(at + step, total)) for at in range(0, total, step)]
 
 
 def norm_of(v):
@@ -555,14 +556,12 @@
     n, d = h.shape[0] - ROWS, h.shape[1]
     w = wt.width
     nw = len(wt.arrays)
-    step = chunked(w, 384)
 
     def kernel(s, h_ref, b_ref, *refs):
         w_refs, (hid_ref, gp_ref, wbuf, sem) = refs[:nw], refs[nw:]
         j = pl.program_id(0)
         now = wt.stream(j, s, w_refs, wbuf, sem)
-        for at in range(0, w, step):
-            cols = slice(at, at + step)
+        for cols in pieces(w):
             u = dotg(h_ref[...], now[:, cols], 1, 0) + b_ref[0, :, cols]
             sq = u * u
             t = jnp.tanh(TANH_C * (u + CUBIC * sq * u))
@@ -653,14 +652,12 @@
     n, d = g.shape
     w = wt.width
     nw = len(wt.arrays)
-    step = chunked(w, 384)
 
     def kernel(s, g_ref, gp_ref, *refs):
         w_refs, (out_ref, sum_ref, wbuf, sem) = refs[:nw], refs[nw:]
         j = pl.program_id(0)
         now = wt.stream(j, s, w_refs, wbuf, sem)
-        for at in range(0, w, step):
-            cols = slice(at, at + step)
+        for cols in pieces(w):
             y = dotg(g_ref[...], now[:, cols], 1, 0) * gp_ref[0, :, cols].astype(F32)
             out_ref[0, :, cols] = y.astype(BF)
             sum_ref[0, :, cols] = jnp.sum(y, axis=0, keepdims=True)
@@ -1136,7 +1133,6 @@
     start(down_way)
     cot = jnp.concatenate(cot_parts)
     ffn_grad = (cot.astype(F32) * mod[5]).astype(BF)
-    ffn_sum = jnp.sum(ffn_grad.astype(F32), axis=0)
 
     def block(ref):
         return ref[0]
@@ -1180,6 +1176,7 @@
         )
     close(*tri_sums)
     tri_got = [across(tri_send[0]), across(tri_send[1])]
+    ffn_sum = jnp.sum(tie(ffn_grad).astype(F32), axis=0)
     tri_sum, send_sum = jnp.concatenate(tri_sums), jnp.concatenate(send_sums)
     pair_sums = jnp.concatenate(
         [
@@ -1191,7 +1188,6 @@
     )
     close()
     start(up_back)
-    down_back.finish(*now)
 
     def beside(first, second):
         shared = geo.n3 - geo.base
@@ -1227,6 +1223,8 @@
     )
     close(pack, *attn_parts)
     attn_back = begin(attn_parts, scatter_steps, False)
+    block_back = [tie(part) for part in block_back]
+    down_shard = down_back.finish(*now)
     latent_back = from_chip(tie(latent_rows))
     opened.extend(latent_back)
     pack = tie(pack)
@@ -1246,7 +1244,7 @@
     close()
     start(attn_back)
     block_out, latent_grad = home(block_back), home(latent_back)
-    down_grad, up_grad = down_back.finish(*now), up_back.finish(*now)
+    down_grad, up_grad = down_shard, up_back.finish(*now)
     attn_grad = attn_back.finish(*now)
     in_grad = attn_grad[:, : 3 * cols].reshape(geo.R, 3, cols).transpose(1, 0, 2)
 

time: 562 us -> 565 us (level)
    ppermute x18, waiting for transfers between devices: 61.3 us -> 68.9 us  [flip_tensor(): return lax.ppermute(x, 'tensor', [(i, i ^ k) for i in range(geo.T)])]
  transfers between devices with their start and end apart: 73 -> 73, of which waited for: 32 -> 32; matrix products, arithmetic and copies ran while one was open for 10% -> 11% of each run, Pallas kernels for 39% -> 38%
where the time goes in v6:
time: 565 us; the launch traced here: 559 us
  Pallas kernels  223 us (39%)
  waiting for transfers between devices  126 us (22%)
  starting transfers between devices  124 us (22%)
  other arithmetic  48.1 us (9%)
  local copies, waits for them, and re-layouts  31.1 us (6%)
    ppermute x18, waiting for transfers between devices, flip_tensor(): return lax.ppermute(x, 'tensor', [(i, i ^ k) for i in range(geo.T)])  68.9 us
    pallas_call x6, Pallas kernels, weight_grad(): pl.pallas_call(kernel, grid_spec=pltpu.PrefetchScalarGridSpec(num_scalar_...  59.8 us
    ppermute x17, starting transfers between devices, flip_core(): return lax.ppermute(x, 'fsdp', [(i, i ^ 1) for i in range(geo.F)])  34.4 us
    ppermute x24, waiting for transfers between devices, flip_pair(): return lax.ppermute(x, 'fsdp', [(i, i ^ 2 * bit) for i in range(geo.F)])  33.1 us
    pallas_call x2, Pallas kernels, attn_bwd(): pl.pallas_call(kernel, grid=(z,), in_specs=[spec(wp), spec(geo.kvw), spec...  29.4 us
    ppermute x18, starting transfers between devices, flip_tensor(): return lax.ppermute(x, 'tensor', [(i, i ^ k) for i in range(geo.T)])  29.3 us
    ppermute x24, starting transfers between devices, flip_pair(): return lax.ppermute(x, 'fsdp', [(i, i ^ 2 * bit) for i in range(geo.F)])  27.6 us
    pallas_call x2, Pallas kernels, attn_fwd(): pl.pallas_call(kernel, grid=(z,), in_specs=[spec(wp), spec(geo.kvw), spec...  20.1 us
  transfers between devices with their start and end apart: 73, of which 32 were waited for; matrix products, arithmetic and copies ran while one was open for 11% of the time, Pallas kernels for 38%

profile of v6, /device:TPU:10, one launch (start us, length us, event | category | flops | bytes accessed | tf_op | source)
XLA Modules:
  0.0 558.8 jit_solution(3905161738128077546)
XLA Ops:
  20.6 13.8 %collective-permute-done.1 = bf16[144,1152]{1,0:T(8,128)(2,1)S(1)} collective-permute-done((bf16[144,1152]{1,0:T(8,128)(2,1)S(1)}, bf16[144,1152]{1,0:T(8,128)(2,1)S(1)}, u32[]{:S(2)}, u32[]{:S(2)}) %collective-permute-start.1) | collective-permute-done | bytes 331808 | tf_op jit(solution)/shard_map/ppermute | solution.py:67
  34.4 8.2 %collective-permute-done.2 = bf16[144,1152]{1,0:T(8,128)(2,1)S(1)} collective-permute-done((bf16[144,1152]{1,0:T(8,128)(2,1)S(1)}, bf16[144,1152]{1,0:T(8,128)(2,1)S(1)}, u32[]{:S(2)}, u32[]{:S(2)}) %collective-permute-start.2) | collective-permute-done | bytes 331808 | tf_op jit(solution)/shard_map/ppermute | solution.py:67
  48.4 7.9 %collective-permute-done.5 = bf16[144,1152]{1,0:T(8,128)(2,1)} collective-permute-done((bf16[144,1152]{1,0:T(8,128)(2,1)}, bf16[144,1152]{1,0:T(8,128)(2,1)}, u32[]{:S(2)}, u32[]{:S(2)}) %collective-permute-start.5) | collective-permute-done | bytes 331808 | tf_op jit(solution)/shard_map/ppermute | solution.py:67
  70.7 11.1 %collective-permute-start.10 = (bf16[2,2,144,1152]{3,2,1,0:T(8,128)(2,1)S(1)}, bf16[2,2,144,1152]{3,2,1,0:T(8,128)(2,1)}, u32[]{:S(2)}, u32[]{:S(2)}) collective-permute-start(bf16[2,2,144,1152]{3,2,1,0:T(8,128)(2,1)S(1)} %pad_maximum_fusion.2.refs_0_.refs_1_.refs_2_), channel_id=1, source_target_pairs={{0,4},{4,0},{8,12},{12,8},{16,20},{20,16},{24,28},{28,24},{1,5},{5... | collective-permute-start | bytes 3981320 | tf_op jit(solution)/shard_map/ppermute | solution.py:63
  149.4 9.8 %attn_fwd.3 = (bf16[2,512,384]{2,1,0:T(8,128)(2,1)}, f32[2,4,512]{2,1,0:T(4,128)}) custom-call(bf16[2,512,384]{2,1,0:T(8,128)(2,1)} %get-tuple-element.246.q_ref, bf16[2,512,640]{2,1,0:T(8,128)(2,1)} %get-tuple-element.179.kv_ref, bf16[2,512,640]{2,1,0:T(8,128)(2,1)} %copy-done.56), custom_call_target="tpu_custom_call" | custom-call | flops 6000000000 | bytes 3932160 | tf_op jit(solution)/shard_map/attn_fwd/pallas_call | solution.py:401
  159.2 10.3 %attn_fwd.2 = (bf16[2,512,384]{2,1,0:T(8,128)(2,1)}, f32[2,4,512]{2,1,0:T(4,128)}) custom-call(bf16[2,512,384]{2,1,0:T(8,128)(2,1)} %get-tuple-element.243.q_ref, bf16[2,512,640]{2,1,0:T(8,128)(2,1)} %get-tuple-element.177.kv_ref, bf16[2,512,640]{2,1,0:T(8,128)(2,1)} %copy-done.55), custom_call_target="tpu_custom_call" | custom-call | flops 6000000000 | bytes 3932160 | tf_op jit(solution)/shard_map/attn_fwd/pallas_call | solution.py:401
  183.1 11.2 %out_proj.1 = (bf16[544,1152]{1,0:T(8,128)(2,1)}, f32[512,1152]{1,0:T(8,128)}, bf16[544,1152]{1,0:T(8,128)(2,1)}) custom-call(s32[3]{0:T(128)} %pad_add_fusion.1.s, bf16[2,512,384]{2,1,0:T(8,128)(2,1)} %get-tuple-element.192.ya_ref.o_ref.refs_6_, bf16[2,512,384]{2,1,0:T(8,128)(2,1)} %get-tuple-element.193.yb_ref.o_ref.refs_7_, f32[6,1152]{1,0:T(8,128)} %reshape.191.m_ref, ...), custom_call_target="tpu_custom_call" | custom-call | flops 1358954496 | bytes 18874368 | tf_op jit(solution)/shard_map/out_proj/pallas_call | solution.py:525
  213.2 15.5 %up_proj.1 = (bf16[4,512,1152]{2,1,0:T(8,128)(2,1)}, bf16[4,512,1152]{2,1,0:T(8,128)(2,1)}) custom-call(s32[3]{0:T(128)} %pad_add_fusion.1.s, bf16[544,1152]{1,0:T(8,128)(2,1)} %get-tuple-element.194.h_ref.refs_0_, f32[4,1,1152]{2,1,0:T(1,128)} %maximum_convert_fusion.b_ref, bf16[4,2,144,1152]{3,2,1,0:T(8,128)(2,1)} %copy-done.5, ...), custom_call_target="tpu_custom_call" | custom-call | flops 5435817984 | bytes 20054016 | tf_op jit(solution)/shard_map/up_proj/pallas_call | solution.py:574
  239.5 8.5 %w_down_send.1 = bf16[4,4,144,1152]{3,2,1,0:T(8,128)(2,1)} custom-call(s32[3]{0:T(128)} %pad_add_fusion.1.s, bf16[512,1152]{1,0:T(8,128)(2,1)} %multiply_convert_fusion.refs_0_.g_ref, bf16[4,512,1152]{2,1,0:T(8,128)(2,1)} %get-tuple-element.201.refs_1_.y_ref), custom_call_target="tpu_custom_call" | custom-call | flops 2717908992 | bytes 15335424 | tf_op jit(solution)/shard_map/w_down_send/pallas_call | solution.py:952
  248.6 14.2 %down_proj.1 = (bf16[512,1152]{1,0:T(8,128)(2,1)}, f32[8,1152]{1,0:T(8,128)}) custom-call(s32[3]{0:T(128)} %pad_add_fusion.1.s, bf16[4,512,1152]{2,1,0:T(8,128)(2,1)} %get-tuple-element.201.refs_1_.y_ref, f32[6,1152]{1,0:T(8,128)} %reshape.191.m_ref, f32[1,1152]{1,0:T(1,128)} %get-tuple-element.391.b_ref, f32[512,1152]{1,0:T(8,128)} %get-tuple-element.206.refs_0_, ...), custom_call_target="tpu_custom_call" | custom-call | flops 5435817984 | bytes 20054016 | tf_op jit(solution)/shard_map/down_proj/pallas_call | solution.py:629
  262.8 10.1 %w_down.1 = (bf16[2,2,144,1152]{3,2,1,0:T(8,128)(2,1)}, bf16[2,2,144,1152]{3,2,1,0:T(8,128)(2,1)}, bf16[2,2,144,1152]{3,2,1,0:T(8,128)(2,1)}, bf16[2,2,144,1152]{3,2,1,0:T(8,128)(2,1)}) custom-call(s32[3]{0:T(128)} %pad_add_fusion.1.s, bf16[512,1152]{1,0:T(8,128)(2,1)} %multiply_convert_fusion.refs_0_.g_ref, ...), custom_call_target="tpu_custom_call" | custom-call | flops 2717908992 | bytes 15335424 | tf_op jit(solution)/shard_map/w_down/pallas_call | solution.py:952
  282.7 13.6 %pre_back.1 = (bf16[4,512,1152]{2,1,0:T(8,128)(2,1)}, f32[4,1,1152]{2,1,0:T(1,128)}) custom-call(s32[3]{0:T(128)} %pad_add_fusion.1.s, bf16[512,1152]{1,0:T(8,128)(2,1)} %multiply_convert_fusion.refs_0_.g_ref, bf16[4,512,1152]{2,1,0:T(8,128)(2,1)} %get-tuple-element.224.gp_ref, bf16[2,2,144,1152]{3,2,1,0:T(8,128)(2,1)} %pad_maximum_fusion.6.refs_2_.refs_0_, ...), custom_call_target="tpu_custom_call" | custom-call | flops 5435817984 | bytes 20054016 | tf_op jit(solution)/shard_map/pre_back/pallas_call | solution.py:666
  296.4 8.4 %w_up_send.1 = bf16[4,4,144,1152]{3,2,1,0:T(8,128)(2,1)} custom-call(s32[3]{0:T(128)} %pad_add_fusion.1.s, bf16[544,1152]{1,0:T(8,128)(2,1)} %get-tuple-element.194.h_ref.refs_0_, bf16[4,512,1152]{2,1,0:T(8,128)(2,1)} %get-tuple-element.225.refs_1_.y_ref), custom_call_target="tpu_custom_call" | custom-call | flops 2717908992 | bytes 15335424 | tf_op jit(solution)/shard_map/w_up_send/pallas_call | solution.py:952
  312.0 16.9 %second_back.1 = (f32[512,1152]{1,0:T(8,128)}, bf16[512,1152]{1,0:T(8,128)(2,1)}, f32[4,8,1152]{2,1,0:T(8,128)}) custom-call(s32[3]{0:T(128)} %pad_add_fusion.1.s, bf16[4,512,1152]{2,1,0:T(8,128)(2,1)} %get-tuple-element.225.refs_1_.y_ref, f32[6,1152]{1,0:T(8,128)} %reshape.191.m_ref, f32[512,1152]{1,0:T(8,128)} %get-tuple-element.206.refs_0_, ...), custom_call_target="tpu_custom_call" | custom-call | flops 5435817984 | bytes 25952256 | tf_op jit(solution)/shard_map/second_back/pallas_call | solution.py:727
  335.9 8.0 %mixed_back.1.do_ref = bf16[4,512,384]{2,1,0:T(8,128)(2,1)} custom-call(s32[3]{0:T(128)} %pad_add_fusion.1.s, bf16[512,1152]{1,0:T(8,128)(2,1)} %get-tuple-element.232.g_ref.refs_1_, bf16[2,2,144,1152]{3,2,1,0:T(8,128)(2,1)} %copy-done.2, bf16[2,2,144,1152]{3,2,1,0:T(8,128)(2,1)} %collective-permute-done.11.refs_1_.refs_2_.refs_3_, ...), custom_call_target="tpu_custom_call" | custom-call | flops 1358954496 | bytes 12976128 | tf_op jit(solution)/shard_map/mixed_back/pallas_call | solution.py:762
  343.9 10.0 %w_up.1 = (bf16[2,2,144,1152]{3,2,1,0:T(8,128)(2,1)}, bf16[2,2,144,1152]{3,2,1,0:T(8,128)(2,1)}, bf16[2,2,144,1152]{3,2,1,0:T(8,128)(2,1)}, bf16[2,2,144,1152]{3,2,1,0:T(8,128)(2,1)}) custom-call(s32[3]{0:T(128)} %pad_add_fusion.1.s, bf16[544,1152]{1,0:T(8,128)(2,1)} %get-tuple-element.194.h_ref.refs_0_, ...), custom_call_target="tpu_custom_call" | custom-call | flops 2717908992 | bytes 15335424 | tf_op jit(solution)/shard_map/w_up/pallas_call | solution.py:952
  355.5 14.7 %attn_bwd.3 = (bf16[2,512,896]{2,1,0:T(8,128)(2,1)}, bf16[2,512,640]{2,1,0:T(8,128)(2,1)}, f32[2,1,896]{2,1,0:T(1,128)}, f32[2,1,640]{2,1,0:T(1,128)}) custom-call(bf16[2,512,384]{2,1,0:T(8,128)(2,1)} %get-tuple-element.246.q_ref, bf16[2,512,640]{2,1,0:T(8,128)(2,1)} %get-tuple-element.179.kv_ref, bf16[2,512,640]{2,1,0:T(8,128)(2,1)} %copy-done.56, ...), custom_call_target="tpu_custom_call" | custom-call | flops 10000000000 | bytes 6291456 | tf_op jit(solution)/shard_map/attn_bwd/pallas_call | solution.py:455
  370.3 14.7 %attn_bwd.2 = (bf16[2,512,896]{2,1,0:T(8,128)(2,1)}, bf16[2,512,640]{2,1,0:T(8,128)(2,1)}, f32[2,1,896]{2,1,0:T(1,128)}, f32[2,1,640]{2,1,0:T(1,128)}) custom-call(bf16[2,512,384]{2,1,0:T(8,128)(2,1)} %get-tuple-element.243.q_ref, bf16[2,512,640]{2,1,0:T(8,128)(2,1)} %get-tuple-element.177.kv_ref, bf16[2,512,640]{2,1,0:T(8,128)(2,1)} %copy-done.55, ...), custom_call_target="tpu_custom_call" | custom-call | flops 10000000000 | bytes 6291456 | tf_op jit(solution)/shard_map/attn_bwd/pallas_call | solution.py:455
  395.0 11.2 %w_attn_send.1 = bf16[4,4,144,1152]{3,2,1,0:T(8,128)(2,1)} custom-call(s32[3]{0:T(128)} %pad_add_fusion.1.s, bf16[512,1152]{1,0:T(8,128)(2,1)} %norm_mod.1.h_ref.refs_0_, bf16[512,1152]{1,0:T(8,128)(2,1)} %get-tuple-element.232.g_ref.refs_1_, bf16[2,512,896]{2,1,0:T(8,128)(2,1)} %get-tuple-element.255.refs_2_.ta, ...), custom_call_target="tpu_custom_call" | custom-call | flops 2717908992 | bytes 15335424 | tf_op jit(solution)/shard_map/w_attn_send/pallas_call | solution.py:952
  419.9 15.2 %first_back.1 = (bf16[512,1152]{1,0:T(8,128)(2,1)}, f32[2,8,1152]{2,1,0:T(8,128)}) custom-call(s32[3]{0:T(128)} %pad_add_fusion.1.s, bf16[2,512,896]{2,1,0:T(8,128)(2,1)} %get-tuple-element.255.refs_2_.ta, bf16[2,512,896]{2,1,0:T(8,128)(2,1)} %get-tuple-element.256.refs_3_.tb, bf16[2,512,640]{2,1,0:T(8,128)(2,1)} %collective-permute-done.53.refs_4_.ga, ...), custom_call_target="tpu_custom_call" | custom-call | flops 4076863488 | bytes 20054016 | tf_op jit(solution)/shard_map/first_back/pallas_call | solution.py:823
  445.0 11.6 %w_attn.1 = (bf16[2,2,144,1152]{3,2,1,0:T(8,128)(2,1)}, bf16[2,2,144,1152]{3,2,1,0:T(8,128)(2,1)}, bf16[2,2,144,1152]{3,2,1,0:T(8,128)(2,1)}, bf16[2,2,144,1152]{3,2,1,0:T(8,128)(2,1)}) custom-call(s32[3]{0:T(128)} %pad_add_fusion.1.s, bf16[512,1152]{1,0:T(8,128)(2,1)} %norm_mod.1.h_ref.refs_0_, bf16[512,1152]{1,0:T(8,128)(2,1)} %get-tuple-element.232.g_ref.refs_1_, ...), custom_call_target="tpu_custom_call" | custom-call | flops 2717908992 | bytes 15335424 | tf_op jit(solution)/shard_map/w_attn/pallas_call | solution.py:952
  485.9 10.9 %all-to-all-done.2 = f32[32,8,128]{2,1,0:T(8,128)S(1)} async-done(((f32[32,8,128]{2,1,0:T(8,128)}), f32[32,8,128]{2,1,0:T(8,128)S(1)}, u32[]{:S(2)}, u32[]{:S(2)}) %all-to-all-start.2) | async-done | bytes 131104 | tf_op jit(solution)/shard_map/all_to_all | solution.py:1241
  532.3 14.8 %collective-permute-done.68 = bf16[144,1152]{1,0:T(8,128)(2,1)S(1)} collective-permute-done((bf16[144,1152]{1,0:T(8,128)(2,1)S(1)}, bf16[144,1152]{1,0:T(8,128)(2,1)S(1)}, u32[]{:S(2)}, u32[]{:S(2)}) %collective-permute-start.68) | collective-permute-done | bytes 331808 | tf_op jit(solution)/shard_map/ppermute | solution.py:67
  547.1 9.2 %collective-permute-done.69 = bf16[144,1152]{1,0:T(8,128)(2,1)S(1)} collective-permute-done((bf16[144,1152]{1,0:T(8,128)(2,1)S(1)}, bf16[144,1152]{1,0:T(8,128)(2,1)S(1)}, u32[]{:S(2)}, u32[]{:S(2)}) %collective-permute-start.69) | collective-permute-done | bytes 331808 | tf_op jit(solution)/shard_map/ppermute | solution.py:67
  (412 shorter events, 276.7 us)
Async XLA Ops:
  4.8 29.6 %collective-permute-start.1 = (bf16[144,1152]{1,0:T(8,128)(2,1)S(1)}, bf16[144,1152]{1,0:T(8,128)(2,1)S(1)}, u32[]{:S(2)}, u32[]{:S(2)}) collective-permute-start(bf16[144,1152]{1,0:T(8,128)(2,1)S(1)} %concatenate.86), channel_id=1, source_target_pairs={{0,2},{1,3},{2,0},{3,1},{4,6},{5,7},{6,4},{7,5},{8,10},{9,11},{10,... | collective-permute-start | bytes 995336 | tf_op jit(solution)/shard_map/ppermute | solution.py:67
  7.9 34.7 %collective-permute-start.2 = (bf16[144,1152]{1,0:T(8,128)(2,1)S(1)}, bf16[144,1152]{1,0:T(8,128)(2,1)S(1)}, u32[]{:S(2)}, u32[]{:S(2)}) collective-permute-start(bf16[144,1152]{1,0:T(8,128)(2,1)S(1)} %concatenate.86), channel_id=1, source_target_pairs={{0,3},{1,2},{2,1},{3,0},{4,7},{5,6},{6,5},{7,4},{8,11},{9,10},{10,... | collective-permute-start | bytes 995336 | tf_op jit(solution)/shard_map/ppermute | solution.py:67
  13.6 34.0 %all-to-all-start = ((f32[32,8,288]{2,1,0:T(8,128)}), f32[32,8,288]{2,1,0:T(8,128)S(1)}, u32[]{:S(2)}, u32[]{:S(2)}) async-start(f32[32,8,288]{2,1,0:T(8,128)} %bitcast.17), calls=%async_computation | async-start | bytes 786432 | tf_op jit(solution)/shard_map/all_to_all | solution.py:1081
  60.4 28.0 %collective-permute-start.12 = (bf16[2,2,144,1152]{3,2,1,0:T(8,128)(2,1)S(1)}, bf16[2,2,144,1152]{3,2,1,0:T(8,128)(2,1)}, u32[]{:S(2)}, u32[]{:S(2)}) collective-permute-start(bf16[2,2,144,1152]{3,2,1,0:T(8,128)(2,1)S(1)} %pad_maximum_fusion.3.refs_0_.refs_5_.refs_4_.refs_6_), channel_id=1, source_target_pairs={{0,8},{4,12},{8,0},{12,4},{16,24},{20,28},{24,16},{28,20},{1,9},{5... | collective-permute-start | bytes 3981320 | tf_op jit(solution)/shard_map/ppermute | solution.py:59
  63.2 27.3 %collective-permute-start.11 = (bf16[2,2,144,1152]{3,2,1,0:T(8,128)(2,1)S(1)}, bf16[2,2,144,1152]{3,2,1,0:T(8,128)(2,1)}, u32[]{:S(2)}, u32[]{:S(2)}) collective-permute-start(bf16[2,2,144,1152]{3,2,1,0:T(8,128)(2,1)S(1)} %pad_maximum_fusion.2.refs_0_.refs_1_.refs_2_), channel_id=1, source_target_pairs={{0,16},{4,20},{8,24},{12,28},{16,0},{20,4},{24,8},{28,12},{1,17},{... | collective-permute-start | bytes 3981320 | tf_op jit(solution)/shard_map/ppermute | solution.py:59
  68.5 46.9 %collective-permute-start.16 = (bf16[2,2,144,1152]{3,2,1,0:T(8,128)(2,1)S(1)}, bf16[2,2,144,1152]{3,2,1,0:T(8,128)(2,1)}, u32[]{:S(2)}, u32[]{:S(2)}) collective-permute-start(bf16[2,2,144,1152]{3,2,1,0:T(8,128)(2,1)S(1)} %pad_maximum_fusion.3.refs_0_.refs_5_.refs_4_.refs_6_), channel_id=1, source_target_pairs={{0,4},{4,0},{8,12},{12,8},{16,20},{20,16},{24,28},{28,24},{1,5},{5... | collective-permute-start | bytes 3981320 | tf_op jit(solution)/shard_map/ppermute | solution.py:63
  70.7 44.7 %collective-permute-start.10 = (bf16[2,2,144,1152]{3,2,1,0:T(8,128)(2,1)S(1)}, bf16[2,2,144,1152]{3,2,1,0:T(8,128)(2,1)}, u32[]{:S(2)}, u32[]{:S(2)}) collective-permute-start(bf16[2,2,144,1152]{3,2,1,0:T(8,128)(2,1)S(1)} %pad_maximum_fusion.2.refs_0_.refs_1_.refs_2_), channel_id=1, source_target_pairs={{0,4},{4,0},{8,12},{12,8},{16,20},{20,16},{24,28},{28,24},{1,5},{5... | collective-permute-start | bytes 3981320 | tf_op jit(solution)/shard_map/ppermute | solution.py:63
  143.3 31.2 %collective-permute-start.27 = (bf16[2,2,144,1152]{3,2,1,0:T(8,128)(2,1)S(1)}, bf16[2,2,144,1152]{3,2,1,0:T(8,128)(2,1)S(1)}, u32[]{:S(2)}, u32[]{:S(2)}) collective-permute-start(bf16[2,2,144,1152]{3,2,1,0:T(8,128)(2,1)S(1)} %pad_maximum_fusion.5), channel_id=1, source_target_pairs={{0,8},{4,12},{8,0},{12,4},{16,24},{20,28},{24,16},{28,20},{1,9},{5... | collective-permute-start | bytes 3981320 | tf_op jit(solution)/shard_map/ppermute | solution.py:59
  144.2 31.0 %collective-permute-start.26 = (bf16[2,2,144,1152]{3,2,1,0:T(8,128)(2,1)S(1)}, bf16[2,2,144,1152]{3,2,1,0:T(8,128)(2,1)S(1)}, u32[]{:S(2)}, u32[]{:S(2)}) collective-permute-start(bf16[2,2,144,1152]{3,2,1,0:T(8,128)(2,1)S(1)} %pad_maximum_fusion.4), channel_id=1, source_target_pairs={{0,16},{4,20},{8,24},{12,28},{16,0},{20,4},{24,8},{28,12},{1,17},{... | collective-permute-start | bytes 3981320 | tf_op jit(solution)/shard_map/ppermute | solution.py:59
  201.1 30.4 %collective-permute-start.34 = (bf16[2,2,144,1152]{3,2,1,0:T(8,128)(2,1)}, bf16[2,2,144,1152]{3,2,1,0:T(8,128)(2,1)}, u32[]{:S(2)}, u32[]{:S(2)}) collective-permute-start(bf16[2,2,144,1152]{3,2,1,0:T(8,128)(2,1)} %pad_maximum_fusion.7.refs_6_.refs_4_), channel_id=1, source_target_pairs={{0,8},{4,12},{8,0},{12,4},{16,24},{20,28},{24,16},{28,20},{1,9},{5... | collective-permute-start | bytes 3981320 | tf_op jit(solution)/shard_map/ppermute | solution.py:59
  204.6 30.2 %collective-permute-start.33 = (bf16[2,2,144,1152]{3,2,1,0:T(8,128)(2,1)}, bf16[2,2,144,1152]{3,2,1,0:T(8,128)(2,1)}, u32[]{:S(2)}, u32[]{:S(2)}) collective-permute-start(bf16[2,2,144,1152]{3,2,1,0:T(8,128)(2,1)} %pad_maximum_fusion.6.refs_2_.refs_0_), channel_id=1, source_target_pairs={{0,16},{4,20},{8,24},{12,28},{16,0},{20,4},{24,8},{28,12},{1,17},{... | collective-permute-start | bytes 3981320 | tf_op jit(solution)/shard_map/ppermute | solution.py:59
  209.8 38.3 %collective-permute-start.38 = (bf16[2,2,144,1152]{3,2,1,0:T(8,128)(2,1)}, bf16[2,2,144,1152]{3,2,1,0:T(8,128)(2,1)}, u32[]{:S(2)}, u32[]{:S(2)}) collective-permute-start(bf16[2,2,144,1152]{3,2,1,0:T(8,128)(2,1)} %pad_maximum_fusion.7.refs_6_.refs_4_), channel_id=1, source_target_pairs={{0,4},{4,0},{8,12},{12,8},{16,20},{20,16},{24,28},{28,24},{1,5},{5... | collective-permute-start | bytes 3981320 | tf_op jit(solution)/shard_map/ppermute | solution.py:63
  272.9 31.9 %collective-permute-start.42 = (bf16[2,2,144,1152]{3,2,1,0:T(8,128)(2,1)}, bf16[2,2,144,1152]{3,2,1,0:T(8,128)(2,1)S(1)}, u32[]{:S(2)}, u32[]{:S(2)}) collective-permute-start(bf16[2,2,144,1152]{3,2,1,0:T(8,128)(2,1)} %get-tuple-element.221), channel_id=1, source_target_pairs={{0,16},{4,20},{8,24},{12,28},{16,0},{20,4},{24,8},{28,12},{1,17},{... | collective-permute-start | bytes 3981320 | tf_op jit(solution)/shard_map/ppermute | solution.py:59
  273.6 31.3 %collective-permute-start.43 = (bf16[2,2,144,1152]{3,2,1,0:T(8,128)(2,1)}, bf16[2,2,144,1152]{3,2,1,0:T(8,128)(2,1)}, u32[]{:S(2)}, u32[]{:S(2)}) collective-permute-start(bf16[2,2,144,1152]{3,2,1,0:T(8,128)(2,1)} %get-tuple-element.222), channel_id=1, source_target_pairs={{0,8},{4,12},{8,0},{12,4},{16,24},{20,28},{24,16},{28,20},{1,9},{5... | collective-permute-start | bytes 3981320 | tf_op jit(solution)/shard_map/ppermute | solution.py:59
  276.8 28.0 %collective-permute-start.41 = (bf16[256,1152]{1,0:T(8,128)(2,1)}, bf16[256,1152]{1,0:T(8,128)(2,1)}, u32[]{:S(2)}, u32[]{:S(2)}) collective-permute-start(bf16[256,1152]{1,0:T(8,128)(2,1)} %get-tuple-element.363), channel_id=1, source_target_pairs={{0,0},{1,1},{4,2},{5,3},{2,4},{3,5},{6,6},{7,7},{8,8},{9,9},{12,10... | collective-permute-start | bytes 1769480 | tf_op jit(solution)/shard_map/ppermute | solution.py:1026
  334.5 50.5 %collective-permute-start.52 = (bf16[144,1152]{1,0:T(8,128)(2,1)}, bf16[144,1152]{1,0:T(8,128)(2,1)S(1)}, u32[]{:S(2)}, u32[]{:S(2)}) collective-permute-start(bf16[144,1152]{1,0:T(8,128)(2,1)} %get-tuple-element.372), channel_id=1, source_target_pairs={{0,2},{1,3},{2,0},{3,1},{4,6},{5,7},{6,4},{7,5},{8,10},{9,11},{10,... | collective-permute-start | bytes 995336 | tf_op jit(solution)/shard_map/ppermute | solution.py:67
  353.9 31.1 %collective-permute-start.50 = (bf16[2,2,144,1152]{3,2,1,0:T(8,128)(2,1)}, bf16[2,2,144,1152]{3,2,1,0:T(8,128)(2,1)S(1)}, u32[]{:S(2)}, u32[]{:S(2)}) collective-permute-start(bf16[2,2,144,1152]{3,2,1,0:T(8,128)(2,1)} %get-tuple-element.241), channel_id=1, source_target_pairs={{0,16},{4,20},{8,24},{12,28},{16,0},{20,4},{24,8},{28,12},{1,17},{... | collective-permute-start | bytes 3981320 | tf_op jit(solution)/shard_map/ppermute | solution.py:59
  354.7 30.4 %collective-permute-start.51 = (bf16[2,2,144,1152]{3,2,1,0:T(8,128)(2,1)}, bf16[2,2,144,1152]{3,2,1,0:T(8,128)(2,1)S(1)}, u32[]{:S(2)}, u32[]{:S(2)}) collective-permute-start(bf16[2,2,144,1152]{3,2,1,0:T(8,128)(2,1)} %get-tuple-element.242), channel_id=1, source_target_pairs={{0,8},{4,12},{8,0},{12,4},{16,24},{20,28},{24,16},{28,20},{1,9},{5... | collective-permute-start | bytes 3981320 | tf_op jit(solution)/shard_map/ppermute | solution.py:59
  463.0 36.1 %collective-permute-start.63 = (bf16[2,2,144,1152]{3,2,1,0:T(8,128)(2,1)}, bf16[2,2,144,1152]{3,2,1,0:T(8,128)(2,1)}, u32[]{:S(2)}, u32[]{:S(2)}) collective-permute-start(bf16[2,2,144,1152]{3,2,1,0:T(8,128)(2,1)} %get-tuple-element.280), channel_id=1, source_target_pairs={{0,16},{4,20},{8,24},{12,28},{16,0},{20,4},{24,8},{28,12},{1,17},{... | collective-permute-start | bytes 3981320 | tf_op jit(solution)/shard_map/ppermute | solution.py:59
  464.5 34.7 %collective-permute-start.64 = (bf16[2,2,144,1152]{3,2,1,0:T(8,128)(2,1)}, bf16[2,2,144,1152]{3,2,1,0:T(8,128)(2,1)}, u32[]{:S(2)}, u32[]{:S(2)}) collective-permute-start(bf16[2,2,144,1152]{3,2,1,0:T(8,128)(2,1)} %get-tuple-element.281), channel_id=1, source_target_pairs={{0,8},{4,12},{8,0},{12,4},{16,24},{20,28},{24,16},{28,20},{1,9},{5... | collective-permute-start | bytes 3981320 | tf_op jit(solution)/shard_map/ppermute | solution.py:59
  467.0 29.8 %all-to-all-start.2 = ((f32[32,8,128]{2,1,0:T(8,128)}), f32[32,8,128]{2,1,0:T(8,128)S(1)}, u32[]{:S(2)}, u32[]{:S(2)}) async-start(f32[32,8,128]{2,1,0:T(8,128)} %bitcast.74), calls=%async_computation.2 | async-start | bytes 262144 | tf_op jit(solution)/shard_map/all_to_all | solution.py:1241
  519.4 27.7 %collective-permute-start.68 = (bf16[144,1152]{1,0:T(8,128)(2,1)S(1)}, bf16[144,1152]{1,0:T(8,128)(2,1)S(1)}, u32[]{:S(2)}, u32[]{:S(2)}) collective-permute-start(bf16[144,1152]{1,0:T(8,128)(2,1)S(1)} %get-tuple-element.369), channel_id=1, source_target_pairs={{0,2},{1,3},{2,0},{3,1},{4,6},{5,7},{6,4},{7,5},{8,10},{9,11},{10,... | collective-permute-start | bytes 995336 | tf_op jit(solution)/shard_map/ppermute | solution.py:67
  527.3 29.0 %collective-permute-start.69 = (bf16[144,1152]{1,0:T(8,128)(2,1)S(1)}, bf16[144,1152]{1,0:T(8,128)(2,1)S(1)}, u32[]{:S(2)}, u32[]{:S(2)}) collective-permute-start(bf16[144,1152]{1,0:T(8,128)(2,1)S(1)} %get-tuple-element.368), channel_id=1, source_target_pairs={{0,3},{1,2},{2,1},{3,0},{4,7},{5,6},{6,5},{7,4},{8,11},{9,10},{10,... | collective-permute-start | bytes 995336 | tf_op jit(solution)/shard_map/ppermute | solution.py:67
  529.7 26.6 %collective-permute-start.67 = (bf16[144,1152]{1,0:T(8,128)(2,1)S(1)}, bf16[144,1152]{1,0:T(8,128)(2,1)S(1)}, u32[]{:S(2)}, u32[]{:S(2)}) collective-permute-start(bf16[144,1152]{1,0:T(8,128)(2,1)S(1)} %slice_bitcast_fusion.4), channel_id=1, source_target_pairs={{0,1},{1,0},{2,3},{3,2},{4,5},{5,4},{6,7},{7,6},{8,9},{9,8},{10,11... | collective-permute-start | bytes 995336 | tf_op jit(solution)/shard_map/ppermute | solution.py:67
  (107 other events, 1346.1 us)

commit v7 on v6

--- a/solution.py
+++ b/solution.py
@@ -1188,6 +1188,7 @@
     )
     close()
     start(up_back)
+    down_back.finish(*now)
 
     def beside(first, second):
         shared = geo.n3 - geo.base
@@ -1224,7 +1225,7 @@
     close(pack, *attn_parts)
     attn_back = begin(attn_parts, scatter_steps, False)
     block_back = [tie(part) for part in block_back]
-    down_shard = down_back.finish(*now)
+    down_shard = tie(down_back.finish())
     latent_back = from_chip(tie(latent_rows))
     opened.extend(latent_back)
     pack = tie(pack)

time: 565 us -> 559 us (0.989)
  starting transfers between devices: 124 us -> 116 us
    ppermute x18, waiting for transfers between devices: 68.9 us -> 62.8 us  [flip_tensor(): return lax.ppermute(x, 'tensor', [(i, i ^ k) for i in range(geo.T)])]
  transfers between devices with their start and end apart: 73 -> 73, of which waited for: 32 -> 32; matrix products, arithmetic and copies ran while one was open for 11% -> 11% of each run, Pallas kernels for 38% -> 39%
where the time goes in v7:
time: 559 us; the launch traced here: 553 us
  Pallas kernels  223 us (40%)
  waiting for transfers between devices  130 us (23%)
  starting transfers between devices  116 us (21%)
  other arithmetic  48.4 us (9%)
  local copies, waits for them, and re-layouts  29.9 us (5%)
    ppermute x18, waiting for transfers between devices, flip_tensor(): return lax.ppermute(x, 'tensor', [(i, i ^ k) for i in range(geo.T)])  62.8 us
    pallas_call x6, Pallas kernels, weight_grad(): pl.pallas_call(kernel, grid_spec=pltpu.PrefetchScalarGridSpec(num_scalar_...  59.8 us
    ppermute x24, waiting for transfers between devices, flip_pair(): return lax.ppermute(x, 'fsdp', [(i, i ^ 2 * bit) for i in range(geo.F)])  35.5 us
    ppermute x17, starting transfers between devices, flip_core(): return lax.ppermute(x, 'fsdp', [(i, i ^ 1) for i in range(geo.F)])  34.5 us
    pallas_call x2, Pallas kernels, attn_bwd(): pl.pallas_call(kernel, grid=(z,), in_specs=[spec(wp), spec(geo.kvw), spec...  29.3 us
    ppermute x24, starting transfers between devices, flip_pair(): return lax.ppermute(x, 'fsdp', [(i, i ^ 2 * bit) for i in range(geo.F)])  27.7 us
    ppermute x18, starting transfers between devices, flip_tensor(): return lax.ppermute(x, 'tensor', [(i, i ^ k) for i in range(geo.T)])  24.8 us
    pallas_call x2, Pallas kernels, attn_fwd(): pl.pallas_call(kernel, grid=(z,), in_specs=[spec(wp), spec(geo.kvw), spec...  20.1 us
  transfers between devices with their start and end apart: 73, of which 32 were waited for; matrix products, arithmetic and copies ran while one was open for 11% of the time, Pallas kernels for 39%

profile of v7, /device:TPU:10, one launch (start us, length us, event | category | flops | bytes accessed | tf_op | source)
XLA Modules:
  0.0 553.1 jit_solution(12263212585123162736)
XLA Ops:
  20.6 13.8 %collective-permute-done.1 = bf16[144,1152]{1,0:T(8,128)(2,1)S(1)} collective-permute-done((bf16[144,1152]{1,0:T(8,128)(2,1)S(1)}, bf16[144,1152]{1,0:T(8,128)(2,1)S(1)}, u32[]{:S(2)}, u32[]{:S(2)}) %collective-permute-start.1) | collective-permute-done | bytes 331808 | tf_op jit(solution)/shard_map/ppermute | solution.py:67
  34.4 8.2 %collective-permute-done.2 = bf16[144,1152]{1,0:T(8,128)(2,1)S(1)} collective-permute-done((bf16[144,1152]{1,0:T(8,128)(2,1)S(1)}, bf16[144,1152]{1,0:T(8,128)(2,1)S(1)}, u32[]{:S(2)}, u32[]{:S(2)}) %collective-permute-start.2) | collective-permute-done | bytes 331808 | tf_op jit(solution)/shard_map/ppermute | solution.py:67
  48.4 7.9 %collective-permute-done.5 = bf16[144,1152]{1,0:T(8,128)(2,1)} collective-permute-done((bf16[144,1152]{1,0:T(8,128)(2,1)}, bf16[144,1152]{1,0:T(8,128)(2,1)}, u32[]{:S(2)}, u32[]{:S(2)}) %collective-permute-start.5) | collective-permute-done | bytes 331808 | tf_op jit(solution)/shard_map/ppermute | solution.py:67
  70.7 11.1 %collective-permute-start.10 = (bf16[2,2,144,1152]{3,2,1,0:T(8,128)(2,1)S(1)}, bf16[2,2,144,1152]{3,2,1,0:T(8,128)(2,1)}, u32[]{:S(2)}, u32[]{:S(2)}) collective-permute-start(bf16[2,2,144,1152]{3,2,1,0:T(8,128)(2,1)S(1)} %pad_maximum_fusion.2.refs_0_.refs_1_.refs_2_), channel_id=1, source_target_pairs={{0,4},{4,0},{8,12},{12,8},{16,20},{20,16},{24,28},{28,24},{1,5},{5... | collective-permute-start | bytes 3981320 | tf_op jit(solution)/shard_map/ppermute | solution.py:63
  149.4 9.8 %attn_fwd.3 = (bf16[2,512,384]{2,1,0:T(8,128)(2,1)}, f32[2,4,512]{2,1,0:T(4,128)}) custom-call(bf16[2,512,384]{2,1,0:T(8,128)(2,1)} %get-tuple-element.247.q_ref, bf16[2,512,640]{2,1,0:T(8,128)(2,1)} %get-tuple-element.180.kv_ref, bf16[2,512,640]{2,1,0:T(8,128)(2,1)} %copy-done.51), custom_call_target="tpu_custom_call" | custom-call | flops 6000000000 | bytes 3932160 | tf_op jit(solution)/shard_map/attn_fwd/pallas_call | solution.py:401
  159.2 10.3 %attn_fwd.2 = (bf16[2,512,384]{2,1,0:T(8,128)(2,1)}, f32[2,4,512]{2,1,0:T(4,128)}) custom-call(bf16[2,512,384]{2,1,0:T(8,128)(2,1)} %get-tuple-element.244.q_ref, bf16[2,512,640]{2,1,0:T(8,128)(2,1)} %get-tuple-element.178.kv_ref, bf16[2,512,640]{2,1,0:T(8,128)(2,1)} %copy-done.50), custom_call_target="tpu_custom_call" | custom-call | flops 6000000000 | bytes 3932160 | tf_op jit(solution)/shard_map/attn_fwd/pallas_call | solution.py:401
  183.0 11.2 %out_proj.1 = (bf16[544,1152]{1,0:T(8,128)(2,1)}, f32[512,1152]{1,0:T(8,128)}, bf16[544,1152]{1,0:T(8,128)(2,1)}) custom-call(s32[3]{0:T(128)} %pad_add_fusion.1.s, bf16[2,512,384]{2,1,0:T(8,128)(2,1)} %get-tuple-element.193.ya_ref.o_ref.refs_6_, bf16[2,512,384]{2,1,0:T(8,128)(2,1)} %get-tuple-element.194.yb_ref.o_ref.refs_7_, f32[6,1152]{1,0:T(8,128)} %reshape.191.m_ref, ...), custom_call_target="tpu_custom_call" | custom-call | flops 1358954496 | bytes 18874368 | tf_op jit(solution)/shard_map/out_proj/pallas_call | solution.py:525
  213.1 15.5 %up_proj.1 = (bf16[4,512,1152]{2,1,0:T(8,128)(2,1)}, bf16[4,512,1152]{2,1,0:T(8,128)(2,1)}) custom-call(s32[3]{0:T(128)} %pad_add_fusion.1.s, bf16[544,1152]{1,0:T(8,128)(2,1)} %get-tuple-element.195.h_ref.refs_0_, f32[4,1,1152]{2,1,0:T(1,128)} %maximum_convert_fusion.b_ref, bf16[4,2,144,1152]{3,2,1,0:T(8,128)(2,1)} %copy-done.5, ...), custom_call_target="tpu_custom_call" | custom-call | flops 5435817984 | bytes 20054016 | tf_op jit(solution)/shard_map/up_proj/pallas_call | solution.py:574
  239.4 8.4 %w_down_send.1 = bf16[4,4,144,1152]{3,2,1,0:T(8,128)(2,1)} custom-call(s32[3]{0:T(128)} %pad_add_fusion.1.s, bf16[512,1152]{1,0:T(8,128)(2,1)} %multiply_convert_fusion.refs_0_.g_ref, bf16[4,512,1152]{2,1,0:T(8,128)(2,1)} %get-tuple-element.202.refs_1_.y_ref), custom_call_target="tpu_custom_call" | custom-call | flops 2717908992 | bytes 15335424 | tf_op jit(solution)/shard_map/w_down_send/pallas_call | solution.py:952
  248.4 14.2 %down_proj.1 = (bf16[512,1152]{1,0:T(8,128)(2,1)}, f32[8,1152]{1,0:T(8,128)}) custom-call(s32[3]{0:T(128)} %pad_add_fusion.1.s, bf16[4,512,1152]{2,1,0:T(8,128)(2,1)} %get-tuple-element.202.refs_1_.y_ref, f32[6,1152]{1,0:T(8,128)} %reshape.191.m_ref, f32[1,1152]{1,0:T(1,128)} %get-tuple-element.393.b_ref, f32[512,1152]{1,0:T(8,128)} %get-tuple-element.207.refs_0_, ...), custom_call_target="tpu_custom_call" | custom-call | flops 5435817984 | bytes 20054016 | tf_op jit(solution)/shard_map/down_proj/pallas_call | solution.py:629
  262.6 10.1 %w_down.1 = (bf16[2,2,144,1152]{3,2,1,0:T(8,128)(2,1)}, bf16[2,2,144,1152]{3,2,1,0:T(8,128)(2,1)}, bf16[2,2,144,1152]{3,2,1,0:T(8,128)(2,1)}, bf16[2,2,144,1152]{3,2,1,0:T(8,128)(2,1)}) custom-call(s32[3]{0:T(128)} %pad_add_fusion.1.s, bf16[512,1152]{1,0:T(8,128)(2,1)} %multiply_convert_fusion.refs_0_.g_ref, ...), custom_call_target="tpu_custom_call" | custom-call | flops 2717908992 | bytes 15335424 | tf_op jit(solution)/shard_map/w_down/pallas_call | solution.py:952
  282.5 13.6 %pre_back.1 = (bf16[4,512,1152]{2,1,0:T(8,128)(2,1)}, f32[4,1,1152]{2,1,0:T(1,128)}) custom-call(s32[3]{0:T(128)} %pad_add_fusion.1.s, bf16[512,1152]{1,0:T(8,128)(2,1)} %multiply_convert_fusion.refs_0_.g_ref, bf16[4,512,1152]{2,1,0:T(8,128)(2,1)} %get-tuple-element.225.gp_ref, bf16[2,2,144,1152]{3,2,1,0:T(8,128)(2,1)} %pad_maximum_fusion.6.refs_2_.refs_0_, ...), custom_call_target="tpu_custom_call" | custom-call | flops 5435817984 | bytes 20054016 | tf_op jit(solution)/shard_map/pre_back/pallas_call | solution.py:666
  296.1 8.4 %w_up_send.1 = bf16[4,4,144,1152]{3,2,1,0:T(8,128)(2,1)} custom-call(s32[3]{0:T(128)} %pad_add_fusion.1.s, bf16[544,1152]{1,0:T(8,128)(2,1)} %get-tuple-element.195.h_ref.refs_0_, bf16[4,512,1152]{2,1,0:T(8,128)(2,1)} %get-tuple-element.226.refs_1_.y_ref), custom_call_target="tpu_custom_call" | custom-call | flops 2717908992 | bytes 15335424 | tf_op jit(solution)/shard_map/w_up_send/pallas_call | solution.py:952
  311.8 16.9 %second_back.1 = (f32[512,1152]{1,0:T(8,128)}, bf16[512,1152]{1,0:T(8,128)(2,1)}, f32[4,8,1152]{2,1,0:T(8,128)}) custom-call(s32[3]{0:T(128)} %pad_add_fusion.1.s, bf16[4,512,1152]{2,1,0:T(8,128)(2,1)} %get-tuple-element.226.refs_1_.y_ref, f32[6,1152]{1,0:T(8,128)} %reshape.191.m_ref, f32[512,1152]{1,0:T(8,128)} %get-tuple-element.207.refs_0_, ...), custom_call_target="tpu_custom_call" | custom-call | flops 5435817984 | bytes 25952256 | tf_op jit(solution)/shard_map/second_back/pallas_call | solution.py:727
  335.7 8.0 %mixed_back.1.do_ref = bf16[4,512,384]{2,1,0:T(8,128)(2,1)} custom-call(s32[3]{0:T(128)} %pad_add_fusion.1.s, bf16[512,1152]{1,0:T(8,128)(2,1)} %get-tuple-element.233.g_ref.refs_1_, bf16[2,2,144,1152]{3,2,1,0:T(8,128)(2,1)} %copy-done.2, bf16[2,2,144,1152]{3,2,1,0:T(8,128)(2,1)} %collective-permute-done.11.refs_1_.refs_2_.refs_3_, ...), custom_call_target="tpu_custom_call" | custom-call | flops 1358954496 | bytes 12976128 | tf_op jit(solution)/shard_map/mixed_back/pallas_call | solution.py:762
  343.7 10.1 %w_up.1 = (bf16[2,2,144,1152]{3,2,1,0:T(8,128)(2,1)}, bf16[2,2,144,1152]{3,2,1,0:T(8,128)(2,1)}, bf16[2,2,144,1152]{3,2,1,0:T(8,128)(2,1)}, bf16[2,2,144,1152]{3,2,1,0:T(8,128)(2,1)}) custom-call(s32[3]{0:T(128)} %pad_add_fusion.1.s, bf16[544,1152]{1,0:T(8,128)(2,1)} %get-tuple-element.195.h_ref.refs_0_, ...), custom_call_target="tpu_custom_call" | custom-call | flops 2717908992 | bytes 15335424 | tf_op jit(solution)/shard_map/w_up/pallas_call | solution.py:952
  355.5 14.7 %attn_bwd.3 = (bf16[2,512,896]{2,1,0:T(8,128)(2,1)}, bf16[2,512,640]{2,1,0:T(8,128)(2,1)}, f32[2,1,896]{2,1,0:T(1,128)}, f32[2,1,640]{2,1,0:T(1,128)}) custom-call(bf16[2,512,384]{2,1,0:T(8,128)(2,1)} %get-tuple-element.247.q_ref, bf16[2,512,640]{2,1,0:T(8,128)(2,1)} %get-tuple-element.180.kv_ref, bf16[2,512,640]{2,1,0:T(8,128)(2,1)} %copy-done.51, ...), custom_call_target="tpu_custom_call" | custom-call | flops 10000000000 | bytes 6291456 | tf_op jit(solution)/shard_map/attn_bwd/pallas_call | solution.py:455
  370.2 14.7 %attn_bwd.2 = (bf16[2,512,896]{2,1,0:T(8,128)(2,1)}, bf16[2,512,640]{2,1,0:T(8,128)(2,1)}, f32[2,1,896]{2,1,0:T(1,128)}, f32[2,1,640]{2,1,0:T(1,128)}) custom-call(bf16[2,512,384]{2,1,0:T(8,128)(2,1)} %get-tuple-element.244.q_ref, bf16[2,512,640]{2,1,0:T(8,128)(2,1)} %get-tuple-element.178.kv_ref, bf16[2,512,640]{2,1,0:T(8,128)(2,1)} %copy-done.50, ...), custom_call_target="tpu_custom_call" | custom-call | flops 10000000000 | bytes 6291456 | tf_op jit(solution)/shard_map/attn_bwd/pallas_call | solution.py:455
  394.8 11.2 %w_attn_send.1 = bf16[4,4,144,1152]{3,2,1,0:T(8,128)(2,1)} custom-call(s32[3]{0:T(128)} %pad_add_fusion.1.s, bf16[512,1152]{1,0:T(8,128)(2,1)} %norm_mod.1.h_ref.refs_0_, bf16[512,1152]{1,0:T(8,128)(2,1)} %get-tuple-element.233.g_ref.refs_1_, bf16[2,512,896]{2,1,0:T(8,128)(2,1)} %get-tuple-element.256.refs_2_.ta, ...), custom_call_target="tpu_custom_call" | custom-call | flops 2717908992 | bytes 15335424 | tf_op jit(solution)/shard_map/w_attn_send/pallas_call | solution.py:952
  419.0 15.2 %first_back.1 = (bf16[512,1152]{1,0:T(8,128)(2,1)}, f32[2,8,1152]{2,1,0:T(8,128)}) custom-call(s32[3]{0:T(128)} %pad_add_fusion.1.s, bf16[2,512,896]{2,1,0:T(8,128)(2,1)} %get-tuple-element.256.refs_2_.ta, bf16[2,512,896]{2,1,0:T(8,128)(2,1)} %get-tuple-element.257.refs_3_.tb, bf16[2,512,640]{2,1,0:T(8,128)(2,1)} %collective-permute-done.53.refs_4_.ga, ...), custom_call_target="tpu_custom_call" | custom-call | flops 4076863488 | bytes 20054016 | tf_op jit(solution)/shard_map/first_back/pallas_call | solution.py:823
  444.7 11.6 %w_attn.1 = (bf16[2,2,144,1152]{3,2,1,0:T(8,128)(2,1)}, bf16[2,2,144,1152]{3,2,1,0:T(8,128)(2,1)}, bf16[2,2,144,1152]{3,2,1,0:T(8,128)(2,1)}, bf16[2,2,144,1152]{3,2,1,0:T(8,128)(2,1)}) custom-call(s32[3]{0:T(128)} %pad_add_fusion.1.s, bf16[512,1152]{1,0:T(8,128)(2,1)} %norm_mod.1.h_ref.refs_0_, bf16[512,1152]{1,0:T(8,128)(2,1)} %get-tuple-element.233.g_ref.refs_1_, ...), custom_call_target="tpu_custom_call" | custom-call | flops 2717908992 | bytes 15335424 | tf_op jit(solution)/shard_map/w_attn/pallas_call | solution.py:952
  476.9 15.5 %all-to-all-done.2 = f32[32,8,128]{2,1,0:T(8,128)S(1)} async-done(((f32[32,8,128]{2,1,0:T(8,128)}), f32[32,8,128]{2,1,0:T(8,128)S(1)}, u32[]{:S(2)}, u32[]{:S(2)}) %all-to-all-start.2) | async-done | bytes 131104 | tf_op jit(solution)/shard_map/all_to_all | solution.py:1242
  526.3 15.0 %collective-permute-done.68 = bf16[144,1152]{1,0:T(8,128)(2,1)S(1)} collective-permute-done((bf16[144,1152]{1,0:T(8,128)(2,1)S(1)}, bf16[144,1152]{1,0:T(8,128)(2,1)S(1)}, u32[]{:S(2)}, u32[]{:S(2)}) %collective-permute-start.68) | collective-permute-done | bytes 331808 | tf_op jit(solution)/shard_map/ppermute | solution.py:67
  541.3 9.2 %collective-permute-done.69 = bf16[144,1152]{1,0:T(8,128)(2,1)S(1)} collective-permute-done((bf16[144,1152]{1,0:T(8,128)(2,1)S(1)}, bf16[144,1152]{1,0:T(8,128)(2,1)S(1)}, u32[]{:S(2)}, u32[]{:S(2)}) %collective-permute-start.69) | collective-permute-done | bytes 331808 | tf_op jit(solution)/shard_map/ppermute | solution.py:67
  (402 shorter events, 266.2 us)
Async XLA Ops:
  4.8 29.6 %collective-permute-start.1 = (bf16[144,1152]{1,0:T(8,128)(2,1)S(1)}, bf16[144,1152]{1,0:T(8,128)(2,1)S(1)}, u32[]{:S(2)}, u32[]{:S(2)}) collective-permute-start(bf16[144,1152]{1,0:T(8,128)(2,1)S(1)} %concatenate.86), channel_id=1, source_target_pairs={{0,2},{1,3},{2,0},{3,1},{4,6},{5,7},{6,4},{7,5},{8,10},{9,11},{10,... | collective-permute-start | bytes 995336 | tf_op jit(solution)/shard_map/ppermute | solution.py:67
  7.9 34.7 %collective-permute-start.2 = (bf16[144,1152]{1,0:T(8,128)(2,1)S(1)}, bf16[144,1152]{1,0:T(8,128)(2,1)S(1)}, u32[]{:S(2)}, u32[]{:S(2)}) collective-permute-start(bf16[144,1152]{1,0:T(8,128)(2,1)S(1)} %concatenate.86), channel_id=1, source_target_pairs={{0,3},{1,2},{2,1},{3,0},{4,7},{5,6},{6,5},{7,4},{8,11},{9,10},{10,... | collective-permute-start | bytes 995336 | tf_op jit(solution)/shard_map/ppermute | solution.py:67
  13.6 34.0 %all-to-all-start = ((f32[32,8,288]{2,1,0:T(8,128)}), f32[32,8,288]{2,1,0:T(8,128)S(1)}, u32[]{:S(2)}, u32[]{:S(2)}) async-start(f32[32,8,288]{2,1,0:T(8,128)} %bitcast.17), calls=%async_computation | async-start | bytes 786432 | tf_op jit(solution)/shard_map/all_to_all | solution.py:1081
  60.4 28.0 %collective-permute-start.12 = (bf16[2,2,144,1152]{3,2,1,0:T(8,128)(2,1)S(1)}, bf16[2,2,144,1152]{3,2,1,0:T(8,128)(2,1)}, u32[]{:S(2)}, u32[]{:S(2)}) collective-permute-start(bf16[2,2,144,1152]{3,2,1,0:T(8,128)(2,1)S(1)} %pad_maximum_fusion.3.refs_0_.refs_5_.refs_4_.refs_6_), channel_id=1, source_target_pairs={{0,8},{4,12},{8,0},{12,4},{16,24},{20,28},{24,16},{28,20},{1,9},{5... | collective-permute-start | bytes 3981320 | tf_op jit(solution)/shard_map/ppermute | solution.py:59
  63.2 27.3 %collective-permute-start.11 = (bf16[2,2,144,1152]{3,2,1,0:T(8,128)(2,1)S(1)}, bf16[2,2,144,1152]{3,2,1,0:T(8,128)(2,1)}, u32[]{:S(2)}, u32[]{:S(2)}) collective-permute-start(bf16[2,2,144,1152]{3,2,1,0:T(8,128)(2,1)S(1)} %pad_maximum_fusion.2.refs_0_.refs_1_.refs_2_), channel_id=1, source_target_pairs={{0,16},{4,20},{8,24},{12,28},{16,0},{20,4},{24,8},{28,12},{1,17},{... | collective-permute-start | bytes 3981320 | tf_op jit(solution)/shard_map/ppermute | solution.py:59
  68.5 46.8 %collective-permute-start.16 = (bf16[2,2,144,1152]{3,2,1,0:T(8,128)(2,1)S(1)}, bf16[2,2,144,1152]{3,2,1,0:T(8,128)(2,1)}, u32[]{:S(2)}, u32[]{:S(2)}) collective-permute-start(bf16[2,2,144,1152]{3,2,1,0:T(8,128)(2,1)S(1)} %pad_maximum_fusion.3.refs_0_.refs_5_.refs_4_.refs_6_), channel_id=1, source_target_pairs={{0,4},{4,0},{8,12},{12,8},{16,20},{20,16},{24,28},{28,24},{1,5},{5... | collective-permute-start | bytes 3981320 | tf_op jit(solution)/shard_map/ppermute | solution.py:63
  70.7 44.6 %collective-permute-start.10 = (bf16[2,2,144,1152]{3,2,1,0:T(8,128)(2,1)S(1)}, bf16[2,2,144,1152]{3,2,1,0:T(8,128)(2,1)}, u32[]{:S(2)}, u32[]{:S(2)}) collective-permute-start(bf16[2,2,144,1152]{3,2,1,0:T(8,128)(2,1)S(1)} %pad_maximum_fusion.2.refs_0_.refs_1_.refs_2_), channel_id=1, source_target_pairs={{0,4},{4,0},{8,12},{12,8},{16,20},{20,16},{24,28},{28,24},{1,5},{5... | collective-permute-start | bytes 3981320 | tf_op jit(solution)/shard_map/ppermute | solution.py:63
  143.3 31.2 %collective-permute-start.27 = (bf16[2,2,144,1152]{3,2,1,0:T(8,128)(2,1)S(1)}, bf16[2,2,144,1152]{3,2,1,0:T(8,128)(2,1)S(1)}, u32[]{:S(2)}, u32[]{:S(2)}) collective-permute-start(bf16[2,2,144,1152]{3,2,1,0:T(8,128)(2,1)S(1)} %pad_maximum_fusion.5), channel_id=1, source_target_pairs={{0,8},{4,12},{8,0},{12,4},{16,24},{20,28},{24,16},{28,20},{1,9},{5... | collective-permute-start | bytes 3981320 | tf_op jit(solution)/shard_map/ppermute | solution.py:59
  144.1 31.0 %collective-permute-start.26 = (bf16[2,2,144,1152]{3,2,1,0:T(8,128)(2,1)S(1)}, bf16[2,2,144,1152]{3,2,1,0:T(8,128)(2,1)S(1)}, u32[]{:S(2)}, u32[]{:S(2)}) collective-permute-start(bf16[2,2,144,1152]{3,2,1,0:T(8,128)(2,1)S(1)} %pad_maximum_fusion.4), channel_id=1, source_target_pairs={{0,16},{4,20},{8,24},{12,28},{16,0},{20,4},{24,8},{28,12},{1,17},{... | collective-permute-start | bytes 3981320 | tf_op jit(solution)/shard_map/ppermute | solution.py:59
  201.0 30.4 %collective-permute-start.34 = (bf16[2,2,144,1152]{3,2,1,0:T(8,128)(2,1)}, bf16[2,2,144,1152]{3,2,1,0:T(8,128)(2,1)}, u32[]{:S(2)}, u32[]{:S(2)}) collective-permute-start(bf16[2,2,144,1152]{3,2,1,0:T(8,128)(2,1)} %pad_maximum_fusion.7.refs_6_.refs_4_), channel_id=1, source_target_pairs={{0,8},{4,12},{8,0},{12,4},{16,24},{20,28},{24,16},{28,20},{1,9},{5... | collective-permute-start | bytes 3981320 | tf_op jit(solution)/shard_map/ppermute | solution.py:59
  204.5 30.2 %collective-permute-start.33 = (bf16[2,2,144,1152]{3,2,1,0:T(8,128)(2,1)}, bf16[2,2,144,1152]{3,2,1,0:T(8,128)(2,1)}, u32[]{:S(2)}, u32[]{:S(2)}) collective-permute-start(bf16[2,2,144,1152]{3,2,1,0:T(8,128)(2,1)} %pad_maximum_fusion.6.refs_2_.refs_0_), channel_id=1, source_target_pairs={{0,16},{4,20},{8,24},{12,28},{16,0},{20,4},{24,8},{28,12},{1,17},{... | collective-permute-start | bytes 3981320 | tf_op jit(solution)/shard_map/ppermute | solution.py:59
  209.7 38.2 %collective-permute-start.38 = (bf16[2,2,144,1152]{3,2,1,0:T(8,128)(2,1)}, bf16[2,2,144,1152]{3,2,1,0:T(8,128)(2,1)}, u32[]{:S(2)}, u32[]{:S(2)}) collective-permute-start(bf16[2,2,144,1152]{3,2,1,0:T(8,128)(2,1)} %pad_maximum_fusion.7.refs_6_.refs_4_), channel_id=1, source_target_pairs={{0,4},{4,0},{8,12},{12,8},{16,20},{20,16},{24,28},{28,24},{1,5},{5... | collective-permute-start | bytes 3981320 | tf_op jit(solution)/shard_map/ppermute | solution.py:63
  272.7 31.9 %collective-permute-start.42 = (bf16[2,2,144,1152]{3,2,1,0:T(8,128)(2,1)}, bf16[2,2,144,1152]{3,2,1,0:T(8,128)(2,1)S(1)}, u32[]{:S(2)}, u32[]{:S(2)}) collective-permute-start(bf16[2,2,144,1152]{3,2,1,0:T(8,128)(2,1)} %get-tuple-element.222), channel_id=1, source_target_pairs={{0,16},{4,20},{8,24},{12,28},{16,0},{20,4},{24,8},{28,12},{1,17},{... | collective-permute-start | bytes 3981320 | tf_op jit(solution)/shard_map/ppermute | solution.py:59
  273.4 31.2 %collective-permute-start.43 = (bf16[2,2,144,1152]{3,2,1,0:T(8,128)(2,1)}, bf16[2,2,144,1152]{3,2,1,0:T(8,128)(2,1)}, u32[]{:S(2)}, u32[]{:S(2)}) collective-permute-start(bf16[2,2,144,1152]{3,2,1,0:T(8,128)(2,1)} %get-tuple-element.223), channel_id=1, source_target_pairs={{0,8},{4,12},{8,0},{12,4},{16,24},{20,28},{24,16},{28,20},{1,9},{5... | collective-permute-start | bytes 3981320 | tf_op jit(solution)/shard_map/ppermute | solution.py:59
  276.6 28.0 %collective-permute-start.41 = (bf16[256,1152]{1,0:T(8,128)(2,1)}, bf16[256,1152]{1,0:T(8,128)(2,1)}, u32[]{:S(2)}, u32[]{:S(2)}) collective-permute-start(bf16[256,1152]{1,0:T(8,128)(2,1)} %get-tuple-element.365), channel_id=1, source_target_pairs={{0,0},{1,1},{4,2},{5,3},{2,4},{3,5},{6,6},{7,7},{8,8},{9,9},{12,10... | collective-permute-start | bytes 1769480 | tf_op jit(solution)/shard_map/ppermute | solution.py:1026
  334.2 50.6 %collective-permute-start.52 = (bf16[144,1152]{1,0:T(8,128)(2,1)}, bf16[144,1152]{1,0:T(8,128)(2,1)S(1)}, u32[]{:S(2)}, u32[]{:S(2)}) collective-permute-start(bf16[144,1152]{1,0:T(8,128)(2,1)} %get-tuple-element.374), channel_id=1, source_target_pairs={{0,2},{1,3},{2,0},{3,1},{4,6},{5,7},{6,4},{7,5},{8,10},{9,11},{10,... | collective-permute-start | bytes 995336 | tf_op jit(solution)/shard_map/ppermute | solution.py:67
  353.8 31.0 %collective-permute-start.50 = (bf16[2,2,144,1152]{3,2,1,0:T(8,128)(2,1)}, bf16[2,2,144,1152]{3,2,1,0:T(8,128)(2,1)S(1)}, u32[]{:S(2)}, u32[]{:S(2)}) collective-permute-start(bf16[2,2,144,1152]{3,2,1,0:T(8,128)(2,1)} %get-tuple-element.242), channel_id=1, source_target_pairs={{0,16},{4,20},{8,24},{12,28},{16,0},{20,4},{24,8},{28,12},{1,17},{... | collective-permute-start | bytes 3981320 | tf_op jit(solution)/shard_map/ppermute | solution.py:59
  354.6 30.3 %collective-permute-start.51 = (bf16[2,2,144,1152]{3,2,1,0:T(8,128)(2,1)}, bf16[2,2,144,1152]{3,2,1,0:T(8,128)(2,1)S(1)}, u32[]{:S(2)}, u32[]{:S(2)}) collective-permute-start(bf16[2,2,144,1152]{3,2,1,0:T(8,128)(2,1)} %get-tuple-element.243), channel_id=1, source_target_pairs={{0,8},{4,12},{8,0},{12,4},{16,24},{20,28},{24,16},{28,20},{1,9},{5... | collective-permute-start | bytes 3981320 | tf_op jit(solution)/shard_map/ppermute | solution.py:59
  410.5 27.1 %collective-permute-start.60 = (bf16[4,4,144,1152]{3,2,1,0:T(8,128)(2,1)}, bf16[4,4,144,1152]{3,2,1,0:T(8,128)(2,1)}, u32[]{:S(2)}, u32[]{:S(2)}) collective-permute-start(bf16[4,4,144,1152]{3,2,1,0:T(8,128)(2,1)} %w_attn_send.1), channel_id=1, source_target_pairs={{0,4},{4,0},{8,12},{12,8},{16,20},{20,16},{24,28},{28,24},{1,5},{5... | collective-permute-start | bytes 15925256 | tf_op jit(solution)/shard_map/ppermute | solution.py:63
  459.2 35.6 %collective-permute-start.63 = (bf16[2,2,144,1152]{3,2,1,0:T(8,128)(2,1)}, bf16[2,2,144,1152]{3,2,1,0:T(8,128)(2,1)}, u32[]{:S(2)}, u32[]{:S(2)}) collective-permute-start(bf16[2,2,144,1152]{3,2,1,0:T(8,128)(2,1)} %get-tuple-element.281), channel_id=1, source_target_pairs={{0,16},{4,20},{8,24},{12,28},{16,0},{20,4},{24,8},{28,12},{1,17},{... | collective-permute-start | bytes 3981320 | tf_op jit(solution)/shard_map/ppermute | solution.py:59
  460.0 34.7 %collective-permute-start.64 = (bf16[2,2,144,1152]{3,2,1,0:T(8,128)(2,1)}, bf16[2,2,144,1152]{3,2,1,0:T(8,128)(2,1)}, u32[]{:S(2)}, u32[]{:S(2)}) collective-permute-start(bf16[2,2,144,1152]{3,2,1,0:T(8,128)(2,1)} %get-tuple-element.282), channel_id=1, source_target_pairs={{0,8},{4,12},{8,0},{12,4},{16,24},{20,28},{24,16},{28,20},{1,9},{5... | collective-permute-start | bytes 3981320 | tf_op jit(solution)/shard_map/ppermute | solution.py:59
  463.3 29.1 %all-to-all-start.2 = ((f32[32,8,128]{2,1,0:T(8,128)}), f32[32,8,128]{2,1,0:T(8,128)S(1)}, u32[]{:S(2)}, u32[]{:S(2)}) async-start(f32[32,8,128]{2,1,0:T(8,128)} %bitcast.74), calls=%async_computation.2 | async-start | bytes 262144 | tf_op jit(solution)/shard_map/all_to_all | solution.py:1242
  521.1 29.5 %collective-permute-start.69 = (bf16[144,1152]{1,0:T(8,128)(2,1)S(1)}, bf16[144,1152]{1,0:T(8,128)(2,1)S(1)}, u32[]{:S(2)}, u32[]{:S(2)}) collective-permute-start(bf16[144,1152]{1,0:T(8,128)(2,1)S(1)} %get-tuple-element.370), channel_id=1, source_target_pairs={{0,3},{1,2},{2,1},{3,0},{4,7},{5,6},{6,5},{7,4},{8,11},{9,10},{10,... | collective-permute-start | bytes 995336 | tf_op jit(solution)/shard_map/ppermute | solution.py:67
  523.9 26.6 %collective-permute-start.67 = (bf16[144,1152]{1,0:T(8,128)(2,1)S(1)}, bf16[144,1152]{1,0:T(8,128)(2,1)S(1)}, u32[]{:S(2)}, u32[]{:S(2)}) collective-permute-start(bf16[144,1152]{1,0:T(8,128)(2,1)S(1)} %slice_bitcast_fusion.4), channel_id=1, source_target_pairs={{0,1},{1,0},{2,3},{3,2},{4,5},{5,4},{6,7},{7,6},{8,9},{9,8},{10,11... | collective-permute-start | bytes 995336 | tf_op jit(solution)/shard_map/ppermute | solution.py:67
  (102 other events, 1349.9 us)

commit v8 on v7

--- a/solution.py
+++ b/solution.py
@@ -591,16 +591,18 @@
     )(scal, h, bias, *wt.arrays)
 
 
-def down_proj(scal, hidden, resid, cot, mod, bias, wt, geo):
+def down_proj(scal, hidden, resid, cot, mod, bias, wt, blocks, geo):
     _, n, w = hidden.shape
     d = geo.D
     nw = len(wt.arrays)
 
     late = Late(resid, cot)
+    rows = n // blocks
 
     def kernel(s, y_ref, m_ref, b_ref, *refs):
         late_in, refs = refs[:2], refs[2:]
-        w_refs, (out_ref, sum_ref, wbuf, sem, acc, *late_buf) = refs[:nw], refs[nw:]
+        w_refs, outs, refs = refs[:nw], refs[nw : nw + blocks], refs[nw + blocks :]
+        sum_ref, wbuf, sem, acc, *late_buf = refs
         j = pl.program_id(0)
         late.start(j, late_in, late_buf)
         now = wt.stream(j, s, w_refs, wbuf, sem)
@@ -619,12 +621,15 @@
         def _():
             r_ref, c_ref = late.wait(late_in, late_buf)
 
-            @pl.loop(0, n // ROWS, unroll=4)
-            def _(i):
-                at = pl.ds(pl.multiple_of(i * ROWS, ROWS), ROWS)
-                ffn = acc[at, :] + b_ref[...]
-                out_ref[at, :] = (r_ref[at, :] + m_ref[5:6, :] * ffn).astype(BF)
-                sum_ref[...] += fold_rows(c_ref[at, :].astype(F32) * ffn)
+            for part, out_ref in enumerate(outs):
+
+                @pl.loop(0, rows // ROWS, unroll=4)
+                def _(i):
+                    here = pl.ds(pl.multiple_of(i * ROWS, ROWS), ROWS)
+                    at = pl.ds(pl.multiple_of(part * rows + i * ROWS, ROWS), ROWS)
+                    ffn = acc[at, :] + b_ref[...]
+                    out_ref[here, :] = (r_ref[at, :] + m_ref[5:6, :] * ffn).astype(BF)
+                    sum_ref[...] += fold_rows(c_ref[at, :].astype(F32) * ffn)
 
     return pl.pallas_call(
         kernel,
@@ -638,10 +643,13 @@
                 *late.specs,
                 *wt.specs(),
             ],
-            out_specs=[whole((n, d)), whole((8, d))],
+            out_specs=[*[whole((rows, d))] * blocks, whole((8, d))],
             scratch_shapes=[*wt.scratch(), pltpu.VMEM((n, d), F32), *late.scratch],
         ),
-        out_shape=[jax.ShapeDtypeStruct((n, d), BF), jax.ShapeDtypeStruct((8, d), F32)],
+        out_shape=[
+            *[jax.ShapeDtypeStruct((rows, d), BF)] * blocks,
+            jax.ShapeDtypeStruct((8, d), F32),
+        ],
         compiler_params=params(),
         cost_estimate=cost(2 * n * d * w * geo.T, 2 * geo.T * w * (d + n) + 8 * n * d),
         name="down_proj",
@@ -1023,7 +1031,7 @@
         got = []
         for k in range(images):
             back = [(dst, src) for src, dst in places(k)]
-            got.append(lax.ppermute(arr[k * row_count : (k + 1) * row_count], BOTH, back))
+            got.append(lax.ppermute(arr[k], BOTH, back))
         return got
 
     def home(parts):
@@ -1145,8 +1153,8 @@
     close(down_half)
     w_down = Gathered(down_way.finish(*now), geo, scal)
     down_got = across(down_half)
-    block_rows, ffn_sums = down_proj(
-        tie(scal), hidden, resid, cot, mod, bias_rows[1:2], w_down, geo
+    *block_rows, ffn_sums = down_proj(
+        tie(scal), hidden, resid, cot, mod, bias_rows[1:2], w_down, images, geo
     )
     close(ffn_sums)
 
@@ -1226,7 +1234,7 @@
     attn_back = begin(attn_parts, scatter_steps, False)
     block_back = [tie(part) for part in block_back]
     down_shard = tie(down_back.finish())
-    latent_back = from_chip(tie(latent_rows))
+    latent_back = from_chip(tie(latent_rows).reshape(images, row_count, width))
     opened.extend(latent_back)
     pack = tie(pack)
     slices = pack.sum(axis=0).reshape(-1)[6 * cols : count]

time: 559 us -> 557 us (level)
  transfers between devices with their start and end apart: 73 -> 73, of which waited for: 32 -> 34; matrix products, arithmetic and copies ran while one was open for 11% -> 10% of each run, Pallas kernels for 39% -> 39%
where the time goes in v8:
time: 557 us; the launch traced here: 551 us
  Pallas kernels  223 us (40%)
  waiting for transfers between devices  129 us (23%)
  starting transfers between devices  117 us (21%)
  other arithmetic  48.4 us (9%)
  local copies, waits for them, and re-layouts  27.4 us (5%)
    ppermute x18, waiting for transfers between devices, flip_tensor(): return lax.ppermute(x, 'tensor', [(i, i ^ k) for i in range(geo.T)])  62.2 us
    pallas_call x6, Pallas kernels, weight_grad(): pl.pallas_call(kernel, grid_spec=pltpu.PrefetchScalarGridSpec(num_scalar_...  59.7 us
    ppermute x24, waiting for transfers between devices, flip_pair(): return lax.ppermute(x, 'fsdp', [(i, i ^ 2 * bit) for i in range(geo.F)])  36.8 us
    ppermute x17, starting transfers between devices, flip_core(): return lax.ppermute(x, 'fsdp', [(i, i ^ 1) for i in range(geo.F)])  32.2 us
    pallas_call x2, Pallas kernels, attn_bwd(): pl.pallas_call(kernel, grid=(z,), in_specs=[spec(wp), spec(geo.kvw), spec...  29.3 us
    ppermute x24, starting transfers between devices, flip_pair(): return lax.ppermute(x, 'fsdp', [(i, i ^ 2 * bit) for i in range(geo.F)])  28.1 us
    ppermute x18, starting transfers between devices, flip_tensor(): return lax.ppermute(x, 'tensor', [(i, i ^ k) for i in range(geo.T)])  26.7 us
    pallas_call x2, Pallas kernels, attn_fwd(): pl.pallas_call(kernel, grid=(z,), in_specs=[spec(wp), spec(geo.kvw), spec...  20.1 us
  transfers between devices with their start and end apart: 73, of which 34 were waited for; matrix products, arithmetic and copies ran while one was open for 10% of the time, Pallas kernels for 39%

profile of v8, /device:TPU:10, one launch (start us, length us, event | category | flops | bytes accessed | tf_op | source)
XLA Modules:
  0.0 550.8 jit_solution(3438501737713018208)
XLA Ops:
  20.6 13.8 %collective-permute-done.1 = bf16[144,1152]{1,0:T(8,128)(2,1)S(1)} collective-permute-done((bf16[144,1152]{1,0:T(8,128)(2,1)S(1)}, bf16[144,1152]{1,0:T(8,128)(2,1)S(1)}, u32[]{:S(2)}, u32[]{:S(2)}) %collective-permute-start.1) | collective-permute-done | bytes 331808 | tf_op jit(solution)/shard_map/ppermute | solution.py:67
  34.4 8.2 %collective-permute-done.2 = bf16[144,1152]{1,0:T(8,128)(2,1)S(1)} collective-permute-done((bf16[144,1152]{1,0:T(8,128)(2,1)S(1)}, bf16[144,1152]{1,0:T(8,128)(2,1)S(1)}, u32[]{:S(2)}, u32[]{:S(2)}) %collective-permute-start.2) | collective-permute-done | bytes 331808 | tf_op jit(solution)/shard_map/ppermute | solution.py:67
  48.4 7.9 %collective-permute-done.5 = bf16[144,1152]{1,0:T(8,128)(2,1)} collective-permute-done((bf16[144,1152]{1,0:T(8,128)(2,1)}, bf16[144,1152]{1,0:T(8,128)(2,1)}, u32[]{:S(2)}, u32[]{:S(2)}) %collective-permute-start.5) | collective-permute-done | bytes 331808 | tf_op jit(solution)/shard_map/ppermute | solution.py:67
  70.7 11.1 %collective-permute-start.10 = (bf16[2,2,144,1152]{3,2,1,0:T(8,128)(2,1)S(1)}, bf16[2,2,144,1152]{3,2,1,0:T(8,128)(2,1)}, u32[]{:S(2)}, u32[]{:S(2)}) collective-permute-start(bf16[2,2,144,1152]{3,2,1,0:T(8,128)(2,1)S(1)} %pad_maximum_fusion.2.refs_0_.refs_1_.refs_2_), channel_id=1, source_target_pairs={{0,4},{4,0},{8,12},{12,8},{16,20},{20,16},{24,28},{28,24},{1,5},{5... | collective-permute-start | bytes 3981320 | tf_op jit(solution)/shard_map/ppermute | solution.py:63
  149.4 9.8 %attn_fwd.3 = (bf16[2,512,384]{2,1,0:T(8,128)(2,1)}, f32[2,4,512]{2,1,0:T(4,128)}) custom-call(bf16[2,512,384]{2,1,0:T(8,128)(2,1)} %get-tuple-element.251.q_ref, bf16[2,512,640]{2,1,0:T(8,128)(2,1)} %get-tuple-element.182.kv_ref, bf16[2,512,640]{2,1,0:T(8,128)(2,1)} %copy-done.51), custom_call_target="tpu_custom_call" | custom-call | flops 6000000000 | bytes 3932160 | tf_op jit(solution)/shard_map/attn_fwd/pallas_call | solution.py:401
  159.2 10.3 %attn_fwd.2 = (bf16[2,512,384]{2,1,0:T(8,128)(2,1)}, f32[2,4,512]{2,1,0:T(4,128)}) custom-call(bf16[2,512,384]{2,1,0:T(8,128)(2,1)} %get-tuple-element.248.q_ref, bf16[2,512,640]{2,1,0:T(8,128)(2,1)} %get-tuple-element.180.kv_ref, bf16[2,512,640]{2,1,0:T(8,128)(2,1)} %copy-done.50), custom_call_target="tpu_custom_call" | custom-call | flops 6000000000 | bytes 3932160 | tf_op jit(solution)/shard_map/attn_fwd/pallas_call | solution.py:401
  183.0 11.2 %out_proj.1 = (bf16[544,1152]{1,0:T(8,128)(2,1)}, f32[512,1152]{1,0:T(8,128)}, bf16[544,1152]{1,0:T(8,128)(2,1)}) custom-call(s32[3]{0:T(128)} %pad_add_fusion.1.s, bf16[2,512,384]{2,1,0:T(8,128)(2,1)} %get-tuple-element.195.ya_ref.o_ref.refs_6_, bf16[2,512,384]{2,1,0:T(8,128)(2,1)} %get-tuple-element.196.yb_ref.o_ref.refs_7_, f32[6,1152]{1,0:T(8,128)} %reshape.196.m_ref, ...), custom_call_target="tpu_custom_call" | custom-call | flops 1358954496 | bytes 18874368 | tf_op jit(solution)/shard_map/out_proj/pallas_call | solution.py:525
  213.0 15.5 %up_proj.1 = (bf16[4,512,1152]{2,1,0:T(8,128)(2,1)}, bf16[4,512,1152]{2,1,0:T(8,128)(2,1)}) custom-call(s32[3]{0:T(128)} %pad_add_fusion.1.s, bf16[544,1152]{1,0:T(8,128)(2,1)} %get-tuple-element.197.h_ref.refs_0_, f32[4,1,1152]{2,1,0:T(1,128)} %maximum_convert_fusion.b_ref, bf16[4,2,144,1152]{3,2,1,0:T(8,128)(2,1)} %copy-done.5, ...), custom_call_target="tpu_custom_call" | custom-call | flops 5435817984 | bytes 20054016 | tf_op jit(solution)/shard_map/up_proj/pallas_call | solution.py:574
  239.4 8.4 %w_down_send.1 = bf16[4,4,144,1152]{3,2,1,0:T(8,128)(2,1)} custom-call(s32[3]{0:T(128)} %pad_add_fusion.1.s, bf16[512,1152]{1,0:T(8,128)(2,1)} %multiply_convert_fusion.refs_0_.g_ref, bf16[4,512,1152]{2,1,0:T(8,128)(2,1)} %get-tuple-element.204.refs_1_.y_ref), custom_call_target="tpu_custom_call" | custom-call | flops 2717908992 | bytes 15335424 | tf_op jit(solution)/shard_map/w_down_send/pallas_call | solution.py:960
  248.3 14.2 %down_proj.1 = (bf16[256,1152]{1,0:T(8,128)(2,1)}, bf16[256,1152]{1,0:T(8,128)(2,1)}, f32[8,1152]{1,0:T(8,128)}) custom-call(s32[3]{0:T(128)} %pad_add_fusion.1.s, bf16[4,512,1152]{2,1,0:T(8,128)(2,1)} %get-tuple-element.204.refs_1_.y_ref, f32[6,1152]{1,0:T(8,128)} %reshape.196.m_ref, f32[1,1152]{1,0:T(1,128)} %get-tuple-element.395.b_ref, ...), custom_call_target="tpu_custom_call" | custom-call | flops 5435817984 | bytes 20054016 | tf_op jit(solution)/shard_map/down_proj/pallas_call | solution.py:634
  262.5 10.1 %w_down.1 = (bf16[2,2,144,1152]{3,2,1,0:T(8,128)(2,1)}, bf16[2,2,144,1152]{3,2,1,0:T(8,128)(2,1)}, bf16[2,2,144,1152]{3,2,1,0:T(8,128)(2,1)}, bf16[2,2,144,1152]{3,2,1,0:T(8,128)(2,1)}) custom-call(s32[3]{0:T(128)} %pad_add_fusion.1.s, bf16[512,1152]{1,0:T(8,128)(2,1)} %multiply_convert_fusion.refs_0_.g_ref, ...), custom_call_target="tpu_custom_call" | custom-call | flops 2717908992 | bytes 15335424 | tf_op jit(solution)/shard_map/w_down/pallas_call | solution.py:960
  280.1 13.6 %pre_back.1 = (bf16[4,512,1152]{2,1,0:T(8,128)(2,1)}, f32[4,1,1152]{2,1,0:T(1,128)}) custom-call(s32[3]{0:T(128)} %pad_add_fusion.1.s, bf16[512,1152]{1,0:T(8,128)(2,1)} %multiply_convert_fusion.refs_0_.g_ref, bf16[4,512,1152]{2,1,0:T(8,128)(2,1)} %get-tuple-element.229.gp_ref, bf16[2,2,144,1152]{3,2,1,0:T(8,128)(2,1)} %pad_maximum_fusion.6.refs_2_.refs_0_, ...), custom_call_target="tpu_custom_call" | custom-call | flops 5435817984 | bytes 20054016 | tf_op jit(solution)/shard_map/pre_back/pallas_call | solution.py:674
  293.7 8.4 %w_up_send.1 = bf16[4,4,144,1152]{3,2,1,0:T(8,128)(2,1)} custom-call(s32[3]{0:T(128)} %pad_add_fusion.1.s, bf16[544,1152]{1,0:T(8,128)(2,1)} %get-tuple-element.197.h_ref.refs_0_, bf16[4,512,1152]{2,1,0:T(8,128)(2,1)} %get-tuple-element.230.refs_1_.y_ref), custom_call_target="tpu_custom_call" | custom-call | flops 2717908992 | bytes 15335424 | tf_op jit(solution)/shard_map/w_up_send/pallas_call | solution.py:960
  309.3 16.9 %second_back.1 = (f32[512,1152]{1,0:T(8,128)}, bf16[512,1152]{1,0:T(8,128)(2,1)}, f32[4,8,1152]{2,1,0:T(8,128)}) custom-call(s32[3]{0:T(128)} %pad_add_fusion.1.s, bf16[4,512,1152]{2,1,0:T(8,128)(2,1)} %get-tuple-element.230.refs_1_.y_ref, f32[6,1152]{1,0:T(8,128)} %reshape.196.m_ref, f32[512,1152]{1,0:T(8,128)} %get-tuple-element.209.refs_0_, ...), custom_call_target="tpu_custom_call" | custom-call | flops 5435817984 | bytes 25952256 | tf_op jit(solution)/shard_map/second_back/pallas_call | solution.py:735
  333.2 8.0 %mixed_back.1.do_ref = bf16[4,512,384]{2,1,0:T(8,128)(2,1)} custom-call(s32[3]{0:T(128)} %pad_add_fusion.1.s, bf16[512,1152]{1,0:T(8,128)(2,1)} %get-tuple-element.237.g_ref.refs_1_, bf16[2,2,144,1152]{3,2,1,0:T(8,128)(2,1)} %copy-done.2, bf16[2,2,144,1152]{3,2,1,0:T(8,128)(2,1)} %collective-permute-done.11.refs_1_.refs_2_.refs_3_, ...), custom_call_target="tpu_custom_call" | custom-call | flops 1358954496 | bytes 12976128 | tf_op jit(solution)/shard_map/mixed_back/pallas_call | solution.py:770
  341.2 10.0 %w_up.1 = (bf16[2,2,144,1152]{3,2,1,0:T(8,128)(2,1)}, bf16[2,2,144,1152]{3,2,1,0:T(8,128)(2,1)}, bf16[2,2,144,1152]{3,2,1,0:T(8,128)(2,1)}, bf16[2,2,144,1152]{3,2,1,0:T(8,128)(2,1)}) custom-call(s32[3]{0:T(128)} %pad_add_fusion.1.s, bf16[544,1152]{1,0:T(8,128)(2,1)} %get-tuple-element.197.h_ref.refs_0_, ...), custom_call_target="tpu_custom_call" | custom-call | flops 2717908992 | bytes 15335424 | tf_op jit(solution)/shard_map/w_up/pallas_call | solution.py:960
  353.1 14.7 %attn_bwd.3 = (bf16[2,512,896]{2,1,0:T(8,128)(2,1)}, bf16[2,512,640]{2,1,0:T(8,128)(2,1)}, f32[2,1,896]{2,1,0:T(1,128)}, f32[2,1,640]{2,1,0:T(1,128)}) custom-call(bf16[2,512,384]{2,1,0:T(8,128)(2,1)} %get-tuple-element.251.q_ref, bf16[2,512,640]{2,1,0:T(8,128)(2,1)} %get-tuple-element.182.kv_ref, bf16[2,512,640]{2,1,0:T(8,128)(2,1)} %copy-done.51, ...), custom_call_target="tpu_custom_call" | custom-call | flops 10000000000 | bytes 6291456 | tf_op jit(solution)/shard_map/attn_bwd/pallas_call | solution.py:455
  367.8 14.7 %attn_bwd.2 = (bf16[2,512,896]{2,1,0:T(8,128)(2,1)}, bf16[2,512,640]{2,1,0:T(8,128)(2,1)}, f32[2,1,896]{2,1,0:T(1,128)}, f32[2,1,640]{2,1,0:T(1,128)}) custom-call(bf16[2,512,384]{2,1,0:T(8,128)(2,1)} %get-tuple-element.248.q_ref, bf16[2,512,640]{2,1,0:T(8,128)(2,1)} %get-tuple-element.180.kv_ref, bf16[2,512,640]{2,1,0:T(8,128)(2,1)} %copy-done.50, ...), custom_call_target="tpu_custom_call" | custom-call | flops 10000000000 | bytes 6291456 | tf_op jit(solution)/shard_map/attn_bwd/pallas_call | solution.py:455
  392.3 11.1 %w_attn_send.1 = bf16[4,4,144,1152]{3,2,1,0:T(8,128)(2,1)} custom-call(s32[3]{0:T(128)} %pad_add_fusion.1.s, bf16[512,1152]{1,0:T(8,128)(2,1)} %norm_mod.1.h_ref.refs_0_, bf16[512,1152]{1,0:T(8,128)(2,1)} %get-tuple-element.237.g_ref.refs_1_, bf16[2,512,896]{2,1,0:T(8,128)(2,1)} %get-tuple-element.260.refs_2_.ta, ...), custom_call_target="tpu_custom_call" | custom-call | flops 2717908992 | bytes 15335424 | tf_op jit(solution)/shard_map/w_attn_send/pallas_call | solution.py:960
  417.0 15.2 %first_back.1 = (bf16[512,1152]{1,0:T(8,128)(2,1)}, f32[2,8,1152]{2,1,0:T(8,128)}) custom-call(s32[3]{0:T(128)} %pad_add_fusion.1.s, bf16[2,512,896]{2,1,0:T(8,128)(2,1)} %get-tuple-element.260.refs_2_.ta, bf16[2,512,896]{2,1,0:T(8,128)(2,1)} %get-tuple-element.261.refs_3_.tb, bf16[2,512,640]{2,1,0:T(8,128)(2,1)} %collective-permute-done.53.refs_4_.ga, ...), custom_call_target="tpu_custom_call" | custom-call | flops 4076863488 | bytes 20054016 | tf_op jit(solution)/shard_map/first_back/pallas_call | solution.py:831
  443.6 11.6 %w_attn.1 = (bf16[2,2,144,1152]{3,2,1,0:T(8,128)(2,1)}, bf16[2,2,144,1152]{3,2,1,0:T(8,128)(2,1)}, bf16[2,2,144,1152]{3,2,1,0:T(8,128)(2,1)}, bf16[2,2,144,1152]{3,2,1,0:T(8,128)(2,1)}) custom-call(s32[3]{0:T(128)} %pad_add_fusion.1.s, bf16[512,1152]{1,0:T(8,128)(2,1)} %norm_mod.1.h_ref.refs_0_, bf16[512,1152]{1,0:T(8,128)(2,1)} %get-tuple-element.237.g_ref.refs_1_, ...), custom_call_target="tpu_custom_call" | custom-call | flops 2717908992 | bytes 15335424 | tf_op jit(solution)/shard_map/w_attn/pallas_call | solution.py:960
  475.6 15.0 %all-to-all-done.2 = f32[32,8,128]{2,1,0:T(8,128)S(1)} async-done(((f32[32,8,128]{2,1,0:T(8,128)}), f32[32,8,128]{2,1,0:T(8,128)S(1)}, u32[]{:S(2)}, u32[]{:S(2)}) %all-to-all-start.2) | async-done | bytes 131104 | tf_op jit(solution)/shard_map/all_to_all | solution.py:1250
  524.6 14.4 %collective-permute-done.68 = bf16[144,1152]{1,0:T(8,128)(2,1)S(1)} collective-permute-done((bf16[144,1152]{1,0:T(8,128)(2,1)S(1)}, bf16[144,1152]{1,0:T(8,128)(2,1)S(1)}, u32[]{:S(2)}, u32[]{:S(2)}) %collective-permute-start.68) | collective-permute-done | bytes 331808 | tf_op jit(solution)/shard_map/ppermute | solution.py:67
  539.1 9.2 %collective-permute-done.69 = bf16[144,1152]{1,0:T(8,128)(2,1)S(1)} collective-permute-done((bf16[144,1152]{1,0:T(8,128)(2,1)S(1)}, bf16[144,1152]{1,0:T(8,128)(2,1)S(1)}, u32[]{:S(2)}, u32[]{:S(2)}) %collective-permute-start.69) | collective-permute-done | bytes 331808 | tf_op jit(solution)/shard_map/ppermute | solution.py:67
  (401 shorter events, 265.3 us)
Async XLA Ops:
  4.8 29.6 %collective-permute-start.1 = (bf16[144,1152]{1,0:T(8,128)(2,1)S(1)}, bf16[144,1152]{1,0:T(8,128)(2,1)S(1)}, u32[]{:S(2)}, u32[]{:S(2)}) collective-permute-start(bf16[144,1152]{1,0:T(8,128)(2,1)S(1)} %concatenate.86), channel_id=1, source_target_pairs={{0,2},{1,3},{2,0},{3,1},{4,6},{5,7},{6,4},{7,5},{8,10},{9,11},{10,... | collective-permute-start | bytes 995336 | tf_op jit(solution)/shard_map/ppermute | solution.py:67
  7.9 34.7 %collective-permute-start.2 = (bf16[144,1152]{1,0:T(8,128)(2,1)S(1)}, bf16[144,1152]{1,0:T(8,128)(2,1)S(1)}, u32[]{:S(2)}, u32[]{:S(2)}) collective-permute-start(bf16[144,1152]{1,0:T(8,128)(2,1)S(1)} %concatenate.86), channel_id=1, source_target_pairs={{0,3},{1,2},{2,1},{3,0},{4,7},{5,6},{6,5},{7,4},{8,11},{9,10},{10,... | collective-permute-start | bytes 995336 | tf_op jit(solution)/shard_map/ppermute | solution.py:67
  13.6 34.0 %all-to-all-start = ((f32[32,8,288]{2,1,0:T(8,128)}), f32[32,8,288]{2,1,0:T(8,128)S(1)}, u32[]{:S(2)}, u32[]{:S(2)}) async-start(f32[32,8,288]{2,1,0:T(8,128)} %bitcast.17), calls=%async_computation | async-start | bytes 786432 | tf_op jit(solution)/shard_map/all_to_all | solution.py:1089
  60.4 28.0 %collective-permute-start.12 = (bf16[2,2,144,1152]{3,2,1,0:T(8,128)(2,1)S(1)}, bf16[2,2,144,1152]{3,2,1,0:T(8,128)(2,1)}, u32[]{:S(2)}, u32[]{:S(2)}) collective-permute-start(bf16[2,2,144,1152]{3,2,1,0:T(8,128)(2,1)S(1)} %pad_maximum_fusion.3.refs_0_.refs_5_.refs_4_.refs_6_), channel_id=1, source_target_pairs={{0,8},{4,12},{8,0},{12,4},{16,24},{20,28},{24,16},{28,20},{1,9},{5... | collective-permute-start | bytes 3981320 | tf_op jit(solution)/shard_map/ppermute | solution.py:59
  63.2 27.3 %collective-permute-start.11 = (bf16[2,2,144,1152]{3,2,1,0:T(8,128)(2,1)S(1)}, bf16[2,2,144,1152]{3,2,1,0:T(8,128)(2,1)}, u32[]{:S(2)}, u32[]{:S(2)}) collective-permute-start(bf16[2,2,144,1152]{3,2,1,0:T(8,128)(2,1)S(1)} %pad_maximum_fusion.2.refs_0_.refs_1_.refs_2_), channel_id=1, source_target_pairs={{0,16},{4,20},{8,24},{12,28},{16,0},{20,4},{24,8},{28,12},{1,17},{... | collective-permute-start | bytes 3981320 | tf_op jit(solution)/shard_map/ppermute | solution.py:59
  68.5 46.9 %collective-permute-start.16 = (bf16[2,2,144,1152]{3,2,1,0:T(8,128)(2,1)S(1)}, bf16[2,2,144,1152]{3,2,1,0:T(8,128)(2,1)}, u32[]{:S(2)}, u32[]{:S(2)}) collective-permute-start(bf16[2,2,144,1152]{3,2,1,0:T(8,128)(2,1)S(1)} %pad_maximum_fusion.3.refs_0_.refs_5_.refs_4_.refs_6_), channel_id=1, source_target_pairs={{0,4},{4,0},{8,12},{12,8},{16,20},{20,16},{24,28},{28,24},{1,5},{5... | collective-permute-start | bytes 3981320 | tf_op jit(solution)/shard_map/ppermute | solution.py:63
  70.7 44.6 %collective-permute-start.10 = (bf16[2,2,144,1152]{3,2,1,0:T(8,128)(2,1)S(1)}, bf16[2,2,144,1152]{3,2,1,0:T(8,128)(2,1)}, u32[]{:S(2)}, u32[]{:S(2)}) collective-permute-start(bf16[2,2,144,1152]{3,2,1,0:T(8,128)(2,1)S(1)} %pad_maximum_fusion.2.refs_0_.refs_1_.refs_2_), channel_id=1, source_target_pairs={{0,4},{4,0},{8,12},{12,8},{16,20},{20,16},{24,28},{28,24},{1,5},{5... | collective-permute-start | bytes 3981320 | tf_op jit(solution)/shard_map/ppermute | solution.py:63
  143.3 31.2 %collective-permute-start.27 = (bf16[2,2,144,1152]{3,2,1,0:T(8,128)(2,1)S(1)}, bf16[2,2,144,1152]{3,2,1,0:T(8,128)(2,1)S(1)}, u32[]{:S(2)}, u32[]{:S(2)}) collective-permute-start(bf16[2,2,144,1152]{3,2,1,0:T(8,128)(2,1)S(1)} %pad_maximum_fusion.5), channel_id=1, source_target_pairs={{0,8},{4,12},{8,0},{12,4},{16,24},{20,28},{24,16},{28,20},{1,9},{5... | collective-permute-start | bytes 3981320 | tf_op jit(solution)/shard_map/ppermute | solution.py:59
  144.1 31.0 %collective-permute-start.26 = (bf16[2,2,144,1152]{3,2,1,0:T(8,128)(2,1)S(1)}, bf16[2,2,144,1152]{3,2,1,0:T(8,128)(2,1)S(1)}, u32[]{:S(2)}, u32[]{:S(2)}) collective-permute-start(bf16[2,2,144,1152]{3,2,1,0:T(8,128)(2,1)S(1)} %pad_maximum_fusion.4), channel_id=1, source_target_pairs={{0,16},{4,20},{8,24},{12,28},{16,0},{20,4},{24,8},{28,12},{1,17},{... | collective-permute-start | bytes 3981320 | tf_op jit(solution)/shard_map/ppermute | solution.py:59
  201.0 30.4 %collective-permute-start.34 = (bf16[2,2,144,1152]{3,2,1,0:T(8,128)(2,1)}, bf16[2,2,144,1152]{3,2,1,0:T(8,128)(2,1)}, u32[]{:S(2)}, u32[]{:S(2)}) collective-permute-start(bf16[2,2,144,1152]{3,2,1,0:T(8,128)(2,1)} %pad_maximum_fusion.7.refs_6_.refs_4_), channel_id=1, source_target_pairs={{0,8},{4,12},{8,0},{12,4},{16,24},{20,28},{24,16},{28,20},{1,9},{5... | collective-permute-start | bytes 3981320 | tf_op jit(solution)/shard_map/ppermute | solution.py:59
  204.5 30.2 %collective-permute-start.33 = (bf16[2,2,144,1152]{3,2,1,0:T(8,128)(2,1)}, bf16[2,2,144,1152]{3,2,1,0:T(8,128)(2,1)}, u32[]{:S(2)}, u32[]{:S(2)}) collective-permute-start(bf16[2,2,144,1152]{3,2,1,0:T(8,128)(2,1)} %pad_maximum_fusion.6.refs_2_.refs_0_), channel_id=1, source_target_pairs={{0,16},{4,20},{8,24},{12,28},{16,0},{20,4},{24,8},{28,12},{1,17},{... | collective-permute-start | bytes 3981320 | tf_op jit(solution)/shard_map/ppermute | solution.py:59
  209.6 38.2 %collective-permute-start.38 = (bf16[2,2,144,1152]{3,2,1,0:T(8,128)(2,1)}, bf16[2,2,144,1152]{3,2,1,0:T(8,128)(2,1)}, u32[]{:S(2)}, u32[]{:S(2)}) collective-permute-start(bf16[2,2,144,1152]{3,2,1,0:T(8,128)(2,1)} %pad_maximum_fusion.7.refs_6_.refs_4_), channel_id=1, source_target_pairs={{0,4},{4,0},{8,12},{12,8},{16,20},{20,16},{24,28},{28,24},{1,5},{5... | collective-permute-start | bytes 3981320 | tf_op jit(solution)/shard_map/ppermute | solution.py:63
  272.6 31.3 %collective-permute-start.42 = (bf16[2,2,144,1152]{3,2,1,0:T(8,128)(2,1)}, bf16[2,2,144,1152]{3,2,1,0:T(8,128)(2,1)S(1)}, u32[]{:S(2)}, u32[]{:S(2)}) collective-permute-start(bf16[2,2,144,1152]{3,2,1,0:T(8,128)(2,1)} %get-tuple-element.225), channel_id=1, source_target_pairs={{0,16},{4,20},{8,24},{12,28},{16,0},{20,4},{24,8},{28,12},{1,17},{... | collective-permute-start | bytes 3981320 | tf_op jit(solution)/shard_map/ppermute | solution.py:59
  273.3 31.1 %collective-permute-start.43 = (bf16[2,2,144,1152]{3,2,1,0:T(8,128)(2,1)}, bf16[2,2,144,1152]{3,2,1,0:T(8,128)(2,1)}, u32[]{:S(2)}, u32[]{:S(2)}) collective-permute-start(bf16[2,2,144,1152]{3,2,1,0:T(8,128)(2,1)} %get-tuple-element.226), channel_id=1, source_target_pairs={{0,8},{4,12},{8,0},{12,4},{16,24},{20,28},{24,16},{28,20},{1,9},{5... | collective-permute-start | bytes 3981320 | tf_op jit(solution)/shard_map/ppermute | solution.py:59
  274.1 28.0 %collective-permute-start.41 = (bf16[256,1152]{1,0:T(8,128)(2,1)}, bf16[256,1152]{1,0:T(8,128)(2,1)}, u32[]{:S(2)}, u32[]{:S(2)}) collective-permute-start(bf16[256,1152]{1,0:T(8,128)(2,1)} %get-tuple-element.223), channel_id=1, source_target_pairs={{0,0},{1,1},{4,2},{5,3},{2,4},{3,5},{6,6},{7,7},{8,8},{9,9},{12,10... | collective-permute-start | bytes 1769480 | tf_op jit(solution)/shard_map/ppermute | solution.py:1034
  331.8 50.6 %collective-permute-start.52 = (bf16[144,1152]{1,0:T(8,128)(2,1)}, bf16[144,1152]{1,0:T(8,128)(2,1)S(1)}, u32[]{:S(2)}, u32[]{:S(2)}) collective-permute-start(bf16[144,1152]{1,0:T(8,128)(2,1)} %get-tuple-element.376), channel_id=1, source_target_pairs={{0,2},{1,3},{2,0},{3,1},{4,6},{5,7},{6,4},{7,5},{8,10},{9,11},{10,... | collective-permute-start | bytes 995336 | tf_op jit(solution)/shard_map/ppermute | solution.py:67
  351.3 31.2 %collective-permute-start.50 = (bf16[2,2,144,1152]{3,2,1,0:T(8,128)(2,1)}, bf16[2,2,144,1152]{3,2,1,0:T(8,128)(2,1)S(1)}, u32[]{:S(2)}, u32[]{:S(2)}) collective-permute-start(bf16[2,2,144,1152]{3,2,1,0:T(8,128)(2,1)} %get-tuple-element.246), channel_id=1, source_target_pairs={{0,16},{4,20},{8,24},{12,28},{16,0},{20,4},{24,8},{28,12},{1,17},{... | collective-permute-start | bytes 3981320 | tf_op jit(solution)/shard_map/ppermute | solution.py:59
  352.1 30.4 %collective-permute-start.51 = (bf16[2,2,144,1152]{3,2,1,0:T(8,128)(2,1)}, bf16[2,2,144,1152]{3,2,1,0:T(8,128)(2,1)S(1)}, u32[]{:S(2)}, u32[]{:S(2)}) collective-permute-start(bf16[2,2,144,1152]{3,2,1,0:T(8,128)(2,1)} %get-tuple-element.247), channel_id=1, source_target_pairs={{0,8},{4,12},{8,0},{12,4},{16,24},{20,28},{24,16},{28,20},{1,9},{5... | collective-permute-start | bytes 3981320 | tf_op jit(solution)/shard_map/ppermute | solution.py:59
  408.2 27.1 %collective-permute-start.60 = (bf16[4,4,144,1152]{3,2,1,0:T(8,128)(2,1)}, bf16[4,4,144,1152]{3,2,1,0:T(8,128)(2,1)}, u32[]{:S(2)}, u32[]{:S(2)}) collective-permute-start(bf16[4,4,144,1152]{3,2,1,0:T(8,128)(2,1)} %w_attn_send.1), channel_id=1, source_target_pairs={{0,4},{4,0},{8,12},{12,8},{16,20},{20,16},{24,28},{28,24},{1,5},{5... | collective-permute-start | bytes 15925256 | tf_op jit(solution)/shard_map/ppermute | solution.py:63
  456.8 36.1 %collective-permute-start.63 = (bf16[2,2,144,1152]{3,2,1,0:T(8,128)(2,1)}, bf16[2,2,144,1152]{3,2,1,0:T(8,128)(2,1)}, u32[]{:S(2)}, u32[]{:S(2)}) collective-permute-start(bf16[2,2,144,1152]{3,2,1,0:T(8,128)(2,1)} %get-tuple-element.285), channel_id=1, source_target_pairs={{0,16},{4,20},{8,24},{12,28},{16,0},{20,4},{24,8},{28,12},{1,17},{... | collective-permute-start | bytes 3981320 | tf_op jit(solution)/shard_map/ppermute | solution.py:59
  457.8 35.2 %collective-permute-start.64 = (bf16[2,2,144,1152]{3,2,1,0:T(8,128)(2,1)}, bf16[2,2,144,1152]{3,2,1,0:T(8,128)(2,1)}, u32[]{:S(2)}, u32[]{:S(2)}) collective-permute-start(bf16[2,2,144,1152]{3,2,1,0:T(8,128)(2,1)} %get-tuple-element.286), channel_id=1, source_target_pairs={{0,8},{4,12},{8,0},{12,4},{16,24},{20,28},{24,16},{28,20},{1,9},{5... | collective-permute-start | bytes 3981320 | tf_op jit(solution)/shard_map/ppermute | solution.py:59
  461.5 29.1 %all-to-all-start.2 = ((f32[32,8,128]{2,1,0:T(8,128)}), f32[32,8,128]{2,1,0:T(8,128)S(1)}, u32[]{:S(2)}, u32[]{:S(2)}) async-start(f32[32,8,128]{2,1,0:T(8,128)} %bitcast.74), calls=%async_computation.2 | async-start | bytes 262144 | tf_op jit(solution)/shard_map/all_to_all | solution.py:1250
  519.4 28.8 %collective-permute-start.69 = (bf16[144,1152]{1,0:T(8,128)(2,1)S(1)}, bf16[144,1152]{1,0:T(8,128)(2,1)S(1)}, u32[]{:S(2)}, u32[]{:S(2)}) collective-permute-start(bf16[144,1152]{1,0:T(8,128)(2,1)S(1)} %get-tuple-element.372), channel_id=1, source_target_pairs={{0,3},{1,2},{2,1},{3,0},{4,7},{5,6},{6,5},{7,4},{8,11},{9,10},{10,... | collective-permute-start | bytes 995336 | tf_op jit(solution)/shard_map/ppermute | solution.py:67
  521.7 26.6 %collective-permute-start.67 = (bf16[144,1152]{1,0:T(8,128)(2,1)S(1)}, bf16[144,1152]{1,0:T(8,128)(2,1)S(1)}, u32[]{:S(2)}, u32[]{:S(2)}) collective-permute-start(bf16[144,1152]{1,0:T(8,128)(2,1)S(1)} %slice_bitcast_fusion.4), channel_id=1, source_target_pairs={{0,1},{1,0},{2,3},{3,2},{4,5},{5,4},{6,7},{7,6},{8,9},{9,8},{10,11... | collective-permute-start | bytes 995336 | tf_op jit(solution)/shard_map/ppermute | solution.py:67
  (102 other events, 1346.5 us)
